TPU v7x, 32 devices: a whole 2x2x4 slice. The times are simulated.
32 devices in a mesh: dp: 8 (over z, core), ctx: 4 (over y, x).
Axes of the slice: x: 2, y: 2, z: 4, core: 2. Of those that a mesh axis runs over, the one named last changes fastest.
Arguments:
- inputs: bfloat16 [8, 1024, 2048], P('dp', 'ctx'), may hold values from -6 to 6
- segments: int32 [8, 1024], P('dp'), may hold values from 0 to 3, never falling along the last dimension, each value on 1 to 512 neighbouring positions
- ln1_gain: bfloat16 [2048], P(('dp', 'ctx')), may hold values from 0.5 to 1.5
- ln1_bias: bfloat16 [2048], P(('dp', 'ctx')), may hold values from -1.5 to 1.5
- qkv_weight: bfloat16 [2048, 6144], P(('dp', 'ctx')), may hold values from -0.125 to 0.125
- qkv_bias: bfloat16 [6144], P(('dp', 'ctx')), may hold values from -2.5 to 2.5
- out_weight: bfloat16 [2048, 2048], P(('dp', 'ctx')), may hold values from -0.5 to 0.5
- ln2_gain: bfloat16 [2048], P(('dp', 'ctx')), may hold values from 0.5 to 1.5
- ln2_bias: bfloat16 [2048], P(('dp', 'ctx')), may hold values from -1.5 to 1.5
- gate_weight: bfloat16 [2048, 5632], P('dp', 'ctx'), may hold values from -0.125 to 0.125
- up_weight: bfloat16 [2048, 5632], P('dp', 'ctx'), may hold values from -0.125 to 0.125
- down_weight: bfloat16 [5632, 2048], P('ctx', 'dp'), may hold values from -0.078125 to 0.078125
- cotangent: bfloat16 [8, 1024, 2048], P('dp', 'ctx'), may hold values from -6 to 6
Outputs:
- output: bfloat16 [8, 1024, 2048], P('dp', 'ctx')
- grad_inputs: float32 [8, 1024, 2048], P('dp', 'ctx')
- grad_ln1_gain: float32 [2048], P(('dp', 'ctx'))
- grad_ln1_bias: float32 [2048], P(('dp', 'ctx'))
- grad_qkv_weight: float32 [2048, 6144], P(('dp', 'ctx'))
- grad_qkv_bias: float32 [6144], P(('dp', 'ctx'))
- grad_out_weight: float32 [2048, 2048], P(('dp', 'ctx'))
- grad_ln2_gain: float32 [2048], P(('dp', 'ctx'))
- grad_ln2_bias: float32 [2048], P(('dp', 'ctx'))
- grad_gate_weight: float32 [2048, 5632], P('dp', 'ctx')
- grad_up_weight: float32 [2048, 5632], P('dp', 'ctx')
- grad_down_weight: float32 [5632, 2048], P('ctx', 'dp')
Inputs may be any that keep to these rules, and one draw needn't show every extreme that they name: `segments`: along each sequence the document numbers never fall; each document holds at most 512 tokens, and some document in the draw holds exactly that many.
All inputs are finite; a program needn't handle non-finite values.
Results may differ from a plain program's by a relative error of at most 0.015.
Values may be sent and summed in bfloat16 or wider, within the bound.
A program may use at most 256 MiB of HBM per device.

v0:
```python
import math

import jax
import jax.numpy as jnp
from jax import lax
from jax.sharding import PartitionSpec as P

D = 2048
H = 32
HD = 64
ROT = 16


norm_eps = 1e-05
masked_value = -1e30


def rotary_tables(positions, rot_dims):
    half_rot = rot_dims // 2
    freq_index = jnp.arange(half_rot, dtype=jnp.float32)
    inverse = jnp.power(jnp.float32(10000.0), -(2.0 * freq_index) / rot_dims)
    angles = positions.astype(jnp.float32)[:, None] * inverse[None, :]
    return (jnp.cos(angles), jnp.sin(angles))


def rotate(values, cosine, sine, rot_dims):
    half_rot = rot_dims // 2
    first_part = values[..., :half_rot]
    second_part = values[..., half_rot:rot_dims]
    cos_wide = cosine[:, None, :]
    sin_wide = sine[:, None, :]
    return jnp.concatenate(
        [
            first_part * cos_wide - second_part * sin_wide,
            second_part * cos_wide + first_part * sin_wide,
            values[..., rot_dims:],
        ],
        axis=-1,
    )


def norm_forward(rows, gain, shift):
    row_mean = jnp.mean(rows, axis=-1, keepdims=True)
    centered = rows - row_mean
    variance = jnp.mean(centered * centered, axis=-1, keepdims=True)
    inv_std = lax.rsqrt(variance + norm_eps)
    scaled = centered * inv_std
    return (scaled * gain + shift, scaled, inv_std)


def norm_backward(grad_normed, scaled, inv_std, gain):
    grad_gain = jnp.sum(grad_normed * scaled, axis=0)
    grad_shift = jnp.sum(grad_normed, axis=0)
    inner_grad = grad_normed * gain
    grad_rows = inv_std * (
        inner_grad
        - jnp.mean(inner_grad, axis=-1, keepdims=True)
        - scaled * jnp.mean(inner_grad * scaled, axis=-1, keepdims=True)
    )
    return (grad_rows, grad_gain, grad_shift)


def attention_scores(queries, keys, allowed, scale):
    raw = jnp.einsum("sqhd,skhd->shqk", queries, keys, preferred_element_type=jnp.float32) * scale
    return jnp.where(allowed[:, None], raw, masked_value)


def shards(
    inputs,
    segments,
    ln1_gain,
    ln1_bias,
    qkv_weight,
    qkv_bias,
    out_weight,
    ln2_gain,
    ln2_bias,
    gate_weight,
    up_weight,
    down_weight,
    cotangent,
):
    seq_count = inputs.shape[0]
    local_len = inputs.shape[1]
    full_len = segments.shape[1]
    row_count = seq_count * local_len
    wide_rows = seq_count * full_len
    scale = 1.0 / math.sqrt(HD)
    offset = lax.axis_index("ctx") * local_len
    positions = offset + jnp.arange(local_len, dtype=jnp.int32)
    cosine, sine = rotary_tables(positions, ROT)
    key_index = jnp.arange(full_len, dtype=jnp.int32)
    query_ids = lax.dynamic_slice_in_dim(segments, offset, local_len, 1)
    allowed = (query_ids[:, :, None] == segments[:, None, :]) & (
        positions[None, :, None] >= key_index[None, None, :]
    )
    attn_set = (
        lax.all_gather(ln1_gain, ("dp", "ctx"), axis=0, tiled=True),
        lax.all_gather(ln1_bias, ("dp", "ctx"), axis=0, tiled=True),
        lax.all_gather(qkv_weight, ("dp", "ctx"), axis=0, tiled=True),
        lax.all_gather(qkv_bias, ("dp", "ctx"), axis=0, tiled=True),
        lax.all_gather(out_weight, ("dp", "ctx"), axis=0, tiled=True),
        lax.all_gather(ln2_gain, ("dp", "ctx"), axis=0, tiled=True),
        lax.all_gather(ln2_bias, ("dp", "ctx"), axis=0, tiled=True),
    )
    gain_one, shift_one, joined_full, joined_shift, out_full, gain_two, shift_two = attn_set
    rows = inputs.reshape(row_count, D).astype(jnp.float32)
    normed_one, scaled_one, inv_one = norm_forward(rows, gain_one, shift_one)
    normed_one = normed_one.astype(jnp.bfloat16)
    joined = jnp.dot(normed_one, joined_full, preferred_element_type=jnp.float32) + joined_shift
    joined = joined.reshape(seq_count, local_len, 3, H, HD)
    queries = rotate(joined[:, :, 0], cosine, sine, ROT).astype(jnp.bfloat16)
    keys_local = rotate(joined[:, :, 1], cosine, sine, ROT).astype(jnp.bfloat16)
    values_local = joined[:, :, 2].astype(jnp.bfloat16)
    keys, values = (
        lax.all_gather(keys_local, "ctx", axis=1, tiled=True),
        lax.all_gather(values_local, "ctx", axis=1, tiled=True),
    )
    scores = attention_scores(queries, keys, allowed, scale)
    top_score = jnp.max(scores, axis=-1, keepdims=True)
    total = jnp.sum(jnp.exp(scores - top_score), axis=-1, keepdims=True)
    log_total = top_score + jnp.log(total)
    probs = jnp.exp(scores - log_total)
    attended = jnp.einsum(
        "shqk,skhd->sqhd", probs.astype(jnp.bfloat16), values, preferred_element_type=jnp.float32
    )
    attended = attended.reshape(row_count, D).astype(jnp.bfloat16)
    resid = rows + jnp.dot(attended, out_full, preferred_element_type=jnp.float32)
    gate_full, up_full, down_full = (
        lax.all_gather(gate_weight, "dp", axis=0, tiled=True),
        lax.all_gather(up_weight, "dp", axis=0, tiled=True),
        lax.all_gather(down_weight, "dp", axis=1, tiled=True),
    )
    normed_two, scaled_two, inv_two = norm_forward(resid, gain_two, shift_two)
    normed_two = normed_two.astype(jnp.bfloat16).reshape(seq_count, local_len, D)
    normed_wide, grad_wide = (
        lax.all_gather(normed_two, "ctx", axis=1, tiled=True),
        lax.all_gather(cotangent, "ctx", axis=1, tiled=True),
    )
    normed_wide = normed_wide.reshape(wide_rows, D)
    grad_wide = grad_wide.reshape(wide_rows, D)
    gate = jnp.dot(normed_wide, gate_full, preferred_element_type=jnp.float32)
    upward = jnp.dot(normed_wide, up_full, preferred_element_type=jnp.float32)
    sigma = jax.nn.sigmoid(gate)
    swish = gate * sigma
    inner = (swish * upward).astype(jnp.bfloat16)
    partial_out = jnp.dot(inner, down_full, preferred_element_type=jnp.float32).reshape(
        seq_count, full_len, D
    )
    branch_out = (
        lax.psum_scatter(partial_out.astype(jnp.bfloat16), "ctx", scatter_dimension=1, tiled=True)
        .astype(jnp.float32)
        .reshape(row_count, D)
    )
    output = (resid + branch_out).astype(jnp.bfloat16).reshape(seq_count, local_len, D)
    grad_float = cotangent.reshape(row_count, D).astype(jnp.float32)
    d_down = jnp.einsum("rf,rd->fd", inner, grad_wide, preferred_element_type=jnp.float32)
    d_inner = jnp.einsum("rd,fd->rf", grad_wide, down_full, preferred_element_type=jnp.float32)
    d_gate = (d_inner * upward * sigma * (1.0 + gate * (1.0 - sigma))).astype(jnp.bfloat16)
    d_upward = (d_inner * swish).astype(jnp.bfloat16)
    d_gate_weight = jnp.einsum("rd,rf->df", normed_wide, d_gate, preferred_element_type=jnp.float32)
    d_up_weight = jnp.einsum("rd,rf->df", normed_wide, d_upward, preferred_element_type=jnp.float32)
    mlp_grads = (
        lax.psum_scatter(
            d_gate_weight.astype(jnp.bfloat16), "dp", scatter_dimension=0, tiled=True
        ).astype(jnp.float32),
        lax.psum_scatter(
            d_up_weight.astype(jnp.bfloat16), "dp", scatter_dimension=0, tiled=True
        ).astype(jnp.float32),
        lax.psum_scatter(d_down.astype(jnp.bfloat16), "dp", scatter_dimension=1, tiled=True).astype(
            jnp.float32
        ),
    )
    d_normed_part = jnp.einsum(
        "rf,df->rd", d_gate, gate_full, preferred_element_type=jnp.float32
    ) + jnp.einsum("rf,df->rd", d_upward, up_full, preferred_element_type=jnp.float32)
    d_normed_two = (
        lax.psum_scatter(
            d_normed_part.reshape(seq_count, full_len, D).astype(jnp.bfloat16),
            "ctx",
            scatter_dimension=1,
            tiled=True,
        )
        .astype(jnp.float32)
        .reshape(row_count, D)
    )
    d_resid_norm, d_gain_two, d_shift_two = norm_backward(
        d_normed_two, scaled_two, inv_two, gain_two
    )
    d_resid = grad_float + d_resid_norm
    gain_one, shift_one, joined_full, joined_shift, out_full = (
        lax.all_gather(ln1_gain, ("dp", "ctx"), axis=0, tiled=True),
        lax.all_gather(ln1_bias, ("dp", "ctx"), axis=0, tiled=True),
        lax.all_gather(qkv_weight, ("dp", "ctx"), axis=0, tiled=True),
        lax.all_gather(qkv_bias, ("dp", "ctx"), axis=0, tiled=True),
        lax.all_gather(out_weight, ("dp", "ctx"), axis=0, tiled=True),
    )
    d_proj = d_resid.astype(jnp.bfloat16)
    d_out_weight = jnp.einsum("rd,re->de", attended, d_proj, preferred_element_type=jnp.float32)
    d_attended = jnp.einsum(
        "re,de->rd", d_proj, out_full, preferred_element_type=jnp.float32
    ).astype(jnp.bfloat16)
    d_attended = d_attended.reshape(seq_count, local_len, H, HD)
    scores = attention_scores(queries, keys, allowed, scale)
    probs = jnp.exp(scores - log_total)
    d_probs = jnp.einsum("sqhd,skhd->shqk", d_attended, values, preferred_element_type=jnp.float32)
    d_values_all = jnp.einsum(
        "shqk,sqhd->skhd",
        probs.astype(jnp.bfloat16),
        d_attended,
        preferred_element_type=jnp.float32,
    )
    d_scores = (probs * (d_probs - jnp.sum(d_probs * probs, axis=-1, keepdims=True))).astype(
        jnp.bfloat16
    )
    d_queries = (
        jnp.einsum("shqk,skhd->sqhd", d_scores, keys, preferred_element_type=jnp.float32) * scale
    )
    d_keys_all = (
        jnp.einsum("shqk,sqhd->skhd", d_scores, queries, preferred_element_type=jnp.float32) * scale
    )
    d_keys, d_values = (
        lax.psum_scatter(
            d_keys_all.astype(jnp.bfloat16), "ctx", scatter_dimension=1, tiled=True
        ).astype(jnp.float32),
        lax.psum_scatter(
            d_values_all.astype(jnp.bfloat16), "ctx", scatter_dimension=1, tiled=True
        ).astype(jnp.float32),
    )
    d_joined = jnp.stack(
        [rotate(d_queries, cosine, -sine, ROT), rotate(d_keys, cosine, -sine, ROT), d_values],
        axis=2,
    )
    d_joined = d_joined.reshape(row_count, 3 * D).astype(jnp.bfloat16)
    d_joined_weight = jnp.einsum(
        "rd,re->de", normed_one, d_joined, preferred_element_type=jnp.float32
    )
    d_joined_shift = jnp.sum(d_joined.astype(jnp.float32), axis=0)
    d_normed_one = jnp.einsum(
        "re,de->rd", d_joined, joined_full, preferred_element_type=jnp.float32
    )
    d_rows_norm, d_gain_one, d_shift_one = norm_backward(
        d_normed_one, scaled_one, inv_one, gain_one
    )
    grad_input = (d_resid + d_rows_norm).reshape(seq_count, local_len, D)
    attn_grads = (
        lax.psum_scatter(d_gain_one, ("dp", "ctx"), scatter_dimension=0, tiled=True),
        lax.psum_scatter(d_shift_one, ("dp", "ctx"), scatter_dimension=0, tiled=True),
        lax.psum_scatter(d_joined_weight, ("dp", "ctx"), scatter_dimension=0, tiled=True),
        lax.psum_scatter(d_joined_shift, ("dp", "ctx"), scatter_dimension=0, tiled=True),
        lax.psum_scatter(d_out_weight, ("dp", "ctx"), scatter_dimension=0, tiled=True),
        lax.psum_scatter(d_gain_two, ("dp", "ctx"), scatter_dimension=0, tiled=True),
        lax.psum_scatter(d_shift_two, ("dp", "ctx"), scatter_dimension=0, tiled=True),
    )
    return (
        output,
        grad_input,
        attn_grads[0],
        attn_grads[1],
        attn_grads[2],
        attn_grads[3],
        attn_grads[4],
        attn_grads[5],
        attn_grads[6],
        mlp_grads[0],
        mlp_grads[1],
        mlp_grads[2],
    )


def solution(mesh):
    return jax.shard_map(
        shards,
        mesh=mesh,
        in_specs=(
            P("dp", "ctx", None),
            P("dp", None),
            P(("dp", "ctx")),
            P(("dp", "ctx")),
            P(("dp", "ctx"), None),
            P(("dp", "ctx")),
            P(("dp", "ctx"), None),
            P(("dp", "ctx")),
            P(("dp", "ctx")),
            P("dp", "ctx"),
            P("dp", "ctx"),
            P("ctx", "dp"),
            P("dp", "ctx", None),
        ),
        out_specs=(
            P("dp", "ctx", None),
            P("dp", "ctx", None),
            P(("dp", "ctx")),
            P(("dp", "ctx")),
            P(("dp", "ctx"), None),
            P(("dp", "ctx")),
            P(("dp", "ctx"), None),
            P(("dp", "ctx")),
            P(("dp", "ctx")),
            P("dp", "ctx"),
            P("dp", "ctx"),
            P("ctx", "dp"),
        ),
        check_vma=False,
    )
```

profile of v0, /device:TPU:0, one launch (start us, length us, event | category | flops | bytes accessed | tf_op | source)
XLA Modules:
  0.0 2006.6 jit_solution(15457265556357874671)
XLA Ops:
  12.2 43.6 %all-reduce.11 = (bf16[6144]{0:T(1024)(128)(2,1)S(1)}, bf16[2048]{0:T(1024)(128)(2,1)S(1)}, bf16[2048]{0:T(1024)(128)(2,1)S(1)}, bf16[2048]{0:T(1024)(128)(2,1)S(1)}, bf16[2048]{0:T(1024)(128)(2,1)S(1)}) all-reduce(bf16[6144]{0:T(1024)(128)(2,1)S(1)} %dynamic-update-slice.2, ...), channel_id=1, replica_groups=mesh['dp'=8,'ctx'=4] {'dp','ctx'}, use_global_device_ids=true, to_apply=%add.2 | all-reduce | flops 14336 | bytes 57344
  55.9 1.5 convert_reduce_fusion.1
  57.4 1.6 fusion.37
  59.7 110.0 %all-gather.12.cloned.1.call-done = bf16[2048,6144]{1,0:T(8,128)(2,1)} async-done(((bf16[64,6144]{1,0:T(8,128)(2,1)}), bf16[2048,6144]{1,0:T(8,128)(2,1)}) %all-gather.12.cloned.1.call-update) | async-done | bytes 25165840 | tf_op jit(solution)/shard_map/all_gather | solution.py:100
  169.8 13.7 convolution_add_fusion
  183.5 6.5 copy.32
  190.0 2.5 slice_bitcast_fusion.1
  194.0 2.7 slice.109
  198.7 46.2 %all-gather.14.cloned.1.call-done = bf16[1,1024,32,64]{1,3,2,0:T(8,128)(2,1)} async-done(((bf16[1,256,32,64]{1,3,2,0:T(8,128)(2,1)}), bf16[1,1024,32,64]{1,3,2,0:T(8,128)(2,1)}) %all-gather.14.cloned.1.call-update) | async-done | bytes 4194320 | tf_op jit(solution)/shard_map/all_gather | solution.py:116
  244.9 16.8 fusion
  261.7 14.9 exponential_reduce_fusion
  276.6 23.2 %all-gather.26.cloned.1.call-done = bf16[1,1024,1,32,64]{1,4,3,2,0:T(8,128)(2,1)} async-done(((bf16[1,256,1,32,64]{1,4,3,2,0:T(8,128)(2,1)}), bf16[1,1024,1,32,64]{1,4,3,2,0:T(8,128)(2,1)}) %all-gather.26.cloned.1.call-update) | async-done | bytes 4194320 | tf_op jit(solution)/shard_map/all_gather | solution.py:117
  299.9 16.9 fusion.50
  316.8 63.5 %all-gather.16.cloned.1.call-done = bf16[2048,2048]{1,0:T(8,128)(2,1)} async-done(((bf16[64,2048]{1,0:T(8,128)(2,1)}), bf16[2048,2048]{1,0:T(8,128)(2,1)}) %all-gather.16.cloned.1.call-update) | async-done | bytes 8388624 | tf_op jit(solution)/shard_map/all_gather | solution.py:102
  380.2 6.1 fusion.83
  386.8 1.4 add_convert_fusion.1
  390.7 50.1 %all-gather.20.cloned.1.call-done = bf16[2048,1408]{1,0:T(8,128)(2,1)} async-done(((bf16[256,1408]{1,0:T(8,128)(2,1)}), bf16[2048,1408]{1,0:T(8,128)(2,1)}) %all-gather.20.cloned.1.call-update) | async-done | bytes 5767184 | tf_op jit(solution)/shard_map/all_gather | solution.py:131
  440.8 53.7 %all-gather.28.cloned.1.call-done = bf16[1024,2048]{1,0:T(8,128)(2,1)} async-done(((bf16[256,2048]{1,0:T(8,128)(2,1)}), bf16[1024,2048]{1,0:T(8,128)(2,1)}) %all-gather.28.cloned.1.call-update) | async-done | bytes 4194320 | tf_op jit(solution)/shard_map/all_gather | solution.py:137
  494.5 11.7 fusion.85
  506.1 50.4 %all-gather.18.cloned.1.call-done = bf16[2048,1408]{1,0:T(8,128)(2,1)} async-done(((bf16[256,1408]{1,0:T(8,128)(2,1)}), bf16[2048,1408]{1,0:T(8,128)(2,1)}) %all-gather.18.cloned.1.call-update) | async-done | bytes 5767184 | tf_op jit(solution)/shard_map/all_gather | solution.py:130
  556.6 11.6 fusion.84
  568.2 41.6 %all-gather.24.cloned.1.call-done = bf16[1,1024,2048]{2,1,0:T(8,128)(2,1)} async-done(((bf16[1,256,2048]{2,1,0:T(8,128)(2,1)}), bf16[1,1024,2048]{2,1,0:T(8,128)(2,1)}) %all-gather.24.cloned.1.call-update) | async-done | bytes 4194320 | tf_op jit(solution)/shard_map/all_gather | solution.py:138
  609.8 62.5 %all-gather.22.cloned.1.call-done = bf16[1408,2048]{1,0:T(8,128)(2,1)} async-done(((bf16[1408,256]{1,0:T(8,128)(2,1)}), bf16[1408,2048]{1,0:T(8,128)(2,1)}) %all-gather.22.cloned.1.call-update) | async-done | bytes 5767184 | tf_op jit(solution)/shard_map/all_gather | solution.py:132
  672.3 16.6 multiply_convert_fusion.2
  688.9 8.7 fusion.86
  697.6 11.4 fusion.3
  709.1 10.9 convert_bitcast_fusion.1
  720.1 40.0 %reduce-scatter.12.cloned.1.call-done = bf16[1,256,2048]{2,1,0:T(8,128)(2,1)} async-done(((bf16[1,1024,2048]{2,1,0:T(8,128)(2,1)}), bf16[1,256,2048]{2,1,0:T(8,128)(2,1)}) %reduce-scatter.12.cloned.1.call-update) | async-done | bytes 1048592 | tf_op jit(solution)/shard_map/reduce_scatter | solution.py:178
  760.1 2.7 fusion.42
  762.8 53.2 %reduce-scatter.10.cloned.1.call-done = bf16[1,256,2048]{2,1,0:T(8,128)(2,1)} async-done(((bf16[1,1024,2048]{2,1,0:T(8,128)(2,1)}), bf16[1,256,2048]{2,1,0:T(8,128)(2,1)}) %reduce-scatter.10.cloned.1.call-update) | async-done | bytes 1048592 | tf_op jit(solution)/shard_map/reduce_scatter | solution.py:151
  816.0 3.5 fusion.40
  819.6 1.3 copy-done.2
  820.9 5.7 convolution_convert_fusion.3
  827.4 26.5 %multiply_reduce_fusion = (f32[32,256]{1,0:T(8,128)S(1)}, f32[32,256,1024]{2,1,0:T(8,128)}) fusion(f32[32,256,1024]{2,1,0:T(8,128)} %get-tuple-element.54, f32[32,256]{1,0:T(8,128)S(1)} %log_add_fusion, pred[256,1024]{1,0:T(8,128)(4,1)S(1)} %fusion.66, bf16[256,32,64]{0,2,1:T(8,128)(2,1)S(1)} %bitcast.173, ...), kind=kOutput, calls=%fused_computation.1 | convolution fusion | flops 1115676672 | bytes 72679424 | tf_op jit(solution)/shard_map/sqhd,skhd->shqk/dot_general | solution.py:206
  853.8 28.0 %multiply_convert_fusion = bf16[32,256,1024]{2,1,0:T(8,128)(2,1)} fusion(f32[32,256,1024]{2,1,0:T(8,128)} %get-tuple-element.58, f32[32,256,1024]{2,1,0:T(8,128)} %get-tuple-element.54, f32[32,256]{1,0:T(8,128)S(1)} %get-tuple-element.57, f32[32,256]{1,0:T(8,128)S(1)} %log_add_fusion, pred[256,1024]{1,0:T(8,128)(4,1)S(1)} %fusion.66), kind=kLoop, calls=%fused_computation | loop fusion | flops 50331648 | bytes 84213760 | tf_op jit(solution)/shard_map/convert_element_type | solution.py:213
  881.9 10.8 fusion.4
  892.7 17.5 convert_bitcast_fusion
  910.3 1.9 copy-done.26
  912.2 11.0 convolution_convert_fusion
  923.2 1.7 copy-done.29
  925.0 10.8 convolution_convert_fusion.1
  935.9 1.8 copy-done.27
  937.7 10.9 convolution_convert_fusion.2
  949.0 1.1 copy-done.3
  950.4 8.6 fusion.68
  959.1 14.1 multiply_bitcast_fusion
  973.2 1.5 slice.74
  974.7 1.6 convert_element_type.235
  976.3 1.2 multiply_subtract_fusion.1
  979.8 21.6 %reduce-scatter.16.cloned.1.call-done = bf16[1,256,32,64]{1,3,2,0:T(8,128)(2,1)} async-done(((bf16[1,1024,32,64]{1,3,2,0:T(8,128)(2,1)}), bf16[1,256,32,64]{1,3,2,0:T(8,128)(2,1)}) %reduce-scatter.16.cloned.1.call-update) | async-done | bytes 1048592 | tf_op jit(solution)/shard_map/reduce_scatter | solution.py:226
  1001.4 3.7 convert_reduce_fusion
  1005.1 21.9 %fusion.55 = f32[2048,6144]{1,0:T(8,128)} fusion(bf16[256,6144]{0,1:T(8,128)(2,1)} %bitcast.171, bf16[1,256,2048]{2,1,0:T(8,128)(2,1)S(1)} %copy-done.1, f32[2048]{0:T(1024)S(1)} %copy-done.15, f32[2048]{0:T(1024)S(1)} %copy-done.13, f32[256]{0:T(256)S(1)} %copy-done.21, f32[256]{0:T(256)S(1)} %copy-done.19), kind=kOutput, calls=%fused_computation.89 | convolution fusion | flops 6445596672 | bytes 54544384 | tf_op jit(solution)/shard_map/rd,re->de/dot_general | solution.py:235
  1027.1 1.4 convert_reduce_fusion.2
  1028.5 40.0 %reduce-scatter.26.cloned.1.call-done = bf16[1408,256]{1,0:T(8,128)(2,1)} async-done(((bf16[1408,2048]{1,0:T(8,128)(2,1)}), bf16[1408,256]{1,0:T(8,128)(2,1)}) %reduce-scatter.26.cloned.1.call-update) | async-done | bytes 720912 | tf_op jit(solution)/shard_map/reduce_scatter | solution.py:170
  1068.5 2.3 convert_element_type.249
  1070.8 63.1 %reduce-scatter.24.cloned.1.call-done = bf16[256,1408]{1,0:T(8,128)(2,1)} async-done(((bf16[2048,1408]{1,0:T(8,128)(2,1)}), bf16[256,1408]{1,0:T(8,128)(2,1)}) %reduce-scatter.24.cloned.1.call-update) | async-done | bytes 720912 | tf_op jit(solution)/shard_map/reduce_scatter | solution.py:167
  1133.9 2.3 convert_element_type.247
  1136.2 63.1 %reduce-scatter.22.cloned.1.call-done = bf16[256,1408]{1,0:T(8,128)(2,1)} async-done(((bf16[2048,1408]{1,0:T(8,128)(2,1)}), bf16[256,1408]{1,0:T(8,128)(2,1)}) %reduce-scatter.22.cloned.1.call-update) | async-done | bytes 720912 | tf_op jit(solution)/shard_map/reduce_scatter | solution.py:164
  1199.3 2.3 convert_element_type.245
  1201.7 14.2 fusion.36
  1215.9 40.7 %all-reduce.10 = (f32[2048]{0:T(1024)S(1)}, f32[2048]{0:T(1024)S(1)}, f32[6144]{0:T(1024)S(1)}, f32[2048]{0:T(1024)S(1)}, f32[2048]{0:T(1024)S(1)}) all-reduce(f32[2048]{0:T(1024)S(1)} %get-tuple-element.14, f32[2048]{0:T(1024)S(1)} %get-tuple-element.17, ...), channel_id=8, replica_groups=mesh['dp'=8,'ctx'=4] {'dp','ctx'}, use_global_device_ids=true, to_apply=%region_16.17.clone | all-reduce | flops 14336 | bytes 114688
  1259.6 3.7 fusion.35
  1263.3 296.2 %reduce-scatter.20.cloned.1.call-done = f32[64,2048]{1,0:T(8,128)} async-done(((f32[2048,2048]{1,0:T(8,128)}), f32[64,2048]{1,0:T(8,128)}) %reduce-scatter.20.cloned.1.call-update) | async-done | bytes 524304 | tf_op jit(solution)/shard_map/reduce_scatter | solution.py:251
  1559.5 440.1 %reduce-scatter.18.cloned.1.call-done = f32[64,6144]{1,0:T(8,128)} async-done(((f32[2048,6144]{1,0:T(8,128)}), f32[64,6144]{1,0:T(8,128)}) %reduce-scatter.18.cloned.1.call-update) | async-done | bytes 1572880 | tf_op jit(solution)/shard_map/reduce_scatter | solution.py:249
  (137 shorter events, 19.1 us)
Async XLA Ops:
  7.2 162.6 %all-gather.12.cloned.1.call-start = ((), (), s32[]{:S(2)}) async-start(), calls=%async_computation.9 | async-start | bytes 25952256 | tf_op jit(solution)/shard_map/all_gather | solution.py:100
  7.9 237.0 %all-gather.14.cloned.1.call-start = ((), (), s32[]{:S(2)}) async-start(), calls=%async_computation.10 | async-start | bytes 5242880 | tf_op jit(solution)/shard_map/all_gather | solution.py:116
  55.8 127.7 %copy-start.12 = (f32[2048]{0:T(1024)}, f32[2048]{0:T(1024)S(1)}, u32[]{:S(2)}) copy-start(f32[2048]{0:T(1024)S(1)} %convert_element_type.204) | copy-start | bytes 24580
  55.8 127.6 %copy-start.14 = (f32[2048]{0:T(1024)}, f32[2048]{0:T(1024)S(1)}, u32[]{:S(2)}) copy-start(f32[2048]{0:T(1024)S(1)} %convert_element_type.205) | copy-start | bytes 24580
  57.3 126.1 %copy-start.18 = (f32[256]{0:T(256)}, f32[256]{0:T(256)S(1)}, u32[]{:S(2)}) copy-start(f32[256]{0:T(256)S(1)} %broadcast_multiply_fusion.5) | copy-start | bytes 3076
  59.0 124.5 %copy-start.20 = (f32[256]{0:T(256)}, f32[256]{0:T(256)S(1)}, u32[]{:S(2)}) copy-start(f32[256]{0:T(256)S(1)} %add_rsqrt_fusion.1) | copy-start | bytes 3076
  59.7 132.9 %copy-start.16 = (f32[256,8]{0,1:T(8,128)}, f32[256,8]{0,1:T(8,128)S(1)}, u32[]{:S(2)}) copy-start(f32[256,8]{0,1:T(8,128)S(1)} %get-tuple-element.52) | copy-start | bytes 24580
  192.7 5.5 copy-start.24
  192.8 52.1 %copy-start.8 = (bf16[256,32,8]{0,2,1:T(8,128)(2,1)}, bf16[256,32,8]{0,2,1:T(8,128)(2,1)S(1)}, u32[]{:S(2)}) copy-start(bf16[256,32,8]{0,2,1:T(8,128)(2,1)S(1)} %get-tuple-element.40) | copy-start | bytes 393220
  192.8 52.1 %copy-start.10 = (bf16[256,32,8]{0,2,1:T(8,128)(2,1)}, bf16[256,32,8]{0,2,1:T(8,128)(2,1)S(1)}, u32[]{:S(2)}) copy-start(bf16[256,32,8]{0,2,1:T(8,128)(2,1)S(1)} %get-tuple-element.41) | copy-start | bytes 393220
  194.0 105.9 %all-gather.26.cloned.1.call-start = ((), (), s32[]{:S(2)}) async-start(), calls=%async_computation.25 | async-start | bytes 5242880 | tf_op jit(solution)/shard_map/all_gather | solution.py:117
  196.8 183.5 %all-gather.16.cloned.1.call-start = ((), (), s32[]{:S(2)}) async-start(), calls=%async_computation.11 | async-start | bytes 8650752 | tf_op jit(solution)/shard_map/all_gather | solution.py:102
  197.3 243.4 %all-gather.20.cloned.1.call-start = ((), (), s32[]{:S(2)}) async-start(), calls=%async_computation.13 | async-start | bytes 6488064 | tf_op jit(solution)/shard_map/all_gather | solution.py:131
  197.9 296.5 %all-gather.28.cloned.1.call-start = ((), (), s32[]{:S(2)}) async-start(), calls=%async_computation.26 | async-start | bytes 5242880 | tf_op jit(solution)/shard_map/all_gather | solution.py:137
  198.7 63.0 %copy-start.4 = (bf16[256,32,48]{0,2,1:T(8,128)(2,1)}, bf16[256,32,48]{0,2,1:T(8,128)(2,1)S(1)}, u32[]{:S(2)}) copy-start(bf16[256,32,48]{0,2,1:T(8,128)(2,1)S(1)} %fusion.67) | copy-start | bytes 2359300
  276.6 103.6 %copy-start = (bf16[1,256,2048]{2,1,0:T(8,128)(2,1)S(1)}, bf16[1,256,2048]{2,1,0:T(8,128)(2,1)}, u32[]{:S(2)}) copy-start(bf16[1,256,2048]{2,1,0:T(8,128)(2,1)} %param.13) | copy-start | bytes 3145732
  388.2 168.4 %all-gather.18.cloned.1.call-start = ((), (), s32[]{:S(2)}) async-start(), calls=%async_computation.12 | async-start | bytes 6488064 | tf_op jit(solution)/shard_map/all_gather | solution.py:130
  389.0 220.9 %all-gather.24.cloned.1.call-start = ((), (), s32[]{:S(2)}) async-start(), calls=%async_computation.16 | async-start | bytes 5242880 | tf_op jit(solution)/shard_map/all_gather | solution.py:138
  389.7 282.6 %all-gather.22.cloned.1.call-start = ((), (), s32[]{:S(2)}) async-start(), calls=%async_computation.14 | async-start | bytes 6488064 | tf_op jit(solution)/shard_map/all_gather | solution.py:132
  390.4 369.6 %reduce-scatter.12.cloned.1.call-start = ((), (), s32[]{:S(2)}) async-start(), calls=%async_computation.17 | async-start | bytes 5242880 | tf_op jit(solution)/shard_map/reduce_scatter | solution.py:178
  672.3 16.6 copy-start.25
  688.9 8.7 copy-start.28
  709.0 107.0 %reduce-scatter.10.cloned.1.call-start = ((), (), s32[]{:S(2)}) async-start(), calls=%async_computation.15 | async-start | bytes 5242880 | tf_op jit(solution)/shard_map/reduce_scatter | solution.py:151
  720.0 96.0 %copy-start.7 = (bf16[1,256,2048]{2,1,0:T(8,128)(2,1)S(1)}, bf16[1,256,2048]{2,1,0:T(8,128)(2,1)}, u32[]{:S(2)}) copy-start(bf16[1,256,2048]{2,1,0:T(8,128)(2,1)} %param.25) | copy-start | bytes 3145732
  720.0 254.7 %reduce-scatter.14.cloned.1.call-start = ((), (), s32[]{:S(2)}) async-start(), calls=%async_computation.18 | async-start | bytes 5242880 | tf_op jit(solution)/shard_map/reduce_scatter | solution.py:223
  819.6 1.3 copy-start.2
  853.8 28.0 %copy-start.5 = (bf16[256,32,48]{0,2,1:T(8,128)(2,1)S(1)}, bf16[256,32,48]{0,2,1:T(8,128)(2,1)}, u32[]{:S(2)}) copy-start(bf16[256,32,48]{0,2,1:T(8,128)(2,1)} %copy-done.4) | copy-start | bytes 2359300
  853.8 28.0 %copy-start.9 = (bf16[256,32,8]{0,2,1:T(8,128)(2,1)S(1)}, bf16[256,32,8]{0,2,1:T(8,128)(2,1)}, u32[]{:S(2)}) copy-start(bf16[256,32,8]{0,2,1:T(8,128)(2,1)} %copy-done.8) | copy-start | bytes 393220
  853.8 28.0 %copy-start.11 = (bf16[256,32,8]{0,2,1:T(8,128)(2,1)S(1)}, bf16[256,32,8]{0,2,1:T(8,128)(2,1)}, u32[]{:S(2)}) copy-start(bf16[256,32,8]{0,2,1:T(8,128)(2,1)} %copy-done.10) | copy-start | bytes 393220
  892.7 108.7 %reduce-scatter.16.cloned.1.call-start = ((), (), s32[]{:S(2)}) async-start(), calls=%async_computation.19 | async-start | bytes 5242880 | tf_op jit(solution)/shard_map/reduce_scatter | solution.py:226
  910.2 2.0 copy-start.26
  910.2 158.2 %reduce-scatter.26.cloned.1.call-start = ((), (), s32[]{:S(2)}) async-start(), calls=%async_computation.24 | async-start | bytes 6488064 | tf_op jit(solution)/shard_map/reduce_scatter | solution.py:170
  923.2 1.8 copy-start.29
  923.2 210.7 %reduce-scatter.24.cloned.1.call-start = ((), (), s32[]{:S(2)}) async-start(), calls=%async_computation.23 | async-start | bytes 6488064 | tf_op jit(solution)/shard_map/reduce_scatter | solution.py:167
  935.8 1.9 copy-start.27
  935.8 263.5 %reduce-scatter.22.cloned.1.call-start = ((), (), s32[]{:S(2)}) async-start(), calls=%async_computation.22 | async-start | bytes 6488064 | tf_op jit(solution)/shard_map/reduce_scatter | solution.py:164
  948.5 1.6 copy-start.3
  948.5 1.9 copy-start.6
  948.6 610.9 %reduce-scatter.20.cloned.1.call-start = ((), (), s32[]{:S(2)}) async-start(), calls=%async_computation.21 | async-start | bytes 17301504 | tf_op jit(solution)/shard_map/reduce_scatter | solution.py:251
  959.0 1040.5 %reduce-scatter.18.cloned.1.call-start = ((), (), s32[]{:S(2)}) async-start(), calls=%async_computation.20 | async-start | bytes 51904512 | tf_op jit(solution)/shard_map/reduce_scatter | solution.py:249
  973.2 3.1 copy-start.17
  973.2 3.1 copy-start.22
  974.7 3.9 slice-start
  978.6 26.5 %copy-start.1 = (bf16[1,256,2048]{2,1,0:T(8,128)(2,1)S(1)}, bf16[1,256,2048]{2,1,0:T(8,128)(2,1)}, u32[]{:S(2)}) copy-start(bf16[1,256,2048]{2,1,0:T(8,128)(2,1)} %param.13) | copy-start | bytes 3145732
  978.6 26.5 %copy-start.13 = (f32[2048]{0:T(1024)S(1)}, f32[2048]{0:T(1024)}, u32[]{:S(2)}) copy-start(f32[2048]{0:T(1024)} %copy-done.12) | copy-start | bytes 24580
  978.6 26.5 %copy-start.15 = (f32[2048]{0:T(1024)S(1)}, f32[2048]{0:T(1024)}, u32[]{:S(2)}) copy-start(f32[2048]{0:T(1024)} %copy-done.14) | copy-start | bytes 24580
  978.6 26.5 %copy-start.19 = (f32[256]{0:T(256)S(1)}, f32[256]{0:T(256)}, u32[]{:S(2)}) copy-start(f32[256]{0:T(256)} %copy-done.18) | copy-start | bytes 3076
  978.6 26.5 %copy-start.21 = (f32[256]{0:T(256)S(1)}, f32[256]{0:T(256)}, u32[]{:S(2)}) copy-start(f32[256]{0:T(256)} %copy-done.20) | copy-start | bytes 3076
  1201.7 14.3 copy-start.23
Sparse Core Ops, SparseCore 0:
  10.9 158.8 all-gather.11
  194.1 50.7 all-gather.13
  247.3 52.5 all-gather.25
  302.6 77.5 all-gather.15
  381.7 59.0 all-gather.19
  443.0 51.3 all-gather.27
  496.1 60.4 all-gather.17
  558.4 51.3 all-gather.23
  611.4 60.8 all-gather.21
  709.2 50.8 reduce-scatter.11
  763.3 52.6 reduce-scatter.9
  892.8 52.6 reduce-scatter.13
  948.7 52.6 reduce-scatter.15
  1003.6 64.8 reduce-scatter.25
  1070.6 63.2 reduce-scatter.23
  1136.0 63.2 reduce-scatter.21
  1202.0 357.4 reduce-scatter.19
  1566.3 433.1 reduce-scatter.17
where the time goes:
time: 2010 us
  waiting for transfers between devices  1520 us (76%)
  matrix products  276 us (14%)
  blocking collectives  84.3 us (4%)
  other arithmetic  77.1 us (4%)
  local copies, waits for them, and re-layouts  29.7 us (1%)
    reduce_scatter x1, waiting for transfers between devices, shards(): lax.psum_scatter(d_joined_weight, ('dp', 'ctx'), scatter_dimension=0, til...  440 us
    reduce_scatter x1, waiting for transfers between devices, shards(): lax.psum_scatter(d_out_weight, ('dp', 'ctx'), scatter_dimension=0, tiled=...  296 us
    all_gather x1, waiting for transfers between devices, shards(): lax.all_gather(qkv_weight, ('dp', 'ctx'), axis=0, tiled=True)  110 us
    unnamed x2, blocking collectives  84.3 us
    all_gather x1, waiting for transfers between devices, shards(): lax.all_gather(out_weight, ('dp', 'ctx'), axis=0, tiled=True)  63.5 us
    reduce_scatter x1, waiting for transfers between devices, shards(): lax.psum_scatter(d_gate_weight.astype(jnp.bfloat16), 'dp', scatter_dimens...  63.1 us
    reduce_scatter x1, waiting for transfers between devices, shards(): lax.psum_scatter(d_up_weight.astype(jnp.bfloat16), 'dp', scatter_dimensio...  63.1 us
    all_gather x1, waiting for transfers between devices, shards(): lax.all_gather(down_weight, 'dp', axis=1, tiled=True)  62.5 us
  transfers between devices with their start and end apart: 18, of which 17 were waited for; matrix products, arithmetic and copies ran while one was open for 12% of the time, Pallas kernels for 0%

commit v1 on v0

v1 whole, which is shorter than its diff:
```python
import functools
import math

import jax
import jax.numpy as jnp
from jax import lax
from jax.experimental import pallas as pl
from jax.experimental.pallas import tpu as pltpu
from jax.sharding import PartitionSpec as P

HD = 64
ROT = 16
DOC_MAX = 512
PAIR = 2 * HD

norm_eps = 1e-05
masked_value = -1e30
f32 = jnp.float32
bf16 = jnp.bfloat16


def dot(a, b):
    return jnp.dot(a, b, preferred_element_type=f32)


def dot_nt(a, b):
    return lax.dot_general(a, b, (((1,), (1,)), ((), ())), preferred_element_type=f32)


def dot_tn(a, b):
    return lax.dot_general(a, b, (((0,), (0,)), ((), ())), preferred_element_type=f32)


def norm_stats(rows):
    row_mean = jnp.mean(rows, axis=-1, keepdims=True)
    centered = rows - row_mean
    variance = jnp.mean(centered * centered, axis=-1, keepdims=True)
    inv_std = lax.rsqrt(variance + norm_eps)
    return centered * inv_std, inv_std


def norm_backward(grad_normed, scaled, inv_std, gain):
    grad_gain = jnp.sum(grad_normed * scaled, axis=0)
    grad_shift = jnp.sum(grad_normed, axis=0)
    inner_grad = grad_normed * gain
    grad_rows = inv_std * (
        inner_grad
        - jnp.mean(inner_grad, axis=-1, keepdims=True)
        - scaled * jnp.mean(inner_grad * scaled, axis=-1, keepdims=True)
    )
    return grad_rows, grad_gain, grad_shift


def partner(n, k):
    return [(c, c ^ k) for c in range(n)]


def hop(x, n, k):
    return lax.ppermute(x, "ctx", partner(n, k))


def gather_relative(block, n):
    if n != 4:
        return [block] + [hop(block, n, k) for k in range(1, n)]
    half = block.shape[0] // 2
    one = hop(block, n, 1)
    two = hop(block, n, 2)
    low = hop(one[:half], n, 2)
    high = hop(two[half:], n, 1)
    return [block, one, two, jnp.concatenate([low, high], axis=0)]


def gather_ctx(block, n):
    me = lax.axis_index("ctx")
    size = block.shape[0]
    parts = gather_relative(block, n)
    full = jnp.zeros((n * size,) + block.shape[1:], block.dtype)
    for k, part in enumerate(parts):
        full = lax.dynamic_update_slice_in_dim(full, part, (me ^ k) * size, 0)
    return full


def scatter_ctx(partial, n):
    me = lax.axis_index("ctx")
    size = partial.shape[0] // n

    def block(k):
        return lax.dynamic_slice_in_dim(partial, (me ^ k) * size, size, 0)

    if n != 4:
        total = block(0).astype(f32)
        for k in range(1, n):
            total = total + hop(block(k).astype(bf16), n, k).astype(f32)
        return total
    half = size // 2
    far = block(3).astype(bf16)
    low = hop(far[:half], n, 1).astype(f32)
    high = hop(far[half:], n, 2).astype(f32)
    one = block(1).astype(f32)
    two = block(2).astype(f32)
    to_one = jnp.concatenate([one[:half], one[half:] + high], axis=0).astype(bf16)
    to_two = jnp.concatenate([two[:half] + low, two[half:]], axis=0).astype(bf16)
    return block(0).astype(f32) + hop(to_one, n, 1).astype(f32) + hop(to_two, n, 2).astype(f32)


def exchange_ctx(blocks, n):
    me = lax.axis_index("ctx")
    got = lax.dynamic_update_slice_in_dim(
        jnp.zeros_like(blocks), lax.dynamic_slice_in_dim(blocks, me, 1, 0), me, 0
    )
    for k in range(1, n):
        sent = lax.dynamic_slice_in_dim(blocks, me ^ k, 1, 0)
        got = lax.dynamic_update_slice_in_dim(got, hop(sent, n, k), me ^ k, 0)
    return got


def turn(x, table_ref):
    return (
        x * table_ref[0]
        + pltpu.roll(x, PAIR - ROT // 2, 1) * table_ref[1]
        + pltpu.roll(x, ROT // 2, 1) * table_ref[2]
    )


def turn_back(x, table_ref):
    return (
        x * table_ref[0]
        - pltpu.roll(x, PAIR - ROT // 2, 1) * table_ref[1]
        - pltpu.roll(x, ROT // 2, 1) * table_ref[2]
    )


def head_lanes(shape):
    return lax.broadcasted_iota(jnp.int32, shape, 1) < HD


def span(full_len, step, at):
    return max(0, (at - DOC_MAX + 1) // step * step), at + step


def block_mask(start, at, step, low, high):
    keys = lax.broadcasted_iota(jnp.int32, (step, high - low), 1) + low
    rows = lax.broadcasted_iota(jnp.int32, (step, high - low), 0) + at
    return (keys >= start) & (keys <= rows)


def attend_kernel(step, joined_ref, bias_ref, table_ref, start_ref, out_ref, qkv_ref, lse_ref):
    full_len = joined_ref.shape[0]
    scale = 1.0 / math.sqrt(HD)
    for t in range(3):
        lanes = slice(t * PAIR, (t + 1) * PAIR)
        x = joined_ref[:, lanes] + bias_ref[:, lanes]
        if t < 2:
            x = turn(x, table_ref)
        qkv_ref[:, lanes] = x.astype(bf16)
    for at in range(0, full_len, step):
        low, high = span(full_len, step, at)
        allowed = block_mask(start_ref[at : at + step, :1], at, step, low, high)
        q = qkv_ref[at : at + step, :PAIR]
        k = qkv_ref[low:high, PAIR : 2 * PAIR]
        v = qkv_ref[low:high, 2 * PAIR :]
        total = jnp.zeros((step, PAIR), f32)
        logs = []
        for head in range(2):
            mine = head_lanes(q.shape) == (head == 0)
            s = dot_nt(jnp.where(mine, q, jnp.zeros_like(q)), k) * scale
            s = jnp.where(allowed, s, masked_value)
            top = jnp.max(s, axis=1, keepdims=True)
            e = jnp.exp(s - top)
            norm = jnp.sum(e, axis=1, keepdims=True)
            probs = (e * (1.0 / norm)).astype(bf16)
            vm = jnp.where(head_lanes(v.shape) == (head == 0), v, jnp.zeros_like(v))
            total = total + dot(probs, vm)
            logs.append(top + jnp.log(norm))
        out_ref[at : at + step, :] = total.astype(bf16)
        lse_ref[at : at + step, :] = jnp.where(head_lanes((step, PAIR)), logs[0], logs[1])


def attend_back_kernel(
    step, qkv_ref, grad_ref, lse_ref, table_ref, start_ref, out_ref, sum_ref, dk_ref, dv_ref
):
    full_len = qkv_ref.shape[0]
    scale = 1.0 / math.sqrt(HD)
    dk_ref[...] = jnp.zeros_like(dk_ref)
    dv_ref[...] = jnp.zeros_like(dv_ref)
    total = jnp.zeros((1, PAIR), f32)
    for at in range(0, full_len, step):
        low, high = span(full_len, step, at)
        rows = slice(at, at + step)
        keys = slice(low, high)
        allowed = block_mask(start_ref[rows, :1], at, step, low, high)
        q = qkv_ref[rows, :PAIR]
        k = qkv_ref[keys, PAIR : 2 * PAIR]
        v = qkv_ref[keys, 2 * PAIR :]
        g = grad_ref[rows, :]
        dq = jnp.zeros((step, PAIR), f32)
        dk = jnp.zeros((high - low, PAIR), f32)
        dv = jnp.zeros((high - low, PAIR), f32)
        for head in range(2):
            mine = head_lanes(q.shape) == (head == 0)
            qm = jnp.where(mine, q, jnp.zeros_like(q))
            gm = jnp.where(mine, g, jnp.zeros_like(g))
            km = jnp.where(head_lanes(k.shape) == (head == 0), k, jnp.zeros_like(k))
            s = dot_nt(qm, k) * scale
            probs = jnp.where(
                allowed, jnp.exp(s - lse_ref[rows, head * HD : head * HD + 1]), 0.0
            )
            dp = dot_nt(gm, v)
            mean = jnp.sum(dp * probs, axis=1, keepdims=True)
            ds = (probs * (dp - mean)).astype(bf16)
            dq = dq + dot(ds, km)
            dk = dk + dot_tn(ds, qm)
            dv = dv + dot_tn(probs.astype(bf16), gm)
        dk_ref[keys, :] += dk
        dv_ref[keys, :] += dv
        dq = turn_back(dq * scale, table_ref.at[:, rows, :]).astype(bf16)
        out_ref[rows, :PAIR] = dq
        total = total + jnp.sum(dq.astype(f32), axis=0, keepdims=True)
    sum_ref[:, :PAIR] = total
    dk = turn_back(dk_ref[...] * scale, table_ref).astype(bf16)
    out_ref[:, PAIR : 2 * PAIR] = dk
    sum_ref[:, PAIR : 2 * PAIR] = jnp.sum(dk.astype(f32), axis=0, keepdims=True)
    dv = dv_ref[...].astype(bf16)
    out_ref[:, 2 * PAIR :] = dv
    sum_ref[:, 2 * PAIR :] = jnp.sum(dv.astype(f32), axis=0, keepdims=True)


def whole(shape):
    return pl.BlockSpec(shape, lambda p: (0,) * len(shape))


def attend_step(full_len):
    return min(256, full_len)


def attend(joined, bias, table, start):
    full_len, width = joined.shape
    pairs = width // (3 * PAIR)
    step = attend_step(full_len)
    seen = sum(span(full_len, step, at)[1] - span(full_len, step, at)[0] for at in range(0, full_len, step)) * step
    wide = pl.BlockSpec((full_len, 3 * PAIR), lambda p: (0, p))
    thin = pl.BlockSpec((full_len, PAIR), lambda p: (0, p))
    return pl.pallas_call(
        functools.partial(attend_kernel, step),
        grid=(pairs,),
        in_specs=[
            wide,
            pl.BlockSpec((1, 3 * PAIR), lambda p: (0, p)),
            whole(table.shape),
            whole(start.shape),
        ],
        out_specs=[thin, wide, thin],
        out_shape=[
            jax.ShapeDtypeStruct((full_len, pairs * PAIR), bf16),
            jax.ShapeDtypeStruct((full_len, width), bf16),
            jax.ShapeDtypeStruct((full_len, pairs * PAIR), f32),
        ],
        compiler_params=pltpu.CompilerParams(vmem_limit_bytes=40 << 20),
        cost_estimate=pl.CostEstimate(
            flops=pairs * seen * PAIR * 8, transcendentals=pairs * seen * 2, bytes_accessed=full_len * width * 8
        ),
    )(joined, bias, table, start)


def attend_back(qkv, grad, lse, table, start):
    full_len, width = qkv.shape
    pairs = width // (3 * PAIR)
    step = attend_step(full_len)
    seen = sum(span(full_len, step, at)[1] - span(full_len, step, at)[0] for at in range(0, full_len, step)) * step
    wide = pl.BlockSpec((full_len, 3 * PAIR), lambda p: (0, p))
    thin = pl.BlockSpec((full_len, PAIR), lambda p: (0, p))
    return pl.pallas_call(
        functools.partial(attend_back_kernel, step),
        grid=(pairs,),
        in_specs=[wide, thin, thin, whole(table.shape), whole(start.shape)],
        out_specs=[wide, pl.BlockSpec((1, 3 * PAIR), lambda p: (0, p))],
        out_shape=[
            jax.ShapeDtypeStruct((full_len, width), bf16),
            jax.ShapeDtypeStruct((1, width), f32),
        ],
        scratch_shapes=[pltpu.VMEM((full_len, PAIR), f32), pltpu.VMEM((full_len, PAIR), f32)],
        compiler_params=pltpu.CompilerParams(vmem_limit_bytes=40 << 20),
        cost_estimate=pl.CostEstimate(
            flops=pairs * seen * PAIR * 20, transcendentals=pairs * seen * 2, bytes_accessed=full_len * width * 8
        ),
    )(qkv, grad, lse, table, start)


def rotary_table(full_len):
    half = ROT // 2
    freq = jnp.arange(half, dtype=f32)
    inverse = jnp.power(f32(10000.0), -(2.0 * freq) / ROT)
    angles = jnp.arange(full_len, dtype=jnp.int32).astype(f32)[:, None] * inverse[None, :]
    cosine, sine = jnp.cos(angles), jnp.sin(angles)
    rest = jnp.zeros((full_len, HD - ROT), f32)
    none = jnp.zeros_like(sine)
    keep = jnp.concatenate([cosine, cosine, rest + 1.0], axis=1)
    ahead = jnp.concatenate([-sine, none, rest], axis=1)
    behind = jnp.concatenate([none, sine, rest], axis=1)
    return jnp.stack([jnp.concatenate([t, t], axis=1) for t in (keep, ahead, behind)])


def shards(
    dp,
    ctx,
    inputs,
    segments,
    ln1_gain,
    ln1_bias,
    qkv_weight,
    qkv_bias,
    out_weight,
    ln2_gain,
    ln2_bias,
    gate_weight,
    up_weight,
    down_weight,
    cotangent,
):
    local_len, width = inputs.shape[1], inputs.shape[2]
    full_len = segments.shape[1]
    heads = width // HD
    near = heads // ctx
    pairs = near // 2
    me = lax.axis_index("ctx")
    own = me * local_len

    small = jnp.concatenate([ln1_gain, ln1_bias, ln2_gain, ln2_bias, qkv_bias])
    small = lax.all_gather(small[None, :], ("dp", "ctx"), axis=0, tiled=True).astype(f32)
    part = ln1_gain.shape[0]
    gain_one, shift_one, gain_two, shift_two = [
        small[:, i * part : (i + 1) * part].reshape(width) for i in range(4)
    ]
    bias = small[:, 4 * part :].reshape(3, pairs, 2, ctx, HD)
    bias = lax.dynamic_index_in_dim(bias, me, 3, keepdims=False)
    bias = bias.transpose(1, 0, 2, 3).reshape(1, near * 3 * HD)

    rows_here = qkv_weight.shape[0]
    blocks = qkv_weight.reshape(rows_here, 3, pairs, 2, ctx, HD).transpose(4, 0, 2, 1, 3, 5)
    blocks = exchange_ctx(blocks.reshape(ctx, rows_here, near * 3 * HD), ctx)
    joined_weight = lax.all_gather(
        blocks.reshape(ctx * rows_here, near * 3 * HD), "dp", axis=0, tiled=True
    )
    if part == HD:
        out_full = lax.all_gather(out_weight, "dp", axis=0, tiled=True)
    else:
        out_full = lax.all_gather(out_weight, ("dp", "ctx"), axis=0, tiled=True)
        out_full = out_full.reshape(near, ctx, HD, width)
        out_full = lax.dynamic_index_in_dim(out_full, me, 1, keepdims=False)
        out_full = out_full.reshape(near * HD, width)
    gate_full = lax.all_gather(gate_weight, "dp", axis=0, tiled=True)
    up_full = lax.all_gather(up_weight, "dp", axis=0, tiled=True)
    down_full = lax.all_gather(down_weight, "dp", axis=1, tiled=True)

    rows = inputs[0]
    rows_wide = gather_ctx(rows, ctx)
    grad_rows = cotangent[0]
    grad_wide = gather_ctx(grad_rows, ctx)

    segment = segments[0]
    start = jnp.sum((segment[None, :] < segment[:, None]).astype(jnp.int32), axis=1)
    start = jnp.broadcast_to(start[:, None], (full_len, 128))
    table = rotary_table(full_len)
    scaled_wide, _ = norm_stats(rows_wide.astype(f32))
    normed_one = (scaled_wide * gain_one + shift_one).astype(bf16)
    joined = dot(normed_one, joined_weight)
    attended, qkv, lse = attend(joined, bias, table, start)
    resid = rows.astype(f32) + scatter_ctx(dot(attended, out_full), ctx)

    scaled_two, inv_two = norm_stats(resid)
    normed_two = (scaled_two * gain_two + shift_two).astype(bf16)
    normed_wide = gather_ctx(normed_two, ctx)
    gate = dot(normed_wide, gate_full)
    upward = dot(normed_wide, up_full)
    sigma = jax.nn.sigmoid(gate)
    swish = gate * sigma
    inner = (swish * upward).astype(bf16)
    d_inner = dot_nt(grad_wide, down_full)
    d_gate = (d_inner * upward * sigma * (1.0 + gate * (1.0 - sigma))).astype(bf16)
    d_upward = (d_inner * swish).astype(bf16)
    d_normed_two = scatter_ctx(dot_nt(d_gate, gate_full) + dot_nt(d_upward, up_full), ctx)
    output = (resid + scatter_ctx(dot(inner, down_full), ctx)).astype(bf16)
    d_down = dot_tn(inner, grad_wide).astype(bf16)
    d_gate_weight = dot_tn(normed_wide, d_gate).astype(bf16)
    d_up_weight = dot_tn(normed_wide, d_upward).astype(bf16)
    d_down = lax.psum_scatter(d_down, "dp", scatter_dimension=1, tiled=True).astype(f32)
    d_gate_weight = lax.psum_scatter(d_gate_weight, "dp", scatter_dimension=0, tiled=True).astype(f32)
    d_up_weight = lax.psum_scatter(d_up_weight, "dp", scatter_dimension=0, tiled=True).astype(f32)

    d_resid_norm, d_gain_two, d_shift_two = norm_backward(d_normed_two, scaled_two, inv_two, gain_two)
    d_resid = grad_rows.astype(f32) + d_resid_norm
    d_proj = gather_ctx(d_resid.astype(bf16), ctx)
    d_attended = dot_nt(d_proj, out_full).astype(bf16)
    d_out_weight = dot_tn(attended, d_proj).astype(bf16)
    if part == HD:
        d_out_weight = lax.psum_scatter(d_out_weight, "dp", scatter_dimension=0, tiled=True)
    else:
        at_me = lax.broadcasted_iota(jnp.int32, (1, ctx, 1, 1), 1) == me
        d_out_weight = jnp.where(at_me, d_out_weight.reshape(near, 1, HD, width), jnp.zeros((), bf16))
        d_out_weight = lax.psum_scatter(
            d_out_weight.reshape(width, width), ("dp", "ctx"), scatter_dimension=0, tiled=True
        )
    d_out_weight = d_out_weight.astype(f32)

    d_joined, d_bias = attend_back(qkv, d_attended, lse, table, start)
    d_normed_one = scatter_ctx(dot_nt(d_joined, joined_weight), ctx)
    d_joined_weight = lax.psum_scatter(
        dot_tn(normed_one, d_joined).astype(bf16), "dp", scatter_dimension=0, tiled=True
    )
    blocks = exchange_ctx(d_joined_weight.reshape(ctx, rows_here, near * 3 * HD), ctx)
    blocks = blocks.reshape(ctx, rows_here, pairs, 3, 2, HD).transpose(1, 3, 2, 4, 0, 5)
    d_joined_weight = blocks.reshape(rows_here, 3 * width).astype(f32)

    scaled_one, inv_one = norm_stats(rows.astype(f32))
    d_rows_norm, d_gain_one, d_shift_one = norm_backward(d_normed_one, scaled_one, inv_one, gain_one)
    grad_input = d_resid + d_rows_norm

    d_bias = d_bias.reshape(pairs, 3, 2, HD).transpose(1, 0, 2, 3)[:, :, :, None, :]
    at_me = (lax.broadcasted_iota(jnp.int32, (1, 1, 1, ctx, 1), 3) == me).astype(f32)
    d_bias = (d_bias * at_me).reshape(dp * ctx, -1)
    small = jnp.concatenate(
        [t.reshape(dp * ctx, part) for t in (d_gain_one, d_shift_one, d_gain_two, d_shift_two)]
        + [d_bias],
        axis=1,
    )
    small = lax.psum_scatter(small, ("dp", "ctx"), scatter_dimension=0, tiled=True)[0]
    d_gain_one, d_shift_one, d_gain_two, d_shift_two = [
        small[i * part : (i + 1) * part] for i in range(4)
    ]
    return (
        output[None],
        grad_input[None],
        d_gain_one,
        d_shift_one,
        d_joined_weight,
        small[4 * part :],
        d_out_weight,
        d_gain_two,
        d_shift_two,
        d_gate_weight,
        d_up_weight,
        d_down,
    )


def solution(mesh):
    every = ("dp", "ctx")
    return jax.shard_map(
        functools.partial(shards, mesh.shape["dp"], mesh.shape["ctx"]),
        mesh=mesh,
        in_specs=(
            P("dp", "ctx", None),
            P("dp", None),
            P(every),
            P(every),
            P(every, None),
            P(every),
            P(every, None),
            P(every),
            P(every),
            P("dp", "ctx"),
            P("dp", "ctx"),
            P("ctx", "dp"),
            P("dp", "ctx", None),
        ),
        out_specs=(
            P("dp", "ctx", None),
            P("dp", "ctx", None),
            P(every),
            P(every),
            P(every, None),
            P(every),
            P(every, None),
            P(every),
            P(every),
            P("dp", "ctx"),
            P("dp", "ctx"),
            P("ctx", "dp"),
        ),
        check_vma=False,
    )
```

time: 2010 us -> 839 us (0.42)
  waiting for transfers between devices: 1520 us -> 347 us
  matrix products: 276 us -> 150 us
  local copies, waits for them, and re-layouts: 29.7 us -> 83.6 us
  starting transfers between devices: 1.52 us -> 43.8 us
  Pallas kernels: 0 us -> 40.2 us
  other arithmetic: 77.1 us -> 55.8 us
    reduce_scatter x9 -> x5, waiting for transfers between devices: 1020 us -> 147 us  [the longest x1 63.2 us: shards(): lax.psum_scatter(d_up_weight, 'dp', scatter_dimension=0, tiled=True)]
    all_gather x9 -> x5, waiting for transfers between devices: 501 us -> 2.44 us  [the longest x1 2.41 us: shards(): down_full = lax.all_gather(down_weight, 'dp', axis=1, tiled=True)]
    ppermute x0 -> x38, waiting for transfers between devices: none -> 196 us  [hop(): return lax.ppermute(x, 'ctx', partner(n, k))]
    dot_general x21 -> x15, matrix products: 276 us -> 150 us  [the longest x5 51.6 us: dot_tn(): lax.dot_general(a, b, (((0,), (0,)), ((), ())), preferred_element_type=f32)]
    ppermute x0 -> x38, starting transfers between devices: none -> 43.4 us  [hop(): return lax.ppermute(x, 'ctx', partner(n, k))]
    pallas_call x0 -> x2, Pallas kernels: none -> 40.2 us  [the longest x1 21.8 us: attend_back(): pl.pallas_call(functools.partial(attend_back_kernel, step), grid=(pairs,)...]
    convert_element_type x12 -> x6, other arithmetic: 37.9 us -> 8.71 us  [the longest x1 2.32 us: shards(): lax.psum_scatter(d_down, 'dp', scatter_dimension=1, tiled=True).astype(f32)]
  transfers between devices with their start and end apart: 18 -> 48, of which waited for: 17 -> 32; matrix products, arithmetic and copies ran while one was open for 12% -> 23% of each run, Pallas kernels for 0% -> 2%
where the time goes in v1:
time: 839 us; the launch traced here: 834 us
  waiting for transfers between devices  347 us (41%)
  matrix products  150 us (18%)
  blocking collectives  98.1 us (12%)
  local copies, waits for them, and re-layouts  83.6 us (10%)
  other arithmetic  55.8 us (7%)
  starting transfers between devices  43.8 us (5%)
  Pallas kernels  40.2 us (5%)
  between operations  15.2 us (2%)
    ppermute x38, waiting for transfers between devices, hop(): return lax.ppermute(x, 'ctx', partner(n, k))  196 us
    unnamed x2, blocking collectives  98.1 us
    reduce_scatter x1, waiting for transfers between devices, shards(): lax.psum_scatter(d_up_weight, 'dp', scatter_dimension=0, tiled=True)  63.2 us
    reduce_scatter x1, waiting for transfers between devices, shards(): lax.psum_scatter(d_down, 'dp', scatter_dimension=1, tiled=True).astype(f32)  63.1 us
    dot_general x5, matrix products, dot_tn(): lax.dot_general(a, b, (((0,), (0,)), ((), ())), preferred_element_type=f32)  51.6 us
    dot_general x5, matrix products, dot(): return jnp.dot(a, b, preferred_element_type=f32)  49.8 us
    dot_general x5, matrix products, dot_nt(): lax.dot_general(a, b, (((1,), (1,)), ((), ())), preferred_element_type=f32)  49.1 us
    ppermute x38, starting transfers between devices, hop(): return lax.ppermute(x, 'ctx', partner(n, k))  43.4 us
  transfers between devices with their start and end apart: 48, of which 32 were waited for; matrix products, arithmetic and copies ran while one was open for 23% of the time, Pallas kernels for 2%

profile of v1, /device:TPU:0, one launch (start us, length us, event | category | flops | bytes accessed | tf_op | source)
XLA Modules:
  0.0 833.7 jit_solution(5522996707447477121)
XLA Ops:
  7.2 2.5 reshape.149
  12.2 3.0 collective-permute-start.4
  16.7 4.2 collective-permute-done.4
  20.9 4.8 collective-permute-done.5
  31.4 3.0 multiply_cosine_fusion
  34.3 58.1 %all-reduce = bf16[14336]{0:T(1024)(128)(2,1)S(1)} all-reduce(bf16[14336]{0:T(1024)(128)(2,1)S(1)} %dynamic-update-slice), channel_id=2, replica_groups=mesh['dp'=8,'ctx'=4] {'dp','ctx'}, use_global_device_ids=true, to_apply=%add | all-reduce | flops 14336 | bytes 57344
  92.7 2.6 concatenate.69
  100.9 2.5 broadcast.124.clone
  111.3 2.4 constant_dynamic-update-slice_fusion.16
  113.6 2.3 constant_dynamic-update-slice_fusion.15
  116.0 3.9 collective-permute-done.3
  123.2 2.8 convert_reduce_fusion
  126.0 3.4 fusion.2
  129.5 13.1 %fusion.30.joined_ref = f32[1024,1536]{1,0:T(8,128)} fusion(bf16[2048,1536]{1,0:T(8,128)(2,1)} %all-gather.7.cloned.1.call-done, bf16[1024,2048]{1,0:T(8,128)(2,1)} %maximum_dynamic-update-slice_fusion, f32[2048]{0:T(1024)S(1)} %add.203, f32[2048]{0:T(1024)S(1)} %mul.268, f32[1024]{0:T(1024)S(1)} %add_rsqrt_fusion, f32[1024]{0:T(1024)S(1)} %broadcast_multiply_fusion.1), kind=kOutput, calls=%fused_computation.138 | convolution fusion | flops 6455033856 | bytes 16801792 | tf_op jit(solution)/shard_map/dot_general | solution.py:23
  142.8 18.4 %shard_map.220 = (bf16[1024,512]{1,0:T(8,128)(2,1)S(1)}, bf16[1024,1536]{1,0:T(8,128)(2,1)S(1)}, f32[1024,512]{1,0:T(8,128)S(1)}) custom-call(f32[1024,1536]{1,0:T(8,128)} %fusion.30.joined_ref, f32[1,1536]{1,0:T(1,128)S(1)} %reshape.153.bias_ref, f32[3,1024,128]{2,1,0:T(8,128)S(1)} %pad_maximum_fusion.table_ref, s32[1024,128]{1,0:T(8,128)S(1)} %broadcast_in_dim.15.start_ref), custom_call_target="tpu_custom_call" | custom-call | flops 2415919104 | bytes 12582912 | tf_op jit(solution)/shard_map/pallas_call | solution.py:243
  164.3 4.0 fusion.38
  168.3 3.3 copy-done.11
  176.1 7.8 collective-permute-done.7
  194.1 19.4 %collective-permute-done.10 = bf16[256,2048]{1,0:T(8,128)(2,1)} collective-permute-done((bf16[256,2048]{1,0:T(8,128)(2,1)}, bf16[256,2048]{1,0:T(8,128)(2,1)}, u32[]{:S(2)}, u32[]{:S(2)}) %collective-permute-start.10) | collective-permute-done | bytes 1048608 | tf_op jit(solution)/shard_map/ppermute | solution.py:59
  213.5 2.8 collective-permute-done.8
  216.2 4.1 fusion.32
  220.7 2.6 broadcast.124.clone.1
  226.5 9.4 %collective-permute-done.20 = bf16[256,2048]{1,0:T(8,128)(2,1)} collective-permute-done((bf16[256,2048]{1,0:T(8,128)(2,1)}, bf16[256,2048]{1,0:T(8,128)(2,1)}, u32[]{:S(2)}, u32[]{:S(2)}) %collective-permute-start.20) | collective-permute-done | bytes 1048608 | tf_op jit(solution)/shard_map/ppermute | solution.py:59
  240.7 2.5 broadcast.124.clone.2
  243.2 2.4 constant_dynamic-update-slice_fusion.8
  245.5 2.3 constant_dynamic-update-slice_fusion.7
  247.9 2.3 constant_dynamic-update-slice_fusion.6
  250.2 8.1 collective-permute-done.12
  261.5 10.8 %collective-permute-done.22 = bf16[128,2048]{1,0:T(8,128)(2,1)S(1)} collective-permute-done((bf16[128,2048]{1,0:T(8,128)(2,1)S(1)}, bf16[128,2048]{1,0:T(8,128)(2,1)S(1)}, u32[]{:S(2)}, u32[]{:S(2)}) %collective-permute-start.22) | collective-permute-done | bytes 524320 | tf_op jit(solution)/shard_map/ppermute | solution.py:59
  275.4 2.6 collective-permute-done.14
  279.1 12.2 %fusion.39 = f32[1024,1408]{1,0:T(8,128)} fusion(bf16[1024,2048]{1,0:T(8,128)(2,1)} %maximum_dynamic-update-slice_fusion.1, bf16[2048,1408]{1,0:T(8,128)(2,1)} %all-gather.11.cloned.1.call-done), kind=kOutput, calls=%fused_computation.146 | convolution fusion | flops 5905580032 | bytes 15728640 | tf_op jit(solution)/shard_map/dot_general | solution.py:23
  291.3 11.9 %fusion.40 = f32[1024,1408]{1,0:T(8,128)} fusion(bf16[1024,2048]{1,0:T(8,128)(2,1)} %maximum_dynamic-update-slice_fusion.1, bf16[2048,1408]{1,0:T(8,128)(2,1)} %all-gather.13.cloned.1.call-done), kind=kOutput, calls=%fused_computation.147 | convolution fusion | flops 5905580032 | bytes 15728640 | tf_op jit(solution)/shard_map/dot_general | solution.py:23
  303.1 2.4 all-gather.15.cloned.1.call-done
  305.6 15.6 %multiply_convert_fusion = (bf16[1024,1408]{1,0:T(8,128)(2,1)S(1)}, bf16[1024,1408]{1,0:T(8,128)(2,1)S(1)}, bf16[1024,1408]{1,0:T(8,128)(2,1)}) fusion(f32[1024,1408]{1,0:T(8,128)} %fusion.39, f32[1024,1408]{1,0:T(8,128)} %fusion.40, bf16[1024,2048]{1,0:T(8,128)(2,1)} %maximum_dynamic-update-slice_fusion.2, bf16[1408,2048]{1,0:T(8,128)(2,1)} %all-gather.15.cloned.1.call-done), kind=kOutput, calls=%fused_computation.12 | convolution fusion | flops 5927206912 | bytes 30146560 | tf_op jit(solution)/shard_map/dot_general | solution.py:27
  321.2 12.9 %fusion.42 = f32[1024,2048]{1,0:T(8,128)} fusion(bf16[1024,1408]{1,0:T(8,128)(2,1)S(1)} %get-tuple-element.40, bf16[2048,1408]{1,0:T(8,128)(2,1)} %all-gather.11.cloned.1.call-done), kind=kOutput, calls=%fused_computation.149 | convolution fusion | flops 5905580032 | bytes 17039360 | tf_op jit(solution)/shard_map/dot_general | solution.py:27
  334.1 9.3 %convolution_add_fusion = f32[1024,2048]{1,0:T(8,128)S(1)} fusion(f32[1024,2048]{1,0:T(8,128)} %fusion.42, bf16[1024,1408]{1,0:T(8,128)(2,1)S(1)} %get-tuple-element.39, bf16[2048,1408]{1,0:T(8,128)(2,1)S(1)} %copy-done.26), kind=kOutput, calls=%fused_computation.18 | convolution fusion | flops 5907677184 | bytes 25427968 | tf_op jit(solution)/shard_map/dot_general | solution.py:27
  346.7 8.7 %fusion.41 = f32[1024,2048]{1,0:T(8,128)S(1)} fusion(bf16[1024,1408]{1,0:T(8,128)(2,1)S(1)} %copy-done.28, bf16[1408,2048]{1,0:T(8,128)(2,1)} %all-gather.15.cloned.1.call-done), kind=kOutput, calls=%fused_computation.148 | convolution fusion | flops 5905580032 | bytes 17039360 | tf_op jit(solution)/shard_map/dot_general | solution.py:23
  362.4 8.1 collective-permute-done.15
  373.8 19.2 %collective-permute-done.26 = bf16[256,2048]{1,0:T(8,128)(2,1)S(1)} collective-permute-done((bf16[256,2048]{1,0:T(8,128)(2,1)S(1)}, bf16[256,2048]{1,0:T(8,128)(2,1)S(1)}, u32[]{:S(2)}, u32[]{:S(2)}) %collective-permute-start.26) | collective-permute-done | bytes 1048608 | tf_op jit(solution)/shard_map/ppermute | solution.py:59
  393.6 20.6 %collective-permute-done.18 = bf16[256,2048]{1,0:T(8,128)(2,1)S(1)} collective-permute-done((bf16[256,2048]{1,0:T(8,128)(2,1)S(1)}, bf16[256,2048]{1,0:T(8,128)(2,1)S(1)}, u32[]{:S(2)}, u32[]{:S(2)}) %collective-permute-start.18) | collective-permute-done | bytes 1048608 | tf_op jit(solution)/shard_map/ppermute | solution.py:59
  415.3 3.8 multiply_reduce_fusion
  419.7 3.5 constant_dynamic-update-slice_fusion.5
  425.2 22.3 %collective-permute-done.28 = bf16[256,2048]{1,0:T(8,128)(2,1)S(1)} collective-permute-done((bf16[256,2048]{1,0:T(8,128)(2,1)S(1)}, bf16[256,2048]{1,0:T(8,128)(2,1)S(1)}, u32[]{:S(2)}, u32[]{:S(2)}) %collective-permute-start.28) | collective-permute-done | bytes 1048608 | tf_op jit(solution)/shard_map/ppermute | solution.py:59
  450.0 9.8 %collective-permute-done.30 = bf16[128,2048]{1,0:T(8,128)(2,1)S(1)} collective-permute-done((bf16[128,2048]{1,0:T(8,128)(2,1)S(1)}, bf16[128,2048]{1,0:T(8,128)(2,1)S(1)}, u32[]{:S(2)}, u32[]{:S(2)}) %collective-permute-start.30) | collective-permute-done | bytes 524320 | tf_op jit(solution)/shard_map/ppermute | solution.py:59
  461.5 2.4 convolution_convert_fusion.5.grad_ref
  465.5 21.8 %shard_map.221 = (bf16[1024,1536]{1,0:T(8,128)(2,1)S(1)}, f32[1,1536]{1,0:T(1,128)S(1)}) custom-call(bf16[1024,1536]{1,0:T(8,128)(2,1)S(1)} %copy-done.1, bf16[1024,512]{1,0:T(8,128)(2,1)S(1)} %convolution_convert_fusion.5.grad_ref, f32[1024,512]{1,0:T(8,128)S(1)} %copy-done.3, f32[3,1024,128]{2,1,0:T(8,128)S(1)} %pad_maximum_fusion.table_ref, ...), custom_call_target="tpu_custom_call" | custom-call | flops 6039797760 | bytes 12582912 | tf_op jit(solution)/shard_map/pallas_call | solution.py:272
  489.0 12.4 %convolution_convert_fusion.3 = bf16[2048,1536]{1,0:T(8,128)(2,1)} fusion(bf16[1024,1536]{1,0:T(8,128)(2,1)S(1)} %get-tuple-element.20, bf16[1024,2048]{1,0:T(8,128)(2,1)} %maximum_dynamic-update-slice_fusion, f32[2048]{0:T(1024)S(1)} %add.203, f32[2048]{0:T(1024)S(1)} %mul.268, f32[1024]{0:T(1024)S(1)} %add_rsqrt_fusion, f32[1024]{0:T(1024)S(1)} %broadcast_multiply_fusion.1), kind=kOutput, calls=%fused_computation.11 | convolution fusion | flops 6458179584 | bytes 13656064 | tf_op jit(solution)/shard_map/dot_general | solution.py:31
  501.4 5.9 convolution_convert_fusion.4
  507.4 11.5 %convolution_convert_fusion.2 = bf16[2048,1408]{1,0:T(8,128)(2,1)} fusion(bf16[1024,2048]{1,0:T(8,128)(2,1)} %maximum_dynamic-update-slice_fusion.1, bf16[1024,1408]{1,0:T(8,128)(2,1)} %copy-done.32), kind=kOutput, calls=%fused_computation.10 | convolution fusion | flops 5908463616 | bytes 12845056 | tf_op jit(solution)/shard_map/dot_general | solution.py:31
  520.8 11.0 %convolution_convert_fusion.1 = bf16[2048,1408]{1,0:T(8,128)(2,1)} fusion(bf16[1024,2048]{1,0:T(8,128)(2,1)} %maximum_dynamic-update-slice_fusion.1, bf16[1024,1408]{1,0:T(8,128)(2,1)S(1)} %copy-done.31), kind=kOutput, calls=%fused_computation.9 | convolution fusion | flops 5908463616 | bytes 12845056 | tf_op jit(solution)/shard_map/dot_general | solution.py:31
  533.6 10.9 %convolution_convert_fusion = bf16[1408,2048]{1,0:T(8,128)(2,1)} fusion(bf16[1024,1408]{1,0:T(8,128)(2,1)S(1)} %copy-done.29, bf16[1024,2048]{1,0:T(8,128)(2,1)} %maximum_dynamic-update-slice_fusion.2), kind=kOutput, calls=%fused_computation.8 | convolution fusion | flops 5908463616 | bytes 12845056 | tf_op jit(solution)/shard_map/dot_general | solution.py:31
  546.4 8.9 %fusion.43 = f32[1024,2048]{1,0:T(8,128)S(1)} fusion(bf16[1024,1536]{1,0:T(8,128)(2,1)S(1)} %copy-done.5, bf16[2048,1536]{1,0:T(8,128)(2,1)} %all-gather.7.cloned.1.call-done), kind=kOutput, calls=%fused_computation.150 | convolution fusion | flops 6442450944 | bytes 17825792 | tf_op jit(solution)/shard_map/dot_general | solution.py:27
  557.2 9.4 %collective-permute-done.31 = bf16[128,2048]{1,0:T(8,128)(2,1)S(1)} collective-permute-done((bf16[128,2048]{1,0:T(8,128)(2,1)S(1)}, bf16[128,2048]{1,0:T(8,128)(2,1)S(1)}, u32[]{:S(2)}, u32[]{:S(2)}) %collective-permute-start.31) | collective-permute-done | bytes 524320 | tf_op jit(solution)/shard_map/ppermute | solution.py:59
  573.9 16.6 %collective-permute-done.34 = bf16[256,2048]{1,0:T(8,128)(2,1)} collective-permute-done((bf16[256,2048]{1,0:T(8,128)(2,1)}, bf16[256,2048]{1,0:T(8,128)(2,1)}, u32[]{:S(2)}, u32[]{:S(2)}) %collective-permute-start.34) | collective-permute-done | bytes 1048608 | tf_op jit(solution)/shard_map/ppermute | solution.py:59
  591.9 5.3 fusion.17
  602.9 3.7 fusion.16
  608.4 40.0 %all-reduce.1 = f32[32,448]{1,0:T(8,128)S(1)} all-reduce(f32[32,448]{1,0:T(8,128)S(1)} %concatenate.81), channel_id=3, replica_groups=mesh['dp'=8,'ctx'=4] {'dp','ctx'}, use_global_device_ids=true, to_apply=%region_15.16.clone | all-reduce | flops 14336 | bytes 114688
  651.4 20.2 %reduce-scatter.10.cloned.1.call-done = bf16[256,1408]{1,0:T(8,128)(2,1)} async-done(((bf16[2048,1408]{1,0:T(8,128)(2,1)}), bf16[256,1408]{1,0:T(8,128)(2,1)}) %reduce-scatter.10.cloned.1.call-update) | async-done | bytes 720912 | tf_op jit(solution)/shard_map/reduce_scatter | solution.py:387
  673.9 63.2 %reduce-scatter.12.cloned.1.call-done = bf16[256,1408]{1,0:T(8,128)(2,1)} async-done(((bf16[2048,1408]{1,0:T(8,128)(2,1)}), bf16[256,1408]{1,0:T(8,128)(2,1)}) %reduce-scatter.12.cloned.1.call-update) | async-done | bytes 720912 | tf_op jit(solution)/shard_map/reduce_scatter | solution.py:388
  739.4 63.1 %reduce-scatter.14.cloned.1.call-done = bf16[1408,256]{1,0:T(8,128)(2,1)} async-done(((bf16[1408,2048]{1,0:T(8,128)(2,1)}), bf16[1408,256]{1,0:T(8,128)(2,1)}) %reduce-scatter.14.cloned.1.call-update) | async-done | bytes 720912 | tf_op jit(solution)/shard_map/reduce_scatter | solution.py:386
  809.4 4.2 collective-permute-done.36
  815.0 4.6 reshape.161
  819.5 3.9 copy.44
  823.4 3.2 reshape.160
  (254 shorter events, 124.8 us)
Async XLA Ops:
  7.2 122.3 %all-gather.7.cloned.1.call-start = ((), (), s32[]{:S(2)}) async-start(), calls=%async_computation.5 | async-start | bytes 7077888 | tf_op jit(solution)/shard_map/all_gather | solution.py:341
  11.0 17.9 %copy-start.8 = (bf16[1,256,2048]{2,1,0:T(8,128)(2,1)S(1)}, bf16[1,256,2048]{2,1,0:T(8,128)(2,1)}, u32[]{:S(2)}) copy-start(bf16[1,256,2048]{2,1,0:T(8,128)(2,1)} %param.13) | copy-start | bytes 3145732
  11.0 20.0 %copy-start.21 = (bf16[64]{0:T(256)(128)(2,1)S(1)}, bf16[64]{0:T(256)(128)(2,1)}, u32[]{:S(2)}) copy-start(bf16[64]{0:T(256)(128)(2,1)} %param.15) | copy-start | bytes 388
  11.0 20.0 %copy-start.22 = (bf16[64]{0:T(256)(128)(2,1)S(1)}, bf16[64]{0:T(256)(128)(2,1)}, u32[]{:S(2)}) copy-start(bf16[64]{0:T(256)(128)(2,1)} %param.16) | copy-start | bytes 388
  11.0 20.0 %copy-start.23 = (bf16[64]{0:T(256)(128)(2,1)S(1)}, bf16[64]{0:T(256)(128)(2,1)}, u32[]{:S(2)}) copy-start(bf16[64]{0:T(256)(128)(2,1)} %param.20) | copy-start | bytes 388
  11.0 20.0 %copy-start.24 = (bf16[64]{0:T(256)(128)(2,1)S(1)}, bf16[64]{0:T(256)(128)(2,1)}, u32[]{:S(2)}) copy-start(bf16[64]{0:T(256)(128)(2,1)} %param.21) | copy-start | bytes 388
  11.0 20.0 %copy-start.25 = (bf16[192]{0:T(256)(128)(2,1)S(1)}, bf16[192]{0:T(256)(128)(2,1)}, u32[]{:S(2)}) copy-start(bf16[192]{0:T(256)(128)(2,1)} %param.18) | copy-start | bytes 1156
  12.2 8.7 %collective-permute-start.4 = (bf16[1,64,1536]{2,1,0:T(8,128)(2,1)S(1)}, bf16[1,64,1536]{2,1,0:T(8,128)(2,1)S(1)}, u32[]{:S(2)}, u32[]{:S(2)}) collective-permute-start(bf16[1,64,1536]{2,1,0:T(8,128)(2,1)S(1)} %get-tuple-element.74), channel_id=1, source_target_pairs={{0,1},{1,0},{2,3},{3,2},{4,5},{5,4},{6,7},{7,6},{8,9},{9,8},{10,11... | collective-permute-start | bytes 589832 | tf_op jit(solution)/shard_map/ppermute | solution.py:59
  15.2 10.6 %collective-permute-start.5 = (bf16[1,64,1536]{2,1,0:T(8,128)(2,1)S(1)}, bf16[1,64,1536]{2,1,0:T(8,128)(2,1)S(1)}, u32[]{:S(2)}, u32[]{:S(2)}) collective-permute-start(bf16[1,64,1536]{2,1,0:T(8,128)(2,1)S(1)} %get-tuple-element.73), channel_id=1, source_target_pairs={{0,2},{1,3},{2,0},{3,1},{4,6},{5,7},{6,4},{7,5},{8,10},{9,11},{10,... | collective-permute-start | bytes 589832 | tf_op jit(solution)/shard_map/ppermute | solution.py:59
  16.7 9.1 %collective-permute-start.6 = (bf16[1,64,1536]{2,1,0:T(8,128)(2,1)S(1)}, bf16[1,64,1536]{2,1,0:T(8,128)(2,1)S(1)}, u32[]{:S(2)}, u32[]{:S(2)}) collective-permute-start(bf16[1,64,1536]{2,1,0:T(8,128)(2,1)S(1)} %get-tuple-element.72), channel_id=1, source_target_pairs={{0,3},{1,2},{2,1},{3,0},{4,7},{5,6},{6,5},{7,4},{8,11},{9,10},{10,... | collective-permute-start | bytes 589832 | tf_op jit(solution)/shard_map/ppermute | solution.py:59
  26.7 137.6 %all-gather.9.cloned.1.call-start = ((), (), s32[]{:S(2)}) async-start(), calls=%async_computation.6 | async-start | bytes 2359296 | tf_op jit(solution)/shard_map/all_gather | solution.py:345
  27.5 251.6 %all-gather.11.cloned.1.call-start = ((), (), s32[]{:S(2)}) async-start(), calls=%async_computation.7 | async-start | bytes 6488064 | tf_op jit(solution)/shard_map/all_gather | solution.py:351
  28.2 263.0 %all-gather.13.cloned.1.call-start = ((), (), s32[]{:S(2)}) async-start(), calls=%async_computation.8 | async-start | bytes 6488064 | tf_op jit(solution)/shard_map/all_gather | solution.py:352
  28.8 276.8 %all-gather.15.cloned.1.call-start = ((), (), s32[]{:S(2)}) async-start(), calls=%async_computation.9 | async-start | bytes 6488064 | tf_op jit(solution)/shard_map/all_gather | solution.py:353
  28.9 79.8 %collective-permute-start = (bf16[256,2048]{1,0:T(8,128)(2,1)S(1)}, bf16[256,2048]{1,0:T(8,128)(2,1)}, u32[]{:S(2)}, u32[]{:S(2)}) collective-permute-start(bf16[256,2048]{1,0:T(8,128)(2,1)S(1)} %bitcast.71), channel_id=1, source_target_pairs={{0,1},{1,0},{2,3},{3,2},{4,5},{5,4},{6,7},{7,6},{8,9},{9,8},{10,11... | collective-permute-start | bytes 3145736 | tf_op jit(solution)/shard_map/ppermute | solution.py:59
  30.1 74.3 %collective-permute-start.1 = (bf16[256,2048]{1,0:T(8,128)(2,1)S(1)}, bf16[256,2048]{1,0:T(8,128)(2,1)}, u32[]{:S(2)}, u32[]{:S(2)}) collective-permute-start(bf16[256,2048]{1,0:T(8,128)(2,1)S(1)} %bitcast.72), channel_id=1, source_target_pairs={{0,2},{1,3},{2,0},{3,1},{4,6},{5,7},{6,4},{7,5},{8,10},{9,11},{10,... | collective-permute-start | bytes 3145736 | tf_op jit(solution)/shard_map/ppermute | solution.py:59
  106.3 13.6 %collective-permute-start.3 = (bf16[128,2048]{1,0:T(8,128)(2,1)}, bf16[128,2048]{1,0:T(8,128)(2,1)S(1)}, u32[]{:S(2)}, u32[]{:S(2)}) collective-permute-start(bf16[128,2048]{1,0:T(8,128)(2,1)} %slice.197), channel_id=1, source_target_pairs={{0,1},{1,0},{2,3},{3,2},{4,5},{5,4},{6,7},{7,6},{8,9},{9,8},{10,11... | collective-permute-start | bytes 1572872 | tf_op jit(solution)/shard_map/ppermute | solution.py:59
  109.7 12.5 %collective-permute-start.2 = (bf16[128,2048]{1,0:T(8,128)(2,1)S(1)}, bf16[128,2048]{1,0:T(8,128)(2,1)S(1)}, u32[]{:S(2)}, u32[]{:S(2)}) collective-permute-start(bf16[128,2048]{1,0:T(8,128)(2,1)S(1)} %slice.196), channel_id=1, source_target_pairs={{0,2},{1,3},{2,0},{3,1},{4,6},{5,7},{6,4},{7,5},{8,10},{9,11},{10,... | collective-permute-start | bytes 1572872 | tf_op jit(solution)/shard_map/ppermute | solution.py:59
  172.8 11.1 %collective-permute-start.7 = (bf16[128,2048]{1,0:T(8,128)(2,1)}, bf16[128,2048]{1,0:T(8,128)(2,1)}, u32[]{:S(2)}, u32[]{:S(2)}) collective-permute-start(bf16[128,2048]{1,0:T(8,128)(2,1)} %get-tuple-element.66), channel_id=1, source_target_pairs={{0,2},{1,3},{2,0},{3,1},{4,6},{5,7},{6,4},{7,5},{8,10},{9,11},{10,... | collective-permute-start | bytes 1572872 | tf_op jit(solution)/shard_map/ppermute | solution.py:59
  173.2 10.7 %collective-permute-start.9 = (bf16[128,2048]{1,0:T(8,128)(2,1)}, bf16[128,2048]{1,0:T(8,128)(2,1)}, u32[]{:S(2)}, u32[]{:S(2)}) collective-permute-start(bf16[128,2048]{1,0:T(8,128)(2,1)} %get-tuple-element.67), channel_id=1, source_target_pairs={{0,1},{1,0},{2,3},{3,2},{4,5},{5,4},{6,7},{7,6},{8,9},{9,8},{10,11... | collective-permute-start | bytes 1572872 | tf_op jit(solution)/shard_map/ppermute | solution.py:59
  174.4 424.0 %reduce-scatter.6.cloned.1.call-start = ((), (), s32[]{:S(2)}) async-start(), calls=%async_computation.10 | async-start | bytes 7077888 | tf_op jit(solution)/shard_map/reduce_scatter | solution.py:407
  187.1 26.4 %collective-permute-start.10 = (bf16[256,2048]{1,0:T(8,128)(2,1)}, bf16[256,2048]{1,0:T(8,128)(2,1)}, u32[]{:S(2)}, u32[]{:S(2)}) collective-permute-start(bf16[256,2048]{1,0:T(8,128)(2,1)} %pad_maximum_fusion.2), channel_id=1, source_target_pairs={{0,2},{1,3},{2,0},{3,1},{4,6},{5,7},{6,4},{7,5},{8,10},{9,11},{10,... | collective-permute-start | bytes 3145736 | tf_op jit(solution)/shard_map/ppermute | solution.py:59
  189.8 26.4 %collective-permute-start.8 = (bf16[256,2048]{1,0:T(8,128)(2,1)}, bf16[256,2048]{1,0:T(8,128)(2,1)}, u32[]{:S(2)}, u32[]{:S(2)}) collective-permute-start(bf16[256,2048]{1,0:T(8,128)(2,1)} %pad_maximum_fusion.1), channel_id=1, source_target_pairs={{0,1},{1,0},{2,3},{3,2},{4,5},{5,4},{6,7},{7,6},{8,9},{9,8},{10,11... | collective-permute-start | bytes 3145736 | tf_op jit(solution)/shard_map/ppermute | solution.py:59
  190.6 48.2 %collective-permute-start.19 = (bf16[256,2048]{1,0:T(8,128)(2,1)}, bf16[256,2048]{1,0:T(8,128)(2,1)}, u32[]{:S(2)}, u32[]{:S(2)}) collective-permute-start(bf16[256,2048]{1,0:T(8,128)(2,1)} %bitcast.10), channel_id=1, source_target_pairs={{0,1},{1,0},{2,3},{3,2},{4,5},{5,4},{6,7},{7,6},{8,9},{9,8},{10,11... | collective-permute-start | bytes 3145736 | tf_op jit(solution)/shard_map/ppermute | solution.py:59
  191.9 44.1 %collective-permute-start.20 = (bf16[256,2048]{1,0:T(8,128)(2,1)}, bf16[256,2048]{1,0:T(8,128)(2,1)}, u32[]{:S(2)}, u32[]{:S(2)}) collective-permute-start(bf16[256,2048]{1,0:T(8,128)(2,1)} %bitcast.10), channel_id=1, source_target_pairs={{0,2},{1,3},{2,0},{3,1},{4,6},{5,7},{6,4},{7,5},{8,10},{9,11},{10,... | collective-permute-start | bytes 3145736 | tf_op jit(solution)/shard_map/ppermute | solution.py:59
  194.0 26.6 %copy-start.17 = (f32[256]{0:T(256)}, f32[256]{0:T(256)S(1)}, u32[]{:S(2)}) copy-start(f32[256]{0:T(256)S(1)} %broadcast_multiply_fusion.4) | copy-start | bytes 3076
  224.7 33.6 %collective-permute-start.12 = (bf16[256,2048]{1,0:T(8,128)(2,1)S(1)}, bf16[256,2048]{1,0:T(8,128)(2,1)S(1)}, u32[]{:S(2)}, u32[]{:S(2)}) collective-permute-start(bf16[256,2048]{1,0:T(8,128)(2,1)S(1)} %get-tuple-element.36), channel_id=1, source_target_pairs={{0,2},{1,3},{2,0},{3,1},{4,6},{5,7},{6,4},{7,5},{8,10},{9,11},{10,... | collective-permute-start | bytes 3145736 | tf_op jit(solution)/shard_map/ppermute | solution.py:59
  224.9 36.2 %collective-permute-start.11 = (bf16[256,2048]{1,0:T(8,128)(2,1)S(1)}, bf16[256,2048]{1,0:T(8,128)(2,1)S(1)}, u32[]{:S(2)}, u32[]{:S(2)}) collective-permute-start(bf16[256,2048]{1,0:T(8,128)(2,1)S(1)} %get-tuple-element.36), channel_id=1, source_target_pairs={{0,1},{1,0},{2,3},{3,2},{4,5},{5,4},{6,7},{7,6},{8,9},{9,8},{10,11... | collective-permute-start | bytes 3145736 | tf_op jit(solution)/shard_map/ppermute | solution.py:59
  237.0 35.3 %collective-permute-start.22 = (bf16[128,2048]{1,0:T(8,128)(2,1)S(1)}, bf16[128,2048]{1,0:T(8,128)(2,1)S(1)}, u32[]{:S(2)}, u32[]{:S(2)}) collective-permute-start(bf16[128,2048]{1,0:T(8,128)(2,1)S(1)} %slice.210), channel_id=1, source_target_pairs={{0,1},{1,0},{2,3},{3,2},{4,5},{5,4},{6,7},{7,6},{8,9},{9,8},{10,11... | collective-permute-start | bytes 1572872 | tf_op jit(solution)/shard_map/ppermute | solution.py:59
  239.8 32.5 %collective-permute-start.21 = (bf16[128,2048]{1,0:T(8,128)(2,1)S(1)}, bf16[128,2048]{1,0:T(8,128)(2,1)S(1)}, u32[]{:S(2)}, u32[]{:S(2)}) collective-permute-start(bf16[128,2048]{1,0:T(8,128)(2,1)S(1)} %slice.209), channel_id=1, source_target_pairs={{0,2},{1,3},{2,0},{3,1},{4,6},{5,7},{6,4},{7,5},{8,10},{9,11},{10,... | collective-permute-start | bytes 1572872 | tf_op jit(solution)/shard_map/ppermute | solution.py:59
  258.3 19.7 %collective-permute-start.14 = (bf16[128,2048]{1,0:T(8,128)(2,1)S(1)}, bf16[128,2048]{1,0:T(8,128)(2,1)S(1)}, u32[]{:S(2)}, u32[]{:S(2)}) collective-permute-start(bf16[128,2048]{1,0:T(8,128)(2,1)S(1)} %slice.206), channel_id=1, source_target_pairs={{0,1},{1,0},{2,3},{3,2},{4,5},{5,4},{6,7},{7,6},{8,9},{9,8},{10,11... | collective-permute-start | bytes 1572872 | tf_op jit(solution)/shard_map/ppermute | solution.py:59
  261.1 16.9 %collective-permute-start.13 = (bf16[128,2048]{1,0:T(8,128)(2,1)S(1)}, bf16[128,2048]{1,0:T(8,128)(2,1)S(1)}, u32[]{:S(2)}, u32[]{:S(2)}) collective-permute-start(bf16[128,2048]{1,0:T(8,128)(2,1)S(1)} %slice.205), channel_id=1, source_target_pairs={{0,2},{1,3},{2,0},{3,1},{4,6},{5,7},{6,4},{7,5},{8,10},{9,11},{10,... | collective-permute-start | bytes 1572872 | tf_op jit(solution)/shard_map/ppermute | solution.py:59
  321.2 12.9 %copy-start.30 = (bf16[1024,1408]{1,0:T(8,128)(2,1)}, bf16[1024,1408]{1,0:T(8,128)(2,1)S(1)}, u32[]{:S(2)}) copy-start(bf16[1024,1408]{1,0:T(8,128)(2,1)S(1)} %get-tuple-element.39) | copy-start | bytes 8650756
  321.2 12.9 %copy-start.26 = (bf16[2048,1408]{1,0:T(8,128)(2,1)S(1)}, bf16[2048,1408]{1,0:T(8,128)(2,1)}, u32[]{:S(2)}) copy-start(bf16[2048,1408]{1,0:T(8,128)(2,1)} %all-gather.13.cloned.1.call-done) | copy-start | bytes 17301508
  343.7 14.1 %collective-permute-start.23 = (bf16[128,2048]{1,0:T(8,128)(2,1)S(1)}, bf16[128,2048]{1,0:T(8,128)(2,1)S(1)}, u32[]{:S(2)}, u32[]{:S(2)}) collective-permute-start(bf16[128,2048]{1,0:T(8,128)(2,1)S(1)} %get-tuple-element.62), channel_id=1, source_target_pairs={{0,2},{1,3},{2,0},{3,1},{4,6},{5,7},{6,4},{7,5},{8,10},{9,11},{10,... | collective-permute-start | bytes 1572872 | tf_op jit(solution)/shard_map/ppermute | solution.py:59
  345.2 14.5 %collective-permute-start.25 = (bf16[128,2048]{1,0:T(8,128)(2,1)S(1)}, bf16[128,2048]{1,0:T(8,128)(2,1)S(1)}, u32[]{:S(2)}, u32[]{:S(2)}) collective-permute-start(bf16[128,2048]{1,0:T(8,128)(2,1)S(1)} %get-tuple-element.63), channel_id=1, source_target_pairs={{0,1},{1,0},{2,3},{3,2},{4,5},{5,4},{6,7},{7,6},{8,9},{9,8},{10,11... | collective-permute-start | bytes 1572872 | tf_op jit(solution)/shard_map/ppermute | solution.py:59
  355.6 14.9 %collective-permute-start.15 = (bf16[128,2048]{1,0:T(8,128)(2,1)S(1)}, bf16[128,2048]{1,0:T(8,128)(2,1)S(1)}, u32[]{:S(2)}, u32[]{:S(2)}) collective-permute-start(bf16[128,2048]{1,0:T(8,128)(2,1)S(1)} %get-tuple-element.64), channel_id=1, source_target_pairs={{0,2},{1,3},{2,0},{3,1},{4,6},{5,7},{6,4},{7,5},{8,10},{9,11},{10,... | collective-permute-start | bytes 1572872 | tf_op jit(solution)/shard_map/ppermute | solution.py:59
  356.2 14.9 %collective-permute-start.17 = (bf16[128,2048]{1,0:T(8,128)(2,1)S(1)}, bf16[128,2048]{1,0:T(8,128)(2,1)S(1)}, u32[]{:S(2)}, u32[]{:S(2)}) collective-permute-start(bf16[128,2048]{1,0:T(8,128)(2,1)S(1)} %get-tuple-element.65), channel_id=1, source_target_pairs={{0,1},{1,0},{2,3},{3,2},{4,5},{5,4},{6,7},{7,6},{8,9},{9,8},{10,11... | collective-permute-start | bytes 1572872 | tf_op jit(solution)/shard_map/ppermute | solution.py:59
  360.2 32.8 %collective-permute-start.26 = (bf16[256,2048]{1,0:T(8,128)(2,1)S(1)}, bf16[256,2048]{1,0:T(8,128)(2,1)S(1)}, u32[]{:S(2)}, u32[]{:S(2)}) collective-permute-start(bf16[256,2048]{1,0:T(8,128)(2,1)S(1)} %pad_maximum_fusion.6), channel_id=1, source_target_pairs={{0,2},{1,3},{2,0},{3,1},{4,6},{5,7},{6,4},{7,5},{8,10},{9,11},{10,... | collective-permute-start | bytes 3145736 | tf_op jit(solution)/shard_map/ppermute | solution.py:59
  360.5 54.8 %copy-start.7 = (f32[256,2048]{1,0:T(8,128)S(1)}, f32[256,2048]{1,0:T(8,128)}, u32[]{:S(2)}) copy-start(f32[256,2048]{1,0:T(8,128)} %copy-done.6) | copy-start | bytes 6291460
  360.5 33.0 %collective-permute-start.24 = (bf16[256,2048]{1,0:T(8,128)(2,1)S(1)}, bf16[256,2048]{1,0:T(8,128)(2,1)S(1)}, u32[]{:S(2)}, u32[]{:S(2)}) collective-permute-start(bf16[256,2048]{1,0:T(8,128)(2,1)S(1)} %pad_maximum_fusion.5), channel_id=1, source_target_pairs={{0,1},{1,0},{2,3},{3,2},{4,5},{5,4},{6,7},{7,6},{8,9},{9,8},{10,11... | collective-permute-start | bytes 3145736 | tf_op jit(solution)/shard_map/ppermute | solution.py:59
  371.5 42.7 %collective-permute-start.18 = (bf16[256,2048]{1,0:T(8,128)(2,1)S(1)}, bf16[256,2048]{1,0:T(8,128)(2,1)S(1)}, u32[]{:S(2)}, u32[]{:S(2)}) collective-permute-start(bf16[256,2048]{1,0:T(8,128)(2,1)S(1)} %pad_maximum_fusion.4), channel_id=1, source_target_pairs={{0,2},{1,3},{2,0},{3,1},{4,6},{5,7},{6,4},{7,5},{8,10},{9,11},{10,... | collective-permute-start | bytes 3145736 | tf_op jit(solution)/shard_map/ppermute | solution.py:59
  373.1 42.2 %collective-permute-start.16 = (bf16[256,2048]{1,0:T(8,128)(2,1)S(1)}, bf16[256,2048]{1,0:T(8,128)(2,1)}, u32[]{:S(2)}, u32[]{:S(2)}) collective-permute-start(bf16[256,2048]{1,0:T(8,128)(2,1)S(1)} %pad_maximum_fusion.3), channel_id=1, source_target_pairs={{0,1},{1,0},{2,3},{3,2},{4,5},{5,4},{6,7},{7,6},{8,9},{9,8},{10,11... | collective-permute-start | bytes 3145736 | tf_op jit(solution)/shard_map/ppermute | solution.py:59
  423.2 38.3 %copy-start.27 = (bf16[512,2048]{1,0:T(8,128)(2,1)S(1)}, bf16[512,2048]{1,0:T(8,128)(2,1)}, u32[]{:S(2)}) copy-start(bf16[512,2048]{1,0:T(8,128)(2,1)} %all-gather.9.cloned.1.call-done) | copy-start | bytes 6291460
  423.2 24.4 %collective-permute-start.28 = (bf16[256,2048]{1,0:T(8,128)(2,1)S(1)}, bf16[256,2048]{1,0:T(8,128)(2,1)S(1)}, u32[]{:S(2)}, u32[]{:S(2)}) collective-permute-start(bf16[256,2048]{1,0:T(8,128)(2,1)S(1)} %get-tuple-element.32), channel_id=1, source_target_pairs={{0,2},{1,3},{2,0},{3,1},{4,6},{5,7},{6,4},{7,5},{8,10},{9,11},{10,... | collective-permute-start | bytes 3145736 | tf_op jit(solution)/shard_map/ppermute | solution.py:59
  423.8 25.4 %collective-permute-start.27 = (bf16[256,2048]{1,0:T(8,128)(2,1)S(1)}, bf16[256,2048]{1,0:T(8,128)(2,1)S(1)}, u32[]{:S(2)}, u32[]{:S(2)}) collective-permute-start(bf16[256,2048]{1,0:T(8,128)(2,1)S(1)} %get-tuple-element.32), channel_id=1, source_target_pairs={{0,1},{1,0},{2,3},{3,2},{4,5},{5,4},{6,7},{7,6},{8,9},{9,8},{10,11... | collective-permute-start | bytes 3145736 | tf_op jit(solution)/shard_map/ppermute | solution.py:59
  447.6 12.3 %collective-permute-start.30 = (bf16[128,2048]{1,0:T(8,128)(2,1)S(1)}, bf16[128,2048]{1,0:T(8,128)(2,1)S(1)}, u32[]{:S(2)}, u32[]{:S(2)}) collective-permute-start(bf16[128,2048]{1,0:T(8,128)(2,1)S(1)} %slice.214), channel_id=1, source_target_pairs={{0,1},{1,0},{2,3},{3,2},{4,5},{5,4},{6,7},{7,6},{8,9},{9,8},{10,11... | collective-permute-start | bytes 1572872 | tf_op jit(solution)/shard_map/ppermute | solution.py:59
  449.3 12.1 %collective-permute-start.29 = (bf16[128,2048]{1,0:T(8,128)(2,1)S(1)}, bf16[128,2048]{1,0:T(8,128)(2,1)S(1)}, u32[]{:S(2)}, u32[]{:S(2)}) collective-permute-start(bf16[128,2048]{1,0:T(8,128)(2,1)S(1)} %slice.213), channel_id=1, source_target_pairs={{0,2},{1,3},{2,0},{3,1},{4,6},{5,7},{6,4},{7,5},{8,10},{9,11},{10,... | collective-permute-start | bytes 1572872 | tf_op jit(solution)/shard_map/ppermute | solution.py:59
  501.4 148.2 %reduce-scatter.8.cloned.1.call-start = ((), (), s32[]{:S(2)}) async-start(), calls=%async_computation.11 | async-start | bytes 2359296 | tf_op jit(solution)/shard_map/reduce_scatter | solution.py:396
  507.3 164.3 %reduce-scatter.10.cloned.1.call-start = ((), (), s32[]{:S(2)}) async-start(), calls=%async_computation.12 | async-start | bytes 6488064 | tf_op jit(solution)/shard_map/reduce_scatter | solution.py:387
  518.9 218.2 %reduce-scatter.12.cloned.1.call-start = ((), (), s32[]{:S(2)}) async-start(), calls=%async_computation.13 | async-start | bytes 6488064 | tf_op jit(solution)/shard_map/reduce_scatter | solution.py:388
  531.8 270.8 %reduce-scatter.14.cloned.1.call-start = ((), (), s32[]{:S(2)}) async-start(), calls=%async_computation.14 | async-start | bytes 6488064 | tf_op jit(solution)/shard_map/reduce_scatter | solution.py:386
  555.6 11.0 %collective-permute-start.31 = (bf16[128,2048]{1,0:T(8,128)(2,1)S(1)}, bf16[128,2048]{1,0:T(8,128)(2,1)S(1)}, u32[]{:S(2)}, u32[]{:S(2)}) collective-permute-start(bf16[128,2048]{1,0:T(8,128)(2,1)S(1)} %get-tuple-element.59), channel_id=1, source_target_pairs={{0,2},{1,3},{2,0},{3,1},{4,6},{5,7},{6,4},{7,5},{8,10},{9,11},{10,... | collective-permute-start | bytes 1572872 | tf_op jit(solution)/shard_map/ppermute | solution.py:59
  555.7 11.4 %collective-permute-start.33 = (bf16[128,2048]{1,0:T(8,128)(2,1)S(1)}, bf16[128,2048]{1,0:T(8,128)(2,1)S(1)}, u32[]{:S(2)}, u32[]{:S(2)}) collective-permute-start(bf16[128,2048]{1,0:T(8,128)(2,1)S(1)} %get-tuple-element.60), channel_id=1, source_target_pairs={{0,1},{1,0},{2,3},{3,2},{4,5},{5,4},{6,7},{7,6},{8,9},{9,8},{10,11... | collective-permute-start | bytes 1572872 | tf_op jit(solution)/shard_map/ppermute | solution.py:59
  557.1 14.5 %copy-start.20 = (f32[256]{0:T(256)S(1)}, f32[256]{0:T(256)}, u32[]{:S(2)}) copy-start(f32[256]{0:T(256)} %get-tuple-element.61) | copy-start | bytes 3076
  557.2 34.8 %copy-start.9 = (bf16[1,256,2048]{2,1,0:T(8,128)(2,1)S(1)}, bf16[1,256,2048]{2,1,0:T(8,128)(2,1)}, u32[]{:S(2)}) copy-start(bf16[1,256,2048]{2,1,0:T(8,128)(2,1)} %param.13) | copy-start | bytes 3145732
  557.2 34.7 %copy-start.18 = (f32[256]{0:T(256)S(1)}, f32[256]{0:T(256)}, u32[]{:S(2)}) copy-start(f32[256]{0:T(256)} %copy-done.17) | copy-start | bytes 3076
  568.5 22.1 %collective-permute-start.34 = (bf16[256,2048]{1,0:T(8,128)(2,1)}, bf16[256,2048]{1,0:T(8,128)(2,1)}, u32[]{:S(2)}, u32[]{:S(2)}) collective-permute-start(bf16[256,2048]{1,0:T(8,128)(2,1)} %pad_maximum_fusion.8), channel_id=1, source_target_pairs={{0,2},{1,3},{2,0},{3,1},{4,6},{5,7},{6,4},{7,5},{8,10},{9,11},{10,... | collective-permute-start | bytes 3145736 | tf_op jit(solution)/shard_map/ppermute | solution.py:59
  570.7 21.2 %collective-permute-start.32 = (bf16[256,2048]{1,0:T(8,128)(2,1)}, bf16[256,2048]{1,0:T(8,128)(2,1)}, u32[]{:S(2)}, u32[]{:S(2)}) collective-permute-start(bf16[256,2048]{1,0:T(8,128)(2,1)} %pad_maximum_fusion.7), channel_id=1, source_target_pairs={{0,1},{1,0},{2,3},{3,2},{4,5},{5,4},{6,7},{7,6},{8,9},{9,8},{10,11... | collective-permute-start | bytes 3145736 | tf_op jit(solution)/shard_map/ppermute | solution.py:59
  571.6 26.7 %copy-start.19 = (f32[256]{0:T(256)}, f32[256]{0:T(256)S(1)}, u32[]{:S(2)}) copy-start(f32[256]{0:T(256)S(1)} %add_rsqrt_fusion.1) | copy-start | bytes 3076
  573.9 29.0 %copy-start.10 = (f32[256,2048]{1,0:T(8,128)S(1)}, f32[256,2048]{1,0:T(8,128)}, u32[]{:S(2)}) copy-start(f32[256,2048]{1,0:T(8,128)} %get-tuple-element.33) | copy-start | bytes 6291460
  601.3 206.5 %collective-permute-start.35 = (bf16[1,64,1536]{2,1,0:T(8,128)(2,1)}, bf16[1,64,1536]{2,1,0:T(8,128)(2,1)}, u32[]{:S(2)}, u32[]{:S(2)}) collective-permute-start(bf16[1,64,1536]{2,1,0:T(8,128)(2,1)} %get-tuple-element.70), channel_id=1, source_target_pairs={{0,1},{1,0},{2,3},{3,2},{4,5},{5,4},{6,7},{7,6},{8,9},{9,8},{10,11... | collective-permute-start | bytes 589832 | tf_op jit(solution)/shard_map/ppermute | solution.py:59
  804.9 8.7 %collective-permute-start.36 = (bf16[1,64,1536]{2,1,0:T(8,128)(2,1)S(1)}, bf16[1,64,1536]{2,1,0:T(8,128)(2,1)S(1)}, u32[]{:S(2)}, u32[]{:S(2)}) collective-permute-start(bf16[1,64,1536]{2,1,0:T(8,128)(2,1)S(1)} %get-tuple-element.69), channel_id=1, source_target_pairs={{0,2},{1,3},{2,0},{3,1},{4,6},{5,7},{6,4},{7,5},{8,10},{9,11},{10,... | collective-permute-start | bytes 589832 | tf_op jit(solution)/shard_map/ppermute | solution.py:59
  806.3 7.9 collective-permute-start.37
  (17 other events, 62.2 us)
Sparse Core Ops, SparseCore 0:
  26.9 65.9 all-gather.6
  94.5 27.8 all-gather.8
  124.0 59.9 all-gather.10
  185.4 59.0 all-gather.12
  246.0 59.5 all-gather.14
  501.5 66.6 reduce-scatter.5
  570.5 33.9 reduce-scatter.7
  606.8 64.7 reduce-scatter.9
  673.9 63.1 reduce-scatter.11
  739.3 63.2 reduce-scatter.13

commit v2 on v1

--- a/solution.py
+++ b/solution.py
@@ -80,7 +80,7 @@
     return full
 
 
-def scatter_ctx(partial, n):
+def scatter_ctx(partial, n, meanwhile=None):
     me = lax.axis_index("ctx")
     size = partial.shape[0] // n
 
@@ -96,6 +96,8 @@
     far = block(3).astype(bf16)
     low = hop(far[:half], n, 1).astype(f32)
     high = hop(far[half:], n, 2).astype(f32)
+    if meanwhile is not None:
+        partial, _ = lax.optimization_barrier((partial, meanwhile))
     one = block(1).astype(f32)
     two = block(2).astype(f32)
     to_one = jnp.concatenate([one[:half], one[half:] + high], axis=0).astype(bf16)
@@ -112,6 +114,354 @@
         sent = lax.dynamic_slice_in_dim(blocks, me ^ k, 1, 0)
         got = lax.dynamic_update_slice_in_dim(got, hop(sent, n, k), me ^ k, 0)
     return got
+
+
+MESH = pl.DeviceIdType.MESH
+ANY = pl.BlockSpec(memory_space=pl.ANY)
+
+
+class Place:
+    def __init__(self, dp):
+        self.row = lax.axis_index("dp")
+        self.col = lax.axis_index("ctx")
+        self.lines = dp // 2
+        self.line = self.row // 2
+        self.core = self.row % 2
+        self.twin = (self.row + 1 - 2 * self.core, self.col)
+
+    def other(self, k):
+        col, bit = self.col, 1
+        while bit <= k:
+            if k & bit:
+                col = col + bit * (1 - 2 * ((self.col // bit) % 2))
+            bit *= 2
+        return col
+
+    def across(self, k):
+        return (self.row, self.other(k))
+
+    def above(self):
+        return (self.row + 2, self.col)
+
+    def below(self):
+        return (self.row - 2, self.col)
+
+
+def greet(place, ctx, column=False):
+    barrier = pltpu.get_barrier_semaphore()
+    for k in range(1, ctx):
+        pl.semaphore_signal(barrier, 1, device_id=place.across(k), device_id_type=MESH)
+    if not column:
+        pl.semaphore_wait(barrier, ctx - 1)
+        return
+    pl.semaphore_signal(barrier, 1, device_id=place.twin, device_id_type=MESH)
+
+    @pl.when(place.line > 0)
+    def _():
+        pl.semaphore_signal(barrier, 1, device_id=place.below(), device_id_type=MESH)
+
+    @pl.when(place.line < place.lines - 1)
+    def _():
+        pl.semaphore_signal(barrier, 1, device_id=place.above(), device_id_type=MESH)
+
+    peers = ctx + (place.line > 0).astype(jnp.int32) + (place.line < place.lines - 1).astype(jnp.int32)
+    pl.semaphore_wait(barrier, peers)
+
+
+def remote(src, dst, send, recv, device):
+    return pltpu.make_async_remote_copy(
+        src_ref=src, dst_ref=dst, send_sem=send, recv_sem=recv, device_id=device, device_id_type=MESH
+    )
+
+
+class LineGather:
+    def __init__(self, place, shard, sems):
+        self.place, self.shard, self.sems = place, shard, sems
+
+    def row(self, line):
+        return line * 2 + self.place.core
+
+    def up(self, hop):
+        part = self.shard(self.row(self.place.line - hop + 1))
+        return remote(part, part, self.sems.at[0, hop], self.sems.at[1, hop], self.place.above())
+
+    def down(self, hop):
+        part = self.shard(self.row(self.place.line + hop - 1))
+        return remote(part, part, self.sems.at[2, hop], self.sems.at[3, hop], self.place.below())
+
+    def over(self, at, row):
+        part = self.shard(row)
+        return remote(part, part, self.sems.at[4, at], self.sems.at[5, at], self.place.twin)
+
+    def sends_up(self, hop):
+        return (self.place.line - hop + 1 >= 0) & (self.place.line < self.place.lines - 1)
+
+    def sends_down(self, hop):
+        return (self.place.line + hop - 1 < self.place.lines) & (self.place.line > 0)
+
+    def send(self, hop):
+        place = self.place
+        pl.when(self.sends_up(hop))(lambda: self.up(hop).start())
+        pl.when(self.sends_down(hop))(lambda: self.down(hop).start())
+        if hop == 1:
+            self.over(0, place.row).start()
+
+    def receive(self, hop):
+        place = self.place
+
+        @pl.when(place.line - hop >= 0)
+        def _():
+            part = self.shard(self.row(place.line - hop))
+            remote(part, part, self.sems.at[0, hop], self.sems.at[1, hop], place.twin).wait_recv()
+            self.over(hop, self.row(place.line - hop)).start()
+
+        @pl.when(place.line + hop < place.lines)
+        def _():
+            part = self.shard(self.row(place.line + hop))
+            remote(part, part, self.sems.at[2, hop], self.sems.at[3, hop], place.twin).wait_recv()
+            self.over(place.lines - 1 + hop, self.row(place.line + hop)).start()
+
+    def finish(self):
+        place = self.place
+        self.over(0, place.row).wait_send()
+        other = 1 - 2 * place.core
+        remote(
+            self.shard(place.row + other), self.shard(place.row + other),
+            self.sems.at[4, 0], self.sems.at[5, 0], place.twin,
+        ).wait_recv()
+        for hop in range(1, place.lines):
+            pl.when(self.sends_up(hop))(lambda: self.up(hop).wait_send())
+            pl.when(self.sends_down(hop))(lambda: self.down(hop).wait_send())
+            for at, line, there in (
+                (hop, place.line - hop, place.line - hop >= 0),
+                (place.lines - 1 + hop, place.line + hop, place.line + hop < place.lines),
+            ):
+
+                @pl.when(there)
+                def _():
+                    row = self.row(line)
+                    self.over(at, row).wait_send()
+                    part = self.shard(row + other)
+                    remote(part, part, self.sems.at[4, at], self.sems.at[5, at], place.twin).wait_recv()
+
+    @staticmethod
+    def scratch(dp):
+        return pltpu.SemaphoreType.DMA((6, dp))
+
+
+class CtxGather:
+    def __init__(self, place, block, full, size, sems):
+        self.place, self.block, self.full, self.size, self.sems = place, block, full, size, sems
+
+    def rows(self, col, start=0, size=None):
+        size = self.size if size is None else size
+        return self.full.at[pl.ds(pl.multiple_of(col * self.size + start, size), size), :]
+
+    def copies(self):
+        place, half = self.place, self.size // 2
+        me = place.col
+        return [
+            remote(self.block, self.rows(me), self.sems.at[0, 0], self.sems.at[1, 0], place.across(1)),
+            remote(self.block, self.rows(me), self.sems.at[0, 1], self.sems.at[1, 1], place.across(2)),
+            remote(
+                self.rows(place.other(1), 0, half), self.rows(place.other(1), 0, half),
+                self.sems.at[0, 2], self.sems.at[1, 2], place.across(2),
+            ),
+            remote(
+                self.rows(place.other(2), half, half), self.rows(place.other(2), half, half),
+                self.sems.at[0, 3], self.sems.at[1, 3], place.across(1),
+            ),
+        ]
+
+    def arrivals(self):
+        place, half = self.place, self.size // 2
+        me = place.col
+        parts = [self.rows(place.other(1)), self.rows(place.other(2)), self.rows(place.other(3), 0, half), self.rows(place.other(3), half, half)]
+        return [
+            remote(part, part, self.sems.at[0, i], self.sems.at[1, i], place.across(1))
+            for i, part in enumerate(parts)
+        ]
+
+    def first(self):
+        copies = self.copies()
+        copies[0].start()
+        copies[1].start()
+
+    def second(self):
+        copies, arrivals = self.copies(), self.arrivals()
+        arrivals[0].wait_recv()
+        copies[2].start()
+        arrivals[1].wait_recv()
+        copies[3].start()
+
+    def finish(self):
+        copies, arrivals = self.copies(), self.arrivals()
+        arrivals[2].wait_recv()
+        arrivals[3].wait_recv()
+        for copy in copies:
+            copy.wait_send()
+
+    @staticmethod
+    def scratch():
+        return pltpu.SemaphoreType.DMA((2, 4))
+
+
+def opening_kernel(
+    dp, ctx,
+    small_ref, blocks_ref, out_weight_ref, rows_ref, cot_ref,
+    small_all, joined_all, out_all, rows_all, cot_all,
+    local_sem, swap_sem, line_small, line_joined, line_out, rows_sem, cot_sem,
+):
+    place = Place(dp)
+    greet(place, ctx, column=True)
+    me, row = place.col, place.row
+    depth = blocks_ref.shape[1]
+    length = rows_ref.shape[0]
+    rows_out = out_weight_ref.shape[0]
+
+    def joined_rows(row, col):
+        return joined_all.at[pl.ds(pl.multiple_of((row * ctx + col) * depth, depth), depth), :]
+
+    def joined_shard(row):
+        return joined_all.at[pl.ds(pl.multiple_of(row * (ctx * depth), ctx * depth), ctx * depth), :]
+
+    def out_shard(row):
+        return out_all.at[pl.ds(pl.multiple_of(row * rows_out, rows_out), rows_out), :]
+
+    local = [
+        pltpu.make_async_copy(small_ref, small_all.at[row, me], local_sem.at[0]),
+        pltpu.make_async_copy(blocks_ref.at[me], joined_rows(row, me), local_sem.at[1]),
+        pltpu.make_async_copy(out_weight_ref, out_shard(row), local_sem.at[2]),
+        pltpu.make_async_copy(rows_ref, rows_all.at[pl.ds(pl.multiple_of(me * length, length), length), :], local_sem.at[3]),
+        pltpu.make_async_copy(cot_ref, cot_all.at[pl.ds(pl.multiple_of(me * length, length), length), :], local_sem.at[4]),
+    ]
+    swaps, arrivals = [], []
+    for k in range(1, ctx):
+        swaps.append(remote(small_ref, small_all.at[row, me], swap_sem.at[0, k], swap_sem.at[1, k], place.across(k)))
+        swaps.append(
+            remote(blocks_ref.at[place.other(k)], joined_rows(row, me), swap_sem.at[2, k], swap_sem.at[3, k], place.across(k))
+        )
+        arrivals.append(
+            remote(small_ref, small_all.at[row, place.other(k)], swap_sem.at[0, k], swap_sem.at[1, k], place.across(k))
+        )
+        part = joined_rows(row, place.other(k))
+        arrivals.append(remote(part, part, swap_sem.at[2, k], swap_sem.at[3, k], place.across(k)))
+    for copy in swaps:
+        copy.start()
+    for copy in local:
+        copy.start()
+    rows_gather = CtxGather(place, rows_ref, rows_all, length, rows_sem)
+    cot_gather = CtxGather(place, cot_ref, cot_all, length, cot_sem)
+    lines = [
+        LineGather(place, lambda row: small_all.at[row], line_small),
+        LineGather(place, joined_shard, line_joined),
+        LineGather(place, out_shard, line_out),
+    ]
+    rows_gather.first()
+    for copy in local[:2]:
+        copy.wait()
+    for copy in arrivals:
+        copy.wait_recv()
+    lines[0].send(1)
+    lines[1].send(1)
+    local[2].wait()
+    lines[2].send(1)
+    rows_gather.second()
+    cot_gather.first()
+    for hop in range(1, place.lines):
+        for line in lines:
+            line.receive(hop)
+            if hop < place.lines - 1:
+                line.send(hop + 1)
+        if hop == 1:
+            cot_gather.second()
+    for line in lines:
+        line.finish()
+    rows_gather.finish()
+    cot_gather.finish()
+    for copy in swaps:
+        copy.wait_send()
+    local[3].wait()
+    local[4].wait()
+
+
+def opening(dp, ctx, small, blocks, out_weight, rows, cot):
+    depth, cols = blocks.shape[1:]
+    shapes = [
+        jax.ShapeDtypeStruct((dp, ctx) + small.shape, small.dtype),
+        jax.ShapeDtypeStruct((dp * ctx * depth, cols), bf16),
+        jax.ShapeDtypeStruct((dp * out_weight.shape[0], out_weight.shape[1]), bf16),
+        jax.ShapeDtypeStruct((ctx * rows.shape[0], rows.shape[1]), bf16),
+        jax.ShapeDtypeStruct((ctx * cot.shape[0], cot.shape[1]), bf16),
+    ]
+    return pl.pallas_call(
+        functools.partial(opening_kernel, dp, ctx),
+        in_specs=[ANY] * 5,
+        out_specs=[ANY] * 5,
+        out_shape=shapes,
+        scratch_shapes=[
+            pltpu.SemaphoreType.DMA((5,)),
+            pltpu.SemaphoreType.DMA((4, ctx)),
+            LineGather.scratch(dp),
+            LineGather.scratch(dp),
+            LineGather.scratch(dp),
+            CtxGather.scratch(),
+            CtxGather.scratch(),
+        ],
+        compiler_params=pltpu.CompilerParams(collective_id=0, has_side_effects=True),
+        cost_estimate=pl.CostEstimate(flops=0, transcendentals=0, bytes_accessed=200 << 20),
+    )(small, blocks, out_weight, rows, cot)
+
+
+def closing_kernel(dp, ctx, parts_ref, out_ref, near, swap_sem, far, line_sem):
+    place = Place(dp)
+    me, row = place.col, place.row
+    barrier = pltpu.get_barrier_semaphore()
+    for k in range(1, ctx):
+        pl.semaphore_signal(barrier, 1, device_id=place.across(k), device_id_type=MESH)
+    for k in range(1, dp):
+        pl.semaphore_signal(barrier, 1, device_id=((row + k) % dp, me), device_id_type=MESH)
+    pl.semaphore_wait(barrier, ctx + dp - 2)
+    swaps = [
+        remote(parts_ref.at[place.other(k)], near.at[k], swap_sem.at[0, k], swap_sem.at[1, k], place.across(k))
+        for k in range(1, ctx)
+    ]
+    for copy in swaps:
+        copy.start()
+    total = parts_ref[me]
+    for k in range(1, ctx):
+        swaps[k - 1].wait()
+        total = total + near[k]
+    near[0] = total
+    sends = [
+        remote(near.at[0, (row + k) % dp], far.at[k], line_sem.at[0, k], line_sem.at[1, k], ((row + k) % dp, me))
+        for k in range(1, dp)
+    ]
+    for copy in sends:
+        copy.start()
+    total = near[0, row]
+    for k in range(1, dp):
+        sends[k - 1].wait()
+        total = total + far[k]
+    out_ref[...] = total
+
+
+def closing(dp, ctx, parts):
+    tile = parts.shape[2:]
+    return pl.pallas_call(
+        functools.partial(closing_kernel, dp, ctx),
+        in_specs=[pl.BlockSpec(memory_space=pltpu.VMEM)],
+        out_specs=pl.BlockSpec(memory_space=pltpu.VMEM),
+        out_shape=jax.ShapeDtypeStruct(tile, f32),
+        scratch_shapes=[
+            pltpu.VMEM((ctx, dp) + tile, f32),
+            pltpu.SemaphoreType.DMA((2, ctx)),
+            pltpu.VMEM((dp,) + tile, f32),
+            pltpu.SemaphoreType.DMA((2, dp)),
+        ],
+        compiler_params=pltpu.CompilerParams(collective_id=1, has_side_effects=True),
+        cost_estimate=pl.CostEstimate(flops=0, transcendentals=0, bytes_accessed=20 << 20),
+    )(parts)
 
 
 def turn(x, table_ref):
@@ -325,37 +675,43 @@
     me = lax.axis_index("ctx")
     own = me * local_len
 
-    small = jnp.concatenate([ln1_gain, ln1_bias, ln2_gain, ln2_bias, qkv_bias])
-    small = lax.all_gather(small[None, :], ("dp", "ctx"), axis=0, tiled=True).astype(f32)
     part = ln1_gain.shape[0]
+    small = jnp.concatenate([ln1_gain, ln1_bias, ln2_gain, ln2_bias, qkv_bias]).astype(f32)
+    count = small.shape[0]
+    small = jnp.pad(small, (0, 1024 - count)).reshape(8, 128)
+    rows_here = qkv_weight.shape[0]
+    blocks = qkv_weight.reshape(rows_here, 3, pairs, 2, ctx, HD).transpose(4, 0, 2, 1, 3, 5)
+    blocks = blocks.reshape(ctx, rows_here, near * 3 * HD)
+    rows, grad_rows = inputs[0], cotangent[0]
+    if ctx == 4 and part == HD:
+        small, joined_weight, out_full, rows_wide, grad_wide = opening(
+            dp, ctx, small, blocks, out_weight, rows, grad_rows
+        )
+        gate_weight, up_weight, down_weight, _ = lax.optimization_barrier(
+            (gate_weight, up_weight, down_weight, rows_wide)
+        )
+    else:
+        small = lax.all_gather(small[None, :], ("dp", "ctx"), axis=0, tiled=True)
+        blocks = exchange_ctx(blocks, ctx)
+        joined_weight = lax.all_gather(
+            blocks.reshape(ctx * rows_here, near * 3 * HD), "dp", axis=0, tiled=True
+        )
+        out_full = lax.all_gather(out_weight, ("dp", "ctx"), axis=0, tiled=True)
+        out_full = out_full.reshape(near, ctx, HD, width)
+        out_full = lax.dynamic_index_in_dim(out_full, me, 1, keepdims=False)
+        out_full = out_full.reshape(near * HD, width)
+        rows_wide = gather_ctx(rows, ctx)
+        grad_wide = gather_ctx(grad_rows, ctx)
+    small = small.reshape(dp * ctx, 1024)[:, :count]
     gain_one, shift_one, gain_two, shift_two = [
         small[:, i * part : (i + 1) * part].reshape(width) for i in range(4)
     ]
     bias = small[:, 4 * part :].reshape(3, pairs, 2, ctx, HD)
     bias = lax.dynamic_index_in_dim(bias, me, 3, keepdims=False)
     bias = bias.transpose(1, 0, 2, 3).reshape(1, near * 3 * HD)
-
-    rows_here = qkv_weight.shape[0]
-    blocks = qkv_weight.reshape(rows_here, 3, pairs, 2, ctx, HD).transpose(4, 0, 2, 1, 3, 5)
-    blocks = exchange_ctx(blocks.reshape(ctx, rows_here, near * 3 * HD), ctx)
-    joined_weight = lax.all_gather(
-        blocks.reshape(ctx * rows_here, near * 3 * HD), "dp", axis=0, tiled=True
-    )
-    if part == HD:
-        out_full = lax.all_gather(out_weight, "dp", axis=0, tiled=True)
-    else:
-        out_full = lax.all_gather(out_weight, ("dp", "ctx"), axis=0, tiled=True)
-        out_full = out_full.reshape(near, ctx, HD, width)
-        out_full = lax.dynamic_index_in_dim(out_full, me, 1, keepdims=False)
-        out_full = out_full.reshape(near * HD, width)
     gate_full = lax.all_gather(gate_weight, "dp", axis=0, tiled=True)
     up_full = lax.all_gather(up_weight, "dp", axis=0, tiled=True)
     down_full = lax.all_gather(down_weight, "dp", axis=1, tiled=True)
-
-    rows = inputs[0]
-    rows_wide = gather_ctx(rows, ctx)
-    grad_rows = cotangent[0]
-    grad_wide = gather_ctx(grad_rows, ctx)
 
     segment = segments[0]
     start = jnp.sum((segment[None, :] < segment[:, None]).astype(jnp.int32), axis=1)
@@ -378,18 +734,21 @@
     d_inner = dot_nt(grad_wide, down_full)
     d_gate = (d_inner * upward * sigma * (1.0 + gate * (1.0 - sigma))).astype(bf16)
     d_upward = (d_inner * swish).astype(bf16)
-    d_normed_two = scatter_ctx(dot_nt(d_gate, gate_full) + dot_nt(d_upward, up_full), ctx)
-    output = (resid + scatter_ctx(dot(inner, down_full), ctx)).astype(bf16)
     d_down = dot_tn(inner, grad_wide).astype(bf16)
+    d_normed_two = scatter_ctx(dot_nt(d_gate, gate_full) + dot_nt(d_upward, up_full), ctx, d_down)
     d_gate_weight = dot_tn(normed_wide, d_gate).astype(bf16)
     d_up_weight = dot_tn(normed_wide, d_upward).astype(bf16)
+    d_normed_two, _, _ = lax.optimization_barrier((d_normed_two, d_gate_weight, d_up_weight))
     d_down = lax.psum_scatter(d_down, "dp", scatter_dimension=1, tiled=True).astype(f32)
     d_gate_weight = lax.psum_scatter(d_gate_weight, "dp", scatter_dimension=0, tiled=True).astype(f32)
     d_up_weight = lax.psum_scatter(d_up_weight, "dp", scatter_dimension=0, tiled=True).astype(f32)
+    branch = dot(inner, down_full)
 
     d_resid_norm, d_gain_two, d_shift_two = norm_backward(d_normed_two, scaled_two, inv_two, gain_two)
     d_resid = grad_rows.astype(f32) + d_resid_norm
     d_proj = gather_ctx(d_resid.astype(bf16), ctx)
+    branch, _ = lax.optimization_barrier((branch, d_proj))
+    output = (resid + scatter_ctx(branch, ctx)).astype(bf16)
     d_attended = dot_nt(d_proj, out_full).astype(bf16)
     d_out_weight = dot_tn(attended, d_proj).astype(bf16)
     if part == HD:
@@ -423,7 +782,8 @@
         + [d_bias],
         axis=1,
     )
-    small = lax.psum_scatter(small, ("dp", "ctx"), scatter_dimension=0, tiled=True)[0]
+    small = jnp.pad(small, ((0, 0), (0, 1024 - count))).reshape(dp, ctx, 8, 128)
+    small = closing(dp, ctx, small.transpose(1, 0, 2, 3)).reshape(1024)[:count]
     d_gain_one, d_shift_one, d_gain_two, d_shift_two = [
         small[i * part : (i + 1) * part] for i in range(4)
     ]

time: 839 us -> 811 us (0.967)
  Pallas kernels: 40.2 us -> 157 us
  blocking collectives: 98.1 us -> 0 us
  local copies, waits for them, and re-layouts: 83.6 us -> 64.6 us
  starting transfers between devices: 43.8 us -> 32.9 us
  waiting for transfers between devices: 347 us -> 337 us
    pallas_call x0 -> x2, Pallas kernels: none -> 117 us  [the longest x1 98.7 us: opening(): pl.pallas_call(functools.partial(opening_kernel, dp, ctx), in_specs=[ANY]...]
    unnamed x2 -> x0, blocking collectives: 98.1 us -> none
    ppermute x38 -> x27, waiting for transfers between devices: 196 us -> 140 us  [hop(): return lax.ppermute(x, 'ctx', partner(n, k))]
    reduce_scatter x1, waiting for transfers between devices: 20.2 us -> 47.6 us  [shards(): lax.psum_scatter(d_gate_weight, 'dp', scatter_dimension=0, tiled=True)]
    all_gather x1, waiting for transfers between devices: 0.01 us -> 20.7 us  [shards(): gate_full = lax.all_gather(gate_weight, 'dp', axis=0, tiled=True)]
    dynamic_update_slice x10 -> x4, local copies, waits for them, and re-layouts: 15 us -> 2.35 us  [gather_ctx(): full = lax.dynamic_update_slice_in_dim(full, part, (me ^ k) * size, 0)]
    ppermute x38 -> x27, starting transfers between devices: 43.4 us -> 32.6 us  [hop(): return lax.ppermute(x, 'ctx', partner(n, k))]
    unnamed x68 -> x72, local copies, waits for them, and re-layouts: 16.4 us -> 18.2 us
  transfers between devices with their start and end apart: 48 -> 35, of which waited for: 32 -> 25; matrix products, arithmetic and copies ran while one was open for 23% -> 19% of each run, Pallas kernels for 2% -> 5%
where the time goes in v2:
time: 811 us; the launch traced here: 805 us
  waiting for transfers between devices  337 us (42%)
  Pallas kernels  157 us (19%)
  matrix products  143 us (18%)
  local copies, waits for them, and re-layouts  64.6 us (8%)
  other arithmetic  55.6 us (7%)
  starting transfers between devices  32.9 us (4%)
  between operations  15.3 us (2%)
    ppermute x27, waiting for transfers between devices, hop(): return lax.ppermute(x, 'ctx', partner(n, k))  140 us
    pallas_call x1, Pallas kernels, opening(): pl.pallas_call(functools.partial(opening_kernel, dp, ctx), in_specs=[ANY]...  98.7 us
    reduce_scatter x1, waiting for transfers between devices, shards(): lax.psum_scatter(d_down, 'dp', scatter_dimension=1, tiled=True).astype(f32)  63.3 us
    reduce_scatter x1, waiting for transfers between devices, shards(): lax.psum_scatter(d_up_weight, 'dp', scatter_dimension=0, tiled=True)  63.2 us
    dot_general x5, matrix products, dot(): return jnp.dot(a, b, preferred_element_type=f32)  51.3 us
    reduce_scatter x1, waiting for transfers between devices, shards(): lax.psum_scatter(d_gate_weight, 'dp', scatter_dimension=0, tiled=True)  47.6 us
    dot_general x5, matrix products, dot_nt(): lax.dot_general(a, b, (((1,), (1,)), ((), ())), preferred_element_type=f32)  46.2 us
    dot_general x5, matrix products, dot_tn(): lax.dot_general(a, b, (((0,), (0,)), ((), ())), preferred_element_type=f32)  45.3 us
  transfers between devices with their start and end apart: 35, of which 25 were waited for; matrix products, arithmetic and copies ran while one was open for 19% of the time, Pallas kernels for 5%

profile of v2, /device:TPU:0, one launch (start us, length us, event | category | flops | bytes accessed | tf_op | source)
XLA Modules:
  0.0 805.2 jit_solution(8814954273397397954)
XLA Ops:
  7.2 3.4 concatenate.59
  11.2 2.5 reshape.157
  15.0 1.7 reshape.158.blocks_ref
  16.7 98.7 %shard_map.220 = (f32[8,4,8,128]{3,2,1,0:T(8,128)}, bf16[2048,1536]{1,0:T(8,128)(2,1)}, bf16[512,2048]{1,0:T(8,128)(2,1)}, bf16[1024,2048]{1,0:T(8,128)(2,1)}, bf16[1024,2048]{1,0:T(8,128)(2,1)}) custom-call(f32[8,128]{1,0:T(8,128)} %bitcast_convert_fusion.small_ref, bf16[4,64,1536]{2,1,0:T(8,128)(2,1)} %reshape.158.blocks_ref, ...), custom_call_target="tpu_custom_call" | custom-call | bytes 209715200 | tf_op jit(solution)/shard_map/pallas_call | solution.py:397
  117.7 1.9 multiply_cosine_fusion
  124.0 3.3 convert_reduce_fusion
  129.0 8.9 %fusion.30.joined_ref = f32[1024,1536]{1,0:T(8,128)} fusion(bf16[2048,1536]{1,0:T(8,128)(2,1)S(1)} %copy-done.26, bf16[1024,2048]{1,0:T(8,128)(2,1)S(1)} %copy-done.12, f32[2048]{0:T(1024)S(1)} %add.185, f32[2048]{0:T(1024)S(1)} %mul.256, f32[1024]{0:T(1024)S(1)} %add_rsqrt_fusion, f32[1024]{0:T(1024)S(1)} %broadcast_multiply_fusion.1), kind=kOutput, calls=%fused_computation.124 | convolution fusion | flops 6455033856 | bytes 16801792 | tf_op jit(solution)/shard_map/dot_general | solution.py:23
  138.2 18.7 %shard_map.221 = (bf16[1024,512]{1,0:T(8,128)(2,1)S(1)}, bf16[1024,1536]{1,0:T(8,128)(2,1)S(1)}, f32[1024,512]{1,0:T(8,128)S(1)}) custom-call(f32[1024,1536]{1,0:T(8,128)} %fusion.30.joined_ref, f32[1,1536]{1,0:T(1,128)S(1)} %reshape.161.bias_ref, f32[3,1024,128]{2,1,0:T(8,128)S(1)} %pad_maximum_fusion.table_ref, s32[1024,128]{1,0:T(8,128)S(1)} %broadcast_in_dim.14.start_ref), custom_call_target="tpu_custom_call" | custom-call | flops 2415919104 | bytes 12582912 | tf_op jit(solution)/shard_map/pallas_call | solution.py:593
  157.0 2.3 fusion.39
  159.8 3.1 copy-done.16
  168.0 10.3 %collective-permute-done = bf16[128,2048]{1,0:T(8,128)(2,1)S(1)} collective-permute-done((bf16[128,2048]{1,0:T(8,128)(2,1)}, bf16[128,2048]{1,0:T(8,128)(2,1)S(1)}, u32[]{:S(2)}, u32[]{:S(2)}) %collective-permute-start) | collective-permute-done | bytes 524320 | tf_op jit(solution)/shard_map/ppermute | solution.py:59
  178.9 1.8 fusion.27
  185.2 21.2 %collective-permute-done.3 = bf16[256,2048]{1,0:T(8,128)(2,1)} collective-permute-done((bf16[256,2048]{1,0:T(8,128)(2,1)}, bf16[256,2048]{1,0:T(8,128)(2,1)}, u32[]{:S(2)}, u32[]{:S(2)}) %collective-permute-start.3) | collective-permute-done | bytes 1048608 | tf_op jit(solution)/shard_map/ppermute | solution.py:59
  206.4 2.0 collective-permute-done.1
  208.4 3.8 fusion.32
  212.5 2.6 broadcast.129.clone
  218.8 20.8 %collective-permute-done.5 = bf16[256,2048]{1,0:T(8,128)(2,1)S(1)} collective-permute-done((bf16[256,2048]{1,0:T(8,128)(2,1)S(1)}, bf16[256,2048]{1,0:T(8,128)(2,1)S(1)}, u32[]{:S(2)}, u32[]{:S(2)}) %collective-permute-start.5) | collective-permute-done | bytes 1048608 | tf_op jit(solution)/shard_map/ppermute | solution.py:59
  240.7 1.9 collective-permute-start.6
  244.8 6.5 collective-permute-done.7
  252.4 11.9 %fusion.42 = f32[1024,1408]{1,0:T(8,128)} fusion(bf16[1024,2048]{1,0:T(8,128)(2,1)} %get-tuple-element.36, bf16[1408,2048]{1,0:T(8,128)(2,1)} %all-gather.8.cloned.1.call-done), kind=kOutput, calls=%fused_computation.135 | convolution fusion | flops 5905580032 | bytes 15728640 | tf_op jit(solution)/shard_map/dot_general | solution.py:27
  264.2 11.8 %fusion.40 = f32[1024,1408]{1,0:T(8,128)} fusion(bf16[1024,2048]{1,0:T(8,128)(2,1)} %maximum_dynamic-update-slice_fusion, bf16[2048,1408]{1,0:T(8,128)(2,1)} %all-gather.6.cloned.1.call-done), kind=kOutput, calls=%fused_computation.133 | convolution fusion | flops 5905580032 | bytes 15728640 | tf_op jit(solution)/shard_map/dot_general | solution.py:23
  276.0 20.7 %all-gather.4.cloned.1.call-done = bf16[2048,1408]{1,0:T(8,128)(2,1)} async-done(((bf16[256,1408]{1,0:T(8,128)(2,1)}), bf16[2048,1408]{1,0:T(8,128)(2,1)}) %all-gather.4.cloned.1.call-update) | async-done | bytes 5767184 | tf_op jit(solution)/shard_map/all_gather | solution.py:712
  296.7 16.3 %multiply_convert_fusion = (bf16[1024,1408]{1,0:T(8,128)(2,1)}, bf16[1024,1408]{1,0:T(8,128)(2,1)S(1)}, bf16[1024,1408]{1,0:T(8,128)(2,1)}) fusion(f32[1024,1408]{1,0:T(8,128)} %fusion.42, f32[1024,1408]{1,0:T(8,128)} %fusion.40, bf16[1024,2048]{1,0:T(8,128)(2,1)} %maximum_dynamic-update-slice_fusion, bf16[2048,1408]{1,0:T(8,128)(2,1)} %all-gather.4.cloned.1.call-done), kind=kOutput, calls=%fused_computation.12 | convolution fusion | flops 5927206912 | bytes 30146560 | tf_op jit(solution)/shard_map/dot_general | solution.py:23
  314.6 10.9 %convolution_convert_fusion.2 = bf16[2048,1408]{1,0:T(8,128)(2,1)} fusion(bf16[1024,2048]{1,0:T(8,128)(2,1)} %maximum_dynamic-update-slice_fusion, bf16[1024,1408]{1,0:T(8,128)(2,1)S(1)} %get-tuple-element.61), kind=kOutput, calls=%fused_computation.10 | convolution fusion | flops 5908463616 | bytes 12845056 | tf_op jit(solution)/shard_map/dot_general | solution.py:31
  325.5 12.0 %fusion.43 = f32[1024,2048]{1,0:T(8,128)} fusion(bf16[1024,1408]{1,0:T(8,128)(2,1)} %copy-done.33, bf16[2048,1408]{1,0:T(8,128)(2,1)} %all-gather.4.cloned.1.call-done), kind=kOutput, calls=%fused_computation.136 | convolution fusion | flops 5905580032 | bytes 17039360 | tf_op jit(solution)/shard_map/dot_general | solution.py:27
  337.5 10.2 %convolution_add_fusion = f32[1024,2048]{1,0:T(8,128)S(1)} fusion(f32[1024,2048]{1,0:T(8,128)} %fusion.43, bf16[1024,1408]{1,0:T(8,128)(2,1)S(1)} %copy-done.31, bf16[2048,1408]{1,0:T(8,128)(2,1)} %all-gather.6.cloned.1.call-done), kind=kOutput, calls=%fused_computation.18 | convolution fusion | flops 5907677184 | bytes 25427968 | tf_op jit(solution)/shard_map/dot_general | solution.py:27
  347.7 3.4 copy-done.17
  355.2 8.1 %convolution_convert_fusion.3 = bf16[1408,2048]{1,0:T(8,128)(2,1)} fusion(bf16[1024,1408]{1,0:T(8,128)(2,1)S(1)} %copy-done.30, bf16[1024,2048]{1,0:T(8,128)(2,1)S(1)} %copy-done.27), kind=kOutput, calls=%fused_computation.11 | convolution fusion | flops 5908463616 | bytes 12845056 | tf_op jit(solution)/shard_map/dot_general | solution.py:31
  367.8 1.8 fusion.25
  373.7 11.3 %convolution_convert_fusion.1 = bf16[2048,1408]{1,0:T(8,128)(2,1)} fusion(bf16[1024,2048]{1,0:T(8,128)(2,1)} %maximum_dynamic-update-slice_fusion, bf16[1024,1408]{1,0:T(8,128)(2,1)S(1)} %copy-done.32), kind=kOutput, calls=%fused_computation.9 | convolution fusion | flops 5908463616 | bytes 12845056 | tf_op jit(solution)/shard_map/dot_general | solution.py:31
  385.0 10.0 %collective-permute-done.11 = bf16[256,2048]{1,0:T(8,128)(2,1)S(1)} collective-permute-done((bf16[256,2048]{1,0:T(8,128)(2,1)}, bf16[256,2048]{1,0:T(8,128)(2,1)S(1)}, u32[]{:S(2)}, u32[]{:S(2)}) %collective-permute-start.11) | collective-permute-done | bytes 1048608 | tf_op jit(solution)/shard_map/ppermute | solution.py:59
  396.5 2.3 convert_add_fusion.2
  401.1 2.3 constant_dynamic-update-slice_fusion.5
  406.2 20.1 %collective-permute-done.13 = bf16[256,2048]{1,0:T(8,128)(2,1)S(1)} collective-permute-done((bf16[256,2048]{1,0:T(8,128)(2,1)S(1)}, bf16[256,2048]{1,0:T(8,128)(2,1)S(1)}, u32[]{:S(2)}, u32[]{:S(2)}) %collective-permute-start.13) | collective-permute-done | bytes 1048608 | tf_op jit(solution)/shard_map/ppermute | solution.py:59
  429.6 9.0 %collective-permute-done.15 = bf16[128,2048]{1,0:T(8,128)(2,1)S(1)} collective-permute-done((bf16[128,2048]{1,0:T(8,128)(2,1)S(1)}, bf16[128,2048]{1,0:T(8,128)(2,1)S(1)}, u32[]{:S(2)}, u32[]{:S(2)}) %collective-permute-start.15) | collective-permute-done | bytes 524320 | tf_op jit(solution)/shard_map/ppermute | solution.py:59
  438.8 2.4 convolution_convert_fusion.5.grad_ref
  442.9 21.6 %shard_map.222 = (bf16[1024,1536]{1,0:T(8,128)(2,1)S(1)}, f32[1,1536]{1,0:T(1,128)S(1)}) custom-call(bf16[1024,1536]{1,0:T(8,128)(2,1)S(1)} %copy-done.1, bf16[1024,512]{1,0:T(8,128)(2,1)S(1)} %convolution_convert_fusion.5.grad_ref, f32[1024,512]{1,0:T(8,128)S(1)} %copy-done.3, f32[3,1024,128]{2,1,0:T(8,128)S(1)} %pad_maximum_fusion.table_ref, ...), custom_call_target="tpu_custom_call" | custom-call | flops 6039797760 | bytes 12582912 | tf_op jit(solution)/shard_map/pallas_call | solution.py:622
  466.1 9.2 %convolution_convert_fusion = bf16[2048,1536]{1,0:T(8,128)(2,1)} fusion(bf16[1024,1536]{1,0:T(8,128)(2,1)S(1)} %get-tuple-element.42, bf16[1024,2048]{1,0:T(8,128)(2,1)S(1)} %copy-done.13, f32[2048]{0:T(1024)S(1)} %add.185, f32[2048]{0:T(1024)S(1)} %mul.256, f32[1024]{0:T(1024)S(1)} %add_rsqrt_fusion, f32[1024]{0:T(1024)S(1)} %broadcast_multiply_fusion.1), kind=kOutput, calls=%fused_computation.8 | convolution fusion | flops 6458179584 | bytes 13656064 | tf_op jit(solution)/shard_map/dot_general | solution.py:31
  476.5 5.9 convolution_convert_fusion.4
  484.6 11.9 %fusion.41 = f32[1024,2048]{1,0:T(8,128)} fusion(bf16[1024,1408]{1,0:T(8,128)(2,1)} %get-tuple-element.62, bf16[1408,2048]{1,0:T(8,128)(2,1)} %all-gather.8.cloned.1.call-done), kind=kOutput, calls=%fused_computation.134 | convolution fusion | flops 5905580032 | bytes 17039360 | tf_op jit(solution)/shard_map/dot_general | solution.py:23
  496.6 9.8 %fusion.44 = f32[1024,2048]{1,0:T(8,128)S(1)} fusion(bf16[1024,1536]{1,0:T(8,128)(2,1)} %copy-done.6, bf16[2048,1536]{1,0:T(8,128)(2,1)} %get-tuple-element.30), kind=kOutput, calls=%fused_computation.137 | convolution fusion | flops 6442450944 | bytes 17825792 | tf_op jit(solution)/shard_map/dot_general | solution.py:27
  506.4 3.3 copy-done.18
  513.0 1.8 dynamic-slice_convert_fusion.1
  516.9 1.7 dynamic-slice_convert_fusion.7
  520.4 5.6 collective-permute-done.20
  527.2 1.9 fusion.21
  533.4 3.8 collective-permute-done.16
  538.4 1.9 fusion.23
  544.8 14.9 %collective-permute-done.23 = bf16[256,2048]{1,0:T(8,128)(2,1)} collective-permute-done((bf16[256,2048]{1,0:T(8,128)(2,1)}, bf16[256,2048]{1,0:T(8,128)(2,1)}, u32[]{:S(2)}, u32[]{:S(2)}) %collective-permute-start.23) | collective-permute-done | bytes 1048608 | tf_op jit(solution)/shard_map/ppermute | solution.py:59
  561.0 4.7 fusion.17
  566.7 18.0 %shard_map.223 = f32[8,128]{1,0:T(8,128)} custom-call(f32[4,8,8,128]{3,2,1,0:T(8,128)} %bitcast.86), custom_call_target="tpu_custom_call" | custom-call | bytes 20971520 | tf_op jit(solution)/shard_map/pallas_call | solution.py:451
  585.9 4.1 fusion.19
  590.0 2.1 fusion.16
  595.8 1.8 convert_element_type.221
  597.6 47.6 %reduce-scatter.10.cloned.1.call-done = bf16[256,1408]{1,0:T(8,128)(2,1)} async-done(((bf16[2048,1408]{1,0:T(8,128)(2,1)}), bf16[256,1408]{1,0:T(8,128)(2,1)}) %reduce-scatter.10.cloned.1.call-update) | async-done | bytes 720912 | tf_op jit(solution)/shard_map/reduce_scatter | solution.py:743
  645.2 2.3 convert_element_type.222
  647.5 63.2 %reduce-scatter.12.cloned.1.call-done = bf16[256,1408]{1,0:T(8,128)(2,1)} async-done(((bf16[2048,1408]{1,0:T(8,128)(2,1)}), bf16[256,1408]{1,0:T(8,128)(2,1)}) %reduce-scatter.12.cloned.1.call-update) | async-done | bytes 720912 | tf_op jit(solution)/shard_map/reduce_scatter | solution.py:744
  710.7 2.3 convert_element_type.223
  713.0 63.3 %reduce-scatter.14.cloned.1.call-done = bf16[1408,256]{1,0:T(8,128)(2,1)} async-done(((bf16[1408,2048]{1,0:T(8,128)(2,1)}), bf16[1408,256]{1,0:T(8,128)(2,1)}) %reduce-scatter.14.cloned.1.call-update) | async-done | bytes 720912 | tf_op jit(solution)/shard_map/reduce_scatter | solution.py:742
  776.2 2.3 convert_element_type.224
  781.5 5.8 collective-permute-done.25
  787.3 3.7 reshape.173
  791.0 3.9 copy.47
  794.9 3.2 reshape.172
  (213 shorter events, 88.5 us)
Async XLA Ops:
  7.2 245.2 %all-gather.8.cloned.1.call-start = ((), (), s32[]{:S(2)}) async-start(), calls=%async_computation.7 | async-start | bytes 6488064 | tf_op jit(solution)/shard_map/all_gather | solution.py:714
  115.5 148.8 %all-gather.6.cloned.1.call-start = ((), (), s32[]{:S(2)}) async-start(), calls=%async_computation.6 | async-start | bytes 6488064 | tf_op jit(solution)/shard_map/all_gather | solution.py:713
  116.2 180.5 %all-gather.4.cloned.1.call-start = ((), (), s32[]{:S(2)}) async-start(), calls=%async_computation.5 | async-start | bytes 6488064 | tf_op jit(solution)/shard_map/all_gather | solution.py:712
  123.3 4.1 copy-start.12
  124.0 5.0 copy-start.26
  138.2 18.8 %copy-start.28 = (bf16[512,2048]{1,0:T(8,128)(2,1)S(1)}, bf16[512,2048]{1,0:T(8,128)(2,1)}, u32[]{:S(2)}) copy-start(bf16[512,2048]{1,0:T(8,128)(2,1)} %get-tuple-element.32) | copy-start | bytes 6291460
  156.9 2.4 copy-start
  156.9 2.4 copy-start.2
  156.9 2.7 copy-start.4
  159.6 3.2 copy-start.16
  163.9 14.4 %collective-permute-start = (bf16[128,2048]{1,0:T(8,128)(2,1)}, bf16[128,2048]{1,0:T(8,128)(2,1)S(1)}, u32[]{:S(2)}, u32[]{:S(2)}) collective-permute-start(bf16[128,2048]{1,0:T(8,128)(2,1)} %get-tuple-element.86), channel_id=1, source_target_pairs={{0,2},{1,3},{2,0},{3,1},{4,6},{5,7},{6,4},{7,5},{8,10},{9,11},{10,... | collective-permute-start | bytes 1572872 | tf_op jit(solution)/shard_map/ppermute | solution.py:59
  164.8 14.1 %collective-permute-start.2 = (bf16[128,2048]{1,0:T(8,128)(2,1)}, bf16[128,2048]{1,0:T(8,128)(2,1)S(1)}, u32[]{:S(2)}, u32[]{:S(2)}) collective-permute-start(bf16[128,2048]{1,0:T(8,128)(2,1)} %get-tuple-element.87), channel_id=1, source_target_pairs={{0,1},{1,0},{2,3},{3,2},{4,5},{5,4},{6,7},{7,6},{8,9},{9,8},{10,11... | collective-permute-start | bytes 1572872 | tf_op jit(solution)/shard_map/ppermute | solution.py:59
  166.3 425.8 %reduce-scatter.6.cloned.1.call-start = ((), (), s32[]{:S(2)}) async-start(), calls=%async_computation.8 | async-start | bytes 7077888 | tf_op jit(solution)/shard_map/reduce_scatter | solution.py:766
  180.7 4.3 copy-start.10
  181.8 24.6 %collective-permute-start.3 = (bf16[256,2048]{1,0:T(8,128)(2,1)}, bf16[256,2048]{1,0:T(8,128)(2,1)}, u32[]{:S(2)}, u32[]{:S(2)}) collective-permute-start(bf16[256,2048]{1,0:T(8,128)(2,1)} %pad_maximum_fusion.2), channel_id=1, source_target_pairs={{0,2},{1,3},{2,0},{3,1},{4,6},{5,7},{6,4},{7,5},{8,10},{9,11},{10,... | collective-permute-start | bytes 3145736 | tf_op jit(solution)/shard_map/ppermute | solution.py:59
  184.0 24.3 %collective-permute-start.1 = (bf16[256,2048]{1,0:T(8,128)(2,1)}, bf16[256,2048]{1,0:T(8,128)(2,1)}, u32[]{:S(2)}, u32[]{:S(2)}) collective-permute-start(bf16[256,2048]{1,0:T(8,128)(2,1)} %pad_maximum_fusion.1), channel_id=1, source_target_pairs={{0,1},{1,0},{2,3},{3,2},{4,5},{5,4},{6,7},{7,6},{8,9},{9,8},{10,11... | collective-permute-start | bytes 3145736 | tf_op jit(solution)/shard_map/ppermute | solution.py:59
  185.2 26.9 %copy-start.22 = (f32[256]{0:T(256)}, f32[256]{0:T(256)S(1)}, u32[]{:S(2)}) copy-start(f32[256]{0:T(256)S(1)} %broadcast_multiply_fusion.4) | copy-start | bytes 3076
  212.1 3.0 copy-start.7
  216.5 23.1 %collective-permute-start.5 = (bf16[256,2048]{1,0:T(8,128)(2,1)S(1)}, bf16[256,2048]{1,0:T(8,128)(2,1)S(1)}, u32[]{:S(2)}, u32[]{:S(2)}) collective-permute-start(bf16[256,2048]{1,0:T(8,128)(2,1)S(1)} %get-tuple-element.57), channel_id=1, source_target_pairs={{0,2},{1,3},{2,0},{3,1},{4,6},{5,7},{6,4},{7,5},{8,10},{9,11},{10,... | collective-permute-start | bytes 3145736 | tf_op jit(solution)/shard_map/ppermute | solution.py:59
  217.4 23.3 %collective-permute-start.4 = (bf16[256,2048]{1,0:T(8,128)(2,1)S(1)}, bf16[256,2048]{1,0:T(8,128)(2,1)S(1)}, u32[]{:S(2)}, u32[]{:S(2)}) collective-permute-start(bf16[256,2048]{1,0:T(8,128)(2,1)S(1)} %get-tuple-element.57), channel_id=1, source_target_pairs={{0,1},{1,0},{2,3},{3,2},{4,5},{5,4},{6,7},{7,6},{8,9},{9,8},{10,11... | collective-permute-start | bytes 3145736 | tf_op jit(solution)/shard_map/ppermute | solution.py:59
  239.6 11.7 %collective-permute-start.7 = (bf16[128,2048]{1,0:T(8,128)(2,1)S(1)}, bf16[128,2048]{1,0:T(8,128)(2,1)S(1)}, u32[]{:S(2)}, u32[]{:S(2)}) collective-permute-start(bf16[128,2048]{1,0:T(8,128)(2,1)S(1)} %slice.180), channel_id=1, source_target_pairs={{0,1},{1,0},{2,3},{3,2},{4,5},{5,4},{6,7},{7,6},{8,9},{9,8},{10,11... | collective-permute-start | bytes 1572872 | tf_op jit(solution)/shard_map/ppermute | solution.py:59
  240.7 10.6 %collective-permute-start.6 = (bf16[128,2048]{1,0:T(8,128)(2,1)S(1)}, bf16[128,2048]{1,0:T(8,128)(2,1)S(1)}, u32[]{:S(2)}, u32[]{:S(2)}) collective-permute-start(bf16[128,2048]{1,0:T(8,128)(2,1)S(1)} %slice.179), channel_id=1, source_target_pairs={{0,2},{1,3},{2,0},{3,1},{4,6},{5,7},{6,4},{7,5},{8,10},{9,11},{10,... | collective-permute-start | bytes 1572872 | tf_op jit(solution)/shard_map/ppermute | solution.py:59
  325.5 12.0 %copy-start.31 = (bf16[1024,1408]{1,0:T(8,128)(2,1)S(1)}, bf16[1024,1408]{1,0:T(8,128)(2,1)}, u32[]{:S(2)}) copy-start(bf16[1024,1408]{1,0:T(8,128)(2,1)} %get-tuple-element.60) | copy-start | bytes 8650756
  337.5 17.7 %copy-start.30 = (bf16[1024,1408]{1,0:T(8,128)(2,1)S(1)}, bf16[1024,1408]{1,0:T(8,128)(2,1)}, u32[]{:S(2)}) copy-start(bf16[1024,1408]{1,0:T(8,128)(2,1)} %get-tuple-element.62) | copy-start | bytes 8650756
  347.7 3.4 copy-start.17
  351.1 4.2 copy-start.27
  352.3 14.3 %collective-permute-start.8 = (bf16[128,2048]{1,0:T(8,128)(2,1)}, bf16[128,2048]{1,0:T(8,128)(2,1)S(1)}, u32[]{:S(2)}, u32[]{:S(2)}) collective-permute-start(bf16[128,2048]{1,0:T(8,128)(2,1)} %get-tuple-element.84), channel_id=1, source_target_pairs={{0,2},{1,3},{2,0},{3,1},{4,6},{5,7},{6,4},{7,5},{8,10},{9,11},{10,... | collective-permute-start | bytes 1572872 | tf_op jit(solution)/shard_map/ppermute | solution.py:59
  353.8 14.0 %collective-permute-start.10 = (bf16[128,2048]{1,0:T(8,128)(2,1)}, bf16[128,2048]{1,0:T(8,128)(2,1)S(1)}, u32[]{:S(2)}, u32[]{:S(2)}) collective-permute-start(bf16[128,2048]{1,0:T(8,128)(2,1)} %get-tuple-element.85), channel_id=1, source_target_pairs={{0,1},{1,0},{2,3},{3,2},{4,5},{5,4},{6,7},{7,6},{8,9},{9,8},{10,11... | collective-permute-start | bytes 1572872 | tf_op jit(solution)/shard_map/ppermute | solution.py:59
  369.6 4.1 copy-start.32
  370.6 24.4 %collective-permute-start.11 = (bf16[256,2048]{1,0:T(8,128)(2,1)}, bf16[256,2048]{1,0:T(8,128)(2,1)S(1)}, u32[]{:S(2)}, u32[]{:S(2)}) collective-permute-start(bf16[256,2048]{1,0:T(8,128)(2,1)} %pad_maximum_fusion.4), channel_id=1, source_target_pairs={{0,2},{1,3},{2,0},{3,1},{4,6},{5,7},{6,4},{7,5},{8,10},{9,11},{10,... | collective-permute-start | bytes 3145736 | tf_op jit(solution)/shard_map/ppermute | solution.py:59
  372.2 24.2 %collective-permute-start.9 = (bf16[256,2048]{1,0:T(8,128)(2,1)}, bf16[256,2048]{1,0:T(8,128)(2,1)}, u32[]{:S(2)}, u32[]{:S(2)}) collective-permute-start(bf16[256,2048]{1,0:T(8,128)(2,1)} %pad_maximum_fusion.3), channel_id=1, source_target_pairs={{0,1},{1,0},{2,3},{3,2},{4,5},{5,4},{6,7},{7,6},{8,9},{9,8},{10,11... | collective-permute-start | bytes 3145736 | tf_op jit(solution)/shard_map/ppermute | solution.py:59
  385.0 13.9 %copy-start.8 = (f32[256,2048]{1,0:T(8,128)S(1)}, f32[256,2048]{1,0:T(8,128)}, u32[]{:S(2)}) copy-start(f32[256,2048]{1,0:T(8,128)} %copy-done.7) | copy-start | bytes 6291460
  403.3 23.0 %collective-permute-start.13 = (bf16[256,2048]{1,0:T(8,128)(2,1)S(1)}, bf16[256,2048]{1,0:T(8,128)(2,1)S(1)}, u32[]{:S(2)}, u32[]{:S(2)}) collective-permute-start(bf16[256,2048]{1,0:T(8,128)(2,1)S(1)} %get-tuple-element.54), channel_id=1, source_target_pairs={{0,2},{1,3},{2,0},{3,1},{4,6},{5,7},{6,4},{7,5},{8,10},{9,11},{10,... | collective-permute-start | bytes 3145736 | tf_op jit(solution)/shard_map/ppermute | solution.py:59
  404.7 24.0 %collective-permute-start.12 = (bf16[256,2048]{1,0:T(8,128)(2,1)S(1)}, bf16[256,2048]{1,0:T(8,128)(2,1)S(1)}, u32[]{:S(2)}, u32[]{:S(2)}) collective-permute-start(bf16[256,2048]{1,0:T(8,128)(2,1)S(1)} %get-tuple-element.54), channel_id=1, source_target_pairs={{0,1},{1,0},{2,3},{3,2},{4,5},{5,4},{6,7},{7,6},{8,9},{9,8},{10,11... | collective-permute-start | bytes 3145736 | tf_op jit(solution)/shard_map/ppermute | solution.py:59
  426.4 12.3 %collective-permute-start.15 = (bf16[128,2048]{1,0:T(8,128)(2,1)S(1)}, bf16[128,2048]{1,0:T(8,128)(2,1)S(1)}, u32[]{:S(2)}, u32[]{:S(2)}) collective-permute-start(bf16[128,2048]{1,0:T(8,128)(2,1)S(1)} %slice.184), channel_id=1, source_target_pairs={{0,1},{1,0},{2,3},{3,2},{4,5},{5,4},{6,7},{7,6},{8,9},{9,8},{10,11... | collective-permute-start | bytes 1572872 | tf_op jit(solution)/shard_map/ppermute | solution.py:59
  428.8 9.9 %collective-permute-start.14 = (bf16[128,2048]{1,0:T(8,128)(2,1)S(1)}, bf16[128,2048]{1,0:T(8,128)(2,1)S(1)}, u32[]{:S(2)}, u32[]{:S(2)}) collective-permute-start(bf16[128,2048]{1,0:T(8,128)(2,1)S(1)} %slice.183), channel_id=1, source_target_pairs={{0,2},{1,3},{2,0},{3,1},{4,6},{5,7},{6,4},{7,5},{8,10},{9,11},{10,... | collective-permute-start | bytes 1572872 | tf_op jit(solution)/shard_map/ppermute | solution.py:59
  429.4 9.4 %copy-start.29 = (bf16[512,2048]{1,0:T(8,128)(2,1)S(1)}, bf16[512,2048]{1,0:T(8,128)(2,1)}, u32[]{:S(2)}) copy-start(bf16[512,2048]{1,0:T(8,128)(2,1)} %get-tuple-element.32) | copy-start | bytes 6291460
  438.8 2.4 copy-start.20
  438.8 3.4 copy-start.1
  438.8 4.0 copy-start.3
  442.8 23.2 %copy-start.13 = (bf16[1024,2048]{1,0:T(8,128)(2,1)S(1)}, bf16[1024,2048]{1,0:T(8,128)(2,1)}, u32[]{:S(2)}) copy-start(bf16[1024,2048]{1,0:T(8,128)(2,1)} %get-tuple-element.28) | copy-start | bytes 12582916
  464.4 1.6 copy-start.6
  475.3 120.5 %reduce-scatter.8.cloned.1.call-start = ((), (), s32[]{:S(2)}) async-start(), calls=%async_computation.9 | async-start | bytes 2359296 | tf_op jit(solution)/shard_map/reduce_scatter | solution.py:755
  482.4 162.7 %reduce-scatter.10.cloned.1.call-start = ((), (), s32[]{:S(2)}) async-start(), calls=%async_computation.10 | async-start | bytes 6488064 | tf_op jit(solution)/shard_map/reduce_scatter | solution.py:743
  483.0 227.7 %reduce-scatter.12.cloned.1.call-start = ((), (), s32[]{:S(2)}) async-start(), calls=%async_computation.11 | async-start | bytes 6488064 | tf_op jit(solution)/shard_map/reduce_scatter | solution.py:744
  483.7 292.5 %reduce-scatter.14.cloned.1.call-start = ((), (), s32[]{:S(2)}) async-start(), calls=%async_computation.12 | async-start | bytes 6488064 | tf_op jit(solution)/shard_map/reduce_scatter | solution.py:742
  506.4 3.3 copy-start.18
  510.9 15.1 %collective-permute-start.20 = (bf16[128,2048]{1,0:T(8,128)(2,1)}, bf16[128,2048]{1,0:T(8,128)(2,1)S(1)}, u32[]{:S(2)}, u32[]{:S(2)}) collective-permute-start(bf16[128,2048]{1,0:T(8,128)(2,1)} %get-tuple-element.79), channel_id=1, source_target_pairs={{0,2},{1,3},{2,0},{3,1},{4,6},{5,7},{6,4},{7,5},{8,10},{9,11},{10,... | collective-permute-start | bytes 1572872 | tf_op jit(solution)/shard_map/ppermute | solution.py:59
  512.1 15.1 %collective-permute-start.22 = (bf16[128,2048]{1,0:T(8,128)(2,1)}, bf16[128,2048]{1,0:T(8,128)(2,1)S(1)}, u32[]{:S(2)}, u32[]{:S(2)}) collective-permute-start(bf16[128,2048]{1,0:T(8,128)(2,1)} %get-tuple-element.80), channel_id=1, source_target_pairs={{0,1},{1,0},{2,3},{3,2},{4,5},{5,4},{6,7},{7,6},{8,9},{9,8},{10,11... | collective-permute-start | bytes 1572872 | tf_op jit(solution)/shard_map/ppermute | solution.py:59
  514.9 22.4 %collective-permute-start.16 = (bf16[128,2048]{1,0:T(8,128)(2,1)S(1)}, bf16[128,2048]{1,0:T(8,128)(2,1)S(1)}, u32[]{:S(2)}, u32[]{:S(2)}) collective-permute-start(bf16[128,2048]{1,0:T(8,128)(2,1)S(1)} %get-tuple-element.82), channel_id=1, source_target_pairs={{0,2},{1,3},{2,0},{3,1},{4,6},{5,7},{6,4},{7,5},{8,10},{9,11},{10,... | collective-permute-start | bytes 1572872 | tf_op jit(solution)/shard_map/ppermute | solution.py:59
  516.3 22.1 %collective-permute-start.18 = (bf16[128,2048]{1,0:T(8,128)(2,1)S(1)}, bf16[128,2048]{1,0:T(8,128)(2,1)S(1)}, u32[]{:S(2)}, u32[]{:S(2)}) collective-permute-start(bf16[128,2048]{1,0:T(8,128)(2,1)S(1)} %get-tuple-element.83), channel_id=1, source_target_pairs={{0,1},{1,0},{2,3},{3,2},{4,5},{5,4},{6,7},{7,6},{8,9},{9,8},{10,11... | collective-permute-start | bytes 1572872 | tf_op jit(solution)/shard_map/ppermute | solution.py:59
  530.1 29.7 %collective-permute-start.23 = (bf16[256,2048]{1,0:T(8,128)(2,1)}, bf16[256,2048]{1,0:T(8,128)(2,1)}, u32[]{:S(2)}, u32[]{:S(2)}) collective-permute-start(bf16[256,2048]{1,0:T(8,128)(2,1)} %pad_maximum_fusion.8), channel_id=1, source_target_pairs={{0,2},{1,3},{2,0},{3,1},{4,6},{5,7},{6,4},{7,5},{8,10},{9,11},{10,... | collective-permute-start | bytes 3145736 | tf_op jit(solution)/shard_map/ppermute | solution.py:59
  531.9 29.1 %collective-permute-start.21 = (bf16[256,2048]{1,0:T(8,128)(2,1)}, bf16[256,2048]{1,0:T(8,128)(2,1)}, u32[]{:S(2)}, u32[]{:S(2)}) collective-permute-start(bf16[256,2048]{1,0:T(8,128)(2,1)} %pad_maximum_fusion.7), channel_id=1, source_target_pairs={{0,1},{1,0},{2,3},{3,2},{4,5},{5,4},{6,7},{7,6},{8,9},{9,8},{10,11... | collective-permute-start | bytes 3145736 | tf_op jit(solution)/shard_map/ppermute | solution.py:59
  540.3 20.7 %copy-start.11 = (bf16[1,256,2048]{2,1,0:T(8,128)(2,1)S(1)}, bf16[1,256,2048]{2,1,0:T(8,128)(2,1)}, u32[]{:S(2)}) copy-start(bf16[1,256,2048]{2,1,0:T(8,128)(2,1)} %param.13) | copy-start | bytes 3145732
  540.3 20.7 %copy-start.23 = (f32[256]{0:T(256)S(1)}, f32[256]{0:T(256)}, u32[]{:S(2)}) copy-start(f32[256]{0:T(256)} %copy-done.22) | copy-start | bytes 3076
  541.4 44.6 %collective-permute-start.19 = (bf16[256,2048]{1,0:T(8,128)(2,1)}, bf16[256,2048]{1,0:T(8,128)(2,1)}, u32[]{:S(2)}, u32[]{:S(2)}) collective-permute-start(bf16[256,2048]{1,0:T(8,128)(2,1)} %pad_maximum_fusion.6), channel_id=1, source_target_pairs={{0,2},{1,3},{2,0},{3,1},{4,6},{5,7},{6,4},{7,5},{8,10},{9,11},{10,... | collective-permute-start | bytes 3145736 | tf_op jit(solution)/shard_map/ppermute | solution.py:59
  543.2 42.7 %collective-permute-start.17 = (bf16[256,2048]{1,0:T(8,128)(2,1)}, bf16[256,2048]{1,0:T(8,128)(2,1)}, u32[]{:S(2)}, u32[]{:S(2)}) collective-permute-start(bf16[256,2048]{1,0:T(8,128)(2,1)} %pad_maximum_fusion.5), channel_id=1, source_target_pairs={{0,1},{1,0},{2,3},{3,2},{4,5},{5,4},{6,7},{7,6},{8,9},{9,8},{10,11... | collective-permute-start | bytes 3145736 | tf_op jit(solution)/shard_map/ppermute | solution.py:59
  544.8 41.1 %copy-start.9 = (f32[256,2048]{1,0:T(8,128)S(1)}, f32[256,2048]{1,0:T(8,128)}, u32[]{:S(2)}) copy-start(f32[256,2048]{1,0:T(8,128)} %copy-done.7) | copy-start | bytes 6291460
  585.9 4.1 copy-start.14
  585.9 4.1 copy-start.15
  590.0 5.2 copy-start.24
  593.5 188.0 %collective-permute-start.24 = (bf16[1,64,1536]{2,1,0:T(8,128)(2,1)S(1)}, bf16[1,64,1536]{2,1,0:T(8,128)(2,1)S(1)}, u32[]{:S(2)}, u32[]{:S(2)}) collective-permute-start(bf16[1,64,1536]{2,1,0:T(8,128)(2,1)S(1)} %get-tuple-element.90), channel_id=1, source_target_pairs={{0,1},{1,0},{2,3},{3,2},{4,5},{5,4},{6,7},{7,6},{8,9},{9,8},{10,11... | collective-permute-start | bytes 589832 | tf_op jit(solution)/shard_map/ppermute | solution.py:59
  778.6 8.7 %collective-permute-start.25 = (bf16[1,64,1536]{2,1,0:T(8,128)(2,1)S(1)}, bf16[1,64,1536]{2,1,0:T(8,128)(2,1)S(1)}, u32[]{:S(2)}, u32[]{:S(2)}) collective-permute-start(bf16[1,64,1536]{2,1,0:T(8,128)(2,1)S(1)} %get-tuple-element.89), channel_id=1, source_target_pairs={{0,2},{1,3},{2,0},{3,1},{4,6},{5,7},{6,4},{7,5},{8,10},{9,11},{10,... | collective-permute-start | bytes 589832 | tf_op jit(solution)/shard_map/ppermute | solution.py:59
  780.0 7.3 collective-permute-start.26
  (5 other events, 6.1 us)
Sparse Core Ops, SparseCore 0:
  115.6 60.0 all-gather.7
  177.3 58.5 all-gather.5
  237.6 59.0 all-gather.3
  475.4 67.6 reduce-scatter.5
  545.3 33.9 reduce-scatter.7
  581.5 63.6 reduce-scatter.9
  647.5 63.1 reduce-scatter.11
  713.0 63.2 reduce-scatter.13

commit v3 on v2

--- a/solution.py
+++ b/solution.py
@@ -413,7 +413,339 @@
     )(small, blocks, out_weight, rows, cot)
 
 
-def closing_kernel(dp, ctx, parts_ref, out_ref, near, swap_sem, far, line_sem):
+CHUNKS = 4
+
+
+class CtxReduce:
+    def __init__(self, place, block, total, sent, got, sems):
+        self.place, self.block, self.total = place, block, total
+        self.sent, self.got, self.sems = sent, got, sems
+        self.size = total.shape[1] // CHUNKS
+
+    def chunk(self, j):
+        return pl.ds(j * self.size, self.size)
+
+    def copy(self, kind, j):
+        way = kind if kind else 1 + j % 2
+        return remote(
+            self.sent.at[kind, self.chunk(j)], self.got.at[kind, self.chunk(j)],
+            self.sems.at[0, kind, j], self.sems.at[1, kind, j], self.place.across(way),
+        )
+
+    def start(self):
+        place = self.place
+        self.sent[0] = self.block(place.other(3)).astype(bf16)
+        for j in range(CHUNKS):
+            self.copy(0, j).start()
+        for kind in (1, 2):
+            self.total[kind - 1] = self.block(place.other(kind))
+            for j in range(CHUNKS):
+                if kind == 1 + j % 2:
+                    self.sent[kind, self.chunk(j)] = self.total[kind - 1, self.chunk(j)].astype(bf16)
+                    self.copy(kind, j).start()
+
+    def relay(self):
+        for j in range(CHUNKS):
+            kind = 2 - j % 2
+            self.copy(0, j).wait_recv()
+            share = self.total[kind - 1, self.chunk(j)] + self.got[0, self.chunk(j)].astype(f32)
+            self.sent[kind, self.chunk(j)] = share.astype(bf16)
+            self.copy(kind, j).start()
+        self.total[0] = self.block(self.place.col)
+
+    def sum(self, j):
+        for kind in (1, 2):
+            self.copy(kind, j).wait_recv()
+        rows = self.chunk(j)
+        return self.total[0, rows] + self.got[1, rows].astype(f32) + self.got[2, rows].astype(f32)
+
+    def finish(self):
+        for kind in range(3):
+            for j in range(CHUNKS):
+                self.copy(kind, j).wait_send()
+
+    @staticmethod
+    def scratch(size, width):
+        return [
+            pltpu.VMEM((2, size, width), f32),
+            pltpu.VMEM((3, size, width), bf16),
+            pltpu.VMEM((3, size, width), bf16),
+            pltpu.SemaphoreType.DMA((2, 3, CHUNKS)),
+        ]
+
+
+class CtxSpread:
+    def __init__(self, place, made, full, sems):
+        self.place, self.made, self.full, self.sems = place, made, full, sems
+        self.size = made.shape[0] // CHUNKS
+
+    def rows(self, col, j):
+        at = (col * CHUNKS + j) * self.size
+        return self.full.at[pl.ds(pl.multiple_of(at, self.size), self.size), :]
+
+    def copy(self, kind, j):
+        place = self.place
+        if kind < 2:
+            part, there = self.made.at[pl.ds(j * self.size, self.size), :], self.rows(place.col, j)
+            way = 1 + kind
+        else:
+            way = 2 - j % 2
+            part = there = self.rows(place.other(3 - way), j)
+        return remote(part, there, self.sems.at[0, kind, j], self.sems.at[1, kind, j], place.across(way))
+
+    def arrived(self, kind, j):
+        part = self.rows(self.place.other(kind + 1), j)
+        remote(
+            part, part, self.sems.at[0, kind, j], self.sems.at[1, kind, j], self.place.across(1)
+        ).wait_recv()
+
+    def local(self, j):
+        part = self.made.at[pl.ds(j * self.size, self.size), :]
+        return pltpu.make_async_copy(part, self.rows(self.place.col, j), self.sems.at[0, 3, j])
+
+    def send(self, j):
+        self.copy(0, j).start()
+        self.copy(1, j).start()
+        self.local(j).start()
+
+    def relay(self, j):
+        way = 2 - j % 2
+        self.arrived(2 - way, j)
+        self.copy(2, j).start()
+
+    def finish(self):
+        for j in range(CHUNKS):
+            way = 2 - j % 2
+            self.arrived(way - 1, j)
+            self.arrived(2, j)
+            self.local(j).wait()
+            for kind in range(3):
+                self.copy(kind, j).wait_send()
+
+    @staticmethod
+    def scratch():
+        return pltpu.SemaphoreType.DMA((2, 4, CHUNKS))
+
+
+def rows_of(ref, col, size):
+    return ref[pl.ds(pl.multiple_of(col * size, size), size), :]
+
+
+def mix_kernel(
+    dp, ctx, attended_ref, weight_ref, rows_ref, gain_ref, shift_ref, resid_ref, wide_ref,
+    total, sent, got, made, reduce_sem, spread_sem,
+):
+    place = Place(dp)
+    greet(place, ctx)
+    size = rows_ref.shape[0]
+    reduce = CtxReduce(
+        place, lambda col: dot(rows_of(attended_ref, col, size), weight_ref[...]), total, sent, got, reduce_sem
+    )
+    spread = CtxSpread(place, made, wide_ref, spread_sem)
+    reduce.start()
+    reduce.relay()
+    for j in range(CHUNKS):
+        rows = reduce.chunk(j)
+        resid = rows_ref[rows, :].astype(f32) + reduce.sum(j)
+        resid_ref[rows, :] = resid
+        scaled, _ = norm_stats(resid)
+        made[rows, :] = (scaled * gain_ref[...] + shift_ref[...]).astype(bf16)
+        spread.send(j)
+        if j:
+            spread.relay(j - 1)
+    spread.relay(CHUNKS - 1)
+    spread.finish()
+    reduce.finish()
+
+
+def mix(dp, ctx, attended, weight, rows, gain, shift):
+    size, width = rows.shape
+    vmem = pl.BlockSpec(memory_space=pltpu.VMEM)
+    return pl.pallas_call(
+        functools.partial(mix_kernel, dp, ctx),
+        in_specs=[vmem] * 5,
+        out_specs=[vmem, ANY],
+        out_shape=[jax.ShapeDtypeStruct((size, width), f32), jax.ShapeDtypeStruct((ctx * size, width), bf16)],
+        scratch_shapes=CtxReduce.scratch(size, width)[:3]
+        + [
+            pltpu.VMEM((size, width), bf16),
+            CtxReduce.scratch(size, width)[3],
+            CtxSpread.scratch(),
+        ],
+        compiler_params=pltpu.CompilerParams(
+            collective_id=2, has_side_effects=True, vmem_limit_bytes=40 << 20
+        ),
+        cost_estimate=pl.CostEstimate(
+            flops=2 * attended.size * width, transcendentals=0, bytes_accessed=180 << 20
+        ),
+    )(attended, weight, rows, gain.reshape(1, width), shift.reshape(1, width))
+
+
+def mix_back_kernel(
+    dp, ctx, gate_ref, up_ref, gate_weight_ref, up_weight_ref, resid_ref, cot_ref, gain_ref,
+    d_resid_ref, sums_ref, wide_ref,
+    total, sent, got, made, reduce_sem, spread_sem,
+):
+    place = Place(dp)
+    greet(place, ctx)
+    size = cot_ref.shape[0]
+
+    def block(col):
+        return dot_nt(rows_of(gate_ref, col, size), gate_weight_ref[...]) + dot_nt(
+            rows_of(up_ref, col, size), up_weight_ref[...]
+        )
+
+    reduce = CtxReduce(place, block, total, sent, got, reduce_sem)
+    spread = CtxSpread(place, made, wide_ref, spread_sem)
+    reduce.start()
+    reduce.relay()
+    sums_ref[...] = jnp.zeros_like(sums_ref)
+    for j in range(CHUNKS):
+        rows = reduce.chunk(j)
+        scaled, inv_std = norm_stats(resid_ref[rows, :])
+        grad, d_gain, d_shift = norm_backward(reduce.sum(j), scaled, inv_std, gain_ref[...])
+        sums_ref[0:1, :] += d_gain[None]
+        sums_ref[1:2, :] += d_shift[None]
+        grad = cot_ref[rows, :].astype(f32) + grad
+        d_resid_ref[rows, :] = grad
+        made[rows, :] = grad.astype(bf16)
+        spread.send(j)
+        if j:
+            spread.relay(j - 1)
+    spread.relay(CHUNKS - 1)
+    spread.finish()
+    reduce.finish()
+
+
+def mix_back(dp, ctx, d_gate, d_up, gate_weight, up_weight, resid, cot, gain):
+    size, width = cot.shape
+    vmem = pl.BlockSpec(memory_space=pltpu.VMEM)
+    return pl.pallas_call(
+        functools.partial(mix_back_kernel, dp, ctx),
+        in_specs=[vmem] * 7,
+        out_specs=[vmem, vmem, ANY],
+        out_shape=[
+            jax.ShapeDtypeStruct((size, width), f32),
+            jax.ShapeDtypeStruct((2, width), f32),
+            jax.ShapeDtypeStruct((ctx * size, width), bf16),
+        ],
+        scratch_shapes=CtxReduce.scratch(size, width)[:3]
+        + [
+            pltpu.VMEM((size, width), bf16),
+            CtxReduce.scratch(size, width)[3],
+            CtxSpread.scratch(),
+        ],
+        compiler_params=pltpu.CompilerParams(
+            collective_id=3, has_side_effects=True, vmem_limit_bytes=56 << 20
+        ),
+        cost_estimate=pl.CostEstimate(
+            flops=4 * d_gate.size * width, transcendentals=0, bytes_accessed=180 << 20
+        ),
+    )(d_gate, d_up, gate_weight, up_weight, resid, cot, gain.reshape(1, width))
+
+
+class LineReduce:
+    def __init__(self, place, parts, pair, got, sems):
+        self.place, self.parts, self.pair, self.got, self.sems = place, parts, pair, got, sems
+
+    def swap(self, line):
+        row = 2 * line + 1 - self.place.core
+        return remote(
+            self.parts.at[row], self.pair.at[line], self.sems.at[0, line], self.sems.at[1, line], self.place.twin
+        )
+
+    def start(self):
+        for line in range(self.place.lines):
+            self.swap(line).start()
+
+    def add(self):
+        for line in range(self.place.lines):
+            self.swap(line).wait_recv()
+            both = self.parts[2 * line + self.place.core].astype(f32) + self.pair[line].astype(f32)
+            self.pair[line] = both.astype(bf16)
+
+    def up(self, far):
+        part = self.place.line + far
+        return remote(
+            self.pair.at[part], self.got.at[part], self.sems.at[2, far], self.sems.at[3, far], self.place.above()
+        )
+
+    def down(self, far):
+        part = self.place.line - far
+        slot = part if far > 1 else self.place.lines
+        return remote(
+            self.pair.at[part], self.got.at[slot], self.sems.at[4, far], self.sems.at[5, far], self.place.below()
+        )
+
+    def came_up(self, far):
+        slot = self.got.at[self.place.line + far]
+        remote(slot, slot, self.sems.at[2, far + 1], self.sems.at[3, far + 1], self.place.twin).wait_recv()
+
+    def came_down(self, far):
+        slot = self.got.at[self.place.line - far if far else self.place.lines]
+        remote(slot, slot, self.sems.at[4, far + 1], self.sems.at[5, far + 1], self.place.twin).wait_recv()
+
+    def send(self, far):
+        place = self.place
+
+        @pl.when(place.line + far < place.lines)
+        def _():
+            @pl.when(place.line > 0)
+            def _():
+                self.came_up(far)
+                part = place.line + far
+                self.pair[part] = (self.pair[part].astype(f32) + self.got[part].astype(f32)).astype(bf16)
+
+            self.up(far).start()
+
+        @pl.when(place.line - far >= 0)
+        def _():
+            @pl.when(place.line < place.lines - 1)
+            def _():
+                self.came_down(far)
+                part = place.line - far
+                self.pair[part] = (self.pair[part].astype(f32) + self.got[part].astype(f32)).astype(bf16)
+
+            self.down(far).start()
+
+    def collect(self, out):
+        place = self.place
+        out[...] = self.pair[place.line].astype(f32)
+
+        @pl.when(place.line > 0)
+        def _():
+            self.came_up(0)
+            out[...] += self.got[place.line].astype(f32)
+
+        @pl.when(place.line < place.lines - 1)
+        def _():
+            self.came_down(0)
+            out[...] += self.got[place.lines].astype(f32)
+
+    def finish(self):
+        place = self.place
+        for line in range(place.lines):
+            self.swap(line).wait_send()
+        for far in range(1, place.lines):
+            pl.when(place.line + far < place.lines)(lambda: self.up(far).wait_send())
+            pl.when(place.line - far >= 0)(lambda: self.down(far).wait_send())
+
+    @staticmethod
+    def scratch(dp, tile):
+        return [
+            pltpu.VMEM((dp // 2,) + tile, bf16),
+            pltpu.VMEM((dp // 2 + 1,) + tile, bf16),
+            pltpu.SemaphoreType.DMA((6, dp // 2)),
+        ]
+
+
+def closing_kernel(
+    dp, ctx,
+    d_joined_ref, weight_ref, qkv_parts_ref, out_parts_ref, rows_ref, d_resid_ref, gain_ref, sums_two_ref, bias_ref,
+    grad_ref, qkv_ref, out_ref, small_ref,
+    total, sent, got, reduce_sem, qkv_pair, qkv_got, qkv_sem, out_pair, out_got, out_sem,
+    sums, tiles, tiles_got, small_sem, mine, swap_out, swap_in, swap_sem,
+):
     place = Place(dp)
     me, row = place.col, place.row
     barrier = pltpu.get_barrier_semaphore()
@@ -422,46 +754,143 @@
     for k in range(1, dp):
         pl.semaphore_signal(barrier, 1, device_id=((row + k) % dp, me), device_id_type=MESH)
     pl.semaphore_wait(barrier, ctx + dp - 2)
+
+    size, width = rows_ref.shape
+    lines = [
+        LineReduce(place, qkv_parts_ref, qkv_pair, qkv_got, qkv_sem),
+        LineReduce(place, out_parts_ref, out_pair, out_got, out_sem),
+    ]
+    for line in lines:
+        line.start()
+    reduce = CtxReduce(
+        place, lambda col: dot_nt(rows_of(d_joined_ref, col, size), weight_ref[...]), total, sent, got, reduce_sem
+    )
+    reduce.start()
+    for line in lines:
+        line.add()
+        line.send(place.lines - 1)
+    reduce.relay()
+    for far in range(place.lines - 2, 1, -1):
+        for line in lines:
+            line.send(far)
+
+    sums[...] = jnp.zeros_like(sums)
+    for j in range(CHUNKS):
+        rows = reduce.chunk(j)
+        scaled, inv_std = norm_stats(rows_ref[rows, :].astype(f32))
+        grad, d_gain, d_shift = norm_backward(reduce.sum(j), scaled, inv_std, gain_ref[...])
+        sums[0:1, :] += d_gain[None]
+        sums[1:2, :] += d_shift[None]
+        grad_ref[rows, :] = d_resid_ref[rows, :] + grad
+    if place.lines > 2:
+        for line in lines:
+            line.send(1)
+
+    part = width // dp
+    tiles[...] = jnp.zeros_like(tiles)
+    for i in range(dp):
+        lanes = slice(i * part, (i + 1) * part)
+        tiles[i, 0:2, :] = sums[:, lanes]
+        tiles[i, 2:4, :] = sums_two_ref[:, lanes]
+        tiles[i, 4:5, :] = bias_ref[i : i + 1, :]
+    sends = [
+        remote(tiles.at[(row + k) % dp], tiles_got.at[k], small_sem.at[0, k], small_sem.at[1, k], ((row + k) % dp, me))
+        for k in range(1, dp)
+    ]
+    for copy in sends:
+        copy.start()
+    tile = tiles[row]
+    for k in range(1, dp):
+        sends[k - 1].wait()
+        tile = tile + tiles_got[k]
+    tiles_got[0] = tile
+    small_ref[me] = tile
+    spreads = [
+        remote(tiles_got.at[0], small_ref.at[me], small_sem.at[2, k], small_sem.at[3, k], place.across(k))
+        for k in range(1, ctx)
+    ]
+    for copy in spreads:
+        copy.start()
+
+    lines[0].collect(mine)
+    depth = mine.shape[0] // ctx
+    swap_out[...] = mine[...].astype(bf16)
     swaps = [
-        remote(parts_ref.at[place.other(k)], near.at[k], swap_sem.at[0, k], swap_sem.at[1, k], place.across(k))
+        remote(
+            swap_out.at[pl.ds(pl.multiple_of(place.other(k) * depth, depth), depth), :], swap_in.at[me],
+            swap_sem.at[0, k], swap_sem.at[1, k], place.across(k),
+        )
         for k in range(1, ctx)
     ]
     for copy in swaps:
         copy.start()
-    total = parts_ref[me]
+    swap_in[me] = rows_of(swap_out, me, depth)
+    lines[1].collect(out_ref)
     for k in range(1, ctx):
-        swaps[k - 1].wait()
-        total = total + near[k]
-    near[0] = total
-    sends = [
-        remote(near.at[0, (row + k) % dp], far.at[k], line_sem.at[0, k], line_sem.at[1, k], ((row + k) % dp, me))
-        for k in range(1, dp)
-    ]
-    for copy in sends:
-        copy.start()
-    total = near[0, row]
-    for k in range(1, dp):
-        sends[k - 1].wait()
-        total = total + far[k]
-    out_ref[...] = total
-
-
-def closing(dp, ctx, parts):
-    tile = parts.shape[2:]
+        part = swap_in.at[place.other(k)]
+        remote(part, part, swap_sem.at[0, k], swap_sem.at[1, k], place.across(k)).wait_recv()
+    low = head_lanes((depth, PAIR))
+    for p in range(mine.shape[1] // (3 * PAIR)):
+        for t in range(3):
+            lanes = slice((3 * p + t) * PAIR, (3 * p + t + 1) * PAIR)
+            for c in range(0, ctx, 2):
+                a = swap_in[c, :, lanes].astype(f32)
+                b = swap_in[c + 1, :, lanes].astype(f32)
+                at = t * width + (2 * p * ctx + c) * HD
+                qkv_ref[:, at : at + PAIR] = jnp.where(low, a, pltpu.roll(b, HD, 1))
+                at = at + ctx * HD
+                qkv_ref[:, at : at + PAIR] = jnp.where(low, pltpu.roll(a, HD, 1), b)
+    for copy in swaps:
+        copy.wait_send()
+    for k in range(1, ctx):
+        spreads[k - 1].wait_send()
+        part = small_ref.at[place.other(k)]
+        remote(part, part, small_sem.at[2, k], small_sem.at[3, k], place.across(k)).wait_recv()
+    for line in lines:
+        line.finish()
+    reduce.finish()
+
+
+def closing(dp, ctx, d_joined, weight, d_qkv, d_out, rows, d_resid, gain, sums_two, bias):
+    size, width = rows.shape
+    near = weight.shape[1]
+    own, tall = width // dp, d_out.shape[0] // dp
+    vmem = pl.BlockSpec(memory_space=pltpu.VMEM)
+    reduce_scratch = CtxReduce.scratch(size, width)
+    max_peers = max(dp, ctx)
     return pl.pallas_call(
         functools.partial(closing_kernel, dp, ctx),
-        in_specs=[pl.BlockSpec(memory_space=pltpu.VMEM)],
-        out_specs=pl.BlockSpec(memory_space=pltpu.VMEM),
-        out_shape=jax.ShapeDtypeStruct(tile, f32),
-        scratch_shapes=[
-            pltpu.VMEM((ctx, dp) + tile, f32),
+        in_specs=[vmem] * 9,
+        out_specs=[vmem] * 4,
+        out_shape=[
+            jax.ShapeDtypeStruct((size, width), f32),
+            jax.ShapeDtypeStruct((own // ctx, 3 * width), f32),
+            jax.ShapeDtypeStruct((tall, width), f32),
+            jax.ShapeDtypeStruct((ctx, 8, own), f32),
+        ],
+        scratch_shapes=reduce_scratch
+        + LineReduce.scratch(dp, (own, near))
+        + LineReduce.scratch(dp, (tall, width))
+        + [
+            pltpu.VMEM((2, width), f32),
+            pltpu.VMEM((dp, 8, own), f32),
+            pltpu.VMEM((dp, 8, own), f32),
+            pltpu.SemaphoreType.DMA((4, max_peers)),
+            pltpu.VMEM((own, near), f32),
+            pltpu.VMEM((own, near), bf16),
+            pltpu.VMEM((ctx, own // ctx, near), bf16),
             pltpu.SemaphoreType.DMA((2, ctx)),
-            pltpu.VMEM((dp,) + tile, f32),
-            pltpu.SemaphoreType.DMA((2, dp)),
         ],
-        compiler_params=pltpu.CompilerParams(collective_id=1, has_side_effects=True),
-        cost_estimate=pl.CostEstimate(flops=0, transcendentals=0, bytes_accessed=20 << 20),
-    )(parts)
+        compiler_params=pltpu.CompilerParams(
+            collective_id=1, has_side_effects=True, vmem_limit_bytes=60 << 20
+        ),
+        cost_estimate=pl.CostEstimate(
+            flops=2 * d_joined.size * width, transcendentals=0, bytes_accessed=200 << 20
+        ),
+    )(
+        d_joined, weight, d_qkv.reshape(dp, own, near), d_out.reshape(dp, tall, width),
+        rows, d_resid, gain.reshape(1, width), sums_two, bias,
+    )
 
 
 def turn(x, table_ref):
@@ -683,12 +1112,10 @@
     blocks = qkv_weight.reshape(rows_here, 3, pairs, 2, ctx, HD).transpose(4, 0, 2, 1, 3, 5)
     blocks = blocks.reshape(ctx, rows_here, near * 3 * HD)
     rows, grad_rows = inputs[0], cotangent[0]
-    if ctx == 4 and part == HD:
+    fused = ctx == 4 and dp % 2 == 0 and part == HD
+    if fused:
         small, joined_weight, out_full, rows_wide, grad_wide = opening(
             dp, ctx, small, blocks, out_weight, rows, grad_rows
-        )
-        gate_weight, up_weight, down_weight, _ = lax.optimization_barrier(
-            (gate_weight, up_weight, down_weight, rows_wide)
         )
     else:
         small = lax.all_gather(small[None, :], ("dp", "ctx"), axis=0, tiled=True)
@@ -721,11 +1148,13 @@
     normed_one = (scaled_wide * gain_one + shift_one).astype(bf16)
     joined = dot(normed_one, joined_weight)
     attended, qkv, lse = attend(joined, bias, table, start)
-    resid = rows.astype(f32) + scatter_ctx(dot(attended, out_full), ctx)
-
-    scaled_two, inv_two = norm_stats(resid)
-    normed_two = (scaled_two * gain_two + shift_two).astype(bf16)
-    normed_wide = gather_ctx(normed_two, ctx)
+    if fused:
+        resid, normed_wide = mix(dp, ctx, attended, out_full, rows, gain_two, shift_two)
+    else:
+        resid = rows.astype(f32) + scatter_ctx(dot(attended, out_full), ctx)
+        scaled_two, inv_two = norm_stats(resid)
+        normed_wide = gather_ctx((scaled_two * gain_two + shift_two).astype(bf16), ctx)
+
     gate = dot(normed_wide, gate_full)
     upward = dot(normed_wide, up_full)
     sigma = jax.nn.sigmoid(gate)
@@ -735,65 +1164,73 @@
     d_gate = (d_inner * upward * sigma * (1.0 + gate * (1.0 - sigma))).astype(bf16)
     d_upward = (d_inner * swish).astype(bf16)
     d_down = dot_tn(inner, grad_wide).astype(bf16)
-    d_normed_two = scatter_ctx(dot_nt(d_gate, gate_full) + dot_nt(d_upward, up_full), ctx, d_down)
+    d_down = lax.psum_scatter(d_down, "dp", scatter_dimension=1, tiled=True).astype(f32)
     d_gate_weight = dot_tn(normed_wide, d_gate).astype(bf16)
     d_up_weight = dot_tn(normed_wide, d_upward).astype(bf16)
-    d_normed_two, _, _ = lax.optimization_barrier((d_normed_two, d_gate_weight, d_up_weight))
-    d_down = lax.psum_scatter(d_down, "dp", scatter_dimension=1, tiled=True).astype(f32)
+    branch = dot(inner, down_full)
+    if fused:
+        d_resid, sums_two, d_proj = mix_back(
+            dp, ctx, d_gate, d_upward, gate_full, up_full, resid, grad_rows, gain_two
+        )
+    else:
+        d_normed_two = scatter_ctx(dot_nt(d_gate, gate_full) + dot_nt(d_upward, up_full), ctx)
+        grad, d_gain_two, d_shift_two = norm_backward(d_normed_two, scaled_two, inv_two, gain_two)
+        d_resid = grad_rows.astype(f32) + grad
+        d_proj = gather_ctx(d_resid.astype(bf16), ctx)
+    branch, d_gate_weight, d_up_weight, _ = lax.optimization_barrier(
+        (branch, d_gate_weight, d_up_weight, d_proj)
+    )
+    output = (resid + scatter_ctx(branch, ctx)).astype(bf16)
     d_gate_weight = lax.psum_scatter(d_gate_weight, "dp", scatter_dimension=0, tiled=True).astype(f32)
     d_up_weight = lax.psum_scatter(d_up_weight, "dp", scatter_dimension=0, tiled=True).astype(f32)
-    branch = dot(inner, down_full)
-
-    d_resid_norm, d_gain_two, d_shift_two = norm_backward(d_normed_two, scaled_two, inv_two, gain_two)
-    d_resid = grad_rows.astype(f32) + d_resid_norm
-    d_proj = gather_ctx(d_resid.astype(bf16), ctx)
-    branch, _ = lax.optimization_barrier((branch, d_proj))
-    output = (resid + scatter_ctx(branch, ctx)).astype(bf16)
+
     d_attended = dot_nt(d_proj, out_full).astype(bf16)
     d_out_weight = dot_tn(attended, d_proj).astype(bf16)
-    if part == HD:
-        d_out_weight = lax.psum_scatter(d_out_weight, "dp", scatter_dimension=0, tiled=True)
+    d_joined, d_bias = attend_back(qkv, d_attended, lse, table, start)
+    d_joined_weight = dot_tn(normed_one, d_joined).astype(bf16)
+    d_bias = d_bias.reshape(pairs, 3, 2, HD).transpose(1, 0, 2, 3)
+    if fused:
+        d_bias = jnp.pad(d_bias.reshape(dp, -1), ((0, 0), (0, width // dp - near * 3 * HD // dp)))
+        grad_input, d_joined_weight, d_out_weight, small = closing(
+            dp, ctx, d_joined, joined_weight, d_joined_weight, d_out_weight, rows, d_resid, gain_one, sums_two, d_bias
+        )
+        vectors = lax.dynamic_slice_in_dim(jnp.sum(small[:, :4], axis=0), me * part, part, 1)
+        d_gain_one, d_shift_one, d_gain_two, d_shift_two = vectors
+        d_bias = small[:, 4, : near * 3 * HD // dp].reshape(ctx, -1, HD).transpose(1, 0, 2)
+        d_bias = lax.dynamic_index_in_dim(d_bias.reshape(ctx, -1), me, 0, keepdims=False)
     else:
         at_me = lax.broadcasted_iota(jnp.int32, (1, ctx, 1, 1), 1) == me
         d_out_weight = jnp.where(at_me, d_out_weight.reshape(near, 1, HD, width), jnp.zeros((), bf16))
         d_out_weight = lax.psum_scatter(
             d_out_weight.reshape(width, width), ("dp", "ctx"), scatter_dimension=0, tiled=True
+        ).astype(f32)
+        d_normed_one = scatter_ctx(dot_nt(d_joined, joined_weight), ctx)
+        scaled_one, inv_one = norm_stats(rows.astype(f32))
+        grad, d_gain_one, d_shift_one = norm_backward(d_normed_one, scaled_one, inv_one, gain_one)
+        grad_input = d_resid + grad
+        d_joined_weight = lax.psum_scatter(d_joined_weight, "dp", scatter_dimension=0, tiled=True)
+        blocks = exchange_ctx(d_joined_weight.reshape(ctx, rows_here, near * 3 * HD), ctx)
+        blocks = blocks.reshape(ctx, rows_here, pairs, 3, 2, HD).transpose(1, 3, 2, 4, 0, 5)
+        d_joined_weight = blocks.reshape(rows_here, 3 * width).astype(f32)
+        at_me = (lax.broadcasted_iota(jnp.int32, (1, 1, 1, ctx, 1), 3) == me).astype(f32)
+        d_bias = (d_bias[:, :, :, None, :] * at_me).reshape(dp * ctx, -1)
+        small = jnp.concatenate(
+            [t.reshape(dp * ctx, part) for t in (d_gain_one, d_shift_one, d_gain_two, d_shift_two)]
+            + [d_bias],
+            axis=1,
         )
-    d_out_weight = d_out_weight.astype(f32)
-
-    d_joined, d_bias = attend_back(qkv, d_attended, lse, table, start)
-    d_normed_one = scatter_ctx(dot_nt(d_joined, joined_weight), ctx)
-    d_joined_weight = lax.psum_scatter(
-        dot_tn(normed_one, d_joined).astype(bf16), "dp", scatter_dimension=0, tiled=True
-    )
-    blocks = exchange_ctx(d_joined_weight.reshape(ctx, rows_here, near * 3 * HD), ctx)
-    blocks = blocks.reshape(ctx, rows_here, pairs, 3, 2, HD).transpose(1, 3, 2, 4, 0, 5)
-    d_joined_weight = blocks.reshape(rows_here, 3 * width).astype(f32)
-
-    scaled_one, inv_one = norm_stats(rows.astype(f32))
-    d_rows_norm, d_gain_one, d_shift_one = norm_backward(d_normed_one, scaled_one, inv_one, gain_one)
-    grad_input = d_resid + d_rows_norm
-
-    d_bias = d_bias.reshape(pairs, 3, 2, HD).transpose(1, 0, 2, 3)[:, :, :, None, :]
-    at_me = (lax.broadcasted_iota(jnp.int32, (1, 1, 1, ctx, 1), 3) == me).astype(f32)
-    d_bias = (d_bias * at_me).reshape(dp * ctx, -1)
-    small = jnp.concatenate(
-        [t.reshape(dp * ctx, part) for t in (d_gain_one, d_shift_one, d_gain_two, d_shift_two)]
-        + [d_bias],
-        axis=1,
-    )
-    small = jnp.pad(small, ((0, 0), (0, 1024 - count))).reshape(dp, ctx, 8, 128)
-    small = closing(dp, ctx, small.transpose(1, 0, 2, 3)).reshape(1024)[:count]
-    d_gain_one, d_shift_one, d_gain_two, d_shift_two = [
-        small[i * part : (i + 1) * part] for i in range(4)
-    ]
+        small = lax.psum_scatter(small, ("dp", "ctx"), scatter_dimension=0, tiled=True)[0]
+        d_gain_one, d_shift_one, d_gain_two, d_shift_two = [
+            small[i * part : (i + 1) * part] for i in range(4)
+        ]
+        d_bias = small[4 * part :]
     return (
         output[None],
         grad_input[None],
         d_gain_one,
         d_shift_one,
         d_joined_weight,
-        small[4 * part :],
+        d_bias,
         d_out_weight,
         d_gain_two,
         d_shift_two,

time: 811 us -> 712 us (0.88)
  Pallas kernels: 157 us -> 516 us
  waiting for transfers between devices: 337 us -> 2.63 us
  matrix products: 143 us -> 110 us
  other arithmetic: 55.6 us -> 23.5 us
  local copies, waits for them, and re-layouts: 64.6 us -> 35 us
  starting transfers between devices: 32.9 us -> 4.84 us
    pallas_call x1 -> x3, Pallas kernels: 18 us -> 312 us  [the longest x1 153 us: closing(): pl.pallas_call(functools.partial(closing_kernel, dp, ctx), in_specs=[vmem...]
    ppermute x27 -> x4, waiting for transfers between devices: 140 us -> 0.01 us  [hop(): return lax.ppermute(x, 'ctx', partner(n, k))]
    pallas_call x1, Pallas kernels: 98.7 us -> 164 us  [opening(): pl.pallas_call(functools.partial(opening_kernel, dp, ctx), in_specs=[ANY]...]
    reduce_scatter x1, waiting for transfers between devices: 63.3 us -> 0.01 us  [shards(): lax.psum_scatter(d_down, 'dp', scatter_dimension=1, tiled=True).astype(f32)]
    reduce_scatter x1, waiting for transfers between devices: 63.2 us -> 0.01 us  [shards(): lax.psum_scatter(d_up_weight, 'dp', scatter_dimension=0, tiled=True)]
    reduce_scatter x1, waiting for transfers between devices: 47.6 us -> 0.01 us  [shards(): lax.psum_scatter(d_gate_weight, 'dp', scatter_dimension=0, tiled=True)]
    ppermute x27 -> x4, starting transfers between devices: 32.6 us -> 4.2 us  [hop(): return lax.ppermute(x, 'ctx', partner(n, k))]
    dot_general x5 -> x2, matrix products: 46.2 us -> 21.5 us  [dot_nt(): lax.dot_general(a, b, (((1,), (1,)), ((), ())), preferred_element_type=f32)]
  transfers between devices with their start and end apart: 35 -> 10, of which waited for: 25 -> 0; matrix products, arithmetic and copies ran while one was open for 19% -> 18% of each run, Pallas kernels for 5% -> 73%
where the time goes in v3:
time: 712 us; the launch traced here: 706 us
  Pallas kernels  516 us (72%)
  matrix products  110 us (15%)
  local copies, waits for them, and re-layouts  35 us (5%)
  other arithmetic  23.5 us (3%)
  between operations  14.8 us (2%)
    pallas_call x1, Pallas kernels, opening(): pl.pallas_call(functools.partial(opening_kernel, dp, ctx), in_specs=[ANY]...  164 us
    pallas_call x1, Pallas kernels, closing(): pl.pallas_call(functools.partial(closing_kernel, dp, ctx), in_specs=[vmem...  153 us
    pallas_call x1, Pallas kernels, mix_back(): pl.pallas_call(functools.partial(mix_back_kernel, dp, ctx), in_specs=[vme...  84.5 us
    pallas_call x1, Pallas kernels, mix(): pl.pallas_call(functools.partial(mix_kernel, dp, ctx), in_specs=[vmem] *...  73.7 us
    dot_general x5, matrix products, dot_tn(): lax.dot_general(a, b, (((0,), (0,)), ((), ())), preferred_element_type=f32)  44.6 us
    dot_general x4, matrix products, dot(): return jnp.dot(a, b, preferred_element_type=f32)  43.3 us
    pallas_call x1, Pallas kernels, attend_back(): pl.pallas_call(functools.partial(attend_back_kernel, step), grid=(pairs,)...  21.8 us
    dot_general x2, matrix products, dot_nt(): lax.dot_general(a, b, (((1,), (1,)), ((), ())), preferred_element_type=f32)  21.5 us
  transfers between devices with their start and end apart: 10, of which 0 were waited for; matrix products, arithmetic and copies ran while one was open for 18% of the time, Pallas kernels for 73%

profile of v3, /device:TPU:0, one launch (start us, length us, event | category | flops | bytes accessed | tf_op | source)
XLA Modules:
  0.0 706.4 jit_solution(12956045019326293431)
XLA Ops:
  7.2 0.7 all-gather.6.cloned.1.call-update
  8.0 0.7 all-gather.4.cloned.1.call-update
  8.7 0.7 all-gather.8.cloned.1.call-update
  9.5 1.9 multiply_cosine_fusion
  11.5 1.1 concatenate.28
  12.6 1.7 concatenate.29
  14.4 3.4 reshape.88
  17.8 2.7 copy.46
  20.5 1.7 reshape.89.blocks_ref
  22.3 0.1 concatenate.26
  22.4 0.6 bitcast_convert_fusion.small_ref
  23.0 164.4 %shard_map.220 = (f32[8,4,8,128]{3,2,1,0:T(8,128)}, bf16[2048,1536]{1,0:T(8,128)(2,1)}, bf16[512,2048]{1,0:T(8,128)(2,1)}, bf16[1024,2048]{1,0:T(8,128)(2,1)}, bf16[1024,2048]{1,0:T(8,128)(2,1)}) custom-call(f32[8,128]{1,0:T(8,128)} %bitcast_convert_fusion.small_ref, bf16[4,64,1536]{2,1,0:T(8,128)(2,1)} %reshape.89.blocks_ref, ...), custom_call_target="tpu_custom_call" | custom-call | bytes 209715200 | tf_op jit(solution)/shard_map/pallas_call | solution.py:397
  187.5 1.0 copy.47
  189.1 1.9 concatenate.27
  191.0 1.5 pad_maximum_fusion.table_ref
  192.5 0.6 convert_reduce_fusion.1
  193.1 3.0 convert_reduce_fusion
  196.1 1.2 fusion.2
  197.3 9.1 %fusion.12.joined_ref = f32[1024,1536]{1,0:T(8,128)} fusion(bf16[2048,1536]{1,0:T(8,128)(2,1)S(1)} %copy-done.23, bf16[1024,2048]{1,0:T(8,128)(2,1)S(1)} %copy-done.13, f32[2048]{0:T(1024)S(1)} %add.78, f32[2048]{0:T(1024)S(1)} %mul.136, f32[1024]{0:T(1024)S(1)} %add_rsqrt_fusion, f32[1024]{0:T(1024)S(1)} %broadcast_multiply_fusion), kind=kOutput, calls=%fused_computation.53 | convolution fusion | flops 6455033856 | bytes 16801792 | tf_op jit(solution)/shard_map/dot_general | solution.py:23
  206.4 0.2 broadcast_in_dim.24.start_ref
  206.6 18.3 %shard_map.221 = (bf16[1024,512]{1,0:T(8,128)(2,1)S(1)}, bf16[1024,1536]{1,0:T(8,128)(2,1)S(1)}, f32[1024,512]{1,0:T(8,128)S(1)}) custom-call(f32[1024,1536]{1,0:T(8,128)} %fusion.12.joined_ref, f32[1,1536]{1,0:T(1,128)S(1)} %reshape.92.bias_ref, f32[3,1024,128]{2,1,0:T(8,128)S(1)} %pad_maximum_fusion.table_ref, s32[1024,128]{1,0:T(8,128)S(1)} %broadcast_in_dim.24.start_ref), custom_call_target="tpu_custom_call" | custom-call | flops 2415919104 | bytes 12582912 | tf_op jit(solution)/shard_map/pallas_call | solution.py:1022
  224.9 1.7 copy-done.5
  226.7 1.3 copy-done.7
  228.0 73.7 %shard_map.222 = (f32[256,2048]{1,0:T(8,128)S(1)}, bf16[1024,2048]{1,0:T(8,128)(2,1)S(1)}) custom-call(bf16[1024,512]{1,0:T(8,128)(2,1)S(1)} %get-tuple-element.37.attended_ref, bf16[512,2048]{1,0:T(8,128)(2,1)S(1)} %copy-done.4, bf16[256,2048]{1,0:T(8,128)(2,1)S(1)} %bitcast.62, f32[1,2048]{1,0:T(1,128)S(1)} %reshape_reshape.8.gain_ref, ...), custom_call_target="tpu_custom_call" | custom-call | flops 2147483648 | bytes 188743680 | tf_op jit(solution)/shard_map/pallas_call | solution.py:564
  301.7 1.3 copy-done
  303.1 2.0 copy-done.11
  305.1 11.7 %fusion.17 = f32[1024,1408]{1,0:T(8,128)} fusion(bf16[1024,2048]{1,0:T(8,128)(2,1)} %copy-done.11, bf16[2048,1408]{1,0:T(8,128)(2,1)} %all-gather.6.cloned.1.call-done.up_weight_ref), kind=kOutput, calls=%fused_computation.57 | convolution fusion | flops 5905580032 | bytes 15728640 | tf_op jit(solution)/shard_map/dot_general | solution.py:23
  316.8 11.7 %fusion.16 = f32[1024,1408]{1,0:T(8,128)} fusion(bf16[1024,2048]{1,0:T(8,128)(2,1)} %copy-done.11, bf16[2048,1408]{1,0:T(8,128)(2,1)} %all-gather.4.cloned.1.call-done.gate_weight_ref), kind=kOutput, calls=%fused_computation.56 | convolution fusion | flops 5905580032 | bytes 15728640 | tf_op jit(solution)/shard_map/dot_general | solution.py:23
  328.5 16.2 %multiply_convert_fusion = (bf16[1024,1408]{1,0:T(8,128)(2,1)}, bf16[1024,1408]{1,0:T(8,128)(2,1)}, bf16[1024,1408]{1,0:T(8,128)(2,1)S(1)}) fusion(f32[1024,1408]{1,0:T(8,128)} %fusion.16, f32[1024,1408]{1,0:T(8,128)} %fusion.17, bf16[1024,2048]{1,0:T(8,128)(2,1)} %get-tuple-element.41, bf16[1408,2048]{1,0:T(8,128)(2,1)} %all-gather.8.cloned.1.call-done), kind=kOutput, calls=%fused_computation.12 | convolution fusion | flops 5927206912 | bytes 30146560 | tf_op jit(solution)/shard_map/dot_general | solution.py:27
  344.7 1.6 copy-done.26
  346.3 8.1 %convolution_convert_fusion = bf16[1408,2048]{1,0:T(8,128)(2,1)} fusion(bf16[1024,1408]{1,0:T(8,128)(2,1)S(1)} %get-tuple-element.58, bf16[1024,2048]{1,0:T(8,128)(2,1)S(1)} %copy-done.24), kind=kOutput, calls=%fused_computation.8 | convolution fusion | flops 5908463616 | bytes 12845056 | tf_op jit(solution)/shard_map/dot_general | solution.py:31
  354.4 0.4 reduce-scatter.6.cloned.1.call-start
  354.9 84.5 %shard_map.223 = (f32[256,2048]{1,0:T(8,128)}, f32[2,2048]{1,0:T(2,128)}, bf16[1024,2048]{1,0:T(8,128)(2,1)}) custom-call(bf16[1024,1408]{1,0:T(8,128)(2,1)} %get-tuple-element.57.gate_ref, bf16[1024,1408]{1,0:T(8,128)(2,1)} %get-tuple-element.56.up_ref, bf16[2048,1408]{1,0:T(8,128)(2,1)} %all-gather.4.cloned.1.call-done.gate_weight_ref, ...), custom_call_target="tpu_custom_call" | custom-call | flops 11811160064 | bytes 188743680 | tf_op jit(solution)/shard_map/pallas_call | solution.py:623
  439.5 10.8 %fusion.18 = f32[1024,2048]{1,0:T(8,128)} fusion(bf16[1024,1408]{1,0:T(8,128)(2,1)S(1)} %copy-done.27, bf16[1408,2048]{1,0:T(8,128)(2,1)} %all-gather.8.cloned.1.call-done), kind=kOutput, calls=%fused_computation.58 | convolution fusion | flops 5905580032 | bytes 17039360 | tf_op jit(solution)/shard_map/dot_general | solution.py:23
  450.3 8.7 %convolution_convert_fusion.2 = bf16[2048,1408]{1,0:T(8,128)(2,1)} fusion(bf16[1024,2048]{1,0:T(8,128)(2,1)S(1)} %copy-done.12, bf16[1024,1408]{1,0:T(8,128)(2,1)S(1)} %copy-done.28), kind=kOutput, calls=%fused_computation.10 | convolution fusion | flops 5908463616 | bytes 12845056 | tf_op jit(solution)/shard_map/dot_general | solution.py:31
  459.0 11.0 %convolution_convert_fusion.3 = bf16[2048,1408]{1,0:T(8,128)(2,1)} fusion(bf16[1024,2048]{1,0:T(8,128)(2,1)} %copy-done.11, bf16[1024,1408]{1,0:T(8,128)(2,1)} %get-tuple-element.57.gate_ref), kind=kOutput, calls=%fused_computation.11 | convolution fusion | flops 5908463616 | bytes 12845056 | tf_op jit(solution)/shard_map/dot_general | solution.py:31
  470.0 0.5 reduce-scatter.4.cloned.1.call-update
  470.6 0.7 broadcast_in_dim_reshape.4.gain_ref
  471.3 5.4 convolution_convert_fusion.5.grad_ref
  476.6 21.8 %shard_map.224 = (bf16[1024,1536]{1,0:T(8,128)(2,1)S(1)}, f32[1,1536]{1,0:T(1,128)S(1)}) custom-call(bf16[1024,1536]{1,0:T(8,128)(2,1)S(1)} %copy-done.6, bf16[1024,512]{1,0:T(8,128)(2,1)S(1)} %convolution_convert_fusion.5.grad_ref, f32[1024,512]{1,0:T(8,128)S(1)} %copy-done.8, f32[3,1024,128]{2,1,0:T(8,128)S(1)} %pad_maximum_fusion.table_ref, ...), custom_call_target="tpu_custom_call" | custom-call | flops 6039797760 | bytes 12582912 | tf_op jit(solution)/shard_map/pallas_call | solution.py:1051
  498.5 1.6 copy-done.9
  500.3 0.6 pad.10.bias_ref
  500.9 2.1 dynamic-slice_convert_fusion
  503.1 1.5 collective-permute-start
  504.6 1.5 collective-permute-start.2
  506.0 1.7 dynamic-slice_convert_fusion.2
  507.8 13.0 %convolution_convert_fusion.1 = bf16[2048,1536]{1,0:T(8,128)(2,1)} fusion(bf16[1024,1536]{1,0:T(8,128)(2,1)S(1)} %copy-done.10, bf16[1024,2048]{1,0:T(8,128)(2,1)} %get-tuple-element.34, f32[2048]{0:T(1024)S(1)} %add.78, f32[2048]{0:T(1024)S(1)} %mul.136, f32[1024]{0:T(1024)S(1)} %add_rsqrt_fusion, f32[1024]{0:T(1024)S(1)} %broadcast_multiply_fusion), kind=kOutput, calls=%fused_computation.9 | convolution fusion | flops 6458179584 | bytes 13656064 | tf_op jit(solution)/shard_map/dot_general | solution.py:31
  520.8 3.8 convolution_convert_fusion.4
  524.6 1.9 fusion.9
  526.6 0.6 collective-permute-start.3
  527.2 1.1 pad_maximum_fusion.1
  528.3 0.6 collective-permute-start.1
  528.8 153.3 %shard_map.225 = (f32[256,2048]{1,0:T(8,128)}, f32[64,6144]{1,0:T(8,128)}, f32[64,2048]{1,0:T(8,128)}, f32[4,8,256]{2,1,0:T(8,128)}) custom-call(bf16[1024,1536]{1,0:T(8,128)(2,1)} %copy-done.9, bf16[2048,1536]{1,0:T(8,128)(2,1)} %get-tuple-element.36.weight_ref, bf16[8,256,1536]{2,1,0:T(8,128)(2,1)} %bitcast.78, bf16[8,64,2048]{2,1,0:T(8,128)(2,1)} %bitcast.79, ...), custom_call_target="tpu_custom_call" | custom-call | flops 6442450944 | bytes 209715200 | tf_op jit(solution)/shard_map/pallas_call | solution.py:861
  682.2 0.8 slice_reduce_fusion.1
  683.1 0.6 constant_dynamic-slice_fusion
  683.7 0.8 slice_reduce_fusion
  684.6 0.5 slice_bitcast_fusion
  685.1 3.8 fusion.7
  688.9 2.5 convert_element_type.112
  691.4 2.3 convert_element_type.110
  693.7 2.4 convert_element_type.109
  696.1 1.3 copy.53
  697.4 1.1 copy.54
  698.6 0.8 copy.55
  (96 shorter events, 1.7 us)
Async XLA Ops:
  7.2 297.9 %all-gather.6.cloned.1.call-start = ((), (), s32[]{:S(2)}) async-start(), calls=%async_computation.4 | async-start | bytes 6488064 | tf_op jit(solution)/shard_map/all_gather | solution.py:1140
  7.9 308.9 %all-gather.4.cloned.1.call-start = ((), (), s32[]{:S(2)}) async-start(), calls=%async_computation.3 | async-start | bytes 6488064 | tf_op jit(solution)/shard_map/all_gather | solution.py:1139
  8.7 319.9 %all-gather.8.cloned.1.call-start = ((), (), s32[]{:S(2)}) async-start(), calls=%async_computation.5 | async-start | bytes 6488064 | tf_op jit(solution)/shard_map/all_gather | solution.py:1141
  9.4 679.5 %reduce-scatter.8.cloned.1.call-start = ((), (), s32[]{:S(2)}) async-start(), calls=%async_computation.8 | async-start | bytes 6488064 | tf_op jit(solution)/shard_map/reduce_scatter | solution.py:1167
  14.3 7.9 %copy-start.18 = (bf16[64]{0:T(256)(128)(2,1)S(1)}, bf16[64]{0:T(256)(128)(2,1)}, u32[]{:S(2)}) copy-start(bf16[64]{0:T(256)(128)(2,1)} %param.15) | copy-start | bytes 388
  14.3 7.9 %copy-start.19 = (bf16[64]{0:T(256)(128)(2,1)S(1)}, bf16[64]{0:T(256)(128)(2,1)}, u32[]{:S(2)}) copy-start(bf16[64]{0:T(256)(128)(2,1)} %param.16) | copy-start | bytes 388
  14.3 7.9 %copy-start.20 = (bf16[64]{0:T(256)(128)(2,1)S(1)}, bf16[64]{0:T(256)(128)(2,1)}, u32[]{:S(2)}) copy-start(bf16[64]{0:T(256)(128)(2,1)} %param.20) | copy-start | bytes 388
  14.3 7.9 %copy-start.21 = (bf16[64]{0:T(256)(128)(2,1)S(1)}, bf16[64]{0:T(256)(128)(2,1)}, u32[]{:S(2)}) copy-start(bf16[64]{0:T(256)(128)(2,1)} %param.21) | copy-start | bytes 388
  14.4 7.9 %copy-start.22 = (bf16[192]{0:T(256)(128)(2,1)S(1)}, bf16[192]{0:T(256)(128)(2,1)}, u32[]{:S(2)}) copy-start(bf16[192]{0:T(256)(128)(2,1)} %param.18) | copy-start | bytes 1156
  187.4 5.1 copy-start.17
  188.7 39.3 %copy-start.3 = (f32[1,2048]{1,0:T(1,128)}, f32[1,2048]{1,0:T(1,128)S(1)}, u32[]{:S(2)}) copy-start(f32[1,2048]{1,0:T(1,128)S(1)} %reshape_reshape.8.gain_ref) | copy-start | bytes 24580
  191.0 5.0 copy-start.13
  193.1 4.2 copy-start.23
  206.6 21.4 %copy-start.2 = (bf16[1,256,2048]{2,1,0:T(8,128)(2,1)S(1)}, bf16[1,256,2048]{2,1,0:T(8,128)(2,1)}, u32[]{:S(2)}) copy-start(bf16[1,256,2048]{2,1,0:T(8,128)(2,1)} %param.13) | copy-start | bytes 3145732
  206.6 21.4 %copy-start.4 = (bf16[512,2048]{1,0:T(8,128)(2,1)S(1)}, bf16[512,2048]{1,0:T(8,128)(2,1)}, u32[]{:S(2)}) copy-start(bf16[512,2048]{1,0:T(8,128)(2,1)} %get-tuple-element.38.weight_ref) | copy-start | bytes 6291460
  224.9 1.7 copy-start.5
  226.7 1.3 copy-start.7
  301.7 1.3 copy-start
  303.1 2.0 copy-start.11
  328.5 17.8 %copy-start.24 = (bf16[1024,2048]{1,0:T(8,128)(2,1)S(1)}, bf16[1024,2048]{1,0:T(8,128)(2,1)}, u32[]{:S(2)}) copy-start(bf16[1024,2048]{1,0:T(8,128)(2,1)} %get-tuple-element.41) | copy-start | bytes 12582916
  344.7 1.6 copy-start.26
  354.4 336.9 %reduce-scatter.6.cloned.1.call-start = ((), (), s32[]{:S(2)}) async-start(), calls=%async_computation.7 | async-start | bytes 6488064 | tf_op jit(solution)/shard_map/reduce_scatter | solution.py:1185
  354.9 84.5 %copy-start.27 = (bf16[1024,1408]{1,0:T(8,128)(2,1)S(1)}, bf16[1024,1408]{1,0:T(8,128)(2,1)}, u32[]{:S(2)}) copy-start(bf16[1024,1408]{1,0:T(8,128)(2,1)} %copy-done.26) | copy-start | bytes 8650756
  439.4 10.8 %copy-start.12 = (bf16[1024,2048]{1,0:T(8,128)(2,1)S(1)}, bf16[1024,2048]{1,0:T(8,128)(2,1)}, u32[]{:S(2)}) copy-start(bf16[1024,2048]{1,0:T(8,128)(2,1)} %copy-done.11) | copy-start | bytes 12582916
  439.5 10.8 %copy-start.28 = (bf16[1024,1408]{1,0:T(8,128)(2,1)S(1)}, bf16[1024,1408]{1,0:T(8,128)(2,1)}, u32[]{:S(2)}) copy-start(bf16[1024,1408]{1,0:T(8,128)(2,1)} %get-tuple-element.56.up_ref) | copy-start | bytes 8650756
  470.0 223.7 %reduce-scatter.4.cloned.1.call-start = ((), (), s32[]{:S(2)}) async-start(), calls=%async_computation.6 | async-start | bytes 6488064 | tf_op jit(solution)/shard_map/reduce_scatter | solution.py:1184
  471.3 5.4 copy-start.6
  471.3 5.4 copy-start.8
  498.4 1.6 copy-start.9
  500.3 7.5 %copy-start.10 = (bf16[1024,1536]{1,0:T(8,128)(2,1)S(1)}, bf16[1024,1536]{1,0:T(8,128)(2,1)}, u32[]{:S(2)}) copy-start(bf16[1024,1536]{1,0:T(8,128)(2,1)} %copy-done.9) | copy-start | bytes 9437188
  503.1 21.6 %collective-permute-start = (bf16[128,2048]{1,0:T(8,128)(2,1)S(1)}, bf16[128,2048]{1,0:T(8,128)(2,1)S(1)}, u32[]{:S(2)}, u32[]{:S(2)}) collective-permute-start(bf16[128,2048]{1,0:T(8,128)(2,1)S(1)} %get-tuple-element.63), channel_id=1, source_target_pairs={{0,2},{1,3},{2,0},{3,1},{4,6},{5,7},{6,4},{7,5},{8,10},{9,11},{10,... | collective-permute-start | bytes 1572872 | tf_op jit(solution)/shard_map/ppermute | solution.py:59
  504.6 20.0 %collective-permute-start.2 = (bf16[128,2048]{1,0:T(8,128)(2,1)S(1)}, bf16[128,2048]{1,0:T(8,128)(2,1)S(1)}, u32[]{:S(2)}, u32[]{:S(2)}) collective-permute-start(bf16[128,2048]{1,0:T(8,128)(2,1)S(1)} %get-tuple-element.64), channel_id=1, source_target_pairs={{0,1},{1,0},{2,3},{3,2},{4,5},{5,4},{6,7},{7,6},{8,9},{9,8},{10,11... | collective-permute-start | bytes 1572872 | tf_op jit(solution)/shard_map/ppermute | solution.py:59
  507.8 13.0 %copy-start.25 = (bf16[1024,2048]{1,0:T(8,128)(2,1)S(1)}, bf16[1024,2048]{1,0:T(8,128)(2,1)}, u32[]{:S(2)}) copy-start(bf16[1024,2048]{1,0:T(8,128)(2,1)} %get-tuple-element.42) | copy-start | bytes 12582916
  526.6 158.5 %collective-permute-start.3 = (bf16[256,2048]{1,0:T(8,128)(2,1)S(1)}, bf16[256,2048]{1,0:T(8,128)(2,1)}, u32[]{:S(2)}, u32[]{:S(2)}) collective-permute-start(bf16[256,2048]{1,0:T(8,128)(2,1)S(1)} %pad_maximum_fusion.2), channel_id=1, source_target_pairs={{0,2},{1,3},{2,0},{3,1},{4,6},{5,7},{6,4},{7,5},{8,10},{9,11},{10,... | collective-permute-start | bytes 3145736 | tf_op jit(solution)/shard_map/ppermute | solution.py:59
  528.3 156.8 %collective-permute-start.1 = (bf16[256,2048]{1,0:T(8,128)(2,1)}, bf16[256,2048]{1,0:T(8,128)(2,1)}, u32[]{:S(2)}, u32[]{:S(2)}) collective-permute-start(bf16[256,2048]{1,0:T(8,128)(2,1)} %pad_maximum_fusion.1), channel_id=1, source_target_pairs={{0,1},{1,0},{2,3},{3,2},{4,5},{5,4},{6,7},{7,6},{8,9},{9,8},{10,11... | collective-permute-start | bytes 3145736 | tf_op jit(solution)/shard_map/ppermute | solution.py:59
  528.8 156.3 %copy-start.1 = (f32[256,2048]{1,0:T(8,128)S(1)}, f32[256,2048]{1,0:T(8,128)}, u32[]{:S(2)}) copy-start(f32[256,2048]{1,0:T(8,128)} %copy-done) | copy-start | bytes 6291460
  688.9 7.2 %copy-start.14 = (f32[256,2048]{1,0:T(8,128)S(1)}, f32[256,2048]{1,0:T(8,128)}, u32[]{:S(2)}) copy-start(f32[256,2048]{1,0:T(8,128)} %get-tuple-element.50) | copy-start | bytes 6291460
  693.7 3.8 copy-start.15
  696.1 2.5 copy-start.16
Sparse Core Ops, SparseCore 0:
  9.7 80.6 all-gather.5
  91.9 85.6 all-gather.3
  179.3 60.7 all-gather.7
  354.6 64.5 reduce-scatter.7
  470.1 64.1 reduce-scatter.5
  536.5 114.3 reduce-scatter.3

commit v4 on v3

--- a/solution.py
+++ b/solution.py
@@ -3,6 +3,7 @@
 
 import jax
 import jax.numpy as jnp
+import numpy as np
 from jax import lax
 from jax.experimental import pallas as pl
 from jax.experimental.pallas import tpu as pltpu
@@ -147,25 +148,11 @@
         return (self.row - 2, self.col)
 
 
-def greet(place, ctx, column=False):
+def greet(place, ctx):
     barrier = pltpu.get_barrier_semaphore()
     for k in range(1, ctx):
         pl.semaphore_signal(barrier, 1, device_id=place.across(k), device_id_type=MESH)
-    if not column:
-        pl.semaphore_wait(barrier, ctx - 1)
-        return
-    pl.semaphore_signal(barrier, 1, device_id=place.twin, device_id_type=MESH)
-
-    @pl.when(place.line > 0)
-    def _():
-        pl.semaphore_signal(barrier, 1, device_id=place.below(), device_id_type=MESH)
-
-    @pl.when(place.line < place.lines - 1)
-    def _():
-        pl.semaphore_signal(barrier, 1, device_id=place.above(), device_id_type=MESH)
-
-    peers = ctx + (place.line > 0).astype(jnp.int32) + (place.line < place.lines - 1).astype(jnp.int32)
-    pl.semaphore_wait(barrier, peers)
+    pl.semaphore_wait(barrier, ctx - 1)
 
 
 def remote(src, dst, send, recv, device):
@@ -306,18 +293,39 @@
         return pltpu.SemaphoreType.DMA((2, 4))
 
 
+def greet_all(place, dp, ctx):
+    barrier = pltpu.get_barrier_semaphore()
+    for k in range(1, ctx):
+        pl.semaphore_signal(barrier, 1, device_id=place.across(k), device_id_type=MESH)
+    for k in range(1, dp):
+        pl.semaphore_signal(barrier, 1, device_id=((place.row + k) % dp, place.col), device_id_type=MESH)
+    pl.semaphore_wait(barrier, ctx + dp - 2)
+
+
 def opening_kernel(
     dp, ctx,
-    small_ref, blocks_ref, out_weight_ref, rows_ref, cot_ref,
-    small_all, joined_all, out_all, rows_all, cot_all,
-    local_sem, swap_sem, line_small, line_joined, line_out, rows_sem, cot_sem,
+    small_ref, qkv_ref, out_weight_ref, rows_ref, cot_ref,
+    small_all, params_ref, joined_all, out_all, normed_ref, cot_all,
+    blocks, rows_all, local_sem, swap_sem, small_sem, line_joined, line_out, rows_sem, cot_sem,
 ):
     place = Place(dp)
-    greet(place, ctx, column=True)
     me, row = place.col, place.row
-    depth = blocks_ref.shape[1]
-    length = rows_ref.shape[0]
+    depth = qkv_ref.shape[0]
+    length, width = rows_ref.shape
     rows_out = out_weight_ref.shape[0]
+
+    low = head_lanes((depth, PAIR))
+    for p in range(width // HD // ctx // 2):
+        for t in range(3):
+            lanes = slice((3 * p + t) * PAIR, (3 * p + t + 1) * PAIR)
+            for c in range(0, ctx, 2):
+                at = t * width + (2 * p * ctx + c) * HD
+                a = qkv_ref[:, at : at + PAIR].astype(f32)
+                at = at + ctx * HD
+                b = qkv_ref[:, at : at + PAIR].astype(f32)
+                blocks[c, :, lanes] = jnp.where(low, a, pltpu.roll(b, HD, 1)).astype(bf16)
+                blocks[c + 1, :, lanes] = jnp.where(low, pltpu.roll(a, HD, 1), b).astype(bf16)
+    greet_all(place, dp, ctx)
 
     def joined_rows(row, col):
         return joined_all.at[pl.ds(pl.multiple_of((row * ctx + col) * depth, depth), depth), :]
@@ -328,44 +336,75 @@
     def out_shard(row):
         return out_all.at[pl.ds(pl.multiple_of(row * rows_out, rows_out), rows_out), :]
 
+    def block(ref, col):
+        return ref.at[pl.ds(pl.multiple_of(col * length, length), length), :]
+
     local = [
-        pltpu.make_async_copy(small_ref, small_all.at[row, me], local_sem.at[0]),
-        pltpu.make_async_copy(blocks_ref.at[me], joined_rows(row, me), local_sem.at[1]),
-        pltpu.make_async_copy(out_weight_ref, out_shard(row), local_sem.at[2]),
-        pltpu.make_async_copy(rows_ref, rows_all.at[pl.ds(pl.multiple_of(me * length, length), length), :], local_sem.at[3]),
-        pltpu.make_async_copy(cot_ref, cot_all.at[pl.ds(pl.multiple_of(me * length, length), length), :], local_sem.at[4]),
+        pltpu.make_async_copy(blocks.at[me], joined_rows(row, me), local_sem.at[0]),
+        pltpu.make_async_copy(out_weight_ref, out_shard(row), local_sem.at[1]),
+        pltpu.make_async_copy(rows_ref, block(rows_all, me), local_sem.at[2]),
+        pltpu.make_async_copy(cot_ref, block(cot_all, me), local_sem.at[3]),
     ]
-    swaps, arrivals = [], []
-    for k in range(1, ctx):
-        swaps.append(remote(small_ref, small_all.at[row, me], swap_sem.at[0, k], swap_sem.at[1, k], place.across(k)))
-        swaps.append(
-            remote(blocks_ref.at[place.other(k)], joined_rows(row, me), swap_sem.at[2, k], swap_sem.at[3, k], place.across(k))
+    swaps = [
+        remote(small_ref, small_all.at[row, me], swap_sem.at[0, k], swap_sem.at[1, k], place.across(k))
+        for k in range(1, ctx)
+    ] + [
+        remote(
+            blocks.at[place.other(k)], joined_rows(row, me), swap_sem.at[2, k], swap_sem.at[3, k], place.across(k)
         )
-        arrivals.append(
-            remote(small_ref, small_all.at[row, place.other(k)], swap_sem.at[0, k], swap_sem.at[1, k], place.across(k))
-        )
-        part = joined_rows(row, place.other(k))
-        arrivals.append(remote(part, part, swap_sem.at[2, k], swap_sem.at[3, k], place.across(k)))
+        for k in range(1, ctx)
+    ]
     for copy in swaps:
         copy.start()
     for copy in local:
         copy.start()
+    small_all[row, me] = small_ref[...]
     rows_gather = CtxGather(place, rows_ref, rows_all, length, rows_sem)
     cot_gather = CtxGather(place, cot_ref, cot_all, length, cot_sem)
-    lines = [
-        LineGather(place, lambda row: small_all.at[row], line_small),
-        LineGather(place, joined_shard, line_joined),
-        LineGather(place, out_shard, line_out),
+    rows_gather.first()
+    for k in range(1, ctx):
+        remote(
+            small_ref, small_all.at[row, place.other(k)], swap_sem.at[0, k], swap_sem.at[1, k], place.across(k)
+        ).wait_recv()
+    small_sends = [
+        remote(
+            small_all.at[row], small_all.at[row], small_sem.at[0, k], small_sem.at[1, k], ((row + k) % dp, me)
+        )
+        for k in range(1, dp)
     ]
-    rows_gather.first()
-    for copy in local[:2]:
-        copy.wait()
-    for copy in arrivals:
-        copy.wait_recv()
+    for copy in small_sends:
+        copy.start()
+    local[0].wait()
+    for k in range(1, ctx):
+        part = joined_rows(row, place.other(k))
+        remote(part, part, swap_sem.at[2, k], swap_sem.at[3, k], place.across(k)).wait_recv()
+    lines = [LineGather(place, joined_shard, line_joined), LineGather(place, out_shard, line_out)]
     lines[0].send(1)
+    local[1].wait()
     lines[1].send(1)
-    local[2].wait()
-    lines[2].send(1)
+
+    for k in range(1, dp):
+        part = small_all.at[(row + dp - k) % dp]
+        remote(part, part, small_sem.at[0, k], small_sem.at[1, k], place.twin).wait_recv()
+    low = head_lanes((1, PAIR))
+    for i in range(dp * ctx // 2):
+        lanes = slice(i * PAIR, (i + 1) * PAIR)
+        a = small_all.at[2 * i // ctx, 2 * i % ctx]
+        b = small_all.at[(2 * i + 1) // ctx, (2 * i + 1) % ctx]
+        for r in range(2):
+            ar, br = a[r : r + 1, :], b[r : r + 1, :]
+            params_ref[2 * r : 2 * r + 1, lanes] = jnp.where(low, ar, pltpu.roll(br, HD, 1))
+            params_ref[2 * r + 1 : 2 * r + 2, lanes] = jnp.where(low, pltpu.roll(ar, HD, 1), br)
+
+    def normalize(col):
+        step = 64
+
+        @pl.loop(0, length // step)
+        def _(i):
+            rows = pl.ds(pl.multiple_of(col * length + i * step, step), step)
+            scaled, _ = norm_stats(rows_all[rows, :].astype(f32))
+            normed_ref[rows, :] = (scaled * params_ref[0:1, :] + params_ref[1:2, :]).astype(bf16)
+
     rows_gather.second()
     cot_gather.first()
     for hop in range(1, place.lines):
@@ -375,42 +414,52 @@
                 line.send(hop + 1)
         if hop == 1:
             cot_gather.second()
+            local[2].wait()
+            for col in (me, place.other(1), place.other(2)):
+                normalize(col)
+    rows_gather.finish()
+    normalize(place.other(3))
     for line in lines:
         line.finish()
-    rows_gather.finish()
     cot_gather.finish()
-    for copy in swaps:
+    for copy in swaps + small_sends:
         copy.wait_send()
     local[3].wait()
-    local[4].wait()
-
-
-def opening(dp, ctx, small, blocks, out_weight, rows, cot):
-    depth, cols = blocks.shape[1:]
-    shapes = [
-        jax.ShapeDtypeStruct((dp, ctx) + small.shape, small.dtype),
-        jax.ShapeDtypeStruct((dp * ctx * depth, cols), bf16),
-        jax.ShapeDtypeStruct((dp * out_weight.shape[0], out_weight.shape[1]), bf16),
-        jax.ShapeDtypeStruct((ctx * rows.shape[0], rows.shape[1]), bf16),
-        jax.ShapeDtypeStruct((ctx * cot.shape[0], cot.shape[1]), bf16),
-    ]
+
+
+def opening(dp, ctx, small, qkv_weight, out_weight, rows, cot):
+    depth, width = qkv_weight.shape[0], rows.shape[1]
+    length = rows.shape[0]
+    near = 3 * width // ctx
+    vmem = pl.BlockSpec(memory_space=pltpu.VMEM)
     return pl.pallas_call(
         functools.partial(opening_kernel, dp, ctx),
-        in_specs=[ANY] * 5,
-        out_specs=[ANY] * 5,
-        out_shape=shapes,
+        in_specs=[vmem, vmem, ANY, ANY, ANY],
+        out_specs=[vmem, vmem, ANY, ANY, vmem, ANY],
+        out_shape=[
+            jax.ShapeDtypeStruct((dp, ctx) + small.shape, f32),
+            jax.ShapeDtypeStruct((4, width), f32),
+            jax.ShapeDtypeStruct((dp * ctx * depth, near), bf16),
+            jax.ShapeDtypeStruct((dp * out_weight.shape[0], width), bf16),
+            jax.ShapeDtypeStruct((ctx * length, width), bf16),
+            jax.ShapeDtypeStruct((ctx * length, width), bf16),
+        ],
         scratch_shapes=[
-            pltpu.SemaphoreType.DMA((5,)),
+            pltpu.VMEM((ctx, depth, near), bf16),
+            pltpu.VMEM((ctx * length, width), bf16),
+            pltpu.SemaphoreType.DMA((4,)),
             pltpu.SemaphoreType.DMA((4, ctx)),
-            LineGather.scratch(dp),
+            pltpu.SemaphoreType.DMA((2, dp)),
             LineGather.scratch(dp),
             LineGather.scratch(dp),
             CtxGather.scratch(),
             CtxGather.scratch(),
         ],
-        compiler_params=pltpu.CompilerParams(collective_id=0, has_side_effects=True),
+        compiler_params=pltpu.CompilerParams(
+            collective_id=0, has_side_effects=True, vmem_limit_bytes=32 << 20
+        ),
         cost_estimate=pl.CostEstimate(flops=0, transcendentals=0, bytes_accessed=200 << 20),
-    )(small, blocks, out_weight, rows, cot)
+    )(small, qkv_weight, out_weight, rows, cot)
 
 
 CHUNKS = 4
@@ -748,13 +797,7 @@
 ):
     place = Place(dp)
     me, row = place.col, place.row
-    barrier = pltpu.get_barrier_semaphore()
-    for k in range(1, ctx):
-        pl.semaphore_signal(barrier, 1, device_id=place.across(k), device_id_type=MESH)
-    for k in range(1, dp):
-        pl.semaphore_signal(barrier, 1, device_id=((row + k) % dp, me), device_id_type=MESH)
-    pl.semaphore_wait(barrier, ctx + dp - 2)
-
+    greet_all(place, dp, ctx)
     size, width = rows_ref.shape
     lines = [
         LineReduce(place, qkv_parts_ref, qkv_pair, qkv_got, qkv_sem),
@@ -1067,16 +1110,14 @@
 
 def rotary_table(full_len):
     half = ROT // 2
-    freq = jnp.arange(half, dtype=f32)
-    inverse = jnp.power(f32(10000.0), -(2.0 * freq) / ROT)
-    angles = jnp.arange(full_len, dtype=jnp.int32).astype(f32)[:, None] * inverse[None, :]
-    cosine, sine = jnp.cos(angles), jnp.sin(angles)
-    rest = jnp.zeros((full_len, HD - ROT), f32)
-    none = jnp.zeros_like(sine)
-    keep = jnp.concatenate([cosine, cosine, rest + 1.0], axis=1)
-    ahead = jnp.concatenate([-sine, none, rest], axis=1)
-    behind = jnp.concatenate([none, sine, rest], axis=1)
-    return jnp.stack([jnp.concatenate([t, t], axis=1) for t in (keep, ahead, behind)])
+    inverse = 10000.0 ** (-2.0 * np.arange(half) / ROT)
+    angles = np.arange(full_len)[:, None] * inverse[None, :]
+    table = np.zeros((3, full_len, HD), np.float32)
+    table[0, :, :half] = table[0, :, half:ROT] = np.cos(angles)
+    table[0, :, ROT:] = 1.0
+    table[1, :, :half] = -np.sin(angles)
+    table[2, :, half:ROT] = np.sin(angles)
+    return jnp.asarray(np.concatenate([table, table], axis=2))
 
 
 def shards(
@@ -1109,17 +1150,21 @@
     count = small.shape[0]
     small = jnp.pad(small, (0, 1024 - count)).reshape(8, 128)
     rows_here = qkv_weight.shape[0]
-    blocks = qkv_weight.reshape(rows_here, 3, pairs, 2, ctx, HD).transpose(4, 0, 2, 1, 3, 5)
-    blocks = blocks.reshape(ctx, rows_here, near * 3 * HD)
     rows, grad_rows = inputs[0], cotangent[0]
     fused = ctx == 4 and dp % 2 == 0 and part == HD
     if fused:
-        small, joined_weight, out_full, rows_wide, grad_wide = opening(
-            dp, ctx, small, blocks, out_weight, rows, grad_rows
+        small, params, joined_weight, out_full, normed_one, grad_wide = opening(
+            dp, ctx, small, qkv_weight, out_weight, rows, grad_rows
         )
+        gain_one, shift_one, gain_two, shift_two = params
+        gate_weight, up_weight, down_weight, _ = lax.optimization_barrier(
+            (gate_weight, up_weight, down_weight, normed_one)
+        )
+        small = small.reshape(dp * ctx, 1024)[:, :count]
     else:
         small = lax.all_gather(small[None, :], ("dp", "ctx"), axis=0, tiled=True)
-        blocks = exchange_ctx(blocks, ctx)
+        blocks = qkv_weight.reshape(rows_here, 3, pairs, 2, ctx, HD).transpose(4, 0, 2, 1, 3, 5)
+        blocks = exchange_ctx(blocks.reshape(ctx, rows_here, near * 3 * HD), ctx)
         joined_weight = lax.all_gather(
             blocks.reshape(ctx * rows_here, near * 3 * HD), "dp", axis=0, tiled=True
         )
@@ -1127,12 +1172,13 @@
         out_full = out_full.reshape(near, ctx, HD, width)
         out_full = lax.dynamic_index_in_dim(out_full, me, 1, keepdims=False)
         out_full = out_full.reshape(near * HD, width)
-        rows_wide = gather_ctx(rows, ctx)
+        small = small.reshape(dp * ctx, 1024)[:, :count]
+        gain_one, shift_one, gain_two, shift_two = [
+            small[:, i * part : (i + 1) * part].reshape(width) for i in range(4)
+        ]
+        scaled_wide, _ = norm_stats(gather_ctx(rows, ctx).astype(f32))
+        normed_one = (scaled_wide * gain_one + shift_one).astype(bf16)
         grad_wide = gather_ctx(grad_rows, ctx)
-    small = small.reshape(dp * ctx, 1024)[:, :count]
-    gain_one, shift_one, gain_two, shift_two = [
-        small[:, i * part : (i + 1) * part].reshape(width) for i in range(4)
-    ]
     bias = small[:, 4 * part :].reshape(3, pairs, 2, ctx, HD)
     bias = lax.dynamic_index_in_dim(bias, me, 3, keepdims=False)
     bias = bias.transpose(1, 0, 2, 3).reshape(1, near * 3 * HD)
@@ -1144,8 +1190,6 @@
     start = jnp.sum((segment[None, :] < segment[:, None]).astype(jnp.int32), axis=1)
     start = jnp.broadcast_to(start[:, None], (full_len, 128))
     table = rotary_table(full_len)
-    scaled_wide, _ = norm_stats(rows_wide.astype(f32))
-    normed_one = (scaled_wide * gain_one + shift_one).astype(bf16)
     joined = dot(normed_one, joined_weight)
     attended, qkv, lse = attend(joined, bias, table, start)
     if fused:
@@ -1168,20 +1212,19 @@
     d_gate_weight = dot_tn(normed_wide, d_gate).astype(bf16)
     d_up_weight = dot_tn(normed_wide, d_upward).astype(bf16)
     branch = dot(inner, down_full)
+    d_gate_ready, d_gate_weight = lax.optimization_barrier((d_gate, d_gate_weight))
+    d_gate_weight = lax.psum_scatter(d_gate_weight, "dp", scatter_dimension=0, tiled=True).astype(f32)
     if fused:
         d_resid, sums_two, d_proj = mix_back(
-            dp, ctx, d_gate, d_upward, gate_full, up_full, resid, grad_rows, gain_two
+            dp, ctx, d_gate_ready, d_upward, gate_full, up_full, resid, grad_rows, gain_two
         )
     else:
         d_normed_two = scatter_ctx(dot_nt(d_gate, gate_full) + dot_nt(d_upward, up_full), ctx)
         grad, d_gain_two, d_shift_two = norm_backward(d_normed_two, scaled_two, inv_two, gain_two)
         d_resid = grad_rows.astype(f32) + grad
         d_proj = gather_ctx(d_resid.astype(bf16), ctx)
-    branch, d_gate_weight, d_up_weight, _ = lax.optimization_barrier(
-        (branch, d_gate_weight, d_up_weight, d_proj)
-    )
+    branch, _ = lax.optimization_barrier((branch, d_proj))
     output = (resid + scatter_ctx(branch, ctx)).astype(bf16)
-    d_gate_weight = lax.psum_scatter(d_gate_weight, "dp", scatter_dimension=0, tiled=True).astype(f32)
     d_up_weight = lax.psum_scatter(d_up_weight, "dp", scatter_dimension=0, tiled=True).astype(f32)
 
     d_attended = dot_nt(d_proj, out_full).astype(bf16)

time: 712 us -> 636 us (0.89)
  Pallas kernels: 516 us -> 407 us
  waiting for transfers between devices: 2.63 us -> 43.1 us
  other arithmetic: 23.5 us -> 15.4 us
    pallas_call x1, Pallas kernels: 164 us -> 104 us  [opening(): pl.pallas_call(functools.partial(opening_kernel, dp, ctx), in_specs=[vmem...]
    pallas_call x1, Pallas kernels: 153 us -> 105 us  [closing(): pl.pallas_call(functools.partial(closing_kernel, dp, ctx), in_specs=[vmem...]
    all_gather x1, waiting for transfers between devices: 0.01 us -> 41.7 us  [shards(): down_full = lax.all_gather(down_weight, 'dp', axis=1, tiled=True)]
    unnamed x62 -> x67, local copies, waits for them, and re-layouts: 13.9 us -> 25.8 us
    reshape x3 -> x0, local copies, waits for them, and re-layouts: 7.9 us -> none  [the longest x2 6.18 us: shards(): qkv_weight.reshape(rows_here, 3, pairs, 2, ctx, HD)]
  transfers between devices with their start and end apart: 10 -> 10, of which waited for: 0 -> 1; matrix products, arithmetic and copies ran while one was open for 18% -> 17% of each run, Pallas kernels for 73% -> 48%
where the time goes in v4:
time: 636 us; the launch traced here: 633 us
  Pallas kernels  407 us (64%)
  matrix products  111 us (17%)
  waiting for transfers between devices  43.1 us (7%)
  local copies, waits for them, and re-layouts  36.9 us (6%)
  other arithmetic  15.4 us (2%)
  between operations  14.7 us (2%)
    pallas_call x1, Pallas kernels, closing(): pl.pallas_call(functools.partial(closing_kernel, dp, ctx), in_specs=[vmem...  105 us
    pallas_call x1, Pallas kernels, opening(): pl.pallas_call(functools.partial(opening_kernel, dp, ctx), in_specs=[vmem...  104 us
    pallas_call x1, Pallas kernels, mix_back(): pl.pallas_call(functools.partial(mix_back_kernel, dp, ctx), in_specs=[vme...  85.1 us
    pallas_call x1, Pallas kernels, mix(): pl.pallas_call(functools.partial(mix_kernel, dp, ctx), in_specs=[vmem] *...  73.7 us
    dot_general x4, matrix products, dot(): return jnp.dot(a, b, preferred_element_type=f32)  47.3 us
    dot_general x5, matrix products, dot_tn(): lax.dot_general(a, b, (((0,), (0,)), ((), ())), preferred_element_type=f32)  45.4 us
    all_gather x1, waiting for transfers between devices, shards(): down_full = lax.all_gather(down_weight, 'dp', axis=1, tiled=True)  41.7 us
    unnamed x67, local copies, waits for them, and re-layouts  25.8 us
  transfers between devices with their start and end apart: 10, of which 1 were waited for; matrix products, arithmetic and copies ran while one was open for 17% of the time, Pallas kernels for 48%

profile of v4, /device:TPU:0, one launch (start us, length us, event | category | flops | bytes accessed | tf_op | source)
XLA Modules:
  0.0 632.9 jit_solution(8156177708449254441)
XLA Ops:
  7.2 3.4 concatenate.11
  10.7 1.2 copy-done.2
  11.9 1.2 copy-done.3
  13.1 1.1 copy-done.5
  14.3 0.9 copy-done.6
  15.2 103.6 %shard_map.229 = (f32[8,4,8,128]{3,2,1,0:T(8,128)S(1)}, f32[4,2048]{1,0:T(4,128)S(1)}, bf16[2048,1536]{1,0:T(8,128)(2,1)S(1)}, bf16[512,2048]{1,0:T(8,128)(2,1)S...) custom-call(f32[8,128]{1,0:T(8,128)S(1)} %bitcast_convert_fusion.small_ref, ...), custom_call_target="tpu_custom_call" | custom-call | bytes 209715200 | tf_op jit(solution)/shard_map/pallas_call | solution.py:435
  118.8 2.7 copy-done.8
  121.5 2.1 copy-done.9
  123.6 2.1 copy-done.11
  125.7 0.7 all-gather.4.cloned.1.call-update
  126.5 0.7 all-gather.8.cloned.1.call-update
  127.2 0.2 reduce-scatter.8.cloned.1.call-start
  127.4 0.1 reshape.58
  127.6 0.1 reshape.59.bias_ref
  127.7 0.6 convert_reduce_fusion
  128.2 12.2 %fusion.6.joined_ref = f32[1024,1536]{1,0:T(8,128)} fusion(bf16[1024,2048]{1,0:T(8,128)(2,1)} %copy-done.9, bf16[2048,1536]{1,0:T(8,128)(2,1)} %copy-done.8), kind=kOutput, calls=%fused_computation.38 | convolution fusion | flops 6442450944 | bytes 16777216 | tf_op jit(solution)/shard_map/dot_general | solution.py:24
  140.4 0.2 broadcast_in_dim.12.start_ref
  140.6 18.2 %shard_map.230 = (bf16[1024,512]{1,0:T(8,128)(2,1)S(1)}, bf16[1024,1536]{1,0:T(8,128)(2,1)S(1)}, f32[1024,512]{1,0:T(8,128)S(1)}) custom-call(f32[1024,1536]{1,0:T(8,128)} %fusion.6.joined_ref, f32[1,1536]{1,0:T(1,128)S(1)} %reshape.59.bias_ref, f32[3,1024,128]{2,1,0:T(8,128)S(1)} %copy-done.13, s32[1024,128]{1,0:T(8,128)S(1)} %broadcast_in_dim.12.start_ref), custom_call_target="tpu_custom_call" | custom-call | flops 2415919104 | bytes 12582912 | tf_op jit(solution)/shard_map/pallas_call | solution.py:1065
  158.9 1.6 copy-done.15
  160.5 1.3 copy-done.17
  161.8 0.6 fusion.5
  162.4 73.7 %shard_map.231 = (f32[256,2048]{1,0:T(8,128)S(1)}, bf16[1024,2048]{1,0:T(8,128)(2,1)S(1)}) custom-call(bf16[1024,512]{1,0:T(8,128)(2,1)S(1)} %get-tuple-element.41.attended_ref, bf16[512,2048]{1,0:T(8,128)(2,1)S(1)} %get-tuple-element.42.weight_ref, bf16[256,2048]{1,0:T(8,128)(2,1)S(1)} %bitcast.60, f32[1,2048]{1,0:T(1,128)S(1)} %get-tuple-element.75.gain_ref, ...), custom_call_target="tpu_custom_call" | custom-call | flops 2147483648 | bytes 188743680 | tf_op jit(solution)/shard_map/pallas_call | solution.py:613
  236.2 1.3 copy-done
  237.5 1.0 copy-done.19
  238.5 2.0 copy-done.22
  240.4 12.1 %fusion.8 = f32[1024,1408]{1,0:T(8,128)} fusion(bf16[1024,2048]{1,0:T(8,128)(2,1)} %copy-done.22, bf16[2048,1408]{1,0:T(8,128)(2,1)} %all-gather.6.cloned.1.call-done.up_weight_ref), kind=kOutput, calls=%fused_computation.40 | convolution fusion | flops 5905580032 | bytes 15728640 | tf_op jit(solution)/shard_map/dot_general | solution.py:24
  252.5 12.1 %fusion.7 = f32[1024,1408]{1,0:T(8,128)} fusion(bf16[1024,2048]{1,0:T(8,128)(2,1)} %copy-done.22, bf16[2048,1408]{1,0:T(8,128)(2,1)} %all-gather.4.cloned.1.call-done.gate_weight_ref), kind=kOutput, calls=%fused_computation.39 | convolution fusion | flops 5905580032 | bytes 15728640 | tf_op jit(solution)/shard_map/dot_general | solution.py:24
  264.7 41.7 %all-gather.8.cloned.1.call-done = bf16[1408,2048]{1,0:T(8,128)(2,1)} async-done(((bf16[1408,256]{1,0:T(8,128)(2,1)}), bf16[1408,2048]{1,0:T(8,128)(2,1)}) %all-gather.8.cloned.1.call-update) | async-done | bytes 5767184 | tf_op jit(solution)/shard_map/all_gather | solution.py:1187
  306.3 16.2 %multiply_convert_fusion = (bf16[1024,1408]{1,0:T(8,128)(2,1)}, bf16[1024,1408]{1,0:T(8,128)(2,1)}, bf16[1024,1408]{1,0:T(8,128)(2,1)S(1)}) fusion(f32[1024,1408]{1,0:T(8,128)} %fusion.7, f32[1024,1408]{1,0:T(8,128)} %fusion.8, bf16[1024,2048]{1,0:T(8,128)(2,1)} %copy-done.11, bf16[1408,2048]{1,0:T(8,128)(2,1)} %all-gather.8.cloned.1.call-done), kind=kOutput, calls=%fused_computation.4 | convolution fusion | flops 5927206912 | bytes 30146560 | tf_op jit(solution)/shard_map/dot_general | solution.py:28
  322.6 1.6 copy-done.29
  324.2 8.1 %convolution_convert_fusion = bf16[1408,2048]{1,0:T(8,128)(2,1)} fusion(bf16[1024,1408]{1,0:T(8,128)(2,1)S(1)} %get-tuple-element.66, bf16[1024,2048]{1,0:T(8,128)(2,1)S(1)} %copy-done.12), kind=kOutput, calls=%fused_computation | convolution fusion | flops 5908463616 | bytes 12845056 | tf_op jit(solution)/shard_map/dot_general | solution.py:32
  332.4 11.0 %convolution_convert_fusion.1 = bf16[2048,1408]{1,0:T(8,128)(2,1)} fusion(bf16[1024,2048]{1,0:T(8,128)(2,1)} %copy-done.22, bf16[1024,1408]{1,0:T(8,128)(2,1)} %get-tuple-element.64.up_ref), kind=kOutput, calls=%fused_computation.1 | convolution fusion | flops 5908463616 | bytes 12845056 | tf_op jit(solution)/shard_map/dot_general | solution.py:32
  343.4 11.2 %convolution_convert_fusion.3 = bf16[2048,1408]{1,0:T(8,128)(2,1)} fusion(bf16[1024,2048]{1,0:T(8,128)(2,1)} %copy-done.22, bf16[1024,1408]{1,0:T(8,128)(2,1)} %get-tuple-element.50.gate_ref), kind=kOutput, calls=%fused_computation.3 | convolution fusion | flops 5908463616 | bytes 12845056 | tf_op jit(solution)/shard_map/dot_general | solution.py:32
  354.7 85.1 %shard_map.232 = (f32[256,2048]{1,0:T(8,128)}, f32[2,2048]{1,0:T(2,128)}, bf16[1024,2048]{1,0:T(8,128)(2,1)}) custom-call(bf16[1024,1408]{1,0:T(8,128)(2,1)} %get-tuple-element.50.gate_ref, bf16[1024,1408]{1,0:T(8,128)(2,1)} %get-tuple-element.64.up_ref, bf16[2048,1408]{1,0:T(8,128)(2,1)} %all-gather.4.cloned.1.call-done.gate_weight_ref, ...), custom_call_target="tpu_custom_call" | custom-call | flops 11811160064 | bytes 188743680 | tf_op jit(solution)/shard_map/pallas_call | solution.py:672
  439.8 10.9 %fusion.9 = f32[1024,2048]{1,0:T(8,128)} fusion(bf16[1024,1408]{1,0:T(8,128)(2,1)S(1)} %copy-done.30, bf16[1408,2048]{1,0:T(8,128)(2,1)} %all-gather.8.cloned.1.call-done), kind=kOutput, calls=%fused_computation.41 | convolution fusion | flops 5905580032 | bytes 17039360 | tf_op jit(solution)/shard_map/dot_general | solution.py:24
  450.7 2.4 convolution_convert_fusion.5.grad_ref
  453.1 0.7 copy-done.18
  453.7 21.6 %shard_map.233 = (bf16[1024,1536]{1,0:T(8,128)(2,1)S(1)}, f32[1,1536]{1,0:T(1,128)S(1)}) custom-call(bf16[1024,1536]{1,0:T(8,128)(2,1)S(1)} %copy-done.16, bf16[1024,512]{1,0:T(8,128)(2,1)S(1)} %convolution_convert_fusion.5.grad_ref, f32[1024,512]{1,0:T(8,128)S(1)} %copy-done.18, f32[3,1024,128]{2,1,0:T(8,128)S(1)} %copy-done.14, ...), custom_call_target="tpu_custom_call" | custom-call | flops 6039797760 | bytes 12582912 | tf_op jit(solution)/shard_map/pallas_call | solution.py:1094
  475.3 1.6 copy-done.21
  477.1 1.9 dynamic-slice_convert_fusion
  479.1 0.1 fusion.4
  479.2 1.5 collective-permute-start
  480.7 1.5 collective-permute-start.2
  482.2 0.6 pad.10.bias_ref
  482.8 1.7 dynamic-slice_convert_fusion.2
  484.5 11.3 %convolution_convert_fusion.2 = bf16[2048,1536]{1,0:T(8,128)(2,1)} fusion(bf16[1024,2048]{1,0:T(8,128)(2,1)S(1)} %copy-done.10, bf16[1024,1536]{1,0:T(8,128)(2,1)} %copy-done.21), kind=kOutput, calls=%fused_computation.2 | convolution fusion | flops 6445596672 | bytes 13631488 | tf_op jit(solution)/shard_map/dot_general | solution.py:32
  495.8 3.8 convolution_convert_fusion.4
  499.6 1.9 fusion.3
  501.6 0.7 collective-permute-start.3
  502.3 1.1 pad_maximum_fusion
  503.4 0.6 collective-permute-start.1
  503.9 104.8 %shard_map.234 = (f32[256,2048]{1,0:T(8,128)}, f32[64,6144]{1,0:T(8,128)}, f32[64,2048]{1,0:T(8,128)}, f32[4,8,256]{2,1,0:T(8,128)}) custom-call(bf16[1024,1536]{1,0:T(8,128)(2,1)} %copy-done.21, bf16[2048,1536]{1,0:T(8,128)(2,1)} %copy-done.8, bf16[8,256,1536]{2,1,0:T(8,128)(2,1)} %bitcast.69, bf16[8,64,2048]{2,1,0:T(8,128)(2,1)} %bitcast.70, ...), custom_call_target="tpu_custom_call" | custom-call | flops 6442450944 | bytes 209715200 | tf_op jit(solution)/shard_map/pallas_call | solution.py:904
  608.7 0.8 slice_reduce_fusion.1
  609.6 0.1 reshape.64
  609.7 0.6 constant_dynamic-slice_fusion
  610.2 0.8 slice_reduce_fusion
  611.1 0.5 slice_bitcast_fusion
  611.6 3.8 fusion.1
  615.4 2.5 convert_element_type.82
  617.9 2.3 convert_element_type.80
  620.2 2.4 convert_element_type.78
  622.6 1.3 copy.45
  624.0 1.1 copy.46
  625.1 0.8 copy.47
  (78 shorter events, 0.9 us)
Async XLA Ops:
  7.2 120.5 %copy-start.26 = (s32[1,1024]{1,0:T(1,128)S(1)}, s32[1,1024]{1,0:T(1,128)}, u32[]{:S(2)}) copy-start(s32[1,1024]{1,0:T(1,128)} %param.15) | copy-start | bytes 12292
  7.2 233.2 %all-gather.6.cloned.1.call-start = ((), (), s32[]{:S(2)}) async-start(), calls=%async_computation.4 | async-start | bytes 6488064 | tf_op jit(solution)/shard_map/all_gather | solution.py:1186
  10.7 1.2 copy-start.2
  11.9 1.2 copy-start.3
  13.1 1.1 copy-start.5
  14.2 0.9 copy-start.6
  118.8 2.7 copy-start.8
  121.5 2.1 copy-start.9
  123.6 2.1 copy-start.11
  125.7 126.8 %all-gather.4.cloned.1.call-start = ((), (), s32[]{:S(2)}) async-start(), calls=%async_computation.3 | async-start | bytes 6488064 | tf_op jit(solution)/shard_map/all_gather | solution.py:1185
  126.4 179.9 %all-gather.8.cloned.1.call-start = ((), (), s32[]{:S(2)}) async-start(), calls=%async_computation.5 | async-start | bytes 6488064 | tf_op jit(solution)/shard_map/all_gather | solution.py:1187
  127.2 488.3 %reduce-scatter.8.cloned.1.call-start = ((), (), s32[]{:S(2)}) async-start(), calls=%async_computation.8 | async-start | bytes 6488064 | tf_op jit(solution)/shard_map/reduce_scatter | solution.py:1211
  128.2 12.4 %copy-start.13 = (f32[3,1024,128]{2,1,0:T(8,128)S(1)}, f32[3,1024,128]{2,1,0:T(8,128)}, u32[]{:S(2)}) copy-start(f32[3,1024,128]{2,1,0:T(8,128)} %constant.36.clone.table_ref) | copy-start | bytes 4718596
  140.6 21.8 %copy-start.4 = (bf16[1,256,2048]{2,1,0:T(8,128)(2,1)S(1)}, bf16[1,256,2048]{2,1,0:T(8,128)(2,1)}, u32[]{:S(2)}) copy-start(bf16[1,256,2048]{2,1,0:T(8,128)(2,1)} %param.14) | copy-start | bytes 3145732
  158.9 1.6 copy-start.15
  160.5 1.3 copy-start.17
  162.4 90.1 %copy-start.7 = (f32[1,2048]{1,0:T(1,128)}, f32[1,2048]{1,0:T(1,128)S(1)}, u32[]{:S(2)}) copy-start(f32[1,2048]{1,0:T(1,128)S(1)} %get-tuple-element.75.gain_ref) | copy-start | bytes 24580
  236.2 1.3 copy-start
  237.5 1.0 copy-start.19
  238.5 2.0 copy-start.22
  306.3 17.9 %copy-start.12 = (bf16[1024,2048]{1,0:T(8,128)(2,1)S(1)}, bf16[1024,2048]{1,0:T(8,128)(2,1)}, u32[]{:S(2)}) copy-start(bf16[1024,2048]{1,0:T(8,128)(2,1)} %copy-done.11) | copy-start | bytes 12582916
  322.6 1.6 copy-start.29
  332.3 285.6 %reduce-scatter.6.cloned.1.call-start = ((), (), s32[]{:S(2)}) async-start(), calls=%async_computation.7 | async-start | bytes 6488064 | tf_op jit(solution)/shard_map/reduce_scatter | solution.py:1228
  343.4 276.8 %reduce-scatter.4.cloned.1.call-start = ((), (), s32[]{:S(2)}) async-start(), calls=%async_computation.6 | async-start | bytes 6488064 | tf_op jit(solution)/shard_map/reduce_scatter | solution.py:1216
  354.7 85.1 %copy-start.30 = (bf16[1024,1408]{1,0:T(8,128)(2,1)S(1)}, bf16[1024,1408]{1,0:T(8,128)(2,1)}, u32[]{:S(2)}) copy-start(bf16[1024,1408]{1,0:T(8,128)(2,1)} %copy-done.29) | copy-start | bytes 8650756
  439.8 10.9 %copy-start.27 = (bf16[1024,2048]{1,0:T(8,128)(2,1)S(1)}, bf16[1024,2048]{1,0:T(8,128)(2,1)}, u32[]{:S(2)}) copy-start(bf16[1024,2048]{1,0:T(8,128)(2,1)} %get-tuple-element.51) | copy-start | bytes 12582916
  450.7 2.4 copy-start.14
  450.7 2.4 copy-start.16
  450.7 3.1 copy-start.18
  475.3 1.6 copy-start.21
  477.1 7.3 %copy-start.10 = (bf16[1024,2048]{1,0:T(8,128)(2,1)S(1)}, bf16[1024,2048]{1,0:T(8,128)(2,1)}, u32[]{:S(2)}) copy-start(bf16[1024,2048]{1,0:T(8,128)(2,1)} %copy-done.9) | copy-start | bytes 12582916
  479.2 20.4 %collective-permute-start = (bf16[128,2048]{1,0:T(8,128)(2,1)S(1)}, bf16[128,2048]{1,0:T(8,128)(2,1)S(1)}, u32[]{:S(2)}, u32[]{:S(2)}) collective-permute-start(bf16[128,2048]{1,0:T(8,128)(2,1)S(1)} %get-tuple-element.71), channel_id=1, source_target_pairs={{0,2},{1,3},{2,0},{3,1},{4,6},{5,7},{6,4},{7,5},{8,10},{9,11},{10,... | collective-permute-start | bytes 1572872 | tf_op jit(solution)/shard_map/ppermute | solution.py:60
  480.7 18.9 %collective-permute-start.2 = (bf16[128,2048]{1,0:T(8,128)(2,1)S(1)}, bf16[128,2048]{1,0:T(8,128)(2,1)S(1)}, u32[]{:S(2)}, u32[]{:S(2)}) collective-permute-start(bf16[128,2048]{1,0:T(8,128)(2,1)S(1)} %get-tuple-element.72), channel_id=1, source_target_pairs={{0,1},{1,0},{2,3},{3,2},{4,5},{5,4},{6,7},{7,6},{8,9},{9,8},{10,11... | collective-permute-start | bytes 1572872 | tf_op jit(solution)/shard_map/ppermute | solution.py:60
  484.5 11.3 %copy-start.20 = (bf16[1024,512]{1,0:T(8,128)(2,1)S(1)}, bf16[1024,512]{1,0:T(8,128)(2,1)}, u32[]{:S(2)}) copy-start(bf16[1024,512]{1,0:T(8,128)(2,1)} %copy-done.19) | copy-start | bytes 3145732
  484.5 11.3 %copy-start.28 = (bf16[1024,2048]{1,0:T(8,128)(2,1)S(1)}, bf16[1024,2048]{1,0:T(8,128)(2,1)}, u32[]{:S(2)}) copy-start(bf16[1024,2048]{1,0:T(8,128)(2,1)} %get-tuple-element.51) | copy-start | bytes 12582916
  501.6 110.0 %collective-permute-start.3 = (bf16[256,2048]{1,0:T(8,128)(2,1)S(1)}, bf16[256,2048]{1,0:T(8,128)(2,1)}, u32[]{:S(2)}, u32[]{:S(2)}) collective-permute-start(bf16[256,2048]{1,0:T(8,128)(2,1)S(1)} %pad_maximum_fusion.1), channel_id=1, source_target_pairs={{0,2},{1,3},{2,0},{3,1},{4,6},{5,7},{6,4},{7,5},{8,10},{9,11},{10,... | collective-permute-start | bytes 3145736 | tf_op jit(solution)/shard_map/ppermute | solution.py:60
  503.4 108.2 %collective-permute-start.1 = (bf16[256,2048]{1,0:T(8,128)(2,1)}, bf16[256,2048]{1,0:T(8,128)(2,1)}, u32[]{:S(2)}, u32[]{:S(2)}) collective-permute-start(bf16[256,2048]{1,0:T(8,128)(2,1)} %pad_maximum_fusion), channel_id=1, source_target_pairs={{0,1},{1,0},{2,3},{3,2},{4,5},{5,4},{6,7},{7,6},{8,9},{9,8},{10,11... | collective-permute-start | bytes 3145736 | tf_op jit(solution)/shard_map/ppermute | solution.py:60
  503.9 107.7 %copy-start.1 = (f32[256,2048]{1,0:T(8,128)S(1)}, f32[256,2048]{1,0:T(8,128)}, u32[]{:S(2)}) copy-start(f32[256,2048]{1,0:T(8,128)} %copy-done) | copy-start | bytes 6291460
  615.4 7.2 %copy-start.23 = (f32[256,2048]{1,0:T(8,128)S(1)}, f32[256,2048]{1,0:T(8,128)}, u32[]{:S(2)}) copy-start(f32[256,2048]{1,0:T(8,128)} %get-tuple-element.59) | copy-start | bytes 6291460
  620.2 3.8 copy-start.24
  622.6 2.5 copy-start.25
Sparse Core Ops, SparseCore 0:
  125.8 58.5 all-gather.5
  186.0 59.0 all-gather.3
  246.8 59.5 all-gather.7
  332.4 63.0 reduce-scatter.7
  397.7 63.2 reduce-scatter.5
  463.1 65.7 reduce-scatter.3

commit v5 on v4

--- a/solution.py
+++ b/solution.py
@@ -208,14 +208,37 @@
             remote(part, part, self.sems.at[2, hop], self.sems.at[3, hop], place.twin).wait_recv()
             self.over(place.lines - 1 + hop, self.row(place.line + hop)).start()
 
+    def came_over(self, at, row):
+        part = self.shard(row)
+        remote(part, part, self.sems.at[4, at], self.sems.at[5, at], self.place.twin).wait_recv()
+
+    def settle(self, hop, use=None):
+        place = self.place
+        other = 1 - 2 * place.core
+        if hop == 0:
+            if use:
+                use(place.row)
+            self.came_over(0, place.row + other)
+            if use:
+                use(place.row + other)
+            return
+        for at, line, there in (
+            (hop, place.line - hop, place.line - hop >= 0),
+            (place.lines - 1 + hop, place.line + hop, place.line + hop < place.lines),
+        ):
+
+            @pl.when(there)
+            def _():
+                row = self.row(line)
+                if use:
+                    use(row)
+                self.came_over(at, row + other)
+                if use:
+                    use(row + other)
+
     def finish(self):
         place = self.place
         self.over(0, place.row).wait_send()
-        other = 1 - 2 * place.core
-        remote(
-            self.shard(place.row + other), self.shard(place.row + other),
-            self.sems.at[4, 0], self.sems.at[5, 0], place.twin,
-        ).wait_recv()
         for hop in range(1, place.lines):
             pl.when(self.sends_up(hop))(lambda: self.up(hop).wait_send())
             pl.when(self.sends_down(hop))(lambda: self.down(hop).wait_send())
@@ -223,13 +246,7 @@
                 (hop, place.line - hop, place.line - hop >= 0),
                 (place.lines - 1 + hop, place.line + hop, place.line + hop < place.lines),
             ):
-
-                @pl.when(there)
-                def _():
-                    row = self.row(line)
-                    self.over(at, row).wait_send()
-                    part = self.shard(row + other)
-                    remote(part, part, self.sems.at[4, at], self.sems.at[5, at], place.twin).wait_recv()
+                pl.when(there)(lambda: self.over(at, self.row(line)).wait_send())
 
     @staticmethod
     def scratch(dp):
@@ -302,10 +319,13 @@
     pl.semaphore_wait(barrier, ctx + dp - 2)
 
 
+PARTS = 2
+
+
 def opening_kernel(
     dp, ctx,
     small_ref, qkv_ref, out_weight_ref, rows_ref, cot_ref,
-    small_all, params_ref, joined_all, out_all, normed_ref, cot_all,
+    small_all, params_ref, weight_ref, out_all, normed_ref, joined_ref, cot_all,
     blocks, rows_all, local_sem, swap_sem, small_sem, line_joined, line_out, rows_sem, cot_sem,
 ):
     place = Place(dp)
@@ -313,6 +333,7 @@
     depth = qkv_ref.shape[0]
     length, width = rows_ref.shape
     rows_out = out_weight_ref.shape[0]
+    tall = ctx * depth
 
     low = head_lanes((depth, PAIR))
     for p in range(width // HD // ctx // 2):
@@ -325,13 +346,11 @@
                 b = qkv_ref[:, at : at + PAIR].astype(f32)
                 blocks[c, :, lanes] = jnp.where(low, a, pltpu.roll(b, HD, 1)).astype(bf16)
                 blocks[c + 1, :, lanes] = jnp.where(low, pltpu.roll(a, HD, 1), b).astype(bf16)
+    small_all[row, me] = small_ref[...]
     greet_all(place, dp, ctx)
 
-    def joined_rows(row, col):
-        return joined_all.at[pl.ds(pl.multiple_of((row * ctx + col) * depth, depth), depth), :]
-
-    def joined_shard(row):
-        return joined_all.at[pl.ds(pl.multiple_of(row * (ctx * depth), ctx * depth), ctx * depth), :]
+    def weight_rows(row, col):
+        return weight_ref.at[pl.ds(pl.multiple_of((row * ctx + col) * depth, depth), depth), :]
 
     def out_shard(row):
         return out_all.at[pl.ds(pl.multiple_of(row * rows_out, rows_out), rows_out), :]
@@ -339,8 +358,15 @@
     def block(ref, col):
         return ref.at[pl.ds(pl.multiple_of(col * length, length), length), :]
 
+    part_cols = weight_ref.shape[1] // PARTS
+
+    def weight_part(i, row):
+        return weight_ref.at[
+            pl.ds(pl.multiple_of(row * tall, tall), tall), pl.ds(i * part_cols, part_cols)
+        ]
+
     local = [
-        pltpu.make_async_copy(blocks.at[me], joined_rows(row, me), local_sem.at[0]),
+        pltpu.make_async_copy(blocks.at[me], weight_rows(row, me), local_sem.at[0]),
         pltpu.make_async_copy(out_weight_ref, out_shard(row), local_sem.at[1]),
         pltpu.make_async_copy(rows_ref, block(rows_all, me), local_sem.at[2]),
         pltpu.make_async_copy(cot_ref, block(cot_all, me), local_sem.at[3]),
@@ -350,7 +376,7 @@
         for k in range(1, ctx)
     ] + [
         remote(
-            blocks.at[place.other(k)], joined_rows(row, me), swap_sem.at[2, k], swap_sem.at[3, k], place.across(k)
+            blocks.at[place.other(k)], weight_rows(row, me), swap_sem.at[2, k], swap_sem.at[3, k], place.across(k)
         )
         for k in range(1, ctx)
     ]
@@ -358,9 +384,14 @@
         copy.start()
     for copy in local:
         copy.start()
-    small_all[row, me] = small_ref[...]
     rows_gather = CtxGather(place, rows_ref, rows_all, length, rows_sem)
     cot_gather = CtxGather(place, cot_ref, cot_all, length, cot_sem)
+    out_line = LineGather(place, out_shard, line_out)
+    lines = [
+        LineGather(place, functools.partial(weight_part, i), line_joined.at[i]) for i in range(PARTS)
+    ] + [out_line]
+    local[1].wait()
+    out_line.send(1)
     rows_gather.first()
     for k in range(1, ctx):
         remote(
@@ -376,12 +407,10 @@
         copy.start()
     local[0].wait()
     for k in range(1, ctx):
-        part = joined_rows(row, place.other(k))
+        part = weight_rows(row, place.other(k))
         remote(part, part, swap_sem.at[2, k], swap_sem.at[3, k], place.across(k)).wait_recv()
-    lines = [LineGather(place, joined_shard, line_joined), LineGather(place, out_shard, line_out)]
-    lines[0].send(1)
-    local[1].wait()
-    lines[1].send(1)
+    for line in lines[:PARTS]:
+        line.send(1)
 
     for k in range(1, dp):
         part = small_all.at[(row + dp - k) % dp]
@@ -389,8 +418,8 @@
     low = head_lanes((1, PAIR))
     for i in range(dp * ctx // 2):
         lanes = slice(i * PAIR, (i + 1) * PAIR)
-        a = small_all.at[2 * i // ctx, 2 * i % ctx]
-        b = small_all.at[(2 * i + 1) // ctx, (2 * i + 1) % ctx]
+        a = small_all[2 * i // ctx, 2 * i % ctx]
+        b = small_all[(2 * i + 1) // ctx, (2 * i + 1) % ctx]
         for r in range(2):
             ar, br = a[r : r + 1, :], b[r : r + 1, :]
             params_ref[2 * r : 2 * r + 1, lanes] = jnp.where(low, ar, pltpu.roll(br, HD, 1))
@@ -405,20 +434,42 @@
             scaled, _ = norm_stats(rows_all[rows, :].astype(f32))
             normed_ref[rows, :] = (scaled * params_ref[0:1, :] + params_ref[1:2, :]).astype(bf16)
 
-    rows_gather.second()
-    cot_gather.first()
-    for hop in range(1, place.lines):
+    def multiply(i, row):
+        at = pl.multiple_of(row * tall, tall)
+        cols = slice(i * part_cols, (i + 1) * part_cols)
+
+        @pl.loop(0, ctx)
+        def _(b):
+            rows = pl.ds(pl.multiple_of(b * length, length), length)
+            joined_ref[rows, cols] += dot(normed_ref[rows, pl.ds(at, tall)], weight_ref[pl.ds(at, tall), cols])
+
+    def forward(hop):
         for line in lines:
             line.receive(hop)
             if hop < place.lines - 1:
                 line.send(hop + 1)
+
+    def absorb(hop):
+        for i in range(PARTS):
+            lines[i].settle(hop, functools.partial(multiply, i))
+
+    joined_ref[...] = jnp.zeros_like(joined_ref)
+    local[2].wait()
+    normalize(me)
+    rows_gather.second()
+    cot_gather.first()
+    for hop in range(1, place.lines):
+        forward(hop)
         if hop == 1:
+            for col in (place.other(1), place.other(2)):
+                normalize(col)
+            rows_gather.finish()
+            normalize(place.other(3))
             cot_gather.second()
-            local[2].wait()
-            for col in (me, place.other(1), place.other(2)):
-                normalize(col)
-    rows_gather.finish()
-    normalize(place.other(3))
+        absorb(hop - 1)
+    absorb(place.lines - 1)
+    for hop in range(place.lines):
+        out_line.settle(hop)
     for line in lines:
         line.finish()
     cot_gather.finish()
@@ -435,13 +486,14 @@
     return pl.pallas_call(
         functools.partial(opening_kernel, dp, ctx),
         in_specs=[vmem, vmem, ANY, ANY, ANY],
-        out_specs=[vmem, vmem, ANY, ANY, vmem, ANY],
+        out_specs=[vmem, vmem, vmem, ANY, vmem, vmem, ANY],
         out_shape=[
             jax.ShapeDtypeStruct((dp, ctx) + small.shape, f32),
             jax.ShapeDtypeStruct((4, width), f32),
             jax.ShapeDtypeStruct((dp * ctx * depth, near), bf16),
             jax.ShapeDtypeStruct((dp * out_weight.shape[0], width), bf16),
             jax.ShapeDtypeStruct((ctx * length, width), bf16),
+            jax.ShapeDtypeStruct((ctx * length, near), f32),
             jax.ShapeDtypeStruct((ctx * length, width), bf16),
         ],
         scratch_shapes=[
@@ -450,15 +502,17 @@
             pltpu.SemaphoreType.DMA((4,)),
             pltpu.SemaphoreType.DMA((4, ctx)),
             pltpu.SemaphoreType.DMA((2, dp)),
-            LineGather.scratch(dp),
+            pltpu.SemaphoreType.DMA((PARTS, 6, dp)),
             LineGather.scratch(dp),
             CtxGather.scratch(),
             CtxGather.scratch(),
         ],
         compiler_params=pltpu.CompilerParams(
-            collective_id=0, has_side_effects=True, vmem_limit_bytes=32 << 20
+            collective_id=0, has_side_effects=True, vmem_limit_bytes=40 << 20
         ),
-        cost_estimate=pl.CostEstimate(flops=0, transcendentals=0, bytes_accessed=200 << 20),
+        cost_estimate=pl.CostEstimate(
+            flops=2 * ctx * length * width * near, transcendentals=0, bytes_accessed=200 << 20
+        ),
     )(small, qkv_weight, out_weight, rows, cot)
 
 
@@ -581,17 +635,27 @@
 
 
 def mix_kernel(
-    dp, ctx, attended_ref, weight_ref, rows_ref, gain_ref, shift_ref, resid_ref, wide_ref,
-    total, sent, got, made, reduce_sem, spread_sem,
+    dp, ctx, attended_ref, weight_ref, rows_ref, gain_ref, shift_ref, down_ref, resid_ref, wide_ref, down_all,
+    total, sent, got, made, reduce_sem, spread_sem, line_sem, local_sem,
 ):
     place = Place(dp)
-    greet(place, ctx)
+    greet_all(place, dp, ctx)
     size = rows_ref.shape[0]
+    cols = down_ref.shape[1]
+
+    def shard(row):
+        return down_all.at[:, pl.ds(pl.multiple_of(row * cols, cols), cols)]
+
+    line = LineGather(place, shard, line_sem)
+    local = pltpu.make_async_copy(down_ref, shard(place.row), local_sem)
+    local.start()
     reduce = CtxReduce(
         place, lambda col: dot(rows_of(attended_ref, col, size), weight_ref[...]), total, sent, got, reduce_sem
     )
     spread = CtxSpread(place, made, wide_ref, spread_sem)
     reduce.start()
+    local.wait()
+    line.send(1)
     reduce.relay()
     for j in range(CHUNKS):
         rows = reduce.chunk(j)
@@ -602,24 +666,41 @@
         spread.send(j)
         if j:
             spread.relay(j - 1)
+        if j == CHUNKS // 2:
+            line.receive(1)
+            if place.lines > 2:
+                line.send(2)
     spread.relay(CHUNKS - 1)
+    for hop in range(2, place.lines):
+        line.receive(hop)
+        if hop < place.lines - 1:
+            line.send(hop + 1)
     spread.finish()
+    for hop in range(place.lines):
+        line.settle(hop)
+    line.finish()
     reduce.finish()
 
 
-def mix(dp, ctx, attended, weight, rows, gain, shift):
+def mix(dp, ctx, attended, weight, rows, gain, shift, down):
     size, width = rows.shape
     vmem = pl.BlockSpec(memory_space=pltpu.VMEM)
     return pl.pallas_call(
         functools.partial(mix_kernel, dp, ctx),
-        in_specs=[vmem] * 5,
-        out_specs=[vmem, ANY],
-        out_shape=[jax.ShapeDtypeStruct((size, width), f32), jax.ShapeDtypeStruct((ctx * size, width), bf16)],
+        in_specs=[vmem] * 5 + [ANY],
+        out_specs=[vmem, ANY, ANY],
+        out_shape=[
+            jax.ShapeDtypeStruct((size, width), f32),
+            jax.ShapeDtypeStruct((ctx * size, width), bf16),
+            jax.ShapeDtypeStruct((down.shape[0], dp * down.shape[1]), bf16),
+        ],
         scratch_shapes=CtxReduce.scratch(size, width)[:3]
         + [
             pltpu.VMEM((size, width), bf16),
             CtxReduce.scratch(size, width)[3],
             CtxSpread.scratch(),
+            LineGather.scratch(dp),
+            pltpu.SemaphoreType.DMA,
         ],
         compiler_params=pltpu.CompilerParams(
             collective_id=2, has_side_effects=True, vmem_limit_bytes=40 << 20
@@ -627,7 +708,7 @@
         cost_estimate=pl.CostEstimate(
             flops=2 * attended.size * width, transcendentals=0, bytes_accessed=180 << 20
         ),
-    )(attended, weight, rows, gain.reshape(1, width), shift.reshape(1, width))
+    )(attended, weight, rows, gain.reshape(1, width), shift.reshape(1, width), down)
 
 
 def mix_back_kernel(
@@ -1153,13 +1234,11 @@
     rows, grad_rows = inputs[0], cotangent[0]
     fused = ctx == 4 and dp % 2 == 0 and part == HD
     if fused:
-        small, params, joined_weight, out_full, normed_one, grad_wide = opening(
+        small, params, joined_weight, out_full, normed_one, joined, grad_wide = opening(
             dp, ctx, small, qkv_weight, out_weight, rows, grad_rows
         )
         gain_one, shift_one, gain_two, shift_two = params
-        gate_weight, up_weight, down_weight, _ = lax.optimization_barrier(
-            (gate_weight, up_weight, down_weight, normed_one)
-        )
+        gate_weight, up_weight, _ = lax.optimization_barrier((gate_weight, up_weight, normed_one))
         small = small.reshape(dp * ctx, 1024)[:, :count]
     else:
         small = lax.all_gather(small[None, :], ("dp", "ctx"), axis=0, tiled=True)
@@ -1184,17 +1263,20 @@
     bias = bias.transpose(1, 0, 2, 3).reshape(1, near * 3 * HD)
     gate_full = lax.all_gather(gate_weight, "dp", axis=0, tiled=True)
     up_full = lax.all_gather(up_weight, "dp", axis=0, tiled=True)
-    down_full = lax.all_gather(down_weight, "dp", axis=1, tiled=True)
 
     segment = segments[0]
     start = jnp.sum((segment[None, :] < segment[:, None]).astype(jnp.int32), axis=1)
     start = jnp.broadcast_to(start[:, None], (full_len, 128))
     table = rotary_table(full_len)
-    joined = dot(normed_one, joined_weight)
+    if not fused:
+        joined = dot(normed_one, joined_weight)
     attended, qkv, lse = attend(joined, bias, table, start)
     if fused:
-        resid, normed_wide = mix(dp, ctx, attended, out_full, rows, gain_two, shift_two)
+        resid, normed_wide, down_full = mix(
+            dp, ctx, attended, out_full, rows, gain_two, shift_two, down_weight
+        )
     else:
+        down_full = lax.all_gather(down_weight, "dp", axis=1, tiled=True)
         resid = rows.astype(f32) + scatter_ctx(dot(attended, out_full), ctx)
         scaled_two, inv_two = norm_stats(resid)
         normed_wide = gather_ctx((scaled_two * gain_two + shift_two).astype(bf16), ctx)
@@ -1204,11 +1286,12 @@
     sigma = jax.nn.sigmoid(gate)
     swish = gate * sigma
     inner = (swish * upward).astype(bf16)
+    d_down = dot_tn(inner, grad_wide).astype(bf16)
+    grad_wide, d_down = lax.optimization_barrier((grad_wide, d_down))
+    d_down = lax.psum_scatter(d_down, "dp", scatter_dimension=1, tiled=True).astype(f32)
     d_inner = dot_nt(grad_wide, down_full)
     d_gate = (d_inner * upward * sigma * (1.0 + gate * (1.0 - sigma))).astype(bf16)
     d_upward = (d_inner * swish).astype(bf16)
-    d_down = dot_tn(inner, grad_wide).astype(bf16)
-    d_down = lax.psum_scatter(d_down, "dp", scatter_dimension=1, tiled=True).astype(f32)
     d_gate_weight = dot_tn(normed_wide, d_gate).astype(bf16)
     d_up_weight = dot_tn(normed_wide, d_upward).astype(bf16)
     branch = dot(inner, down_full)

time: 636 us -> 670 us (1.053); the launches traced: 633 us -> 658 us
  Pallas kernels: 407 us -> 494 us
  waiting for transfers between devices: 43.1 us -> 1.12 us
  matrix products: 111 us -> 95.5 us
    pallas_call x1, Pallas kernels: 73.7 us -> 130 us  [mix(): pl.pallas_call(functools.partial(mix_kernel, dp, ctx), in_specs=[vmem] *...]
    all_gather x1 -> x0, waiting for transfers between devices: 41.7 us -> none  [shards(): down_full = lax.all_gather(down_weight, 'dp', axis=1, tiled=True)]
    pallas_call x1, Pallas kernels: 105 us -> 122 us  [closing(): pl.pallas_call(functools.partial(closing_kernel, dp, ctx), in_specs=[vmem...]
    pallas_call x1, Pallas kernels: 104 us -> 117 us  [opening(): pl.pallas_call(functools.partial(opening_kernel, dp, ctx), in_specs=[vmem...]
    dot_general x4 -> x3, matrix products: 47.3 us -> 34.7 us  [dot(): return jnp.dot(a, b, preferred_element_type=f32)]
    unnamed x67 -> x71, local copies, waits for them, and re-layouts: 25.8 us -> 26.6 us
  transfers between devices with their start and end apart: 10 -> 9, of which waited for: 1 -> 0; matrix products, arithmetic and copies ran while one was open for 17% -> 10% of each run, Pallas kernels for 48% -> 57%
where the time goes in v5:
time: 670 us; the launch traced here: 658 us
  Pallas kernels  494 us (74%)
  matrix products  95.5 us (14%)
  local copies, waits for them, and re-layouts  34.3 us (5%)
  between operations  14.3 us (2%)
  other arithmetic  13.9 us (2%)
    pallas_call x1, Pallas kernels, mix(): pl.pallas_call(functools.partial(mix_kernel, dp, ctx), in_specs=[vmem] *...  130 us
    pallas_call x1, Pallas kernels, closing(): pl.pallas_call(functools.partial(closing_kernel, dp, ctx), in_specs=[vmem...  122 us
    pallas_call x1, Pallas kernels, opening(): pl.pallas_call(functools.partial(opening_kernel, dp, ctx), in_specs=[vmem...  117 us
    pallas_call x1, Pallas kernels, mix_back(): pl.pallas_call(functools.partial(mix_back_kernel, dp, ctx), in_specs=[vme...  85.2 us
    dot_general x5, matrix products, dot_tn(): lax.dot_general(a, b, (((0,), (0,)), ((), ())), preferred_element_type=f32)  40.6 us
    dot_general x3, matrix products, dot(): return jnp.dot(a, b, preferred_element_type=f32)  34.7 us
    unnamed x71, local copies, waits for them, and re-layouts  26.6 us
    pallas_call x1, Pallas kernels, attend_back(): pl.pallas_call(functools.partial(attend_back_kernel, step), grid=(pairs,)...  21.6 us
  transfers between devices with their start and end apart: 9, of which 0 were waited for; matrix products, arithmetic and copies ran while one was open for 10% of the time, Pallas kernels for 57%

profile of v5, /device:TPU:0, one launch (start us, length us, event | category | flops | bytes accessed | tf_op | source)
XLA Modules:
  0.0 658.3 jit_solution(14581616831371749897)
XLA Ops:
  7.2 3.4 concatenate.11
  10.7 1.2 copy-done.3
  11.9 1.2 copy-done.4
  13.1 1.1 copy-done.6
  14.2 0.9 copy-done.8
  15.2 117.2 %shard_map.229 = (f32[8,4,8,128]{3,2,1,0:T(8,128)S(1)}, f32[4,2048]{1,0:T(4,128)S(1)}, bf16[2048,1536]{1,0:T(8,128)(2,1)}, bf16[512,2048]{1,0:T(8,128)(2,1)S(1)}...) custom-call(f32[8,128]{1,0:T(8,128)S(1)} %bitcast_convert_fusion.small_ref, ...), custom_call_target="tpu_custom_call" | custom-call | flops 6442450944 | bytes 209715200 | tf_op jit(solution)/shard_map/pallas_call | solution.py:486
  132.4 1.9 copy-done.21
  134.3 2.1 copy-done.23
  136.5 0.7 all-gather.5.cloned.1.call-update
  137.2 0.3 reduce-scatter.6.cloned.1.call-start
  137.5 0.1 reshape.58
  137.7 0.1 reshape.59.bias_ref
  137.7 0.6 convert_reduce_fusion
  138.3 0.2 broadcast_in_dim.12.start_ref
  138.5 1.4 copy-done.9
  139.9 18.4 %shard_map.230 = (bf16[1024,512]{1,0:T(8,128)(2,1)S(1)}, bf16[1024,1536]{1,0:T(8,128)(2,1)S(1)}, f32[1024,512]{1,0:T(8,128)S(1)}) custom-call(f32[1024,1536]{1,0:T(8,128)} %get-tuple-element.41.joined_ref, f32[1,1536]{1,0:T(1,128)S(1)} %reshape.59.bias_ref, f32[3,1024,128]{2,1,0:T(8,128)S(1)} %copy-done.9, s32[1024,128]{1,0:T(8,128)S(1)} %broadcast_in_dim.12.start_ref), custom_call_target="tpu_custom_call" | custom-call | flops 2415919104 | bytes 12582912 | tf_op jit(solution)/shard_map/pallas_call | solution.py:1146
  158.3 1.6 copy-done.11
  159.9 1.3 copy-done.13
  161.2 0.6 fusion.5
  161.8 130.3 %shard_map.231 = (f32[256,2048]{1,0:T(8,128)S(1)}, bf16[1024,2048]{1,0:T(8,128)(2,1)S(1)}, bf16[1408,2048]{1,0:T(8,128)(2,1)}) custom-call(bf16[1024,512]{1,0:T(8,128)(2,1)S(1)} %get-tuple-element.43.attended_ref, bf16[512,2048]{1,0:T(8,128)(2,1)S(1)} %get-tuple-element.44.weight_ref, bf16[256,2048]{1,0:T(8,128)(2,1)S(1)} %bitcast.59, ...), custom_call_target="tpu_custom_call" | custom-call | flops 2147483648 | bytes 188743680 | tf_op jit(solution)/shard_map/pallas_call | solution.py:688
  292.2 1.3 copy-done
  293.5 1.0 copy-done.15
  294.4 2.1 copy-done.17
  296.5 11.7 %fusion.6 = f32[1024,1408]{1,0:T(8,128)} fusion(bf16[1024,2048]{1,0:T(8,128)(2,1)} %copy-done.17, bf16[2048,1408]{1,0:T(8,128)(2,1)} %all-gather.3.cloned.1.call-done.gate_weight_ref), kind=kOutput, calls=%fused_computation.38 | convolution fusion | flops 5905580032 | bytes 15728640 | tf_op jit(solution)/shard_map/dot_general | solution.py:24
  308.3 13.3 %multiply_convert_fusion.2 = (bf16[1024,1408]{1,0:T(8,128)(2,1)S(1)}, f32[1024,1408]{1,0:T(8,128)}) fusion(f32[1024,1408]{1,0:T(8,128)} %fusion.6, bf16[1024,2048]{1,0:T(8,128)(2,1)} %copy-done.17, bf16[2048,1408]{1,0:T(8,128)(2,1)} %all-gather.5.cloned.1.call-done.up_weight_ref), kind=kOutput, calls=%fused_computation.6 | convolution fusion | flops 5914230784 | bytes 24379392 | tf_op jit(solution)/shard_map/dot_general | solution.py:24
  321.6 1.6 copy-done.31
  323.2 8.2 %convolution_convert_fusion.3 = bf16[1408,2048]{1,0:T(8,128)(2,1)} fusion(bf16[1024,1408]{1,0:T(8,128)(2,1)S(1)} %get-tuple-element.85, bf16[1024,2048]{1,0:T(8,128)(2,1)S(1)} %copy-done.22), kind=kOutput, calls=%fused_computation.3 | convolution fusion | flops 5908463616 | bytes 12845056 | tf_op jit(solution)/shard_map/dot_general | solution.py:32
  331.3 15.4 %multiply_convert_fusion = (bf16[1024,1408]{1,0:T(8,128)(2,1)S(1)}, bf16[1024,1408]{1,0:T(8,128)(2,1)}) fusion(f32[1024,1408]{1,0:T(8,128)} %fusion.6, f32[1024,1408]{1,0:T(8,128)} %get-tuple-element.86, bf16[1024,2048]{1,0:T(8,128)(2,1)} %copy-done.21, bf16[1408,2048]{1,0:T(8,128)(2,1)} %get-tuple-element.51), kind=kOutput, calls=%fused_computation.4 | convolution fusion | flops 5924323328 | bytes 27262976 | tf_op jit(solution)/shard_map/dot_general | solution.py:28
  346.7 1.6 copy-done.32
  348.3 8.6 %convolution_convert_fusion = bf16[2048,1408]{1,0:T(8,128)(2,1)} fusion(bf16[1024,2048]{1,0:T(8,128)(2,1)S(1)} %copy-done.18, bf16[1024,1408]{1,0:T(8,128)(2,1)S(1)} %get-tuple-element.70.up_ref), kind=kOutput, calls=%fused_computation | convolution fusion | flops 5908463616 | bytes 12845056 | tf_op jit(solution)/shard_map/dot_general | solution.py:32
  356.9 11.0 %convolution_convert_fusion.2 = bf16[2048,1408]{1,0:T(8,128)(2,1)} fusion(bf16[1024,2048]{1,0:T(8,128)(2,1)} %copy-done.17, bf16[1024,1408]{1,0:T(8,128)(2,1)} %get-tuple-element.54.gate_ref), kind=kOutput, calls=%fused_computation.2 | convolution fusion | flops 5908463616 | bytes 12845056 | tf_op jit(solution)/shard_map/dot_general | solution.py:32
  368.0 0.2 reduce-scatter.8.cloned.1.call-start
  368.2 0.4 reduce-scatter.8.cloned.1.call-update
  368.6 85.2 %shard_map.232 = (f32[256,2048]{1,0:T(8,128)}, f32[2,2048]{1,0:T(2,128)}, bf16[1024,2048]{1,0:T(8,128)(2,1)}) custom-call(bf16[1024,1408]{1,0:T(8,128)(2,1)} %get-tuple-element.54.gate_ref, bf16[1024,1408]{1,0:T(8,128)(2,1)} %copy-done.32, bf16[2048,1408]{1,0:T(8,128)(2,1)} %all-gather.3.cloned.1.call-done.gate_weight_ref, ...), custom_call_target="tpu_custom_call" | custom-call | flops 11811160064 | bytes 188743680 | tf_op jit(solution)/shard_map/pallas_call | solution.py:753
  453.8 4.7 convolution_convert_fusion.5.grad_ref
  458.6 21.6 %shard_map.233 = (bf16[1024,1536]{1,0:T(8,128)(2,1)S(1)}, f32[1,1536]{1,0:T(1,128)S(1)}) custom-call(bf16[1024,1536]{1,0:T(8,128)(2,1)S(1)} %copy-done.12, bf16[1024,512]{1,0:T(8,128)(2,1)S(1)} %convolution_convert_fusion.5.grad_ref, f32[1024,512]{1,0:T(8,128)S(1)} %copy-done.14, f32[3,1024,128]{2,1,0:T(8,128)S(1)} %copy-done.10, ...), custom_call_target="tpu_custom_call" | custom-call | flops 6039797760 | bytes 12582912 | tf_op jit(solution)/shard_map/pallas_call | solution.py:1175
  480.2 1.7 copy-done.19
  482.0 9.7 %fusion.7 = f32[1024,2048]{1,0:T(8,128)S(1)} fusion(bf16[1024,1408]{1,0:T(8,128)(2,1)} %copy-done.31, bf16[1408,2048]{1,0:T(8,128)(2,1)} %get-tuple-element.51), kind=kOutput, calls=%fused_computation.39 | convolution fusion | flops 5905580032 | bytes 17039360 | tf_op jit(solution)/shard_map/dot_general | solution.py:24
  491.8 0.1 dynamic-slice_convert_fusion
  492.0 0.1 fusion.4
  492.1 1.5 collective-permute-start
  493.6 0.6 collective-permute-start.2
  494.2 0.6 pad.10.bias_ref
  494.8 0.1 dynamic-slice_convert_fusion.2
  495.0 1.2 copy-done.20
  496.1 9.1 %convolution_convert_fusion.1 = bf16[2048,1536]{1,0:T(8,128)(2,1)} fusion(bf16[1024,2048]{1,0:T(8,128)(2,1)S(1)} %copy-done.24, bf16[1024,1536]{1,0:T(8,128)(2,1)S(1)} %copy-done.20), kind=kOutput, calls=%fused_computation.1 | convolution fusion | flops 6445596672 | bytes 13631488 | tf_op jit(solution)/shard_map/dot_general | solution.py:32
  505.3 3.8 convolution_convert_fusion.4
  509.1 0.3 fusion.3
  509.5 1.4 collective-permute-start.1
  510.9 1.1 pad_maximum_fusion.1
  512.0 0.7 collective-permute-start.3
  512.7 121.6 %shard_map.234 = (f32[256,2048]{1,0:T(8,128)}, f32[64,6144]{1,0:T(8,128)}, f32[64,2048]{1,0:T(8,128)}, f32[4,8,256]{2,1,0:T(8,128)}) custom-call(bf16[1024,1536]{1,0:T(8,128)(2,1)} %copy-done.19, bf16[2048,1536]{1,0:T(8,128)(2,1)} %get-tuple-element.60.weight_ref, bf16[8,256,1536]{2,1,0:T(8,128)(2,1)} %bitcast.67, bf16[8,64,2048]{2,1,0:T(8,128)(2,1)} %bitcast.68, ...), custom_call_target="tpu_custom_call" | custom-call | flops 6442450944 | bytes 209715200 | tf_op jit(solution)/shard_map/pallas_call | solution.py:985
  634.4 0.8 slice_reduce_fusion.1
  635.3 0.1 reshape.64
  635.3 0.6 constant_dynamic-slice_fusion
  635.9 0.8 slice_reduce_fusion
  636.8 0.5 slice_bitcast_fusion
  637.3 3.8 fusion.1
  641.1 2.5 convert_element_type.81
  643.6 2.3 convert_element_type.79
  645.9 2.4 convert_element_type.82
  648.3 1.3 copy.45
  649.7 1.1 copy.46
  650.8 0.8 copy.47
  (78 shorter events, 0.8 us)
Async XLA Ops:
  7.2 289.4 %all-gather.3.cloned.1.call-start = ((), (), s32[]{:S(2)}) async-start(), calls=%async_computation.3 | async-start | bytes 6488064 | tf_op jit(solution)/shard_map/all_gather | solution.py:1264
  10.7 1.2 copy-start.3
  11.9 1.2 copy-start.4
  13.1 1.1 copy-start.6
  14.2 0.9 copy-start.8
  15.2 122.6 %copy-start.29 = (s32[1,1024]{1,0:T(1,128)S(1)}, s32[1,1024]{1,0:T(1,128)}, u32[]{:S(2)}) copy-start(s32[1,1024]{1,0:T(1,128)} %param.15) | copy-start | bytes 12292
  132.4 1.9 copy-start.21
  134.3 2.1 copy-start.23
  136.5 171.8 %all-gather.5.cloned.1.call-start = ((), (), s32[]{:S(2)}) async-start(), calls=%async_computation.4 | async-start | bytes 6488064 | tf_op jit(solution)/shard_map/all_gather | solution.py:1265
  137.2 503.9 %reduce-scatter.6.cloned.1.call-start = ((), (), s32[]{:S(2)}) async-start(), calls=%async_computation.6 | async-start | bytes 6488064 | tf_op jit(solution)/shard_map/reduce_scatter | solution.py:1311
  138.5 1.4 copy-start.9
  139.9 21.9 %copy-start.5 = (bf16[1,256,2048]{2,1,0:T(8,128)(2,1)S(1)}, bf16[1,256,2048]{2,1,0:T(8,128)(2,1)}, u32[]{:S(2)}) copy-start(bf16[1,256,2048]{2,1,0:T(8,128)(2,1)} %param.14) | copy-start | bytes 3145732
  139.9 21.9 %copy-start.7 = (bf16[1408,256]{1,0:T(8,128)(2,1)S(1)}, bf16[1408,256]{1,0:T(8,128)(2,1)}, u32[]{:S(2)}) copy-start(bf16[1408,256]{1,0:T(8,128)(2,1)} %down_ref.1) | copy-start | bytes 2162692
  158.3 1.6 copy-start.11
  159.9 1.3 copy-start.13
  161.8 146.4 %copy-start.2 = (f32[1,2048]{1,0:T(1,128)}, f32[1,2048]{1,0:T(1,128)S(1)}, u32[]{:S(2)}) copy-start(f32[1,2048]{1,0:T(1,128)S(1)} %get-tuple-element.80.gain_ref) | copy-start | bytes 24580
  292.2 1.3 copy-start
  293.5 1.0 copy-start.15
  294.4 2.1 copy-start.17
  308.3 14.9 %copy-start.22 = (bf16[1024,2048]{1,0:T(8,128)(2,1)S(1)}, bf16[1024,2048]{1,0:T(8,128)(2,1)}, u32[]{:S(2)}) copy-start(bf16[1024,2048]{1,0:T(8,128)(2,1)} %copy-done.21) | copy-start | bytes 12582916
  321.6 1.6 copy-start.31
  331.3 17.0 %copy-start.18 = (bf16[1024,2048]{1,0:T(8,128)(2,1)S(1)}, bf16[1024,2048]{1,0:T(8,128)(2,1)}, u32[]{:S(2)}) copy-start(bf16[1024,2048]{1,0:T(8,128)(2,1)} %copy-done.17) | copy-start | bytes 12582916
  346.7 1.6 copy-start.32
  356.9 286.7 %reduce-scatter.4.cloned.1.call-start = ((), (), s32[]{:S(2)}) async-start(), calls=%async_computation.5 | async-start | bytes 6488064 | tf_op jit(solution)/shard_map/reduce_scatter | solution.py:1299
  368.0 277.9 %reduce-scatter.8.cloned.1.call-start = ((), (), s32[]{:S(2)}) async-start(), calls=%async_computation.7 | async-start | bytes 6488064 | tf_op jit(solution)/shard_map/reduce_scatter | solution.py:1291
  453.8 4.8 copy-start.10
  453.8 4.8 copy-start.12
  453.8 4.8 copy-start.14
  480.2 1.7 copy-start.19
  482.0 12.9 %copy-start.24 = (bf16[1024,2048]{1,0:T(8,128)(2,1)S(1)}, bf16[1024,2048]{1,0:T(8,128)(2,1)}, u32[]{:S(2)}) copy-start(bf16[1024,2048]{1,0:T(8,128)(2,1)} %copy-done.23) | copy-start | bytes 12582916
  491.8 17.3 %copy-start.25 = (f32[1024,2048]{1,0:T(8,128)}, f32[1024,2048]{1,0:T(8,128)S(1)}, u32[]{:S(2)}) copy-start(f32[1024,2048]{1,0:T(8,128)S(1)} %fusion.7) | copy-start | bytes 25165828
  491.8 4.3 copy-start.20
  492.1 17.0 %collective-permute-start = (bf16[128,2048]{1,0:T(8,128)(2,1)S(1)}, bf16[128,2048]{1,0:T(8,128)(2,1)S(1)}, u32[]{:S(2)}, u32[]{:S(2)}) collective-permute-start(bf16[128,2048]{1,0:T(8,128)(2,1)S(1)} %get-tuple-element.76), channel_id=1, source_target_pairs={{0,2},{1,3},{2,0},{3,1},{4,6},{5,7},{6,4},{7,5},{8,10},{9,11},{10,... | collective-permute-start | bytes 1572872 | tf_op jit(solution)/shard_map/ppermute | solution.py:60
  493.6 15.5 %collective-permute-start.2 = (bf16[128,2048]{1,0:T(8,128)(2,1)S(1)}, bf16[128,2048]{1,0:T(8,128)(2,1)S(1)}, u32[]{:S(2)}, u32[]{:S(2)}) collective-permute-start(bf16[128,2048]{1,0:T(8,128)(2,1)S(1)} %get-tuple-element.77), channel_id=1, source_target_pairs={{0,1},{1,0},{2,3},{3,2},{4,5},{5,4},{6,7},{7,6},{8,9},{9,8},{10,11... | collective-permute-start | bytes 1572872 | tf_op jit(solution)/shard_map/ppermute | solution.py:60
  496.1 9.2 %copy-start.16 = (bf16[1024,512]{1,0:T(8,128)(2,1)S(1)}, bf16[1024,512]{1,0:T(8,128)(2,1)}, u32[]{:S(2)}) copy-start(bf16[1024,512]{1,0:T(8,128)(2,1)} %copy-done.15) | copy-start | bytes 3145732
  496.1 9.2 %copy-start.30 = (bf16[1024,2048]{1,0:T(8,128)(2,1)S(1)}, bf16[1024,2048]{1,0:T(8,128)(2,1)}, u32[]{:S(2)}) copy-start(bf16[1024,2048]{1,0:T(8,128)(2,1)} %get-tuple-element.55) | copy-start | bytes 12582916
  509.5 127.8 %collective-permute-start.1 = (bf16[256,2048]{1,0:T(8,128)(2,1)S(1)}, bf16[256,2048]{1,0:T(8,128)(2,1)}, u32[]{:S(2)}, u32[]{:S(2)}) collective-permute-start(bf16[256,2048]{1,0:T(8,128)(2,1)S(1)} %pad_maximum_fusion), channel_id=1, source_target_pairs={{0,1},{1,0},{2,3},{3,2},{4,5},{5,4},{6,7},{7,6},{8,9},{9,8},{10,11... | collective-permute-start | bytes 3145736 | tf_op jit(solution)/shard_map/ppermute | solution.py:60
  512.0 125.3 %collective-permute-start.3 = (bf16[256,2048]{1,0:T(8,128)(2,1)}, bf16[256,2048]{1,0:T(8,128)(2,1)}, u32[]{:S(2)}, u32[]{:S(2)}) collective-permute-start(bf16[256,2048]{1,0:T(8,128)(2,1)} %pad_maximum_fusion.1), channel_id=1, source_target_pairs={{0,2},{1,3},{2,0},{3,1},{4,6},{5,7},{6,4},{7,5},{8,10},{9,11},{10,... | collective-permute-start | bytes 3145736 | tf_op jit(solution)/shard_map/ppermute | solution.py:60
  512.7 124.6 %copy-start.1 = (f32[256,2048]{1,0:T(8,128)S(1)}, f32[256,2048]{1,0:T(8,128)}, u32[]{:S(2)}) copy-start(f32[256,2048]{1,0:T(8,128)} %copy-done) | copy-start | bytes 6291460
  641.1 7.2 %copy-start.26 = (f32[256,2048]{1,0:T(8,128)S(1)}, f32[256,2048]{1,0:T(8,128)}, u32[]{:S(2)}) copy-start(f32[256,2048]{1,0:T(8,128)} %get-tuple-element.64) | copy-start | bytes 6291460
  645.9 3.8 copy-start.27
  648.3 2.5 copy-start.28
Sparse Core Ops, SparseCore 0:
  136.6 69.3 all-gather.2
  207.7 80.5 all-gather.4
  357.0 64.1 reduce-scatter.5
  423.3 63.1 reduce-scatter.3
  488.7 82.5 reduce-scatter.7

commit v6 on v5

--- a/solution.py
+++ b/solution.py
@@ -216,11 +216,9 @@
         place = self.place
         other = 1 - 2 * place.core
         if hop == 0:
-            if use:
-                use(place.row)
             self.came_over(0, place.row + other)
             if use:
-                use(place.row + other)
+                use(place.line)
             return
         for at, line, there in (
             (hop, place.line - hop, place.line - hop >= 0),
@@ -229,12 +227,9 @@
 
             @pl.when(there)
             def _():
-                row = self.row(line)
+                self.came_over(at, self.row(line) + other)
                 if use:
-                    use(row)
-                self.came_over(at, row + other)
-                if use:
-                    use(row + other)
+                    use(line)
 
     def finish(self):
         place = self.place
@@ -310,13 +305,15 @@
         return pltpu.SemaphoreType.DMA((2, 4))
 
 
-def greet_all(place, dp, ctx):
+def greet_all(place, dp, ctx, signal=True, wait=True):
     barrier = pltpu.get_barrier_semaphore()
-    for k in range(1, ctx):
-        pl.semaphore_signal(barrier, 1, device_id=place.across(k), device_id_type=MESH)
-    for k in range(1, dp):
-        pl.semaphore_signal(barrier, 1, device_id=((place.row + k) % dp, place.col), device_id_type=MESH)
-    pl.semaphore_wait(barrier, ctx + dp - 2)
+    if signal:
+        for k in range(1, ctx):
+            pl.semaphore_signal(barrier, 1, device_id=place.across(k), device_id_type=MESH)
+        for k in range(1, dp):
+            pl.semaphore_signal(barrier, 1, device_id=((place.row + k) % dp, place.col), device_id_type=MESH)
+    if wait:
+        pl.semaphore_wait(barrier, ctx + dp - 2)
 
 
 PARTS = 2
@@ -324,9 +321,9 @@
 
 def opening_kernel(
     dp, ctx,
-    small_ref, qkv_ref, out_weight_ref, rows_ref, cot_ref,
+    gain_one, shift_one, gain_two, shift_two, bias, qkv_hbm, out_weight_ref, rows_ref, cot_ref,
     small_all, params_ref, weight_ref, out_all, normed_ref, joined_ref, cot_all,
-    blocks, rows_all, local_sem, swap_sem, small_sem, line_joined, line_out, rows_sem, cot_sem,
+    small_ref, qkv_ref, blocks, rows_all, local_sem, swap_sem, small_sem, line_joined, line_out, rows_sem, cot_sem,
 ):
     place = Place(dp)
     me, row = place.col, place.row
@@ -334,6 +331,19 @@
     length, width = rows_ref.shape
     rows_out = out_weight_ref.shape[0]
     tall = ctx * depth
+
+    qkv_copy = pltpu.make_async_copy(qkv_hbm, qkv_ref, local_sem.at[4])
+    qkv_copy.start()
+    greet_all(place, dp, ctx, wait=False)
+    small_ref[...] = jnp.zeros_like(small_ref)
+    for i, vector in enumerate((gain_one, shift_one, gain_two, shift_two)):
+        small_ref[i // 2 : i // 2 + 1, i % 2 * HD : (i % 2 + 1) * HD] = vector[...].astype(f32)
+    for i in range(bias.shape[1] // HD):
+        small_ref[2 + i // 2 : 3 + i // 2, i % 2 * HD : (i % 2 + 1) * HD] = bias[
+            :, i * HD : (i + 1) * HD
+        ].astype(f32)
+    small_all[row, me] = small_ref[...]
+    qkv_copy.wait()
 
     low = head_lanes((depth, PAIR))
     for p in range(width // HD // ctx // 2):
@@ -346,8 +356,7 @@
                 b = qkv_ref[:, at : at + PAIR].astype(f32)
                 blocks[c, :, lanes] = jnp.where(low, a, pltpu.roll(b, HD, 1)).astype(bf16)
                 blocks[c + 1, :, lanes] = jnp.where(low, pltpu.roll(a, HD, 1), b).astype(bf16)
-    small_all[row, me] = small_ref[...]
-    greet_all(place, dp, ctx)
+    greet_all(place, dp, ctx, signal=False)
 
     def weight_rows(row, col):
         return weight_ref.at[pl.ds(pl.multiple_of((row * ctx + col) * depth, depth), depth), :]
@@ -434,14 +443,16 @@
             scaled, _ = norm_stats(rows_all[rows, :].astype(f32))
             normed_ref[rows, :] = (scaled * params_ref[0:1, :] + params_ref[1:2, :]).astype(bf16)
 
-    def multiply(i, row):
-        at = pl.multiple_of(row * tall, tall)
+    def multiply(i, line):
+        at = pl.multiple_of(line * (2 * tall), 2 * tall)
         cols = slice(i * part_cols, (i + 1) * part_cols)
 
         @pl.loop(0, ctx)
         def _(b):
             rows = pl.ds(pl.multiple_of(b * length, length), length)
-            joined_ref[rows, cols] += dot(normed_ref[rows, pl.ds(at, tall)], weight_ref[pl.ds(at, tall), cols])
+            joined_ref[rows, cols] += dot(
+                normed_ref[rows, pl.ds(at, 2 * tall)], weight_ref[pl.ds(at, 2 * tall), cols]
+            )
 
     def forward(hop):
         for line in lines:
@@ -465,6 +476,7 @@
                 normalize(col)
             rows_gather.finish()
             normalize(place.other(3))
+        if hop == min(2, place.lines - 1):
             cot_gather.second()
         absorb(hop - 1)
     absorb(place.lines - 1)
@@ -478,17 +490,17 @@
     local[3].wait()
 
 
-def opening(dp, ctx, small, qkv_weight, out_weight, rows, cot):
+def opening(dp, ctx, vectors, qkv_weight, out_weight, rows, cot):
     depth, width = qkv_weight.shape[0], rows.shape[1]
     length = rows.shape[0]
     near = 3 * width // ctx
     vmem = pl.BlockSpec(memory_space=pltpu.VMEM)
     return pl.pallas_call(
         functools.partial(opening_kernel, dp, ctx),
-        in_specs=[vmem, vmem, ANY, ANY, ANY],
+        in_specs=[vmem] * len(vectors) + [ANY] * 4,
         out_specs=[vmem, vmem, vmem, ANY, vmem, vmem, ANY],
         out_shape=[
-            jax.ShapeDtypeStruct((dp, ctx) + small.shape, f32),
+            jax.ShapeDtypeStruct((dp, ctx, 8, PAIR), f32),
             jax.ShapeDtypeStruct((4, width), f32),
             jax.ShapeDtypeStruct((dp * ctx * depth, near), bf16),
             jax.ShapeDtypeStruct((dp * out_weight.shape[0], width), bf16),
@@ -497,9 +509,11 @@
             jax.ShapeDtypeStruct((ctx * length, width), bf16),
         ],
         scratch_shapes=[
+            pltpu.VMEM((8, PAIR), f32),
+            pltpu.VMEM((depth, 3 * width), bf16),
             pltpu.VMEM((ctx, depth, near), bf16),
             pltpu.VMEM((ctx * length, width), bf16),
-            pltpu.SemaphoreType.DMA((4,)),
+            pltpu.SemaphoreType.DMA((5,)),
             pltpu.SemaphoreType.DMA((4, ctx)),
             pltpu.SemaphoreType.DMA((2, dp)),
             pltpu.SemaphoreType.DMA((PARTS, 6, dp)),
@@ -513,7 +527,7 @@
         cost_estimate=pl.CostEstimate(
             flops=2 * ctx * length * width * near, transcendentals=0, bytes_accessed=200 << 20
         ),
-    )(small, qkv_weight, out_weight, rows, cot)
+    )(*vectors, qkv_weight, out_weight, rows, cot)
 
 
 CHUNKS = 4
@@ -635,27 +649,17 @@
 
 
 def mix_kernel(
-    dp, ctx, attended_ref, weight_ref, rows_ref, gain_ref, shift_ref, down_ref, resid_ref, wide_ref, down_all,
-    total, sent, got, made, reduce_sem, spread_sem, line_sem, local_sem,
+    dp, ctx, attended_ref, weight_ref, rows_ref, gain_ref, shift_ref, resid_ref, wide_ref,
+    total, sent, got, made, reduce_sem, spread_sem,
 ):
     place = Place(dp)
-    greet_all(place, dp, ctx)
+    greet(place, ctx)
     size = rows_ref.shape[0]
-    cols = down_ref.shape[1]
-
-    def shard(row):
-        return down_all.at[:, pl.ds(pl.multiple_of(row * cols, cols), cols)]
-
-    line = LineGather(place, shard, line_sem)
-    local = pltpu.make_async_copy(down_ref, shard(place.row), local_sem)
-    local.start()
     reduce = CtxReduce(
         place, lambda col: dot(rows_of(attended_ref, col, size), weight_ref[...]), total, sent, got, reduce_sem
     )
     spread = CtxSpread(place, made, wide_ref, spread_sem)
     reduce.start()
-    local.wait()
-    line.send(1)
     reduce.relay()
     for j in range(CHUNKS):
         rows = reduce.chunk(j)
@@ -666,41 +670,24 @@
         spread.send(j)
         if j:
             spread.relay(j - 1)
-        if j == CHUNKS // 2:
-            line.receive(1)
-            if place.lines > 2:
-                line.send(2)
     spread.relay(CHUNKS - 1)
-    for hop in range(2, place.lines):
-        line.receive(hop)
-        if hop < place.lines - 1:
-            line.send(hop + 1)
     spread.finish()
-    for hop in range(place.lines):
-        line.settle(hop)
-    line.finish()
     reduce.finish()
 
 
-def mix(dp, ctx, attended, weight, rows, gain, shift, down):
+def mix(dp, ctx, attended, weight, rows, gain, shift):
     size, width = rows.shape
     vmem = pl.BlockSpec(memory_space=pltpu.VMEM)
     return pl.pallas_call(
         functools.partial(mix_kernel, dp, ctx),
-        in_specs=[vmem] * 5 + [ANY],
-        out_specs=[vmem, ANY, ANY],
-        out_shape=[
-            jax.ShapeDtypeStruct((size, width), f32),
-            jax.ShapeDtypeStruct((ctx * size, width), bf16),
-            jax.ShapeDtypeStruct((down.shape[0], dp * down.shape[1]), bf16),
-        ],
+        in_specs=[vmem] * 5,
+        out_specs=[vmem, ANY],
+        out_shape=[jax.ShapeDtypeStruct((size, width), f32), jax.ShapeDtypeStruct((ctx * size, width), bf16)],
         scratch_shapes=CtxReduce.scratch(size, width)[:3]
         + [
             pltpu.VMEM((size, width), bf16),
             CtxReduce.scratch(size, width)[3],
             CtxSpread.scratch(),
-            LineGather.scratch(dp),
-            pltpu.SemaphoreType.DMA,
         ],
         compiler_params=pltpu.CompilerParams(
             collective_id=2, has_side_effects=True, vmem_limit_bytes=40 << 20
@@ -708,29 +695,79 @@
         cost_estimate=pl.CostEstimate(
             flops=2 * attended.size * width, transcendentals=0, bytes_accessed=180 << 20
         ),
-    )(attended, weight, rows, gain.reshape(1, width), shift.reshape(1, width), down)
+    )(attended, weight, rows, gain.reshape(1, width), shift.reshape(1, width))
 
 
 def mix_back_kernel(
-    dp, ctx, gate_ref, up_ref, gate_weight_ref, up_weight_ref, resid_ref, cot_ref, gain_ref,
-    d_resid_ref, sums_ref, wide_ref,
-    total, sent, got, made, reduce_sem, spread_sem,
+    dp, ctx, gate_ref, up_ref, gate_weight_hbm, up_weight_hbm, inner_hbm, down_hbm, normed_hbm,
+    resid_ref, cot_ref, gain_ref,
+    d_resid_ref, sums_ref, wide_ref, branch_hbm, d_up_hbm,
+    total, sent, got, made, gate_weight_ref, up_weight_ref, inner_ref, down_ref, normed_ref, branch, d_up,
+    reduce_sem, spread_sem, load_sem, branch_sem, d_up_sem,
 ):
     place = Place(dp)
+    loads = [
+        pltpu.make_async_copy(src, dst, load_sem.at[i])
+        for i, (src, dst) in enumerate(
+            (
+                (gate_weight_hbm, gate_weight_ref), (up_weight_hbm, up_weight_ref), (normed_hbm, normed_ref),
+                (inner_hbm, inner_ref), (down_hbm, down_ref),
+            )
+        )
+    ]
+    for load in loads[:2]:
+        load.start()
     greet(place, ctx)
-    size = cot_ref.shape[0]
+    size, width = cot_ref.shape
+    cols = width // ctx // 2
+    for load in loads[:2]:
+        load.wait()
 
     def block(col):
         return dot_nt(rows_of(gate_ref, col, size), gate_weight_ref[...]) + dot_nt(
             rows_of(up_ref, col, size), up_weight_ref[...]
         )
 
+    def d_up_copy(i):
+        return pltpu.make_async_copy(
+            d_up.at[i % 2], d_up_hbm.at[pl.ds(i * cols, cols), :], d_up_sem.at[i % 2]
+        )
+
+    def branch_copy(i):
+        return pltpu.make_async_copy(
+            branch.at[i % 2], branch_hbm.at[pl.ds(i * size, size), :], branch_sem.at[i % 2]
+        )
+
+    def d_up_piece(i):
+        if i == 0:
+            loads[2].wait()
+        if i > 1:
+            d_up_copy(i - 2).wait()
+        d_up[i % 2] = dot_tn(normed_ref[:, i * cols : (i + 1) * cols], up_ref[...]).astype(bf16)
+        d_up_copy(i).start()
+
+    def branch_piece(i):
+        if i == 0:
+            loads[3].wait()
+            loads[4].wait()
+        if i > 1:
+            branch_copy(i - 2).wait()
+        branch[i % 2] = dot(inner_ref[i * size : (i + 1) * size, :], down_ref[...]).astype(bf16)
+        branch_copy(i).start()
+
+    pieces = [functools.partial(d_up_piece, i) for i in range(2 * ctx)]
+    pieces += [functools.partial(branch_piece, i) for i in range(ctx)]
+
     reduce = CtxReduce(place, block, total, sent, got, reduce_sem)
     spread = CtxSpread(place, made, wide_ref, spread_sem)
     reduce.start()
+    for load in loads[2:]:
+        load.start()
     reduce.relay()
     sums_ref[...] = jnp.zeros_like(sums_ref)
     for j in range(CHUNKS):
+        for piece in pieces[2 * j : 2 * j + 2]:
+            piece()
         rows = reduce.chunk(j)
         scaled, inv_std = norm_stats(resid_ref[rows, :])
         grad, d_gain, d_shift = norm_backward(reduce.sum(j), scaled, inv_std, gain_ref[...])
@@ -742,36 +779,55 @@
         spread.send(j)
         if j:
             spread.relay(j - 1)
+    pieces[2 * CHUNKS]()
     spread.relay(CHUNKS - 1)
+    for piece in pieces[2 * CHUNKS + 1 :]:
+        piece()
     spread.finish()
     reduce.finish()
-
-
-def mix_back(dp, ctx, d_gate, d_up, gate_weight, up_weight, resid, cot, gain):
+    for i in (1, 2):
+        d_up_copy(2 * ctx - i).wait()
+        branch_copy(ctx - i).wait()
+
+
+def mix_back(dp, ctx, d_gate, d_up, gate_weight, up_weight, inner, down, normed, resid, cot, gain):
     size, width = cot.shape
+    hidden = d_up.shape[1]
     vmem = pl.BlockSpec(memory_space=pltpu.VMEM)
     return pl.pallas_call(
         functools.partial(mix_back_kernel, dp, ctx),
-        in_specs=[vmem] * 7,
-        out_specs=[vmem, vmem, ANY],
+        in_specs=[vmem] * 2 + [ANY] * 5 + [vmem] * 3,
+        out_specs=[vmem, vmem, ANY, ANY, ANY],
         out_shape=[
             jax.ShapeDtypeStruct((size, width), f32),
             jax.ShapeDtypeStruct((2, width), f32),
             jax.ShapeDtypeStruct((ctx * size, width), bf16),
+            jax.ShapeDtypeStruct((ctx * size, width), bf16),
+            jax.ShapeDtypeStruct((width, hidden), bf16),
         ],
         scratch_shapes=CtxReduce.scratch(size, width)[:3]
         + [
             pltpu.VMEM((size, width), bf16),
+            pltpu.VMEM((width, hidden), bf16),
+            pltpu.VMEM((width, hidden), bf16),
+            pltpu.VMEM((ctx * size, hidden), bf16),
+            pltpu.VMEM((hidden, width), bf16),
+            pltpu.VMEM((ctx * size, width), bf16),
+            pltpu.VMEM((2, size, width), bf16),
+            pltpu.VMEM((2, width // ctx // 2, hidden), bf16),
             CtxReduce.scratch(size, width)[3],
             CtxSpread.scratch(),
+            pltpu.SemaphoreType.DMA((5,)),
+            pltpu.SemaphoreType.DMA((2,)),
+            pltpu.SemaphoreType.DMA((2,)),
         ],
         compiler_params=pltpu.CompilerParams(
-            collective_id=3, has_side_effects=True, vmem_limit_bytes=56 << 20
+            collective_id=3, has_side_effects=True, vmem_limit_bytes=60 << 20
         ),
         cost_estimate=pl.CostEstimate(
-            flops=4 * d_gate.size * width, transcendentals=0, bytes_accessed=180 << 20
+            flops=8 * d_gate.size * width, transcendentals=0, bytes_accessed=180 << 20
         ),
-    )(d_gate, d_up, gate_weight, up_weight, resid, cot, gain.reshape(1, width))
+    )(d_gate, d_up, gate_weight, up_weight, inner, down, normed, resid, cot, gain.reshape(1, width))
 
 
 class LineReduce:
@@ -1227,21 +1283,23 @@
     own = me * local_len
 
     part = ln1_gain.shape[0]
-    small = jnp.concatenate([ln1_gain, ln1_bias, ln2_gain, ln2_bias, qkv_bias]).astype(f32)
-    count = small.shape[0]
-    small = jnp.pad(small, (0, 1024 - count)).reshape(8, 128)
+    vectors = [v[None, :] for v in (ln1_gain, ln1_bias, ln2_gain, ln2_bias, qkv_bias)]
+    count = 4 * part + qkv_bias.shape[0]
     rows_here = qkv_weight.shape[0]
     rows, grad_rows = inputs[0], cotangent[0]
     fused = ctx == 4 and dp % 2 == 0 and part == HD
     if fused:
         small, params, joined_weight, out_full, normed_one, joined, grad_wide = opening(
-            dp, ctx, small, qkv_weight, out_weight, rows, grad_rows
+            dp, ctx, vectors, qkv_weight, out_weight, rows, grad_rows
         )
         gain_one, shift_one, gain_two, shift_two = params
-        gate_weight, up_weight, _ = lax.optimization_barrier((gate_weight, up_weight, normed_one))
+        gate_weight, up_weight, down_weight, _ = lax.optimization_barrier(
+            (gate_weight, up_weight, down_weight, normed_one)
+        )
         small = small.reshape(dp * ctx, 1024)[:, :count]
     else:
-        small = lax.all_gather(small[None, :], ("dp", "ctx"), axis=0, tiled=True)
+        small = jnp.concatenate(vectors, axis=1).astype(f32)
+        small = lax.all_gather(small, ("dp", "ctx"), axis=0, tiled=True)
         blocks = qkv_weight.reshape(rows_here, 3, pairs, 2, ctx, HD).transpose(4, 0, 2, 1, 3, 5)
         blocks = exchange_ctx(blocks.reshape(ctx, rows_here, near * 3 * HD), ctx)
         joined_weight = lax.all_gather(
@@ -1251,7 +1309,6 @@
         out_full = out_full.reshape(near, ctx, HD, width)
         out_full = lax.dynamic_index_in_dim(out_full, me, 1, keepdims=False)
         out_full = out_full.reshape(near * HD, width)
-        small = small.reshape(dp * ctx, 1024)[:, :count]
         gain_one, shift_one, gain_two, shift_two = [
             small[:, i * part : (i + 1) * part].reshape(width) for i in range(4)
         ]
@@ -1263,6 +1320,7 @@
     bias = bias.transpose(1, 0, 2, 3).reshape(1, near * 3 * HD)
     gate_full = lax.all_gather(gate_weight, "dp", axis=0, tiled=True)
     up_full = lax.all_gather(up_weight, "dp", axis=0, tiled=True)
+    down_full = lax.all_gather(down_weight, "dp", axis=1, tiled=True)
 
     segment = segments[0]
     start = jnp.sum((segment[None, :] < segment[:, None]).astype(jnp.int32), axis=1)
@@ -1272,11 +1330,8 @@
         joined = dot(normed_one, joined_weight)
     attended, qkv, lse = attend(joined, bias, table, start)
     if fused:
-        resid, normed_wide, down_full = mix(
-            dp, ctx, attended, out_full, rows, gain_two, shift_two, down_weight
-        )
+        resid, normed_wide = mix(dp, ctx, attended, out_full, rows, gain_two, shift_two)
     else:
-        down_full = lax.all_gather(down_weight, "dp", axis=1, tiled=True)
         resid = rows.astype(f32) + scatter_ctx(dot(attended, out_full), ctx)
         scaled_two, inv_two = norm_stats(resid)
         normed_wide = gather_ctx((scaled_two * gain_two + shift_two).astype(bf16), ctx)
@@ -1293,28 +1348,30 @@
     d_gate = (d_inner * upward * sigma * (1.0 + gate * (1.0 - sigma))).astype(bf16)
     d_upward = (d_inner * swish).astype(bf16)
     d_gate_weight = dot_tn(normed_wide, d_gate).astype(bf16)
-    d_up_weight = dot_tn(normed_wide, d_upward).astype(bf16)
-    branch = dot(inner, down_full)
     d_gate_ready, d_gate_weight = lax.optimization_barrier((d_gate, d_gate_weight))
     d_gate_weight = lax.psum_scatter(d_gate_weight, "dp", scatter_dimension=0, tiled=True).astype(f32)
     if fused:
-        d_resid, sums_two, d_proj = mix_back(
-            dp, ctx, d_gate_ready, d_upward, gate_full, up_full, resid, grad_rows, gain_two
+        d_resid, sums_two, d_proj, branch, d_up_weight = mix_back(
+            dp, ctx, d_gate_ready, d_upward, gate_full, up_full, inner, down_full, normed_wide, resid,
+            grad_rows, gain_two,
         )
     else:
+        branch = dot(inner, down_full)
+        d_up_weight = dot_tn(normed_wide, d_upward).astype(bf16)
         d_normed_two = scatter_ctx(dot_nt(d_gate, gate_full) + dot_nt(d_upward, up_full), ctx)
         grad, d_gain_two, d_shift_two = norm_backward(d_normed_two, scaled_two, inv_two, gain_two)
         d_resid = grad_rows.astype(f32) + grad
         d_proj = gather_ctx(d_resid.astype(bf16), ctx)
-    branch, _ = lax.optimization_barrier((branch, d_proj))
-    output = (resid + scatter_ctx(branch, ctx)).astype(bf16)
     d_up_weight = lax.psum_scatter(d_up_weight, "dp", scatter_dimension=0, tiled=True).astype(f32)
 
     d_attended = dot_nt(d_proj, out_full).astype(bf16)
     d_out_weight = dot_tn(attended, d_proj).astype(bf16)
+    d_attended, d_down = lax.optimization_barrier((d_attended, d_down))
     d_joined, d_bias = attend_back(qkv, d_attended, lse, table, start)
+    output = (resid + scatter_ctx(branch, ctx, d_joined)).astype(bf16)
     d_joined_weight = dot_tn(normed_one, d_joined).astype(bf16)
     d_bias = d_bias.reshape(pairs, 3, 2, HD).transpose(1, 0, 2, 3)
+    d_joined, d_gate_weight = lax.optimization_barrier((d_joined, d_gate_weight))
     if fused:
         d_bias = jnp.pad(d_bias.reshape(dp, -1), ((0, 0), (0, width // dp - near * 3 * HD // dp)))
         grad_input, d_joined_weight, d_out_weight, small = closing(

time: 670 us -> 602 us (0.90)
  Pallas kernels: 494 us -> 400 us
  waiting for transfers between devices: 1.12 us -> 45.2 us
  matrix products: 95.5 us -> 74.6 us
    pallas_call x1, Pallas kernels: 130 us -> 72.5 us  [mix(): pl.pallas_call(functools.partial(mix_kernel, dp, ctx), in_specs=[vmem] *...]
    all_gather x0 -> x1, waiting for transfers between devices: none -> 38.4 us  [shards(): down_full = lax.all_gather(down_weight, 'dp', axis=1, tiled=True)]
    pallas_call x1, Pallas kernels: 117 us -> 97.3 us  [opening(): pl.pallas_call(functools.partial(opening_kernel, dp, ctx), in_specs=[vmem...]
    pallas_call x1, Pallas kernels: 122 us -> 104 us  [closing(): pl.pallas_call(functools.partial(closing_kernel, dp, ctx), in_specs=[vmem...]
    dot_general x3 -> x2, matrix products: 34.7 us -> 24.7 us  [dot(): return jnp.dot(a, b, preferred_element_type=f32)]
    dot_general x5 -> x4, matrix products: 40.6 us -> 32.2 us  [dot_tn(): lax.dot_general(a, b, (((0,), (0,)), ((), ())), preferred_element_type=f32)]
    unnamed x71 -> x77, local copies, waits for them, and re-layouts: 26.6 us -> 31.9 us
  transfers between devices with their start and end apart: 9 -> 10, of which waited for: 0 -> 2; matrix products, arithmetic and copies ran while one was open for 10% -> 16% of each run, Pallas kernels for 57% -> 51%
where the time goes in v6:
time: 602 us; the launch traced here: 596 us
  Pallas kernels  400 us (66%)
  matrix products  74.6 us (12%)
  waiting for transfers between devices  45.2 us (8%)
  local copies, waits for them, and re-layouts  40 us (7%)
  other arithmetic  15.9 us (3%)
  between operations  14.6 us (2%)
    pallas_call x1, Pallas kernels, closing(): pl.pallas_call(functools.partial(closing_kernel, dp, ctx), in_specs=[vmem...  104 us
    pallas_call x1, Pallas kernels, opening(): pl.pallas_call(functools.partial(opening_kernel, dp, ctx), in_specs=[vmem...  97.3 us
    pallas_call x1, Pallas kernels, mix_back(): pl.pallas_call(functools.partial(mix_back_kernel, dp, ctx), in_specs=[vme...  86 us
    pallas_call x1, Pallas kernels, mix(): pl.pallas_call(functools.partial(mix_kernel, dp, ctx), in_specs=[vmem] *...  72.5 us
    all_gather x1, waiting for transfers between devices, shards(): down_full = lax.all_gather(down_weight, 'dp', axis=1, tiled=True)  38.4 us
    dot_general x4, matrix products, dot_tn(): lax.dot_general(a, b, (((0,), (0,)), ((), ())), preferred_element_type=f32)  32.2 us
    unnamed x77, local copies, waits for them, and re-layouts  31.9 us
    dot_general x2, matrix products, dot(): return jnp.dot(a, b, preferred_element_type=f32)  24.7 us
  transfers between devices with their start and end apart: 10, of which 2 were waited for; matrix products, arithmetic and copies ran while one was open for 16% of the time, Pallas kernels for 51%

profile of v6, /device:TPU:0, one launch (start us, length us, event | category | flops | bytes accessed | tf_op | source)
XLA Modules:
  0.0 595.7 jit_solution(2396676461860326418)
XLA Ops:
  7.2 0.7 broadcast_in_dim.31.bias
  7.9 1.2 copy-done.3
  9.1 1.2 copy-done.4
  10.3 1.1 copy-done.6
  11.5 0.9 copy-done.7
  12.4 0.7 copy-done.8
  13.1 0.7 copy-done.9
  13.7 0.7 copy-done.10
  14.4 0.7 copy-done.11
  15.0 97.3 %shard_map.229 = (f32[8,4,8,128]{3,2,1,0:T(8,128)S(1)}, f32[4,2048]{1,0:T(4,128)S(1)}, bf16[2048,1536]{1,0:T(8,128)(2,1)}, bf16[512,2048]{1,0:T(8,128)(2,1)S(1)}...) custom-call(bf16[1,64]{1,0:T(2,128)(2,1)S(1)} %bitcast.57, ...), custom_call_target="tpu_custom_call" | custom-call | flops 6442450944 | bytes 209715200 | tf_op jit(solution)/shard_map/pallas_call | solution.py:498
  112.3 1.3 copy-done.22
  113.6 2.0 copy-done.25
  115.6 1.9 copy-done.27
  117.6 0.7 all-gather.6.cloned.1.call-update
  118.4 0.7 all-gather.8.cloned.1.call-update
  119.0 0.5 reduce-scatter.4.cloned.1.call-start
  119.8 0.6 convert_reduce_fusion
  120.6 1.4 copy-done.12
  122.0 18.4 %shard_map.230 = (bf16[1024,512]{1,0:T(8,128)(2,1)S(1)}, bf16[1024,1536]{1,0:T(8,128)(2,1)S(1)}, f32[1024,512]{1,0:T(8,128)S(1)}) custom-call(f32[1024,1536]{1,0:T(8,128)} %get-tuple-element.47.joined_ref, f32[1,1536]{1,0:T(1,128)S(1)} %reshape.52.bias_ref, f32[3,1024,128]{2,1,0:T(8,128)S(1)} %copy-done.12, s32[1024,128]{1,0:T(8,128)S(1)} %broadcast_in_dim.32.start_ref), custom_call_target="tpu_custom_call" | custom-call | flops 2415919104 | bytes 12582912 | tf_op jit(solution)/shard_map/pallas_call | solution.py:1202
  140.4 1.6 copy-done.14
  142.1 1.3 copy-done.16
  143.4 0.6 fusion.2
  144.0 72.5 %shard_map.231 = (f32[256,2048]{1,0:T(8,128)S(1)}, bf16[1024,2048]{1,0:T(8,128)(2,1)S(1)}) custom-call(bf16[1024,512]{1,0:T(8,128)(2,1)S(1)} %get-tuple-element.49.attended_ref, bf16[512,2048]{1,0:T(8,128)(2,1)S(1)} %copy-done.23, bf16[256,2048]{1,0:T(8,128)(2,1)S(1)} %bitcast.56, f32[1,2048]{1,0:T(1,128)S(1)} %get-tuple-element.92.gain_ref, ...), custom_call_target="tpu_custom_call" | custom-call | flops 2147483648 | bytes 188743680 | tf_op jit(solution)/shard_map/pallas_call | solution.py:681
  216.5 1.4 copy-done
  217.9 2.1 copy-done.20
  220.0 11.8 %fusion.3 = f32[1024,1408]{1,0:T(8,128)} fusion(bf16[1024,2048]{1,0:T(8,128)(2,1)} %copy-done.20, bf16[2048,1408]{1,0:T(8,128)(2,1)} %all-gather.4.cloned.1.call-done.gate_weight_hbm), kind=kOutput, calls=%fused_computation.34 | convolution fusion | flops 5905580032 | bytes 15728640 | tf_op jit(solution)/shard_map/dot_general | solution.py:24
  231.8 5.4 all-gather.6.cloned.1.call-done.up_weight_hbm
  237.1 12.9 %multiply_convert_fusion.2 = (bf16[1024,1408]{1,0:T(8,128)(2,1)S(1)}, f32[1024,1408]{1,0:T(8,128)}) fusion(f32[1024,1408]{1,0:T(8,128)} %fusion.3, bf16[1024,2048]{1,0:T(8,128)(2,1)} %copy-done.20, bf16[2048,1408]{1,0:T(8,128)(2,1)} %all-gather.6.cloned.1.call-done.up_weight_hbm), kind=kOutput, calls=%fused_computation.5 | convolution fusion | flops 5914230784 | bytes 24379392 | tf_op jit(solution)/shard_map/dot_general | solution.py:24
  250.1 1.6 copy-done.34
  251.7 8.1 %convolution_convert_fusion.2 = bf16[1408,2048]{1,0:T(8,128)(2,1)} fusion(bf16[1024,1408]{1,0:T(8,128)(2,1)S(1)} %get-tuple-element.97.inner_hbm, bf16[1024,2048]{1,0:T(8,128)(2,1)S(1)} %copy-done.26), kind=kOutput, calls=%fused_computation.2 | convolution fusion | flops 5908463616 | bytes 12845056 | tf_op jit(solution)/shard_map/dot_general | solution.py:32
  259.9 38.4 %all-gather.8.cloned.1.call-done.down_hbm = bf16[1408,2048]{1,0:T(8,128)(2,1)} async-done(((bf16[1408,256]{1,0:T(8,128)(2,1)}), bf16[1408,2048]{1,0:T(8,128)(2,1)}) %all-gather.8.cloned.1.call-update) | async-done | bytes 5767184 | tf_op jit(solution)/shard_map/all_gather | solution.py:1323
  298.3 15.4 %multiply_convert_fusion = (bf16[1024,1408]{1,0:T(8,128)(2,1)}, bf16[1024,1408]{1,0:T(8,128)(2,1)S(1)}) fusion(f32[1024,1408]{1,0:T(8,128)} %fusion.3, f32[1024,1408]{1,0:T(8,128)} %get-tuple-element.98, bf16[1024,2048]{1,0:T(8,128)(2,1)} %copy-done.25, bf16[1408,2048]{1,0:T(8,128)(2,1)} %all-gather.8.cloned.1.call-done.down_hbm), kind=kOutput, calls=%fused_computation.3 | convolution fusion | flops 5924323328 | bytes 27262976 | tf_op jit(solution)/shard_map/dot_general | solution.py:28
  313.7 1.6 copy-done.35
  315.3 8.5 %convolution_convert_fusion.1 = bf16[2048,1408]{1,0:T(8,128)(2,1)} fusion(bf16[1024,2048]{1,0:T(8,128)(2,1)S(1)} %copy-done.21, bf16[1024,1408]{1,0:T(8,128)(2,1)S(1)} %get-tuple-element.60.gate_ref), kind=kOutput, calls=%fused_computation.1 | convolution fusion | flops 5908463616 | bytes 12845056 | tf_op jit(solution)/shard_map/dot_general | solution.py:32
  324.3 86.0 %shard_map.232 = (f32[256,2048]{1,0:T(8,128)}, f32[2,2048]{1,0:T(2,128)}, bf16[1024,2048]{1,0:T(8,128)(2,1)}, bf16[1024,2048]{1,0:T(8,128)(2,1)}, bf16[2048,1408]{1,0:T(8,128)(2,1)}) custom-call(bf16[1024,1408]{1,0:T(8,128)(2,1)} %copy-done.35, bf16[1024,1408]{1,0:T(8,128)(2,1)} %get-tuple-element.82.up_ref, ...), custom_call_target="tpu_custom_call" | custom-call | flops 23622320128 | bytes 188743680 | tf_op jit(solution)/shard_map/pallas_call | solution.py:797
  410.3 2.3 constant_dynamic-slice_fusion
  412.6 0.6 collective-permute-start
  413.2 0.5 collective-permute-start.2
  413.8 6.5 %convolution_convert_fusion.3 = bf16[512,2048]{1,0:T(8,128)(2,1)} fusion(bf16[1024,512]{1,0:T(8,128)(2,1)S(1)} %get-tuple-element.49.attended_ref, bf16[1024,2048]{1,0:T(8,128)(2,1)} %get-tuple-element.63), kind=kOutput, calls=%fused_computation.9 | convolution fusion | flops 2148532224 | bytes 7340032 | tf_op jit(solution)/shard_map/dot_general | solution.py:32
  420.2 2.4 convolution_convert_fusion.4.grad_ref
  422.6 2.3 convert_element_type.67
  425.0 1.9 copy-done.15
  426.9 1.6 copy-done.17
  428.5 21.6 %shard_map.233 = (bf16[1024,1536]{1,0:T(8,128)(2,1)S(1)}, f32[1,1536]{1,0:T(1,128)S(1)}) custom-call(bf16[1024,1536]{1,0:T(8,128)(2,1)S(1)} %copy-done.15, bf16[1024,512]{1,0:T(8,128)(2,1)S(1)} %convolution_convert_fusion.4.grad_ref, f32[1024,512]{1,0:T(8,128)S(1)} %copy-done.17, f32[3,1024,128]{2,1,0:T(8,128)S(1)} %copy-done.13, ...), custom_call_target="tpu_custom_call" | custom-call | flops 6039797760 | bytes 12582912 | tf_op jit(solution)/shard_map/pallas_call | solution.py:1231
  450.1 1.7 copy-done.18
  451.9 2.3 convert_element_type.74
  454.2 1.3 constant_dynamic-slice_fusion.1
  455.6 2.1 add_convert_fusion.2
  457.7 1.1 pad_maximum_fusion.1
  458.8 1.5 collective-permute-start.3
  460.2 1.1 pad_maximum_fusion
  461.3 1.4 collective-permute-start.1
  462.7 0.6 pad.4.bias_ref
  463.4 9.0 %convolution_convert_fusion = bf16[2048,1536]{1,0:T(8,128)(2,1)} fusion(bf16[1024,2048]{1,0:T(8,128)(2,1)S(1)} %copy-done.28, bf16[1024,1536]{1,0:T(8,128)(2,1)S(1)} %copy-done.19), kind=kOutput, calls=%fused_computation | convolution fusion | flops 6445596672 | bytes 13631488 | tf_op jit(solution)/shard_map/dot_general | solution.py:32
  472.4 104.3 %shard_map.234 = (f32[256,2048]{1,0:T(8,128)}, f32[64,6144]{1,0:T(8,128)}, f32[64,2048]{1,0:T(8,128)}, f32[4,8,256]{2,1,0:T(8,128)}) custom-call(bf16[1024,1536]{1,0:T(8,128)(2,1)} %copy-done.18, bf16[2048,1536]{1,0:T(8,128)(2,1)} %get-tuple-element.71.weight_ref, bf16[8,256,1536]{2,1,0:T(8,128)(2,1)} %bitcast.68, bf16[8,64,2048]{2,1,0:T(8,128)(2,1)} %bitcast.69, ...), custom_call_target="tpu_custom_call" | custom-call | flops 6442450944 | bytes 209715200 | tf_op jit(solution)/shard_map/pallas_call | solution.py:1041
  576.7 0.8 slice_reduce_fusion.1
  577.7 2.5 convert_element_type.77
  580.2 0.6 constant_dynamic-slice_fusion.2
  580.7 0.8 slice_reduce_fusion
  581.6 0.5 slice_bitcast_fusion
  582.1 3.2 fusion.1
  585.4 1.3 copy.45
  586.7 1.1 copy.46
  587.8 0.8 copy.47
  (83 shorter events, 1.7 us)
Async XLA Ops:
  7.2 212.8 %all-gather.4.cloned.1.call-start = ((), (), s32[]{:S(2)}) async-start(), calls=%async_computation.3 | async-start | bytes 6488064 | tf_op jit(solution)/shard_map/all_gather | solution.py:1321
  7.9 1.2 copy-start.3
  9.1 1.2 copy-start.4
  10.3 1.1 copy-start.6
  11.5 0.9 copy-start.7
  12.4 0.7 copy-start.8
  13.1 0.7 copy-start.9
  13.7 0.7 copy-start.10
  14.4 0.7 copy-start.11
  15.0 104.8 %copy-start.32 = (s32[1,1024]{1,0:T(1,128)S(1)}, s32[1,1024]{1,0:T(1,128)}, u32[]{:S(2)}) copy-start(s32[1,1024]{1,0:T(1,128)} %param.15) | copy-start | bytes 12292
  112.3 1.3 copy-start.22
  113.6 2.0 copy-start.25
  115.6 1.9 copy-start.27
  117.6 119.6 %all-gather.6.cloned.1.call-start = ((), (), s32[]{:S(2)}) async-start(), calls=%async_computation.4 | async-start | bytes 6488064 | tf_op jit(solution)/shard_map/all_gather | solution.py:1322
  118.3 180.0 %all-gather.8.cloned.1.call-start = ((), (), s32[]{:S(2)}) async-start(), calls=%async_computation.5 | async-start | bytes 6488064 | tf_op jit(solution)/shard_map/all_gather | solution.py:1323
  119.0 303.6 %reduce-scatter.4.cloned.1.call-start = ((), (), s32[]{:S(2)}) async-start(), calls=%async_computation.6 | async-start | bytes 6488064 | tf_op jit(solution)/shard_map/reduce_scatter | solution.py:1346
  120.6 1.4 copy-start.12
  122.0 22.0 %copy-start.5 = (bf16[1,256,2048]{2,1,0:T(8,128)(2,1)S(1)}, bf16[1,256,2048]{2,1,0:T(8,128)(2,1)}, u32[]{:S(2)}) copy-start(bf16[1,256,2048]{2,1,0:T(8,128)(2,1)} %param.14) | copy-start | bytes 3145732
  122.0 22.0 %copy-start.23 = (bf16[512,2048]{1,0:T(8,128)(2,1)S(1)}, bf16[512,2048]{1,0:T(8,128)(2,1)}, u32[]{:S(2)}) copy-start(bf16[512,2048]{1,0:T(8,128)(2,1)} %copy-done.22) | copy-start | bytes 6291460
  140.4 1.7 copy-start.14
  142.1 1.3 copy-start.16
  144.0 87.8 %copy-start.2 = (f32[1,2048]{1,0:T(1,128)}, f32[1,2048]{1,0:T(1,128)S(1)}, u32[]{:S(2)}) copy-start(f32[1,2048]{1,0:T(1,128)S(1)} %get-tuple-element.92.gain_ref) | copy-start | bytes 24580
  216.5 1.4 copy-start
  217.9 2.1 copy-start.20
  237.1 14.6 %copy-start.26 = (bf16[1024,2048]{1,0:T(8,128)(2,1)S(1)}, bf16[1024,2048]{1,0:T(8,128)(2,1)}, u32[]{:S(2)}) copy-start(bf16[1024,2048]{1,0:T(8,128)(2,1)} %copy-done.25) | copy-start | bytes 12582916
  250.1 1.6 copy-start.34
  259.8 192.1 %reduce-scatter.6.cloned.1.call-start = ((), (), s32[]{:S(2)}) async-start(), calls=%async_computation.7 | async-start | bytes 6488064 | tf_op jit(solution)/shard_map/reduce_scatter | solution.py:1352
  298.3 17.0 %copy-start.21 = (bf16[1024,2048]{1,0:T(8,128)(2,1)S(1)}, bf16[1024,2048]{1,0:T(8,128)(2,1)}, u32[]{:S(2)}) copy-start(bf16[1024,2048]{1,0:T(8,128)(2,1)} %copy-done.20) | copy-start | bytes 12582916
  313.7 1.6 copy-start.35
  323.8 253.9 %reduce-scatter.8.cloned.1.call-start = ((), (), s32[]{:S(2)}) async-start(), calls=%async_computation.8 | async-start | bytes 6488064 | tf_op jit(solution)/shard_map/reduce_scatter | solution.py:1365
  412.6 43.0 %collective-permute-start = (bf16[128,2048]{1,0:T(8,128)(2,1)}, bf16[128,2048]{1,0:T(8,128)(2,1)}, u32[]{:S(2)}, u32[]{:S(2)}) collective-permute-start(bf16[128,2048]{1,0:T(8,128)(2,1)} %get-tuple-element.88), channel_id=1, source_target_pairs={{0,2},{1,3},{2,0},{3,1},{4,6},{5,7},{6,4},{7,5},{8,10},{9,11},{10,... | collective-permute-start | bytes 1572872 | tf_op jit(solution)/shard_map/ppermute | solution.py:60
  413.2 42.3 %collective-permute-start.2 = (bf16[128,2048]{1,0:T(8,128)(2,1)}, bf16[128,2048]{1,0:T(8,128)(2,1)}, u32[]{:S(2)}, u32[]{:S(2)}) collective-permute-start(bf16[128,2048]{1,0:T(8,128)(2,1)} %get-tuple-element.89), channel_id=1, source_target_pairs={{0,1},{1,0},{2,3},{3,2},{4,5},{5,4},{6,7},{7,6},{8,9},{9,8},{10,11... | collective-permute-start | bytes 1572872 | tf_op jit(solution)/shard_map/ppermute | solution.py:60
  413.7 6.5 %copy-start.24 = (bf16[512,2048]{1,0:T(8,128)(2,1)S(1)}, bf16[512,2048]{1,0:T(8,128)(2,1)}, u32[]{:S(2)}) copy-start(bf16[512,2048]{1,0:T(8,128)(2,1)} %copy-done.22) | copy-start | bytes 6291460
  413.8 6.5 %copy-start.33 = (bf16[1024,2048]{1,0:T(8,128)(2,1)S(1)}, bf16[1024,2048]{1,0:T(8,128)(2,1)}, u32[]{:S(2)}) copy-start(bf16[1024,2048]{1,0:T(8,128)(2,1)} %get-tuple-element.63) | copy-start | bytes 12582916
  420.2 4.7 copy-start.13
  425.0 1.9 copy-start.15
  426.9 1.6 copy-start.17
  450.1 1.7 copy-start.18
  455.6 7.8 %copy-start.19 = (bf16[1024,1536]{1,0:T(8,128)(2,1)S(1)}, bf16[1024,1536]{1,0:T(8,128)(2,1)}, u32[]{:S(2)}) copy-start(bf16[1024,1536]{1,0:T(8,128)(2,1)} %copy-done.18) | copy-start | bytes 9437188
  455.6 7.8 %copy-start.28 = (bf16[1024,2048]{1,0:T(8,128)(2,1)S(1)}, bf16[1024,2048]{1,0:T(8,128)(2,1)}, u32[]{:S(2)}) copy-start(bf16[1024,2048]{1,0:T(8,128)(2,1)} %copy-done.27) | copy-start | bytes 12582916
  458.8 123.4 %collective-permute-start.3 = (bf16[256,2048]{1,0:T(8,128)(2,1)}, bf16[256,2048]{1,0:T(8,128)(2,1)S(1)}, u32[]{:S(2)}, u32[]{:S(2)}) collective-permute-start(bf16[256,2048]{1,0:T(8,128)(2,1)} %pad_maximum_fusion.1), channel_id=1, source_target_pairs={{0,2},{1,3},{2,0},{3,1},{4,6},{5,7},{6,4},{7,5},{8,10},{9,11},{10,... | collective-permute-start | bytes 3145736 | tf_op jit(solution)/shard_map/ppermute | solution.py:60
  461.3 120.8 %collective-permute-start.1 = (bf16[256,2048]{1,0:T(8,128)(2,1)}, bf16[256,2048]{1,0:T(8,128)(2,1)}, u32[]{:S(2)}, u32[]{:S(2)}) collective-permute-start(bf16[256,2048]{1,0:T(8,128)(2,1)} %pad_maximum_fusion), channel_id=1, source_target_pairs={{0,1},{1,0},{2,3},{3,2},{4,5},{5,4},{6,7},{7,6},{8,9},{9,8},{10,11... | collective-permute-start | bytes 3145736 | tf_op jit(solution)/shard_map/ppermute | solution.py:60
  472.4 109.7 %copy-start.1 = (f32[256,2048]{1,0:T(8,128)S(1)}, f32[256,2048]{1,0:T(8,128)}, u32[]{:S(2)}) copy-start(f32[256,2048]{1,0:T(8,128)} %copy-done) | copy-start | bytes 6291460
  577.7 7.7 %copy-start.29 = (f32[256,2048]{1,0:T(8,128)S(1)}, f32[256,2048]{1,0:T(8,128)}, u32[]{:S(2)}) copy-start(f32[256,2048]{1,0:T(8,128)} %get-tuple-element.75) | copy-start | bytes 6291460
  582.1 4.6 copy-start.30
  585.4 2.5 copy-start.31
Sparse Core Ops, SparseCore 0:
  117.7 58.6 all-gather.3
  178.0 59.0 all-gather.5
  238.7 59.5 all-gather.7
  300.4 63.0 reduce-scatter.3
  365.7 63.2 reduce-scatter.5
  431.1 65.2 reduce-scatter.7

commit v7 on v6

--- a/solution.py
+++ b/solution.py
@@ -81,7 +81,7 @@
     return full
 
 
-def scatter_ctx(partial, n, meanwhile=None):
+def scatter_ctx(partial, n):
     me = lax.axis_index("ctx")
     size = partial.shape[0] // n
 
@@ -97,8 +97,6 @@
     far = block(3).astype(bf16)
     low = hop(far[:half], n, 1).astype(f32)
     high = hop(far[half:], n, 2).astype(f32)
-    if meanwhile is not None:
-        partial, _ = lax.optimization_barrier((partial, meanwhile))
     one = block(1).astype(f32)
     two = block(2).astype(f32)
     to_one = jnp.concatenate([one[:half], one[half:] + high], axis=0).astype(bf16)
@@ -118,7 +116,7 @@
 
 
 MESH = pl.DeviceIdType.MESH
-ANY = pl.BlockSpec(memory_space=pl.ANY)
+HBM = pl.BlockSpec(memory_space=pltpu.HBM)
 
 
 class Place:
@@ -322,8 +320,8 @@
 def opening_kernel(
     dp, ctx,
     gain_one, shift_one, gain_two, shift_two, bias, qkv_hbm, out_weight_ref, rows_ref, cot_ref,
-    small_all, params_ref, weight_ref, out_all, normed_ref, joined_ref, cot_all,
-    small_ref, qkv_ref, blocks, rows_all, local_sem, swap_sem, small_sem, line_joined, line_out, rows_sem, cot_sem,
+    small_all, params_ref, weight_hbm, out_all, normed_hbm, joined_ref, cot_all,
+    small_ref, qkv_ref, blocks, rows_all, weight_ref, normed_ref, normed_sem, weight_sem, local_sem, swap_sem, small_sem, line_joined, line_out, rows_sem, cot_sem,
 ):
     place = Place(dp)
     me, row = place.col, place.row
@@ -443,7 +441,20 @@
             scaled, _ = norm_stats(rows_all[rows, :].astype(f32))
             normed_ref[rows, :] = (scaled * params_ref[0:1, :] + params_ref[1:2, :]).astype(bf16)
 
+        normed_copy(col).start()
+
+    def normed_copy(col):
+        return pltpu.make_async_copy(block(normed_ref, col), block(normed_hbm, col), normed_sem.at[col])
+
+    def weight_copy(i, line):
+        part = (
+            pl.ds(pl.multiple_of(line * (2 * tall), 2 * tall), 2 * tall),
+            pl.ds(i * part_cols, part_cols),
+        )
+        return pltpu.make_async_copy(weight_ref.at[part], weight_hbm.at[part], weight_sem.at[i, line])
+
     def multiply(i, line):
+        weight_copy(i, line).start()
         at = pl.multiple_of(line * (2 * tall), 2 * tall)
         cols = slice(i * part_cols, (i + 1) * part_cols)
 
@@ -488,6 +499,11 @@
     for copy in swaps + small_sends:
         copy.wait_send()
     local[3].wait()
+    for col in range(ctx):
+        normed_copy(col).wait()
+    for line in range(place.lines):
+        for i in range(PARTS):
+            weight_copy(i, line).wait()
 
 
 def opening(dp, ctx, vectors, qkv_weight, out_weight, rows, cot):
@@ -497,8 +513,8 @@
     vmem = pl.BlockSpec(memory_space=pltpu.VMEM)
     return pl.pallas_call(
         functools.partial(opening_kernel, dp, ctx),
-        in_specs=[vmem] * len(vectors) + [ANY] * 4,
-        out_specs=[vmem, vmem, vmem, ANY, vmem, vmem, ANY],
+        in_specs=[vmem] * len(vectors) + [HBM] * 4,
+        out_specs=[vmem, vmem, HBM, HBM, HBM, vmem, HBM],
         out_shape=[
             jax.ShapeDtypeStruct((dp, ctx, 8, PAIR), f32),
             jax.ShapeDtypeStruct((4, width), f32),
@@ -513,6 +529,10 @@
             pltpu.VMEM((depth, 3 * width), bf16),
             pltpu.VMEM((ctx, depth, near), bf16),
             pltpu.VMEM((ctx * length, width), bf16),
+            pltpu.VMEM((dp * ctx * depth, near), bf16),
+            pltpu.VMEM((ctx * length, width), bf16),
+            pltpu.SemaphoreType.DMA((ctx,)),
+            pltpu.SemaphoreType.DMA((PARTS, dp // 2)),
             pltpu.SemaphoreType.DMA((5,)),
             pltpu.SemaphoreType.DMA((4, ctx)),
             pltpu.SemaphoreType.DMA((2, dp)),
@@ -550,10 +570,16 @@
         )
 
     def start(self):
-        place = self.place
-        self.sent[0] = self.block(place.other(3)).astype(bf16)
+        self.start_far()
+        self.start_near()
+
+    def start_far(self):
+        self.sent[0] = self.block(self.place.other(3)).astype(bf16)
         for j in range(CHUNKS):
             self.copy(0, j).start()
+
+    def start_near(self):
+        place = self.place
         for kind in (1, 2):
             self.total[kind - 1] = self.block(place.other(kind))
             for j in range(CHUNKS):
@@ -649,8 +675,8 @@
 
 
 def mix_kernel(
-    dp, ctx, attended_ref, weight_ref, rows_ref, gain_ref, shift_ref, resid_ref, wide_ref,
-    total, sent, got, made, reduce_sem, spread_sem,
+    dp, ctx, attended_ref, weight_ref, rows_ref, gain_ref, shift_ref, resid_hbm, wide_ref,
+    total, sent, got, made, resid_ref, reduce_sem, spread_sem, resid_sem,
 ):
     place = Place(dp)
     greet(place, ctx)
@@ -661,10 +687,16 @@
     spread = CtxSpread(place, made, wide_ref, spread_sem)
     reduce.start()
     reduce.relay()
+
+    def resid_copy(j):
+        rows = reduce.chunk(j)
+        return pltpu.make_async_copy(resid_ref.at[rows, :], resid_hbm.at[rows, :], resid_sem.at[j])
+
     for j in range(CHUNKS):
         rows = reduce.chunk(j)
         resid = rows_ref[rows, :].astype(f32) + reduce.sum(j)
         resid_ref[rows, :] = resid
+        resid_copy(j).start()
         scaled, _ = norm_stats(resid)
         made[rows, :] = (scaled * gain_ref[...] + shift_ref[...]).astype(bf16)
         spread.send(j)
@@ -673,6 +705,8 @@
     spread.relay(CHUNKS - 1)
     spread.finish()
     reduce.finish()
+    for j in range(CHUNKS):
+        resid_copy(j).wait()
 
 
 def mix(dp, ctx, attended, weight, rows, gain, shift):
@@ -681,13 +715,15 @@
     return pl.pallas_call(
         functools.partial(mix_kernel, dp, ctx),
         in_specs=[vmem] * 5,
-        out_specs=[vmem, ANY],
+        out_specs=[HBM, HBM],
         out_shape=[jax.ShapeDtypeStruct((size, width), f32), jax.ShapeDtypeStruct((ctx * size, width), bf16)],
         scratch_shapes=CtxReduce.scratch(size, width)[:3]
         + [
             pltpu.VMEM((size, width), bf16),
+            pltpu.VMEM((size, width), f32),
             CtxReduce.scratch(size, width)[3],
             CtxSpread.scratch(),
+            pltpu.SemaphoreType.DMA((CHUNKS,)),
         ],
         compiler_params=pltpu.CompilerParams(
             collective_id=2, has_side_effects=True, vmem_limit_bytes=40 << 20
@@ -701,9 +737,9 @@
 def mix_back_kernel(
     dp, ctx, gate_ref, up_ref, gate_weight_hbm, up_weight_hbm, inner_hbm, down_hbm, normed_hbm,
     resid_ref, cot_ref, gain_ref,
-    d_resid_ref, sums_ref, wide_ref, branch_hbm, d_up_hbm,
-    total, sent, got, made, gate_weight_ref, up_weight_ref, inner_ref, down_ref, normed_ref, branch, d_up,
-    reduce_sem, spread_sem, load_sem, branch_sem, d_up_sem,
+    d_resid_hbm, sums_ref, wide_ref, branch_hbm, d_up_hbm,
+    total, sent, got, made, d_resid_ref, gate_weight_ref, up_weight_ref, inner_ref, down_ref, normed_ref, branch, d_up,
+    reduce_sem, spread_sem, load_sem, branch_sem, d_up_sem, d_resid_sem,
 ):
     place = Place(dp)
     loads = [
@@ -754,6 +790,10 @@
             branch_copy(i - 2).wait()
         branch[i % 2] = dot(inner_ref[i * size : (i + 1) * size, :], down_ref[...]).astype(bf16)
         branch_copy(i).start()
+
+    def d_resid_copy(j):
+        rows = reduce.chunk(j)
+        return pltpu.make_async_copy(d_resid_ref.at[rows, :], d_resid_hbm.at[rows, :], d_resid_sem.at[j])
 
     pieces = [functools.partial(d_up_piece, i) for i in range(2 * ctx)]
     pieces += [functools.partial(branch_piece, i) for i in range(ctx)]
@@ -775,6 +815,7 @@
         sums_ref[1:2, :] += d_shift[None]
         grad = cot_ref[rows, :].astype(f32) + grad
         d_resid_ref[rows, :] = grad
+        d_resid_copy(j).start()
         made[rows, :] = grad.astype(bf16)
         spread.send(j)
         if j:
@@ -788,6 +829,8 @@
     for i in (1, 2):
         d_up_copy(2 * ctx - i).wait()
         branch_copy(ctx - i).wait()
+    for j in range(CHUNKS):
+        d_resid_copy(j).wait()
 
 
 def mix_back(dp, ctx, d_gate, d_up, gate_weight, up_weight, inner, down, normed, resid, cot, gain):
@@ -796,8 +839,8 @@
     vmem = pl.BlockSpec(memory_space=pltpu.VMEM)
     return pl.pallas_call(
         functools.partial(mix_back_kernel, dp, ctx),
-        in_specs=[vmem] * 2 + [ANY] * 5 + [vmem] * 3,
-        out_specs=[vmem, vmem, ANY, ANY, ANY],
+        in_specs=[vmem] * 2 + [HBM] * 5 + [vmem] * 3,
+        out_specs=[HBM, vmem, HBM, HBM, HBM],
         out_shape=[
             jax.ShapeDtypeStruct((size, width), f32),
             jax.ShapeDtypeStruct((2, width), f32),
@@ -808,6 +851,7 @@
         scratch_shapes=CtxReduce.scratch(size, width)[:3]
         + [
             pltpu.VMEM((size, width), bf16),
+            pltpu.VMEM((size, width), f32),
             pltpu.VMEM((width, hidden), bf16),
             pltpu.VMEM((width, hidden), bf16),
             pltpu.VMEM((ctx * size, hidden), bf16),
@@ -820,6 +864,7 @@
             pltpu.SemaphoreType.DMA((5,)),
             pltpu.SemaphoreType.DMA((2,)),
             pltpu.SemaphoreType.DMA((2,)),
+            pltpu.SemaphoreType.DMA((CHUNKS,)),
         ],
         compiler_params=pltpu.CompilerParams(
             collective_id=3, has_side_effects=True, vmem_limit_bytes=60 << 20
@@ -831,8 +876,13 @@
 
 
 class LineReduce:
-    def __init__(self, place, parts, pair, got, sems):
-        self.place, self.parts, self.pair, self.got, self.sems = place, parts, pair, got, sems
+    def __init__(self, place, parts, own, pair, got, sems):
+        self.place, self.parts, self.own, self.pair, self.got, self.sems = place, parts, own, pair, got, sems
+
+    def load(self, line):
+        return pltpu.make_async_copy(
+            self.parts.at[2 * line + self.place.core], self.own.at[line], self.sems.at[6, line]
+        )
 
     def swap(self, line):
         row = 2 * line + 1 - self.place.core
@@ -846,9 +896,9 @@
 
     def add(self):
         for line in range(self.place.lines):
+            self.load(line).wait()
             self.swap(line).wait_recv()
-            both = self.parts[2 * line + self.place.core].astype(f32) + self.pair[line].astype(f32)
-            self.pair[line] = both.astype(bf16)
+            self.pair[line] = (self.own[line].astype(f32) + self.pair[line].astype(f32)).astype(bf16)
 
     def up(self, far):
         part = self.place.line + far
@@ -920,41 +970,127 @@
     def scratch(dp, tile):
         return [
             pltpu.VMEM((dp // 2,) + tile, bf16),
+            pltpu.VMEM((dp // 2,) + tile, bf16),
             pltpu.VMEM((dp // 2 + 1,) + tile, bf16),
-            pltpu.SemaphoreType.DMA((6, dp // 2)),
+            pltpu.SemaphoreType.DMA((7, dp // 2)),
         ]
+
+
+class CtxReduceReady:
+    def __init__(self, place, full, have, got, sems, load_sems):
+        self.place, self.full, self.have, self.got, self.sems, self.load_sems = place, full, have, got, sems, load_sems
+        self.height = have.shape[1]
+        self.size = self.height // CHUNKS
+
+    def chunk(self, j):
+        return pl.ds(j * self.size, self.size)
+
+    def load(self, kind):
+        col = self.place.other(kind)
+        rows = pl.ds(pl.multiple_of(col * self.height, self.height), self.height)
+        return pltpu.make_async_copy(self.full.at[rows, :], self.have.at[kind], self.load_sems.at[kind])
+
+    def copy(self, kind, j):
+        place = self.place
+        if kind:
+            part, way = self.have.at[kind, self.chunk(j)], kind
+        else:
+            at = (place.other(3) * CHUNKS + j) * self.size
+            part, way = self.full.at[pl.ds(pl.multiple_of(at, self.size), self.size), :], 1 + j % 2
+        return remote(
+            part, self.got.at[kind, self.chunk(j)], self.sems.at[0, kind, j], self.sems.at[1, kind, j],
+            place.across(way),
+        )
+
+    def start(self):
+        for j in range(CHUNKS):
+            self.copy(0, j).start()
+        for kind in (1, 2):
+            self.load(kind).wait()
+            for j in range(CHUNKS):
+                if kind == 1 + j % 2:
+                    self.copy(kind, j).start()
+
+    def relay(self):
+        for j in range(CHUNKS):
+            kind, rows = 2 - j % 2, self.chunk(j)
+            self.copy(0, j).wait_recv()
+            share = self.have[kind, rows].astype(f32) + self.got[0, rows].astype(f32)
+            self.have[kind, rows] = share.astype(bf16)
+            self.copy(kind, j).start()
+
+    def sum(self, j):
+        for kind in (1, 2):
+            self.copy(kind, j).wait_recv()
+        rows = self.chunk(j)
+        return self.have[0, rows].astype(f32) + self.got[1, rows].astype(f32) + self.got[2, rows].astype(f32)
+
+    def finish(self):
+        for kind in range(3):
+            for j in range(CHUNKS):
+                self.copy(kind, j).wait_send()
 
 
 def closing_kernel(
     dp, ctx,
-    d_joined_ref, weight_ref, qkv_parts_ref, out_parts_ref, rows_ref, d_resid_ref, gain_ref, sums_two_ref, bias_ref,
-    grad_ref, qkv_ref, out_ref, small_ref,
-    total, sent, got, reduce_sem, qkv_pair, qkv_got, qkv_sem, out_pair, out_got, out_sem,
-    sums, tiles, tiles_got, small_sem, mine, swap_out, swap_in, swap_sem,
+    d_joined_hbm, weight_hbm, qkv_parts, out_parts, branch_hbm, rows_hbm, d_resid_hbm, resid_hbm,
+    gain_ref, sums_two_ref, bias_ref,
+    grad_ref, qkv_ref, out_ref, output_ref, vectors_ref, d_bias_ref,
+    d_joined_ref, weight_ref, rows_ref, d_resid_ref, resid_ref, load_sem,
+    total, sent, got, reduce_sem, qkv_own, qkv_pair, qkv_got, qkv_sem, out_own, out_pair, out_got, out_sem,
+    have, branch_got, branch_sem, branch_load_sem,
+    sums, tiles, tiles_got, small, small_sem, mine, swap_out, swap_in, swap_sem,
 ):
     place = Place(dp)
     me, row = place.col, place.row
+    lines = [
+        LineReduce(place, qkv_parts, qkv_own, qkv_pair, qkv_got, qkv_sem),
+        LineReduce(place, out_parts, out_own, out_pair, out_got, out_sem),
+    ]
+    loads = [
+        pltpu.make_async_copy(src, dst, load_sem.at[i])
+        for i, (src, dst) in enumerate(
+            (
+                (d_joined_hbm, d_joined_ref), (weight_hbm, weight_ref), (rows_hbm, rows_ref),
+                (d_resid_hbm, d_resid_ref), (resid_hbm, resid_ref),
+            )
+        )
+    ]
+    for load in loads[:2]:
+        load.start()
     greet_all(place, dp, ctx)
-    size, width = rows_ref.shape
-    lines = [
-        LineReduce(place, qkv_parts_ref, qkv_pair, qkv_got, qkv_sem),
-        LineReduce(place, out_parts_ref, out_pair, out_got, out_sem),
-    ]
     for line in lines:
         line.start()
+    for i in range(place.lines):
+        for line in lines:
+            line.load(i).start()
+    branch = CtxReduceReady(place, branch_hbm, have, branch_got, branch_sem, branch_load_sem)
+    for kind in range(3):
+        branch.load(kind).start()
+    for load in loads[2:]:
+        load.start()
+
+    size, width = rows_ref.shape
+    for load in loads[:2]:
+        load.wait()
     reduce = CtxReduce(
         place, lambda col: dot_nt(rows_of(d_joined_ref, col, size), weight_ref[...]), total, sent, got, reduce_sem
     )
-    reduce.start()
+    reduce.start_far()
     for line in lines:
         line.add()
         line.send(place.lines - 1)
+    reduce.start_near()
+    branch.start()
     reduce.relay()
     for far in range(place.lines - 2, 1, -1):
         for line in lines:
             line.send(far)
 
     sums[...] = jnp.zeros_like(sums)
+    for load in loads[2:]:
+        load.wait()
+    branch.load(0).wait()
     for j in range(CHUNKS):
         rows = reduce.chunk(j)
         scaled, inv_std = norm_stats(rows_ref[rows, :].astype(f32))
@@ -962,6 +1098,7 @@
         sums[0:1, :] += d_gain[None]
         sums[1:2, :] += d_shift[None]
         grad_ref[rows, :] = d_resid_ref[rows, :] + grad
+    branch.relay()
     if place.lines > 2:
         for line in lines:
             line.send(1)
@@ -984,13 +1121,34 @@
         sends[k - 1].wait()
         tile = tile + tiles_got[k]
     tiles_got[0] = tile
-    small_ref[me] = tile
+    small[me] = tile
     spreads = [
-        remote(tiles_got.at[0], small_ref.at[me], small_sem.at[2, k], small_sem.at[3, k], place.across(k))
+        remote(tiles_got.at[0], small.at[me], small_sem.at[2, k], small_sem.at[3, k], place.across(k))
         for k in range(1, ctx)
     ]
     for copy in spreads:
         copy.start()
+
+    for j in range(CHUNKS):
+        rows = branch.chunk(j)
+        output_ref[rows, :] = (resid_ref[rows, :] + branch.sum(j)).astype(bf16)
+
+    for k in range(1, ctx):
+        spreads[k - 1].wait_send()
+        part = small.at[place.other(k)]
+        remote(part, part, small_sem.at[2, k], small_sem.at[3, k], place.across(k)).wait_recv()
+    four = sum(small[c, 0:4, :] for c in range(ctx))
+    piece = vectors_ref.shape[1]
+    slots = d_bias_ref.shape[1] // HD
+    vectors = four[:, :piece]
+    biases = [small[i % ctx, 4:5, i // ctx * HD : (i // ctx + 1) * HD] for i in range(slots * ctx)]
+    chosen = biases[:slots]
+    for c in range(1, ctx):
+        vectors = jnp.where(me == c, four[:, c * piece : (c + 1) * piece], vectors)
+        chosen = [jnp.where(me == c, biases[slots * c + i], chosen[i]) for i in range(slots)]
+    vectors_ref[...] = vectors
+    for i in range(slots):
+        d_bias_ref[:, i * HD : (i + 1) * HD] = chosen[i]
 
     lines[0].collect(mine)
     depth = mine.shape[0] // ctx
@@ -1022,16 +1180,13 @@
                 qkv_ref[:, at : at + PAIR] = jnp.where(low, pltpu.roll(a, HD, 1), b)
     for copy in swaps:
         copy.wait_send()
-    for k in range(1, ctx):
-        spreads[k - 1].wait_send()
-        part = small_ref.at[place.other(k)]
-        remote(part, part, small_sem.at[2, k], small_sem.at[3, k], place.across(k)).wait_recv()
     for line in lines:
         line.finish()
+    branch.finish()
     reduce.finish()
 
 
-def closing(dp, ctx, d_joined, weight, d_qkv, d_out, rows, d_resid, gain, sums_two, bias):
+def closing(dp, ctx, d_joined, weight, d_qkv, d_out, branch, rows, d_resid, resid, gain, sums_two, bias):
     size, width = rows.shape
     near = weight.shape[1]
     own, tall = width // dp, d_out.shape[0] // dp
@@ -1040,21 +1195,34 @@
     max_peers = max(dp, ctx)
     return pl.pallas_call(
         functools.partial(closing_kernel, dp, ctx),
-        in_specs=[vmem] * 9,
-        out_specs=[vmem] * 4,
+        in_specs=[HBM] * 8 + [vmem] * 3,
+        out_specs=[vmem] * 6,
         out_shape=[
             jax.ShapeDtypeStruct((size, width), f32),
             jax.ShapeDtypeStruct((own // ctx, 3 * width), f32),
             jax.ShapeDtypeStruct((tall, width), f32),
-            jax.ShapeDtypeStruct((ctx, 8, own), f32),
+            jax.ShapeDtypeStruct((size, width), bf16),
+            jax.ShapeDtypeStruct((4, own // ctx), f32),
+            jax.ShapeDtypeStruct((1, 3 * own // ctx), f32),
         ],
-        scratch_shapes=reduce_scratch
+        scratch_shapes=[
+            pltpu.VMEM((ctx * size, near), bf16),
+            pltpu.VMEM((width, near), bf16),
+            pltpu.VMEM((size, width), bf16),
+            pltpu.VMEM((size, width), f32),
+            pltpu.VMEM((size, width), f32),
+            pltpu.SemaphoreType.DMA((5,)),
+        ]
+        + reduce_scratch
         + LineReduce.scratch(dp, (own, near))
         + LineReduce.scratch(dp, (tall, width))
+        + reduce_scratch[1:]
         + [
+            pltpu.SemaphoreType.DMA((3,)),
             pltpu.VMEM((2, width), f32),
             pltpu.VMEM((dp, 8, own), f32),
             pltpu.VMEM((dp, 8, own), f32),
+            pltpu.VMEM((ctx, 8, own), f32),
             pltpu.SemaphoreType.DMA((4, max_peers)),
             pltpu.VMEM((own, near), f32),
             pltpu.VMEM((own, near), bf16),
@@ -1062,14 +1230,14 @@
             pltpu.SemaphoreType.DMA((2, ctx)),
         ],
         compiler_params=pltpu.CompilerParams(
-            collective_id=1, has_side_effects=True, vmem_limit_bytes=60 << 20
+            collective_id=1, has_side_effects=True, vmem_limit_bytes=62 << 20
         ),
         cost_estimate=pl.CostEstimate(
             flops=2 * d_joined.size * width, transcendentals=0, bytes_accessed=200 << 20
         ),
     )(
-        d_joined, weight, d_qkv.reshape(dp, own, near), d_out.reshape(dp, tall, width),
-        rows, d_resid, gain.reshape(1, width), sums_two, bias,
+        d_joined, weight, d_qkv.reshape(dp, own, near), d_out.reshape(dp, tall, width), branch,
+        rows, d_resid, resid, gain.reshape(1, width), sums_two, bias,
     )
 
 
@@ -1293,9 +1461,7 @@
             dp, ctx, vectors, qkv_weight, out_weight, rows, grad_rows
         )
         gain_one, shift_one, gain_two, shift_two = params
-        gate_weight, up_weight, down_weight, _ = lax.optimization_barrier(
-            (gate_weight, up_weight, down_weight, normed_one)
-        )
+        up_weight, down_weight, _ = lax.optimization_barrier((up_weight, down_weight, normed_one))
         small = small.reshape(dp * ctx, 1024)[:, :count]
     else:
         small = jnp.concatenate(vectors, axis=1).astype(f32)
@@ -1368,20 +1534,19 @@
     d_out_weight = dot_tn(attended, d_proj).astype(bf16)
     d_attended, d_down = lax.optimization_barrier((d_attended, d_down))
     d_joined, d_bias = attend_back(qkv, d_attended, lse, table, start)
-    output = (resid + scatter_ctx(branch, ctx, d_joined)).astype(bf16)
     d_joined_weight = dot_tn(normed_one, d_joined).astype(bf16)
     d_bias = d_bias.reshape(pairs, 3, 2, HD).transpose(1, 0, 2, 3)
     d_joined, d_gate_weight = lax.optimization_barrier((d_joined, d_gate_weight))
     if fused:
         d_bias = jnp.pad(d_bias.reshape(dp, -1), ((0, 0), (0, width // dp - near * 3 * HD // dp)))
-        grad_input, d_joined_weight, d_out_weight, small = closing(
-            dp, ctx, d_joined, joined_weight, d_joined_weight, d_out_weight, rows, d_resid, gain_one, sums_two, d_bias
-        )
-        vectors = lax.dynamic_slice_in_dim(jnp.sum(small[:, :4], axis=0), me * part, part, 1)
+        grad_input, d_joined_weight, d_out_weight, output, vectors, d_bias = closing(
+            dp, ctx, d_joined, joined_weight, d_joined_weight, d_out_weight, branch, rows, d_resid, resid,
+            gain_one, sums_two, d_bias,
+        )
         d_gain_one, d_shift_one, d_gain_two, d_shift_two = vectors
-        d_bias = small[:, 4, : near * 3 * HD // dp].reshape(ctx, -1, HD).transpose(1, 0, 2)
-        d_bias = lax.dynamic_index_in_dim(d_bias.reshape(ctx, -1), me, 0, keepdims=False)
+        d_bias = d_bias[0]
     else:
+        output = (resid + scatter_ctx(branch, ctx)).astype(bf16)
         at_me = lax.broadcasted_iota(jnp.int32, (1, ctx, 1, 1), 1) == me
         d_out_weight = jnp.where(at_me, d_out_weight.reshape(near, 1, HD, width), jnp.zeros((), bf16))
         d_out_weight = lax.psum_scatter(

time: 602 us -> 592 us (0.983)
  waiting for transfers between devices: 45.2 us -> 1.45 us
  Pallas kernels: 400 us -> 443 us
  other arithmetic: 15.9 us -> 8.17 us
    all_gather x1, waiting for transfers between devices: 38.4 us -> 0.02 us  [shards(): down_full = lax.all_gather(down_weight, 'dp', axis=1, tiled=True)]
    pallas_call x1, Pallas kernels: 97.3 us -> 134 us  [opening(): pl.pallas_call(functools.partial(opening_kernel, dp, ctx), in_specs=[vmem...]
    pallas_call x1, Pallas kernels: 104 us -> 112 us  [closing(): pl.pallas_call(functools.partial(closing_kernel, dp, ctx), in_specs=[HBM]...]
    unnamed x77 -> x81, local copies, waits for them, and re-layouts: 31.9 us -> 35.5 us
  transfers between devices with their start and end apart: 10 -> 6, of which waited for: 2 -> 0; matrix products, arithmetic and copies ran while one was open for 16% -> 15% of each run, Pallas kernels for 51% -> 76%
where the time goes in v7:
time: 592 us; the launch traced here: 586 us
  Pallas kernels  443 us (75%)
  matrix products  78 us (13%)
  local copies, waits for them, and re-layouts  39.3 us (7%)
  between operations  14.6 us (2%)
  other arithmetic  8.17 us (1%)
    pallas_call x1, Pallas kernels, opening(): pl.pallas_call(functools.partial(opening_kernel, dp, ctx), in_specs=[vmem...  134 us
    pallas_call x1, Pallas kernels, closing(): pl.pallas_call(functools.partial(closing_kernel, dp, ctx), in_specs=[HBM]...  112 us
    pallas_call x1, Pallas kernels, mix_back(): pl.pallas_call(functools.partial(mix_back_kernel, dp, ctx), in_specs=[vme...  84.1 us
    pallas_call x1, Pallas kernels, mix(): pl.pallas_call(functools.partial(mix_kernel, dp, ctx), in_specs=[vmem] *...  73 us
    unnamed x81, local copies, waits for them, and re-layouts  35.5 us
    dot_general x4, matrix products, dot_tn(): lax.dot_general(a, b, (((0,), (0,)), ((), ())), preferred_element_type=f32)  33.9 us
    dot_general x2, matrix products, dot(): return jnp.dot(a, b, preferred_element_type=f32)  24.8 us
    pallas_call x1, Pallas kernels, attend_back(): pl.pallas_call(functools.partial(attend_back_kernel, step), grid=(pairs,)...  21.9 us
  transfers between devices with their start and end apart: 6, of which 0 were waited for; matrix products, arithmetic and copies ran while one was open for 15% of the time, Pallas kernels for 76%

profile of v7, /device:TPU:0, one launch (start us, length us, event | category | flops | bytes accessed | tf_op | source)
XLA Modules:
  0.0 586.0 jit_solution(14569236666079390342)
XLA Ops:
  7.2 0.0 all-gather.4.cloned.1.call-start
  7.2 0.7 all-gather.4.cloned.1.call-update
  7.9 0.0 all-gather.6.cloned.1.call-start
  8.0 0.7 broadcast_in_dim.31.bias
  8.6 1.2 copy-done.2
  9.8 1.2 copy-done.7
  11.1 1.1 copy-done.8
  12.2 0.9 copy-done.9
  13.2 0.7 copy-done.10
  13.8 0.7 copy-done.11
  14.5 0.7 copy-done.12
  15.1 0.7 copy-done.13
  15.8 133.7 %shard_map.229 = (f32[8,4,8,128]{3,2,1,0:T(8,128)S(1)}, f32[4,2048]{1,0:T(4,128)S(1)}, bf16[2048,1536]{1,0:T(8,128)(2,1)}, bf16[512,2048]{1,0:T(8,128)(2,1)S(1)}...) custom-call(bf16[1,64]{1,0:T(2,128)(2,1)S(1)} %bitcast.55, ...), custom_call_target="tpu_custom_call" | custom-call | flops 6442450944 | bytes 209715200 | tf_op jit(solution)/shard_map/pallas_call | solution.py:514
  149.5 1.3 copy-done.22
  150.8 1.9 copy-done.25
  152.7 2.1 copy-done.28
  154.8 0.0 all-gather.8.cloned.1.call-start
  154.8 0.7 all-gather.8.cloned.1.call-update
  155.5 0.5 reduce-scatter.4.cloned.1.call-start
  156.1 0.1 reshape.48
  156.2 0.1 reshape.49.bias_ref
  156.3 0.6 convert_reduce_fusion
  156.9 0.2 broadcast_in_dim.32.start_ref
  157.1 18.3 %shard_map.230 = (bf16[1024,512]{1,0:T(8,128)(2,1)S(1)}, bf16[1024,1536]{1,0:T(8,128)(2,1)S(1)}, f32[1024,512]{1,0:T(8,128)S(1)}) custom-call(f32[1024,1536]{1,0:T(8,128)} %get-tuple-element.47.joined_ref, f32[1,1536]{1,0:T(1,128)S(1)} %reshape.49.bias_ref, f32[3,1024,128]{2,1,0:T(8,128)S(1)} %copy-done.14, s32[1024,128]{1,0:T(8,128)S(1)} %broadcast_in_dim.32.start_ref), custom_call_target="tpu_custom_call" | custom-call | flops 2415919104 | bytes 12582912 | tf_op jit(solution)/shard_map/pallas_call | solution.py:1370
  175.5 1.7 copy-done.16
  177.2 1.3 copy-done.18
  178.5 0.6 fusion.1
  179.1 73.0 %shard_map.231 = (f32[256,2048]{1,0:T(8,128)S(1)}, bf16[1024,2048]{1,0:T(8,128)(2,1)S(1)}) custom-call(bf16[1024,512]{1,0:T(8,128)(2,1)S(1)} %get-tuple-element.51.attended_ref, bf16[512,2048]{1,0:T(8,128)(2,1)S(1)} %copy-done.23, bf16[256,2048]{1,0:T(8,128)(2,1)S(1)} %bitcast.51, f32[1,2048]{1,0:T(1,128)S(1)} %get-tuple-element.86.gain_ref, ...), custom_call_target="tpu_custom_call" | custom-call | flops 2147483648 | bytes 188743680 | tf_op jit(solution)/shard_map/pallas_call | solution.py:715
  252.2 1.4 copy-done.1
  253.6 2.1 copy-done.20
  255.7 11.8 %fusion.2 = f32[1024,1408]{1,0:T(8,128)} fusion(bf16[1024,2048]{1,0:T(8,128)(2,1)} %copy-done.20, bf16[2048,1408]{1,0:T(8,128)(2,1)} %all-gather.4.cloned.1.call-done.gate_weight_hbm), kind=kOutput, calls=%fused_computation.20 | convolution fusion | flops 5905580032 | bytes 15728640 | tf_op jit(solution)/shard_map/dot_general | solution.py:24
  267.5 13.1 %multiply_convert_fusion.2 = (bf16[1024,1408]{1,0:T(8,128)(2,1)S(1)}, f32[1024,1408]{1,0:T(8,128)}) fusion(f32[1024,1408]{1,0:T(8,128)} %fusion.2, bf16[1024,2048]{1,0:T(8,128)(2,1)} %copy-done.20, bf16[2048,1408]{1,0:T(8,128)(2,1)} %all-gather.6.cloned.1.call-done.up_weight_hbm), kind=kOutput, calls=%fused_computation.5 | convolution fusion | flops 5914230784 | bytes 24379392 | tf_op jit(solution)/shard_map/dot_general | solution.py:24
  280.5 1.6 copy-done.35
  282.1 8.1 %convolution_convert_fusion.2 = bf16[1408,2048]{1,0:T(8,128)(2,1)} fusion(bf16[1024,1408]{1,0:T(8,128)(2,1)S(1)} %get-tuple-element.91.inner_hbm, bf16[1024,2048]{1,0:T(8,128)(2,1)S(1)} %copy-done.26), kind=kOutput, calls=%fused_computation.2 | convolution fusion | flops 5908463616 | bytes 12845056 | tf_op jit(solution)/shard_map/dot_general | solution.py:32
  290.2 0.0 reduce-scatter.6.cloned.1.call-start
  290.3 0.0 all-gather.8.cloned.1.call-done.down_hbm
  290.3 15.9 %multiply_convert_fusion = (bf16[1024,1408]{1,0:T(8,128)(2,1)}, bf16[1024,1408]{1,0:T(8,128)(2,1)S(1)}) fusion(f32[1024,1408]{1,0:T(8,128)} %fusion.2, f32[1024,1408]{1,0:T(8,128)} %get-tuple-element.92, bf16[1024,2048]{1,0:T(8,128)(2,1)} %copy-done.25, bf16[1408,2048]{1,0:T(8,128)(2,1)} %all-gather.8.cloned.1.call-done.down_hbm), kind=kOutput, calls=%fused_computation.3 | convolution fusion | flops 5924323328 | bytes 27262976 | tf_op jit(solution)/shard_map/dot_general | solution.py:28
  306.2 1.6 copy-done.36
  307.8 8.5 %convolution_convert_fusion.1 = bf16[2048,1408]{1,0:T(8,128)(2,1)} fusion(bf16[1024,2048]{1,0:T(8,128)(2,1)S(1)} %copy-done.21, bf16[1024,1408]{1,0:T(8,128)(2,1)S(1)} %get-tuple-element.59.gate_ref), kind=kOutput, calls=%fused_computation.1 | convolution fusion | flops 5908463616 | bytes 12845056 | tf_op jit(solution)/shard_map/dot_general | solution.py:32
  316.4 0.4 reduce-scatter.8.cloned.1.call-start
  316.8 84.1 %shard_map.232 = (f32[256,2048]{1,0:T(8,128)}, f32[2,2048]{1,0:T(2,128)}, bf16[1024,2048]{1,0:T(8,128)(2,1)}, bf16[1024,2048]{1,0:T(8,128)(2,1)}, bf16[2048,1408]{1,0:T(8,128)(2,1)}) custom-call(bf16[1024,1408]{1,0:T(8,128)(2,1)} %copy-done.36, bf16[1024,1408]{1,0:T(8,128)(2,1)} %get-tuple-element.82.up_ref, ...), custom_call_target="tpu_custom_call" | custom-call | flops 23622320128 | bytes 188743680 | tf_op jit(solution)/shard_map/pallas_call | solution.py:840
  400.9 0.0 reduce-scatter.8.cloned.1.call-update
  401.0 6.1 %convolution_convert_fusion.3 = bf16[512,2048]{1,0:T(8,128)(2,1)} fusion(bf16[1024,512]{1,0:T(8,128)(2,1)S(1)} %get-tuple-element.51.attended_ref, bf16[1024,2048]{1,0:T(8,128)(2,1)} %get-tuple-element.61), kind=kOutput, calls=%fused_computation.9 | convolution fusion | flops 2148532224 | bytes 7340032 | tf_op jit(solution)/shard_map/dot_general | solution.py:32
  407.1 3.3 convolution_convert_fusion.4.grad_ref
  410.4 2.3 convert_element_type.45
  412.7 1.1 copy-done.5
  413.8 1.4 copy-done.15
  415.2 1.9 copy-done.17
  417.1 1.6 copy-done.19
  418.7 1.2 copy-done.27
  419.9 21.9 %shard_map.233 = (bf16[1024,1536]{1,0:T(8,128)(2,1)S(1)}, f32[1,1536]{1,0:T(1,128)S(1)}) custom-call(bf16[1024,1536]{1,0:T(8,128)(2,1)S(1)} %copy-done.17, bf16[1024,512]{1,0:T(8,128)(2,1)S(1)} %copy-done.27, f32[1024,512]{1,0:T(8,128)S(1)} %copy-done.19, f32[3,1024,128]{2,1,0:T(8,128)S(1)} %copy-done.15, s32[1024,128]{1,0:T(8,128)S(1)} %copy-done.5), custom_call_target="tpu_custom_call" | custom-call | flops 6039797760 | bytes 12582912 | tf_op jit(solution)/shard_map/pallas_call | solution.py:1399
  441.9 0.1 reshape.52
  442.0 0.1 reshape.53
  442.1 2.8 convert_element_type.46
  444.9 0.6 pad.4.bias_ref
  445.5 11.2 %convolution_convert_fusion = bf16[2048,1536]{1,0:T(8,128)(2,1)} fusion(bf16[1024,2048]{1,0:T(8,128)(2,1)} %copy-done.28, bf16[1024,1536]{1,0:T(8,128)(2,1)S(1)} %get-tuple-element.67.d_joined_hbm), kind=kOutput, calls=%fused_computation | convolution fusion | flops 6445596672 | bytes 13631488 | tf_op jit(solution)/shard_map/dot_general | solution.py:32
  456.7 112.3 %shard_map.234 = (f32[256,2048]{1,0:T(8,128)}, f32[64,6144]{1,0:T(8,128)}, f32[64,2048]{1,0:T(8,128)}, bf16[256,2048]{1,0:T(8,128)(2,1)}, f32[4,64]{1,0:T(4,128)}, /*index=5*/f32[1,192]{1,0:T(1,128)}) custom-call(bf16[1024,1536]{1,0:T(8,128)(2,1)} %copy-done, bf16[2048,1536]{1,0:T(8,128)(2,1)} %get-tuple-element.68.weight_hbm, ...), custom_call_target="tpu_custom_call" | custom-call | flops 6442450944 | bytes 209715200 | tf_op jit(solution)/shard_map/pallas_call | solution.py:1196
  569.1 1.4 slice_bitcast_fusion
  570.4 2.4 convert_element_type.49
  572.9 2.3 copy.43
  575.2 1.3 copy.44
  576.5 1.1 copy.45
  577.6 0.6 copy.46
  578.2 0.8 copy.47
  (66 shorter events, 0.2 us)
Async XLA Ops:
  7.2 248.5 %all-gather.4.cloned.1.call-start = ((), (), s32[]{:S(2)}) async-start(), calls=%async_computation.3 | async-start | bytes 6488064 | tf_op jit(solution)/shard_map/all_gather | solution.py:1487
  7.9 259.5 %all-gather.6.cloned.1.call-start = ((), (), s32[]{:S(2)}) async-start(), calls=%async_computation.4 | async-start | bytes 6488064 | tf_op jit(solution)/shard_map/all_gather | solution.py:1488
  8.6 1.2 copy-start.2
  9.8 1.2 copy-start.7
  11.1 1.1 copy-start.8
  12.2 0.9 copy-start.9
  13.2 0.7 copy-start.10
  13.8 0.7 copy-start.11
  14.5 0.7 copy-start.12
  15.1 0.7 copy-start.13
  15.8 140.5 %copy-start.32 = (s32[1,1024]{1,0:T(1,128)S(1)}, s32[1,1024]{1,0:T(1,128)}, u32[]{:S(2)}) copy-start(s32[1,1024]{1,0:T(1,128)} %param.15) | copy-start | bytes 12292
  15.8 141.3 %copy-start.14 = (f32[3,1024,128]{2,1,0:T(8,128)S(1)}, f32[3,1024,128]{2,1,0:T(8,128)}, u32[]{:S(2)}) copy-start(f32[3,1024,128]{2,1,0:T(8,128)} %constant.17.clone.table_ref) | copy-start | bytes 4718596
  149.5 1.3 copy-start.22
  150.8 1.9 copy-start.25
  152.7 2.1 copy-start.28
  154.8 135.5 %all-gather.8.cloned.1.call-start = ((), (), s32[]{:S(2)}) async-start(), calls=%async_computation.5 | async-start | bytes 6488064 | tf_op jit(solution)/shard_map/all_gather | solution.py:1489
  155.5 254.9 %reduce-scatter.4.cloned.1.call-start = ((), (), s32[]{:S(2)}) async-start(), calls=%async_computation.6 | async-start | bytes 6488064 | tf_op jit(solution)/shard_map/reduce_scatter | solution.py:1512
  157.1 18.4 %copy-start.4 = (s32[1024,128]{1,0:T(8,128)}, s32[1024,128]{1,0:T(8,128)S(1)}, u32[]{:S(2)}) copy-start(s32[1024,128]{1,0:T(8,128)S(1)} %broadcast_in_dim.32.start_ref) | copy-start | bytes 1572868
  157.1 22.0 %copy-start.3 = (bf16[1,256,2048]{2,1,0:T(8,128)(2,1)S(1)}, bf16[1,256,2048]{2,1,0:T(8,128)(2,1)}, u32[]{:S(2)}) copy-start(bf16[1,256,2048]{2,1,0:T(8,128)(2,1)} %param.14) | copy-start | bytes 3145732
  157.1 22.0 %copy-start.23 = (bf16[512,2048]{1,0:T(8,128)(2,1)S(1)}, bf16[512,2048]{1,0:T(8,128)(2,1)}, u32[]{:S(2)}) copy-start(bf16[512,2048]{1,0:T(8,128)(2,1)} %copy-done.22) | copy-start | bytes 6291460
  175.5 1.7 copy-start.16
  177.2 1.4 copy-start.18
  179.1 88.3 %copy-start.6 = (f32[1,2048]{1,0:T(1,128)}, f32[1,2048]{1,0:T(1,128)S(1)}, u32[]{:S(2)}) copy-start(f32[1,2048]{1,0:T(1,128)S(1)} %get-tuple-element.86.gain_ref) | copy-start | bytes 24580
  252.2 1.4 copy-start.1
  253.6 2.1 copy-start.20
  267.4 14.6 %copy-start.26 = (bf16[1024,2048]{1,0:T(8,128)(2,1)S(1)}, bf16[1024,2048]{1,0:T(8,128)(2,1)}, u32[]{:S(2)}) copy-start(bf16[1024,2048]{1,0:T(8,128)(2,1)} %copy-done.25) | copy-start | bytes 12582916
  280.5 1.6 copy-start.35
  290.2 151.9 %reduce-scatter.6.cloned.1.call-start = ((), (), s32[]{:S(2)}) async-start(), calls=%async_computation.7 | async-start | bytes 6488064 | tf_op jit(solution)/shard_map/reduce_scatter | solution.py:1518
  290.3 17.5 %copy-start.21 = (bf16[1024,2048]{1,0:T(8,128)(2,1)S(1)}, bf16[1024,2048]{1,0:T(8,128)(2,1)}, u32[]{:S(2)}) copy-start(bf16[1024,2048]{1,0:T(8,128)(2,1)} %copy-done.20) | copy-start | bytes 12582916
  306.2 1.6 copy-start.36
  316.4 254.1 %reduce-scatter.8.cloned.1.call-start = ((), (), s32[]{:S(2)}) async-start(), calls=%async_computation.8 | async-start | bytes 6488064 | tf_op jit(solution)/shard_map/reduce_scatter | solution.py:1531
  401.0 6.1 %copy-start.24 = (bf16[512,2048]{1,0:T(8,128)(2,1)S(1)}, bf16[512,2048]{1,0:T(8,128)(2,1)}, u32[]{:S(2)}) copy-start(bf16[512,2048]{1,0:T(8,128)(2,1)} %copy-done.22) | copy-start | bytes 6291460
  401.0 6.1 %copy-start.34 = (bf16[1024,2048]{1,0:T(8,128)(2,1)S(1)}, bf16[1024,2048]{1,0:T(8,128)(2,1)}, u32[]{:S(2)}) copy-start(bf16[1024,2048]{1,0:T(8,128)(2,1)} %get-tuple-element.61) | copy-start | bytes 12582916
  412.7 1.1 copy-start.5
  413.8 1.4 copy-start.15
  415.2 1.9 copy-start.17
  417.1 1.6 copy-start.19
  418.7 1.2 copy-start.27
  441.9 14.9 %copy-start = (bf16[1024,1536]{1,0:T(8,128)(2,1)}, bf16[1024,1536]{1,0:T(8,128)(2,1)S(1)}, u32[]{:S(2)}) copy-start(bf16[1024,1536]{1,0:T(8,128)(2,1)S(1)} %get-tuple-element.67.d_joined_hbm) | copy-start | bytes 9437188
  569.1 6.1 %copy-start.29 = (f32[256,2048]{1,0:T(8,128)S(1)}, f32[256,2048]{1,0:T(8,128)}, u32[]{:S(2)}) copy-start(f32[256,2048]{1,0:T(8,128)} %get-tuple-element.74) | copy-start | bytes 6291460
  570.4 6.1 %copy-start.30 = (f32[64,6144]{1,0:T(8,128)S(1)}, f32[64,6144]{1,0:T(8,128)}, u32[]{:S(2)}) copy-start(f32[64,6144]{1,0:T(8,128)} %get-tuple-element.109) | copy-start | bytes 4718596
  575.2 2.5 copy-start.33
  575.2 3.0 copy-start.31
Sparse Core Ops, SparseCore 0:
  9.7 87.2 all-gather.3
  154.9 59.5 all-gather.5
  216.1 59.5 all-gather.7
  290.3 63.3 reduce-scatter.3
  355.8 63.2 reduce-scatter.5
  421.3 77.8 reduce-scatter.7

commit v8 on v7

--- a/solution.py
+++ b/solution.py
@@ -314,243 +314,8 @@
         pl.semaphore_wait(barrier, ctx + dp - 2)
 
 
+CHUNKS = 4
 PARTS = 2
-
-
-def opening_kernel(
-    dp, ctx,
-    gain_one, shift_one, gain_two, shift_two, bias, qkv_hbm, out_weight_ref, rows_ref, cot_ref,
-    small_all, params_ref, weight_hbm, out_all, normed_hbm, joined_ref, cot_all,
-    small_ref, qkv_ref, blocks, rows_all, weight_ref, normed_ref, normed_sem, weight_sem, local_sem, swap_sem, small_sem, line_joined, line_out, rows_sem, cot_sem,
-):
-    place = Place(dp)
-    me, row = place.col, place.row
-    depth = qkv_ref.shape[0]
-    length, width = rows_ref.shape
-    rows_out = out_weight_ref.shape[0]
-    tall = ctx * depth
-
-    qkv_copy = pltpu.make_async_copy(qkv_hbm, qkv_ref, local_sem.at[4])
-    qkv_copy.start()
-    greet_all(place, dp, ctx, wait=False)
-    small_ref[...] = jnp.zeros_like(small_ref)
-    for i, vector in enumerate((gain_one, shift_one, gain_two, shift_two)):
-        small_ref[i // 2 : i // 2 + 1, i % 2 * HD : (i % 2 + 1) * HD] = vector[...].astype(f32)
-    for i in range(bias.shape[1] // HD):
-        small_ref[2 + i // 2 : 3 + i // 2, i % 2 * HD : (i % 2 + 1) * HD] = bias[
-            :, i * HD : (i + 1) * HD
-        ].astype(f32)
-    small_all[row, me] = small_ref[...]
-    qkv_copy.wait()
-
-    low = head_lanes((depth, PAIR))
-    for p in range(width // HD // ctx // 2):
-        for t in range(3):
-            lanes = slice((3 * p + t) * PAIR, (3 * p + t + 1) * PAIR)
-            for c in range(0, ctx, 2):
-                at = t * width + (2 * p * ctx + c) * HD
-                a = qkv_ref[:, at : at + PAIR].astype(f32)
-                at = at + ctx * HD
-                b = qkv_ref[:, at : at + PAIR].astype(f32)
-                blocks[c, :, lanes] = jnp.where(low, a, pltpu.roll(b, HD, 1)).astype(bf16)
-                blocks[c + 1, :, lanes] = jnp.where(low, pltpu.roll(a, HD, 1), b).astype(bf16)
-    greet_all(place, dp, ctx, signal=False)
-
-    def weight_rows(row, col):
-        return weight_ref.at[pl.ds(pl.multiple_of((row * ctx + col) * depth, depth), depth), :]
-
-    def out_shard(row):
-        return out_all.at[pl.ds(pl.multiple_of(row * rows_out, rows_out), rows_out), :]
-
-    def block(ref, col):
-        return ref.at[pl.ds(pl.multiple_of(col * length, length), length), :]
-
-    part_cols = weight_ref.shape[1] // PARTS
-
-    def weight_part(i, row):
-        return weight_ref.at[
-            pl.ds(pl.multiple_of(row * tall, tall), tall), pl.ds(i * part_cols, part_cols)
-        ]
-
-    local = [
-        pltpu.make_async_copy(blocks.at[me], weight_rows(row, me), local_sem.at[0]),
-        pltpu.make_async_copy(out_weight_ref, out_shard(row), local_sem.at[1]),
-        pltpu.make_async_copy(rows_ref, block(rows_all, me), local_sem.at[2]),
-        pltpu.make_async_copy(cot_ref, block(cot_all, me), local_sem.at[3]),
-    ]
-    swaps = [
-        remote(small_ref, small_all.at[row, me], swap_sem.at[0, k], swap_sem.at[1, k], place.across(k))
-        for k in range(1, ctx)
-    ] + [
-        remote(
-            blocks.at[place.other(k)], weight_rows(row, me), swap_sem.at[2, k], swap_sem.at[3, k], place.across(k)
-        )
-        for k in range(1, ctx)
-    ]
-    for copy in swaps:
-        copy.start()
-    for copy in local:
-        copy.start()
-    rows_gather = CtxGather(place, rows_ref, rows_all, length, rows_sem)
-    cot_gather = CtxGather(place, cot_ref, cot_all, length, cot_sem)
-    out_line = LineGather(place, out_shard, line_out)
-    lines = [
-        LineGather(place, functools.partial(weight_part, i), line_joined.at[i]) for i in range(PARTS)
-    ] + [out_line]
-    local[1].wait()
-    out_line.send(1)
-    rows_gather.first()
-    for k in range(1, ctx):
-        remote(
-            small_ref, small_all.at[row, place.other(k)], swap_sem.at[0, k], swap_sem.at[1, k], place.across(k)
-        ).wait_recv()
-    small_sends = [
-        remote(
-            small_all.at[row], small_all.at[row], small_sem.at[0, k], small_sem.at[1, k], ((row + k) % dp, me)
-        )
-        for k in range(1, dp)
-    ]
-    for copy in small_sends:
-        copy.start()
-    local[0].wait()
-    for k in range(1, ctx):
-        part = weight_rows(row, place.other(k))
-        remote(part, part, swap_sem.at[2, k], swap_sem.at[3, k], place.across(k)).wait_recv()
-    for line in lines[:PARTS]:
-        line.send(1)
-
-    for k in range(1, dp):
-        part = small_all.at[(row + dp - k) % dp]
-        remote(part, part, small_sem.at[0, k], small_sem.at[1, k], place.twin).wait_recv()
-    low = head_lanes((1, PAIR))
-    for i in range(dp * ctx // 2):
-        lanes = slice(i * PAIR, (i + 1) * PAIR)
-        a = small_all[2 * i // ctx, 2 * i % ctx]
-        b = small_all[(2 * i + 1) // ctx, (2 * i + 1) % ctx]
-        for r in range(2):
-            ar, br = a[r : r + 1, :], b[r : r + 1, :]
-            params_ref[2 * r : 2 * r + 1, lanes] = jnp.where(low, ar, pltpu.roll(br, HD, 1))
-            params_ref[2 * r + 1 : 2 * r + 2, lanes] = jnp.where(low, pltpu.roll(ar, HD, 1), br)
-
-    def normalize(col):
-        step = 64
-
-        @pl.loop(0, length // step)
-        def _(i):
-            rows = pl.ds(pl.multiple_of(col * length + i * step, step), step)
-            scaled, _ = norm_stats(rows_all[rows, :].astype(f32))
-            normed_ref[rows, :] = (scaled * params_ref[0:1, :] + params_ref[1:2, :]).astype(bf16)
-
-        normed_copy(col).start()
-
-    def normed_copy(col):
-        return pltpu.make_async_copy(block(normed_ref, col), block(normed_hbm, col), normed_sem.at[col])
-
-    def weight_copy(i, line):
-        part = (
-            pl.ds(pl.multiple_of(line * (2 * tall), 2 * tall), 2 * tall),
-            pl.ds(i * part_cols, part_cols),
-        )
-        return pltpu.make_async_copy(weight_ref.at[part], weight_hbm.at[part], weight_sem.at[i, line])
-
-    def multiply(i, line):
-        weight_copy(i, line).start()
-        at = pl.multiple_of(line * (2 * tall), 2 * tall)
-        cols = slice(i * part_cols, (i + 1) * part_cols)
-
-        @pl.loop(0, ctx)
-        def _(b):
-            rows = pl.ds(pl.multiple_of(b * length, length), length)
-            joined_ref[rows, cols] += dot(
-                normed_ref[rows, pl.ds(at, 2 * tall)], weight_ref[pl.ds(at, 2 * tall), cols]
-            )
-
-    def forward(hop):
-        for line in lines:
-            line.receive(hop)
-            if hop < place.lines - 1:
-                line.send(hop + 1)
-
-    def absorb(hop):
-        for i in range(PARTS):
-            lines[i].settle(hop, functools.partial(multiply, i))
-
-    joined_ref[...] = jnp.zeros_like(joined_ref)
-    local[2].wait()
-    normalize(me)
-    rows_gather.second()
-    cot_gather.first()
-    for hop in range(1, place.lines):
-        forward(hop)
-        if hop == 1:
-            for col in (place.other(1), place.other(2)):
-                normalize(col)
-            rows_gather.finish()
-            normalize(place.other(3))
-        if hop == min(2, place.lines - 1):
-            cot_gather.second()
-        absorb(hop - 1)
-    absorb(place.lines - 1)
-    for hop in range(place.lines):
-        out_line.settle(hop)
-    for line in lines:
-        line.finish()
-    cot_gather.finish()
-    for copy in swaps + small_sends:
-        copy.wait_send()
-    local[3].wait()
-    for col in range(ctx):
-        normed_copy(col).wait()
-    for line in range(place.lines):
-        for i in range(PARTS):
-            weight_copy(i, line).wait()
-
-
-def opening(dp, ctx, vectors, qkv_weight, out_weight, rows, cot):
-    depth, width = qkv_weight.shape[0], rows.shape[1]
-    length = rows.shape[0]
-    near = 3 * width // ctx
-    vmem = pl.BlockSpec(memory_space=pltpu.VMEM)
-    return pl.pallas_call(
-        functools.partial(opening_kernel, dp, ctx),
-        in_specs=[vmem] * len(vectors) + [HBM] * 4,
-        out_specs=[vmem, vmem, HBM, HBM, HBM, vmem, HBM],
-        out_shape=[
-            jax.ShapeDtypeStruct((dp, ctx, 8, PAIR), f32),
-            jax.ShapeDtypeStruct((4, width), f32),
-            jax.ShapeDtypeStruct((dp * ctx * depth, near), bf16),
-            jax.ShapeDtypeStruct((dp * out_weight.shape[0], width), bf16),
-            jax.ShapeDtypeStruct((ctx * length, width), bf16),
-            jax.ShapeDtypeStruct((ctx * length, near), f32),
-            jax.ShapeDtypeStruct((ctx * length, width), bf16),
-        ],
-        scratch_shapes=[
-            pltpu.VMEM((8, PAIR), f32),
-            pltpu.VMEM((depth, 3 * width), bf16),
-            pltpu.VMEM((ctx, depth, near), bf16),
-            pltpu.VMEM((ctx * length, width), bf16),
-            pltpu.VMEM((dp * ctx * depth, near), bf16),
-            pltpu.VMEM((ctx * length, width), bf16),
-            pltpu.SemaphoreType.DMA((ctx,)),
-            pltpu.SemaphoreType.DMA((PARTS, dp // 2)),
-            pltpu.SemaphoreType.DMA((5,)),
-            pltpu.SemaphoreType.DMA((4, ctx)),
-            pltpu.SemaphoreType.DMA((2, dp)),
-            pltpu.SemaphoreType.DMA((PARTS, 6, dp)),
-            LineGather.scratch(dp),
-            CtxGather.scratch(),
-            CtxGather.scratch(),
-        ],
-        compiler_params=pltpu.CompilerParams(
-            collective_id=0, has_side_effects=True, vmem_limit_bytes=40 << 20
-        ),
-        cost_estimate=pl.CostEstimate(
-            flops=2 * ctx * length * width * near, transcendentals=0, bytes_accessed=200 << 20
-        ),
-    )(*vectors, qkv_weight, out_weight, rows, cot)
-
-
-CHUNKS = 4
 
 
 class CtxReduce:
@@ -672,66 +437,6 @@
 
 def rows_of(ref, col, size):
     return ref[pl.ds(pl.multiple_of(col * size, size), size), :]
-
-
-def mix_kernel(
-    dp, ctx, attended_ref, weight_ref, rows_ref, gain_ref, shift_ref, resid_hbm, wide_ref,
-    total, sent, got, made, resid_ref, reduce_sem, spread_sem, resid_sem,
-):
-    place = Place(dp)
-    greet(place, ctx)
-    size = rows_ref.shape[0]
-    reduce = CtxReduce(
-        place, lambda col: dot(rows_of(attended_ref, col, size), weight_ref[...]), total, sent, got, reduce_sem
-    )
-    spread = CtxSpread(place, made, wide_ref, spread_sem)
-    reduce.start()
-    reduce.relay()
-
-    def resid_copy(j):
-        rows = reduce.chunk(j)
-        return pltpu.make_async_copy(resid_ref.at[rows, :], resid_hbm.at[rows, :], resid_sem.at[j])
-
-    for j in range(CHUNKS):
-        rows = reduce.chunk(j)
-        resid = rows_ref[rows, :].astype(f32) + reduce.sum(j)
-        resid_ref[rows, :] = resid
-        resid_copy(j).start()
-        scaled, _ = norm_stats(resid)
-        made[rows, :] = (scaled * gain_ref[...] + shift_ref[...]).astype(bf16)
-        spread.send(j)
-        if j:
-            spread.relay(j - 1)
-    spread.relay(CHUNKS - 1)
-    spread.finish()
-    reduce.finish()
-    for j in range(CHUNKS):
-        resid_copy(j).wait()
-
-
-def mix(dp, ctx, attended, weight, rows, gain, shift):
-    size, width = rows.shape
-    vmem = pl.BlockSpec(memory_space=pltpu.VMEM)
-    return pl.pallas_call(
-        functools.partial(mix_kernel, dp, ctx),
-        in_specs=[vmem] * 5,
-        out_specs=[HBM, HBM],
-        out_shape=[jax.ShapeDtypeStruct((size, width), f32), jax.ShapeDtypeStruct((ctx * size, width), bf16)],
-        scratch_shapes=CtxReduce.scratch(size, width)[:3]
-        + [
-            pltpu.VMEM((size, width), bf16),
-            pltpu.VMEM((size, width), f32),
-            CtxReduce.scratch(size, width)[3],
-            CtxSpread.scratch(),
-            pltpu.SemaphoreType.DMA((CHUNKS,)),
-        ],
-        compiler_params=pltpu.CompilerParams(
-            collective_id=2, has_side_effects=True, vmem_limit_bytes=40 << 20
-        ),
-        cost_estimate=pl.CostEstimate(
-            flops=2 * attended.size * width, transcendentals=0, bytes_accessed=180 << 20
-        ),
-    )(attended, weight, rows, gain.reshape(1, width), shift.reshape(1, width))
 
 
 def mix_back_kernel(
@@ -1265,10 +970,20 @@
     return max(0, (at - DOC_MAX + 1) // step * step), at + step
 
 
-def block_mask(start, at, step, low, high):
-    keys = lax.broadcasted_iota(jnp.int32, (step, high - low), 1) + low
-    rows = lax.broadcasted_iota(jnp.int32, (step, high - low), 0) + at
-    return (keys >= start) & (keys <= rows)
+def parts_of(low, at, step):
+    return ([(low, at, False)] if low < at else []) + [(at, at + step, True)]
+
+
+def masked(scores, start, first, causal):
+    keys = lax.broadcasted_iota(jnp.int32, scores.shape, 1)
+    allowed = keys >= start - first
+    if causal:
+        allowed = allowed & (keys <= lax.broadcasted_iota(jnp.int32, scores.shape, 0))
+    return jnp.where(allowed, scores, masked_value)
+
+
+def one_head(x, head):
+    return jnp.where(head_lanes(x.shape) == (head == 0), x, jnp.zeros_like(x))
 
 
 def attend_kernel(step, joined_ref, bias_ref, table_ref, start_ref, out_ref, qkv_ref, lse_ref):
@@ -1281,23 +996,25 @@
             x = turn(x, table_ref)
         qkv_ref[:, lanes] = x.astype(bf16)
     for at in range(0, full_len, step):
-        low, high = span(full_len, step, at)
-        allowed = block_mask(start_ref[at : at + step, :1], at, step, low, high)
-        q = qkv_ref[at : at + step, :PAIR]
-        k = qkv_ref[low:high, PAIR : 2 * PAIR]
-        v = qkv_ref[low:high, 2 * PAIR :]
+        parts = parts_of(span(full_len, step, at)[0], at, step)
+        start = start_ref[at : at + step, :1]
+        q = qkv_ref[at : at + step, :PAIR] * bf16(scale)
         total = jnp.zeros((step, PAIR), f32)
         logs = []
         for head in range(2):
-            mine = head_lanes(q.shape) == (head == 0)
-            s = dot_nt(jnp.where(mine, q, jnp.zeros_like(q)), k) * scale
-            s = jnp.where(allowed, s, masked_value)
-            top = jnp.max(s, axis=1, keepdims=True)
-            e = jnp.exp(s - top)
-            norm = jnp.sum(e, axis=1, keepdims=True)
-            probs = (e * (1.0 / norm)).astype(bf16)
-            vm = jnp.where(head_lanes(v.shape) == (head == 0), v, jnp.zeros_like(v))
-            total = total + dot(probs, vm)
+            qm = one_head(q, head)
+            scores = [
+                masked(dot_nt(qm, qkv_ref[low:high, PAIR : 2 * PAIR]), start, low, causal)
+                for low, high, causal in parts
+            ]
+            tops = [jnp.max(s, axis=1, keepdims=True) for s in scores]
+            top = functools.reduce(jnp.maximum, tops)
+            norm, sums = 0.0, 0.0
+            for s, (low, high, _) in zip(scores, parts):
+                e = jnp.exp(s - top)
+                norm = norm + jnp.sum(e, axis=1, keepdims=True)
+                sums = sums + dot(e.astype(bf16), one_head(qkv_ref[low:high, 2 * PAIR :], head))
+            total = total + sums * (1.0 / norm)
             logs.append(top + jnp.log(norm))
         out_ref[at : at + step, :] = total.astype(bf16)
         lse_ref[at : at + step, :] = jnp.where(head_lanes((step, PAIR)), logs[0], logs[1])
@@ -1312,39 +1029,36 @@
     dv_ref[...] = jnp.zeros_like(dv_ref)
     total = jnp.zeros((1, PAIR), f32)
     for at in range(0, full_len, step):
-        low, high = span(full_len, step, at)
         rows = slice(at, at + step)
-        keys = slice(low, high)
-        allowed = block_mask(start_ref[rows, :1], at, step, low, high)
-        q = qkv_ref[rows, :PAIR]
-        k = qkv_ref[keys, PAIR : 2 * PAIR]
-        v = qkv_ref[keys, 2 * PAIR :]
+        parts = parts_of(span(full_len, step, at)[0], at, step)
+        start = start_ref[rows, :1]
+        q = qkv_ref[rows, :PAIR] * bf16(scale)
         g = grad_ref[rows, :]
         dq = jnp.zeros((step, PAIR), f32)
-        dk = jnp.zeros((high - low, PAIR), f32)
-        dv = jnp.zeros((high - low, PAIR), f32)
+        dk = [jnp.zeros((high - low, PAIR), f32) for low, high, _ in parts]
+        dv = [jnp.zeros((high - low, PAIR), f32) for low, high, _ in parts]
         for head in range(2):
-            mine = head_lanes(q.shape) == (head == 0)
-            qm = jnp.where(mine, q, jnp.zeros_like(q))
-            gm = jnp.where(mine, g, jnp.zeros_like(g))
-            km = jnp.where(head_lanes(k.shape) == (head == 0), k, jnp.zeros_like(k))
-            s = dot_nt(qm, k) * scale
-            probs = jnp.where(
-                allowed, jnp.exp(s - lse_ref[rows, head * HD : head * HD + 1]), 0.0
-            )
-            dp = dot_nt(gm, v)
-            mean = jnp.sum(dp * probs, axis=1, keepdims=True)
-            ds = (probs * (dp - mean)).astype(bf16)
-            dq = dq + dot(ds, km)
-            dk = dk + dot_tn(ds, qm)
-            dv = dv + dot_tn(probs.astype(bf16), gm)
-        dk_ref[keys, :] += dk
-        dv_ref[keys, :] += dv
+            qm, gm = one_head(q, head), one_head(g, head)
+            lse = lse_ref[rows, head * HD : head * HD + 1]
+            probs, dps, mean = [], [], 0.0
+            for low, high, causal in parts:
+                s = masked(dot_nt(qm, qkv_ref[low:high, PAIR : 2 * PAIR]), start, low, causal)
+                probs.append(jnp.exp(s - lse))
+                dps.append(dot_nt(gm, qkv_ref[low:high, 2 * PAIR :]))
+                mean = mean + jnp.sum(dps[-1] * probs[-1], axis=1, keepdims=True)
+            for i, (low, high, _) in enumerate(parts):
+                ds = (probs[i] * (dps[i] - mean)).astype(bf16)
+                dq = dq + dot(ds, one_head(qkv_ref[low:high, PAIR : 2 * PAIR], head))
+                dk[i] = dk[i] + dot_tn(ds, qm)
+                dv[i] = dv[i] + dot_tn(probs[i].astype(bf16), gm)
+        for i, (low, high, _) in enumerate(parts):
+            dk_ref[low:high, :] += dk[i]
+            dv_ref[low:high, :] += dv[i]
         dq = turn_back(dq * scale, table_ref.at[:, rows, :]).astype(bf16)
         out_ref[rows, :PAIR] = dq
         total = total + jnp.sum(dq.astype(f32), axis=0, keepdims=True)
     sum_ref[:, :PAIR] = total
-    dk = turn_back(dk_ref[...] * scale, table_ref).astype(bf16)
+    dk = turn_back(dk_ref[...], table_ref).astype(bf16)
     out_ref[:, PAIR : 2 * PAIR] = dk
     sum_ref[:, PAIR : 2 * PAIR] = jnp.sum(dk.astype(f32), axis=0, keepdims=True)
     dv = dv_ref[...].astype(bf16)
@@ -1413,6 +1127,383 @@
     )(qkv, grad, lse, table, start)
 
 
+def forward_kernel(
+    dp, ctx, step,
+    gain_one, shift_one, gain_two, shift_two, bias, start_ref, table_hbm,
+    qkv_hbm, out_weight_ref, rows_ref, cot_ref, gate_hbm, up_hbm,
+    params_ref, weight_hbm, out_hbm, normed_hbm, cot_all, attended_hbm, heads_hbm, lse_hbm, resid_hbm, wide_ref,
+    gate_all, up_all,
+    small_all, table_ref, small_ref, qkv_ref, blocks, rows_all, weight_ref, normed_ref, joined_ref, bias_ref, out_all,
+    attended_ref, heads_ref, lse_ref, total, sent, got, made, resid_ref,
+    normed_sem, weight_sem, local_sem, swap_sem, small_sem, line_joined, line_out, line_gate, line_up, rows_sem, cot_sem,
+    late_sem, reduce_sem, spread_sem, resid_sem,
+):
+    place = Place(dp)
+    me, row = place.col, place.row
+    depth = qkv_ref.shape[0]
+    length, width = rows_ref.shape
+    rows_out = out_weight_ref.shape[0]
+    tall = ctx * depth
+
+    qkv_copy = pltpu.make_async_copy(qkv_hbm, qkv_ref, local_sem.at[4])
+    qkv_copy.start()
+    table_copy = pltpu.make_async_copy(table_hbm, table_ref, late_sem.at[0])
+    table_copy.start()
+    greet_all(place, dp, ctx, wait=False)
+    small_ref[...] = jnp.zeros_like(small_ref)
+    for i, vector in enumerate((gain_one, shift_one, gain_two, shift_two)):
+        small_ref[i // 2 : i // 2 + 1, i % 2 * HD : (i % 2 + 1) * HD] = vector[...].astype(f32)
+    for i in range(bias.shape[1] // HD):
+        small_ref[2 + i // 2 : 3 + i // 2, i % 2 * HD : (i % 2 + 1) * HD] = bias[
+            :, i * HD : (i + 1) * HD
+        ].astype(f32)
+    small_all[row, me] = small_ref[...]
+    qkv_copy.wait()
+
+    low = head_lanes((depth, PAIR))
+    for p in range(width // HD // ctx // 2):
+        for t in range(3):
+            lanes = slice((3 * p + t) * PAIR, (3 * p + t + 1) * PAIR)
+            for c in range(0, ctx, 2):
+                at = t * width + (2 * p * ctx + c) * HD
+                a = qkv_ref[:, at : at + PAIR].astype(f32)
+                at = at + ctx * HD
+                b = qkv_ref[:, at : at + PAIR].astype(f32)
+                blocks[c, :, lanes] = jnp.where(low, a, pltpu.roll(b, HD, 1)).astype(bf16)
+                blocks[c + 1, :, lanes] = jnp.where(low, pltpu.roll(a, HD, 1), b).astype(bf16)
+    greet_all(place, dp, ctx, signal=False)
+
+    def weight_rows(row, col):
+        return weight_ref.at[pl.ds(pl.multiple_of((row * ctx + col) * depth, depth), depth), :]
+
+    def out_shard(row):
+        return out_all.at[pl.ds(pl.multiple_of(row * rows_out, rows_out), rows_out), :]
+
+    def block(ref, col):
+        return ref.at[pl.ds(pl.multiple_of(col * length, length), length), :]
+
+    part_cols = weight_ref.shape[1] // PARTS
+
+    def weight_part(i, row):
+        return weight_ref.at[
+            pl.ds(pl.multiple_of(row * tall, tall), tall), pl.ds(i * part_cols, part_cols)
+        ]
+
+    local = [
+        pltpu.make_async_copy(blocks.at[me], weight_rows(row, me), local_sem.at[0]),
+        pltpu.make_async_copy(out_weight_ref, out_shard(row), local_sem.at[1]),
+        pltpu.make_async_copy(rows_ref, block(rows_all, me), local_sem.at[2]),
+        pltpu.make_async_copy(cot_ref, block(cot_all, me), local_sem.at[3]),
+    ]
+    swaps = [
+        remote(small_ref, small_all.at[row, me], swap_sem.at[0, k], swap_sem.at[1, k], place.across(k))
+        for k in range(1, ctx)
+    ] + [
+        remote(
+            blocks.at[place.other(k)], weight_rows(row, me), swap_sem.at[2, k], swap_sem.at[3, k], place.across(k)
+        )
+        for k in range(1, ctx)
+    ]
+    for copy in swaps:
+        copy.start()
+    for copy in local:
+        copy.start()
+    def gate_shard(row):
+        tall = gate_hbm.shape[0]
+        return gate_all.at[pl.ds(pl.multiple_of(row * tall, tall), tall), :]
+
+    def up_shard(row):
+        tall = up_hbm.shape[0]
+        return up_all.at[pl.ds(pl.multiple_of(row * tall, tall), tall), :]
+
+    gate_line, up_line = LineGather(place, gate_shard, line_gate), LineGather(place, up_shard, line_up)
+    late = [
+        pltpu.make_async_copy(gate_hbm, gate_shard(row), late_sem.at[1]),
+        pltpu.make_async_copy(up_hbm, up_shard(row), late_sem.at[2]),
+    ]
+    rows_gather = CtxGather(place, rows_ref, rows_all, length, rows_sem)
+    cot_gather = CtxGather(place, cot_ref, cot_all, length, cot_sem)
+    out_line = LineGather(place, out_shard, line_out)
+    lines = [
+        LineGather(place, functools.partial(weight_part, i), line_joined.at[i]) for i in range(PARTS)
+    ] + [out_line]
+    local[1].wait()
+    out_line.send(1)
+    rows_gather.first()
+    for k in range(1, ctx):
+        remote(
+            small_ref, small_all.at[row, place.other(k)], swap_sem.at[0, k], swap_sem.at[1, k], place.across(k)
+        ).wait_recv()
+    small_sends = [
+        remote(
+            small_all.at[row], small_all.at[row], small_sem.at[0, k], small_sem.at[1, k], ((row + k) % dp, me)
+        )
+        for k in range(1, dp)
+    ]
+    for copy in small_sends:
+        copy.start()
+    local[0].wait()
+    for k in range(1, ctx):
+        part = weight_rows(row, place.other(k))
+        remote(part, part, swap_sem.at[2, k], swap_sem.at[3, k], place.across(k)).wait_recv()
+    for line in lines[:PARTS]:
+        line.send(1)
+
+    for k in range(1, dp):
+        part = small_all.at[(row + dp - k) % dp]
+        remote(part, part, small_sem.at[0, k], small_sem.at[1, k], place.twin).wait_recv()
+    low = head_lanes((1, PAIR))
+    for i in range(dp * ctx // 2):
+        lanes = slice(i * PAIR, (i + 1) * PAIR)
+        a = small_all[2 * i // ctx, 2 * i % ctx]
+        b = small_all[(2 * i + 1) // ctx, (2 * i + 1) % ctx]
+        for r in range(2):
+            ar, br = a[r : r + 1, :], b[r : r + 1, :]
+            params_ref[2 * r : 2 * r + 1, lanes] = jnp.where(low, ar, pltpu.roll(br, HD, 1))
+            params_ref[2 * r + 1 : 2 * r + 2, lanes] = jnp.where(low, pltpu.roll(ar, HD, 1), br)
+
+    def normalize(col):
+        step = 64
+
+        @pl.loop(0, length // step)
+        def _(i):
+            rows = pl.ds(pl.multiple_of(col * length + i * step, step), step)
+            scaled, _ = norm_stats(rows_all[rows, :].astype(f32))
+            normed_ref[rows, :] = (scaled * params_ref[0:1, :] + params_ref[1:2, :]).astype(bf16)
+
+        normed_copy(col).start()
+
+    def normed_copy(col):
+        return pltpu.make_async_copy(block(normed_ref, col), block(normed_hbm, col), normed_sem.at[col])
+
+    def weight_copy(i, line):
+        part = (
+            pl.ds(pl.multiple_of(line * (2 * tall), 2 * tall), 2 * tall),
+            pl.ds(i * part_cols, part_cols),
+        )
+        return pltpu.make_async_copy(weight_ref.at[part], weight_hbm.at[part], weight_sem.at[i, line])
+
+    def multiply(i, line):
+        weight_copy(i, line).start()
+        at = pl.multiple_of(line * (2 * tall), 2 * tall)
+        cols = slice(i * part_cols, (i + 1) * part_cols)
+
+        @pl.loop(0, ctx)
+        def _(b):
+            rows = pl.ds(pl.multiple_of(b * length, length), length)
+            joined_ref[rows, cols] += dot(
+                normed_ref[rows, pl.ds(at, 2 * tall)], weight_ref[pl.ds(at, 2 * tall), cols]
+            )
+
+    def forward(hop):
+        for line in lines:
+            line.receive(hop)
+            if hop < place.lines - 1:
+                line.send(hop + 1)
+
+    def absorb(hop):
+        for i in range(PARTS):
+            lines[i].settle(hop, functools.partial(multiply, i))
+
+    joined_ref[...] = jnp.zeros_like(joined_ref)
+    local[2].wait()
+    normalize(me)
+    rows_gather.second()
+    cot_gather.first()
+    for hop in range(1, place.lines):
+        forward(hop)
+        if hop == 1:
+            for col in (place.other(1), place.other(2)):
+                normalize(col)
+            rows_gather.finish()
+            normalize(place.other(3))
+        if hop == min(2, place.lines - 1):
+            cot_gather.second()
+        absorb(hop - 1)
+    late[0].start()
+    late[1].start()
+    absorb(place.lines - 1)
+    late[0].wait()
+    late[1].wait()
+    gate_line.send(1)
+
+    low = head_lanes((1, PAIR))
+    pairs = joined_ref.shape[1] // (3 * PAIR)
+    per_device = bias.shape[1] // HD
+    for p in range(pairs):
+        for t in range(3):
+            chosen = [None, None]
+            for c in range(ctx):
+                for half in range(2):
+                    slot = t * (width // HD) + (2 * p + half) * ctx + c
+                    owner, at = slot // per_device, slot % per_device
+                    piece = small_all[owner // ctx, owner % ctx, 2 + at // 2 : 3 + at // 2, :]
+                    if at % 2 != half:
+                        piece = pltpu.roll(piece, HD, 1)
+                    chosen[half] = piece if c == 0 else jnp.where(me == c, piece, chosen[half])
+            lanes = slice((3 * p + t) * PAIR, (3 * p + t + 1) * PAIR)
+            bias_ref[:, lanes] = jnp.where(low, chosen[0], chosen[1])
+
+    def heads_copies():
+        return [
+            pltpu.make_async_copy(attended_ref, attended_hbm, late_sem.at[3]),
+            pltpu.make_async_copy(heads_ref, heads_hbm, late_sem.at[4]),
+            pltpu.make_async_copy(lse_ref, lse_hbm, late_sem.at[5]),
+            pltpu.make_async_copy(out_all, out_hbm, late_sem.at[6]),
+        ]
+
+    def attend_pairs(first, last):
+        @pl.loop(first, last)
+        def _(p):
+            wide = pl.ds(pl.multiple_of(p * (3 * PAIR), 3 * PAIR), 3 * PAIR)
+            thin = pl.ds(pl.multiple_of(p * PAIR, PAIR), PAIR)
+            attend_kernel(
+                step, joined_ref.at[:, wide], bias_ref.at[:, wide], table_ref, start_ref,
+                attended_ref.at[:, thin], heads_ref.at[:, wide], lse_ref.at[:, thin],
+            )
+
+    def pass_on(line, hop):
+        line.receive(hop)
+        if hop < place.lines - 1:
+            line.send(hop + 1)
+
+    table_copy.wait()
+    attend_pairs(0, pairs // 2)
+    if place.lines > 1:
+        pass_on(gate_line, 1)
+    attend_pairs(pairs // 2, pairs)
+    for hop in range(place.lines):
+        out_line.settle(hop)
+    for line in lines:
+        line.finish()
+    cot_gather.finish()
+    for copy in heads_copies():
+        copy.start()
+
+    reduce = CtxReduce(
+        place, lambda col: dot(rows_of(attended_ref, col, length), out_all[...]), total, sent, got, reduce_sem
+    )
+    spread = CtxSpread(place, made, wide_ref, spread_sem)
+
+    def resid_copy(j):
+        rows = reduce.chunk(j)
+        return pltpu.make_async_copy(resid_ref.at[rows, :], resid_hbm.at[rows, :], resid_sem.at[j])
+
+    reduce.start()
+    if place.lines > 2:
+        pass_on(gate_line, 2)
+    up_line.send(1)
+    reduce.relay()
+    for j in range(CHUNKS):
+        rows = reduce.chunk(j)
+        at = pl.multiple_of(me * length + j * reduce.size, reduce.size)
+        resid = rows_all[pl.ds(at, reduce.size), :].astype(f32) + reduce.sum(j)
+        resid_ref[rows, :] = resid
+        resid_copy(j).start()
+        scaled, _ = norm_stats(resid)
+        made[rows, :] = (scaled * params_ref[2:3, :] + params_ref[3:4, :]).astype(bf16)
+        spread.send(j)
+        if j:
+            spread.relay(j - 1)
+        if j == 1 and place.lines > 1:
+            pass_on(up_line, 1)
+    spread.relay(CHUNKS - 1)
+    for hop in range(3, place.lines):
+        pass_on(gate_line, hop)
+    for hop in range(2, place.lines):
+        pass_on(up_line, hop)
+    spread.finish()
+    for line in (gate_line, up_line):
+        for hop in range(place.lines):
+            line.settle(hop)
+        line.finish()
+    reduce.finish()
+    for copy in swaps + small_sends:
+        copy.wait_send()
+    local[3].wait()
+    for col in range(ctx):
+        normed_copy(col).wait()
+    for line in range(place.lines):
+        for i in range(PARTS):
+            weight_copy(i, line).wait()
+    for j in range(CHUNKS):
+        resid_copy(j).wait()
+    for copy in heads_copies():
+        copy.wait()
+
+
+def forward(dp, ctx, vectors, start, table, qkv_weight, out_weight, rows, cot, gate_weight, up_weight):
+    depth, width = qkv_weight.shape[0], rows.shape[1]
+    length = rows.shape[0]
+    full_len = ctx * length
+    near = 3 * width // ctx
+    thin = near // 3
+    hidden = gate_weight.shape[1]
+    vmem = pl.BlockSpec(memory_space=pltpu.VMEM)
+    reduce_scratch = CtxReduce.scratch(length, width)
+    return pl.pallas_call(
+        functools.partial(forward_kernel, dp, ctx, attend_step(full_len)),
+        in_specs=[vmem] * (len(vectors) + 1) + [HBM] * 7,
+        out_specs=[vmem] + [HBM] * 11,
+        out_shape=[
+            jax.ShapeDtypeStruct((4, width), f32),
+            jax.ShapeDtypeStruct((dp * ctx * depth, near), bf16),
+            jax.ShapeDtypeStruct((dp * out_weight.shape[0], width), bf16),
+            jax.ShapeDtypeStruct((full_len, width), bf16),
+            jax.ShapeDtypeStruct((full_len, width), bf16),
+            jax.ShapeDtypeStruct((full_len, thin), bf16),
+            jax.ShapeDtypeStruct((full_len, near), bf16),
+            jax.ShapeDtypeStruct((full_len, thin), f32),
+            jax.ShapeDtypeStruct((length, width), f32),
+            jax.ShapeDtypeStruct((full_len, width), bf16),
+            jax.ShapeDtypeStruct((dp * gate_weight.shape[0], hidden), bf16),
+            jax.ShapeDtypeStruct((dp * up_weight.shape[0], hidden), bf16),
+        ],
+        scratch_shapes=[
+            pltpu.VMEM((dp, ctx, 8, PAIR), f32),
+            pltpu.VMEM(table.shape, f32),
+            pltpu.VMEM((8, PAIR), f32),
+            pltpu.VMEM((depth, 3 * width), bf16),
+            pltpu.VMEM((ctx, depth, near), bf16),
+            pltpu.VMEM((full_len, width), bf16),
+            pltpu.VMEM((dp * ctx * depth, near), bf16),
+            pltpu.VMEM((full_len, width), bf16),
+            pltpu.VMEM((full_len, near), f32),
+            pltpu.VMEM((1, near), f32),
+            pltpu.VMEM((dp * out_weight.shape[0], width), bf16),
+            pltpu.VMEM((full_len, thin), bf16),
+            pltpu.VMEM((full_len, near), bf16),
+            pltpu.VMEM((full_len, thin), f32),
+        ]
+        + reduce_scratch[:3]
+        + [
+            pltpu.VMEM((length, width), bf16),
+            pltpu.VMEM((length, width), f32),
+            pltpu.SemaphoreType.DMA((ctx,)),
+            pltpu.SemaphoreType.DMA((PARTS, dp // 2)),
+            pltpu.SemaphoreType.DMA((5,)),
+            pltpu.SemaphoreType.DMA((4, ctx)),
+            pltpu.SemaphoreType.DMA((2, dp)),
+            pltpu.SemaphoreType.DMA((PARTS, 6, dp)),
+            LineGather.scratch(dp),
+            LineGather.scratch(dp),
+            LineGather.scratch(dp),
+            CtxGather.scratch(),
+            CtxGather.scratch(),
+            pltpu.SemaphoreType.DMA((7,)),
+            reduce_scratch[3],
+            CtxSpread.scratch(),
+            pltpu.SemaphoreType.DMA((CHUNKS,)),
+        ],
+        compiler_params=pltpu.CompilerParams(
+            collective_id=0, has_side_effects=True, vmem_limit_bytes=62 << 20
+        ),
+        cost_estimate=pl.CostEstimate(
+            flops=2 * full_len * width * near, transcendentals=0, bytes_accessed=400 << 20
+        ),
+    )(*vectors, start, table, qkv_weight, out_weight, rows, cot, gate_weight, up_weight)
+
+
 def rotary_table(full_len):
     half = ROT // 2
     inverse = 10000.0 ** (-2.0 * np.arange(half) / ROT)
@@ -1450,19 +1541,24 @@
     me = lax.axis_index("ctx")
     own = me * local_len
 
+    segment = segments[0]
+    start = jnp.sum((segment[None, :] < segment[:, None]).astype(jnp.int32), axis=1)
+    start = jnp.broadcast_to(start[:, None], (full_len, 128))
+    table = rotary_table(full_len)
     part = ln1_gain.shape[0]
     vectors = [v[None, :] for v in (ln1_gain, ln1_bias, ln2_gain, ln2_bias, qkv_bias)]
-    count = 4 * part + qkv_bias.shape[0]
     rows_here = qkv_weight.shape[0]
     rows, grad_rows = inputs[0], cotangent[0]
     fused = ctx == 4 and dp % 2 == 0 and part == HD
     if fused:
-        small, params, joined_weight, out_full, normed_one, joined, grad_wide = opening(
-            dp, ctx, vectors, qkv_weight, out_weight, rows, grad_rows
-        )
-        gain_one, shift_one, gain_two, shift_two = params
-        up_weight, down_weight, _ = lax.optimization_barrier((up_weight, down_weight, normed_one))
-        small = small.reshape(dp * ctx, 1024)[:, :count]
+        (
+            params, joined_weight, out_full, normed_one, grad_wide, attended, qkv, lse, resid, normed_wide,
+            gate_full, up_full,
+        ) = forward(
+            dp, ctx, vectors, start, table, qkv_weight, out_weight, rows, grad_rows, gate_weight, up_weight
+        )
+        gain_one, _, gain_two, _ = params
+        down_weight, _ = lax.optimization_barrier((down_weight, normed_wide))
     else:
         small = jnp.concatenate(vectors, axis=1).astype(f32)
         small = lax.all_gather(small, ("dp", "ctx"), axis=0, tiled=True)
@@ -1481,26 +1577,16 @@
         scaled_wide, _ = norm_stats(gather_ctx(rows, ctx).astype(f32))
         normed_one = (scaled_wide * gain_one + shift_one).astype(bf16)
         grad_wide = gather_ctx(grad_rows, ctx)
-    bias = small[:, 4 * part :].reshape(3, pairs, 2, ctx, HD)
-    bias = lax.dynamic_index_in_dim(bias, me, 3, keepdims=False)
-    bias = bias.transpose(1, 0, 2, 3).reshape(1, near * 3 * HD)
-    gate_full = lax.all_gather(gate_weight, "dp", axis=0, tiled=True)
-    up_full = lax.all_gather(up_weight, "dp", axis=0, tiled=True)
-    down_full = lax.all_gather(down_weight, "dp", axis=1, tiled=True)
-
-    segment = segments[0]
-    start = jnp.sum((segment[None, :] < segment[:, None]).astype(jnp.int32), axis=1)
-    start = jnp.broadcast_to(start[:, None], (full_len, 128))
-    table = rotary_table(full_len)
-    if not fused:
-        joined = dot(normed_one, joined_weight)
-    attended, qkv, lse = attend(joined, bias, table, start)
-    if fused:
-        resid, normed_wide = mix(dp, ctx, attended, out_full, rows, gain_two, shift_two)
-    else:
+        bias = small[:, 4 * part :].reshape(3, pairs, 2, ctx, HD)
+        bias = lax.dynamic_index_in_dim(bias, me, 3, keepdims=False)
+        bias = bias.transpose(1, 0, 2, 3).reshape(1, near * 3 * HD)
+        attended, qkv, lse = attend(dot(normed_one, joined_weight), bias, table, start)
         resid = rows.astype(f32) + scatter_ctx(dot(attended, out_full), ctx)
         scaled_two, inv_two = norm_stats(resid)
         normed_wide = gather_ctx((scaled_two * gain_two + shift_two).astype(bf16), ctx)
+        gate_full = lax.all_gather(gate_weight, "dp", axis=0, tiled=True)
+        up_full = lax.all_gather(up_weight, "dp", axis=0, tiled=True)
+    down_full = lax.all_gather(down_weight, "dp", axis=1, tiled=True)
 
     gate = dot(normed_wide, gate_full)
     upward = dot(normed_wide, up_full)

time: 592 us -> 617 us (1.042)
  waiting for transfers between devices: 1.45 us -> 31.4 us
  Pallas kernels: 443 us -> 464 us
  local copies, waits for them, and re-layouts: 39.3 us -> 20.3 us
    all_gather x1, waiting for transfers between devices: 0.02 us -> 31.3 us  [shards(): down_full = lax.all_gather(down_weight, 'dp', axis=1, tiled=True)]
    unnamed x81 -> x47, local copies, waits for them, and re-layouts: 35.5 us -> 15.2 us
    pallas_call x3 -> x1, Pallas kernels: 225 us -> 244 us  [forward(): pl.pallas_call(functools.partial(forward_kernel, dp, ctx, attend_step(ful...]
  transfers between devices with their start and end apart: 6 -> 4, of which waited for: 0 -> 1; matrix products, arithmetic and copies ran while one was open for 15% -> 13% of each run, Pallas kernels for 76% -> 36%
where the time goes in v8:
time: 617 us; the launch traced here: 611 us
  Pallas kernels  464 us (75%)
  matrix products  72.2 us (12%)
  waiting for transfers between devices  31.4 us (5%)
  local copies, waits for them, and re-layouts  20.3 us (3%)
  between operations  14.2 us (2%)
  other arithmetic  8.38 us (1%)
    pallas_call x1, Pallas kernels, forward(): pl.pallas_call(functools.partial(forward_kernel, dp, ctx, attend_step(ful...  244 us
    pallas_call x1, Pallas kernels, closing(): pl.pallas_call(functools.partial(closing_kernel, dp, ctx), in_specs=[HBM]...  113 us
    pallas_call x1, Pallas kernels, mix_back(): pl.pallas_call(functools.partial(mix_back_kernel, dp, ctx), in_specs=[vme...  85.5 us
    dot_general x4, matrix products, dot_tn(): lax.dot_general(a, b, (((0,), (0,)), ((), ())), preferred_element_type=f32)  34.2 us
    all_gather x1, waiting for transfers between devices, shards(): down_full = lax.all_gather(down_weight, 'dp', axis=1, tiled=True)  31.3 us
    pallas_call x1, Pallas kernels, attend_back(): pl.pallas_call(functools.partial(attend_back_kernel, step), grid=(pairs,)...  22.2 us
    dot_general x2, matrix products, dot(): return jnp.dot(a, b, preferred_element_type=f32)  19.2 us
    dot_general x2, matrix products, dot_nt(): lax.dot_general(a, b, (((1,), (1,)), ((), ())), preferred_element_type=f32)  18.7 us
  transfers between devices with their start and end apart: 4, of which 1 were waited for; matrix products, arithmetic and copies ran while one was open for 13% of the time, Pallas kernels for 36%

profile of v8, /device:TPU:0, one launch (start us, length us, event | category | flops | bytes accessed | tf_op | source)
XLA Modules:
  0.0 611.1 jit_solution(2074297742009136050)
XLA Ops:
  7.2 0.0 all-gather.2.cloned.1.call-start
  7.2 1.2 broadcast_in_dim.31.bias
  8.4 1.3 convert_reduce_fusion
  9.8 1.0 broadcast_in_dim.32.start_ref
  10.8 243.5 %shard_map.229 = (f32[4,2048]{1,0:T(4,128)}, bf16[2048,1536]{1,0:T(8,128)(2,1)}, bf16[512,2048]{1,0:T(8,128)(2,1)}, bf16[1024,2048]{1,0:T(8,128)(2,1)}, bf16[102...) custom-call(bf16[1,64]{1,0:T(2,128)(2,1)} %bitcast.50, ...), custom_call_target="tpu_custom_call" | custom-call | flops 6442450944 | bytes 419430400 | tf_op jit(solution)/shard_map/pallas_call | solution.py:1444
  254.3 0.0 all-gather.2.cloned.1.call-update
  254.3 0.4 reduce-scatter.4.cloned.1.call-start
  254.8 0.0 copy-start.16
  254.8 0.0 copy-start.17
  254.8 10.6 %fusion.2 = f32[1024,1408]{1,0:T(8,128)S(1)} fusion(bf16[1024,2048]{1,0:T(8,128)(2,1)} %get-tuple-element.48.normed_hbm, bf16[2048,1408]{1,0:T(8,128)(2,1)} %get-tuple-element.49.gate_weight_hbm), kind=kOutput, calls=%fused_computation.17 | convolution fusion | flops 5905580032 | bytes 15728640 | tf_op jit(solution)/shard_map/dot_general | solution.py:24
  265.4 0.0 copy-start.19
  265.4 0.0 copy-done.16
  265.4 0.0 copy-done.17
  265.4 0.0 copy-start.13
  265.4 8.6 %multiply_convert_fusion.2 = (bf16[1024,1408]{1,0:T(8,128)(2,1)S(1)}, f32[1024,1408]{1,0:T(8,128)}) fusion(f32[1024,1408]{1,0:T(8,128)S(1)} %fusion.2, bf16[1024,2048]{1,0:T(8,128)(2,1)S(1)} %copy-done.17, bf16[2048,1408]{1,0:T(8,128)(2,1)S(1)} %copy-done.16), kind=kOutput, calls=%fused_computation.5 | convolution fusion | flops 5914230784 | bytes 24379392 | tf_op jit(solution)/shard_map/dot_general | solution.py:24
  274.1 0.0 copy-done.19
  274.1 0.0 copy-done.13
  274.1 8.1 %convolution_convert_fusion.2 = bf16[1408,2048]{1,0:T(8,128)(2,1)} fusion(bf16[1024,1408]{1,0:T(8,128)(2,1)S(1)} %get-tuple-element.88.inner_hbm, bf16[1024,2048]{1,0:T(8,128)(2,1)S(1)} %copy-done.13), kind=kOutput, calls=%fused_computation.2 | convolution fusion | flops 5908463616 | bytes 12845056 | tf_op jit(solution)/shard_map/dot_general | solution.py:32
  282.2 0.0 copy-done.15
  282.2 0.0 reduce-scatter.4.cloned.1.call-update
  282.3 0.0 reduce-scatter.6.cloned.1.call-start
  282.3 31.3 %all-gather.2.cloned.1.call-done.down_hbm = bf16[1408,2048]{1,0:T(8,128)(2,1)} async-done(((bf16[1408,256]{1,0:T(8,128)(2,1)}), bf16[1408,2048]{1,0:T(8,128)(2,1)}) %all-gather.2.cloned.1.call-update) | async-done | bytes 5767184 | tf_op jit(solution)/shard_map/all_gather | solution.py:1589
  313.6 15.4 %multiply_convert_fusion = (bf16[1024,1408]{1,0:T(8,128)(2,1)}, bf16[1024,1408]{1,0:T(8,128)(2,1)S(1)}) fusion(f32[1024,1408]{1,0:T(8,128)} %copy-done.19, f32[1024,1408]{1,0:T(8,128)} %get-tuple-element.89, bf16[1024,2048]{1,0:T(8,128)(2,1)} %get-tuple-element.51, bf16[1408,2048]{1,0:T(8,128)(2,1)} %all-gather.2.cloned.1.call-done.down_hbm), kind=kOutput, calls=%fused_computation.3 | convolution fusion | flops 5924323328 | bytes 27262976 | tf_op jit(solution)/shard_map/dot_general | solution.py:28
  329.0 0.0 copy-done.18
  329.0 8.6 %convolution_convert_fusion.1 = bf16[2048,1408]{1,0:T(8,128)(2,1)} fusion(bf16[1024,2048]{1,0:T(8,128)(2,1)S(1)} %copy-done.18, bf16[1024,1408]{1,0:T(8,128)(2,1)S(1)} %get-tuple-element.53.gate_ref), kind=kOutput, calls=%fused_computation.1 | convolution fusion | flops 5908463616 | bytes 12845056 | tf_op jit(solution)/shard_map/dot_general | solution.py:32
  337.6 0.0 copy-done.20
  337.6 0.0 reduce-scatter.6.cloned.1.call-update
  337.6 0.2 reduce-scatter.8.cloned.1.call-start
  337.8 0.5 copy-done.9
  338.3 0.6 fusion.1
  338.9 85.5 %shard_map.230 = (f32[256,2048]{1,0:T(8,128)}, f32[2,2048]{1,0:T(2,128)}, bf16[1024,2048]{1,0:T(8,128)(2,1)}, bf16[1024,2048]{1,0:T(8,128)(2,1)}, bf16[2048,1408]{1,0:T(8,128)(2,1)}) custom-call(bf16[1024,1408]{1,0:T(8,128)(2,1)} %copy-done.20, bf16[1024,1408]{1,0:T(8,128)(2,1)} %get-tuple-element.80.up_ref, ...), custom_call_target="tpu_custom_call" | custom-call | flops 23622320128 | bytes 188743680 | tf_op jit(solution)/shard_map/pallas_call | solution.py:545
  424.4 0.0 copy-start.12
  424.4 0.0 reduce-scatter.8.cloned.1.call-update
  424.4 1.2 copy-done.12
  425.7 6.3 %convolution_convert_fusion.3 = bf16[512,2048]{1,0:T(8,128)(2,1)} fusion(bf16[1024,512]{1,0:T(8,128)(2,1)S(1)} %copy-done.12, bf16[1024,2048]{1,0:T(8,128)(2,1)} %get-tuple-element.56), kind=kOutput, calls=%fused_computation.9 | convolution fusion | flops 2148532224 | bytes 7340032 | tf_op jit(solution)/shard_map/dot_general | solution.py:32
  432.0 0.0 copy-done.11
  432.0 0.0 copy-done.14
  432.0 3.3 convolution_convert_fusion.4.grad_ref
  435.3 2.3 convert_element_type.45
  437.6 1.0 copy-done.1
  438.7 1.4 copy-done.2
  440.1 1.3 copy-done.3
  441.3 1.9 copy-done.4
  443.3 1.6 copy-done.5
  444.9 22.2 %shard_map.231 = (bf16[1024,1536]{1,0:T(8,128)(2,1)S(1)}, f32[1,1536]{1,0:T(1,128)S(1)}) custom-call(bf16[1024,1536]{1,0:T(8,128)(2,1)S(1)} %copy-done.4, bf16[1024,512]{1,0:T(8,128)(2,1)S(1)} %copy-done.3, f32[1024,512]{1,0:T(8,128)S(1)} %copy-done.5, f32[3,1024,128]{2,1,0:T(8,128)S(1)} %copy-done.2, s32[1024,128]{1,0:T(8,128)S(1)} %copy-done.1), custom_call_target="tpu_custom_call" | custom-call | flops 6039797760 | bytes 12582912 | tf_op jit(solution)/shard_map/pallas_call | solution.py:1113
  467.1 0.0 copy-start
  467.1 0.1 reshape.40
  467.2 0.1 reshape.41
  467.3 0.8 pad.4.bias_ref
  468.1 11.2 %convolution_convert_fusion = bf16[2048,1536]{1,0:T(8,128)(2,1)} fusion(bf16[1024,2048]{1,0:T(8,128)(2,1)} %get-tuple-element.65, bf16[1024,1536]{1,0:T(8,128)(2,1)S(1)} %get-tuple-element.63.d_joined_hbm), kind=kOutput, calls=%fused_computation | convolution fusion | flops 6445596672 | bytes 13631488 | tf_op jit(solution)/shard_map/dot_general | solution.py:32
  479.3 0.0 copy-done
  479.3 2.3 convert_element_type.46
  481.6 112.8 %shard_map.232 = (f32[256,2048]{1,0:T(8,128)}, f32[64,6144]{1,0:T(8,128)}, f32[64,2048]{1,0:T(8,128)}, bf16[256,2048]{1,0:T(8,128)(2,1)}, f32[4,64]{1,0:T(4,128)}, /*index=5*/f32[1,192]{1,0:T(1,128)}) custom-call(bf16[1024,1536]{1,0:T(8,128)(2,1)} %copy-done, bf16[2048,1536]{1,0:T(8,128)(2,1)} %get-tuple-element.64.weight_hbm, ...), custom_call_target="tpu_custom_call" | custom-call | flops 6442450944 | bytes 209715200 | tf_op jit(solution)/shard_map/pallas_call | solution.py:901
  594.4 0.0 copy-start.6
  594.4 1.4 slice_bitcast_fusion
  595.8 2.4 convert_element_type.49
  598.2 2.3 copy.35
  600.5 0.0 copy-done.6
  600.5 1.3 copy.36
  601.8 0.0 copy-done.7
  601.9 1.1 copy.37
  603.0 0.6 copy.38
  603.6 0.0 copy-done.8
  603.6 0.8 copy.39
  (20 shorter events, 0.1 us)
Async XLA Ops:
  7.2 306.4 %all-gather.2.cloned.1.call-start = ((), (), s32[]{:S(2)}) async-start(), calls=%async_computation.3 | async-start | bytes 6488064 | tf_op jit(solution)/shard_map/all_gather | solution.py:1589
  254.3 181.0 %reduce-scatter.4.cloned.1.call-start = ((), (), s32[]{:S(2)}) async-start(), calls=%async_computation.4 | async-start | bytes 6488064 | tf_op jit(solution)/shard_map/reduce_scatter | solution.py:1598
  254.8 10.6 %copy-start.16 = (bf16[2048,1408]{1,0:T(8,128)(2,1)S(1)}, bf16[2048,1408]{1,0:T(8,128)(2,1)}, u32[]{:S(2)}) copy-start(bf16[2048,1408]{1,0:T(8,128)(2,1)} %get-tuple-element.50.up_weight_hbm) | copy-start | bytes 17301508
  254.8 10.6 %copy-start.17 = (bf16[1024,2048]{1,0:T(8,128)(2,1)S(1)}, bf16[1024,2048]{1,0:T(8,128)(2,1)}, u32[]{:S(2)}) copy-start(bf16[1024,2048]{1,0:T(8,128)(2,1)} %get-tuple-element.48.normed_hbm) | copy-start | bytes 12582916
  265.4 8.7 %copy-start.19 = (f32[1024,1408]{1,0:T(8,128)}, f32[1024,1408]{1,0:T(8,128)S(1)}, u32[]{:S(2)}) copy-start(f32[1024,1408]{1,0:T(8,128)S(1)} %fusion.2) | copy-start | bytes 17301508
  265.4 8.7 %copy-start.13 = (bf16[1024,2048]{1,0:T(8,128)(2,1)S(1)}, bf16[1024,2048]{1,0:T(8,128)(2,1)}, u32[]{:S(2)}) copy-start(bf16[1024,2048]{1,0:T(8,128)(2,1)} %get-tuple-element.51) | copy-start | bytes 12582916
  274.1 8.2 %copy-start.15 = (bf16[1024,1408]{1,0:T(8,128)(2,1)}, bf16[1024,1408]{1,0:T(8,128)(2,1)S(1)}, u32[]{:S(2)}) copy-start(bf16[1024,1408]{1,0:T(8,128)(2,1)S(1)} %get-tuple-element.88.inner_hbm) | copy-start | bytes 8650756
  282.3 197.1 %reduce-scatter.6.cloned.1.call-start = ((), (), s32[]{:S(2)}) async-start(), calls=%async_computation.5 | async-start | bytes 6488064 | tf_op jit(solution)/shard_map/reduce_scatter | solution.py:1604
  313.6 15.4 %copy-start.18 = (bf16[1024,2048]{1,0:T(8,128)(2,1)S(1)}, bf16[1024,2048]{1,0:T(8,128)(2,1)}, u32[]{:S(2)}) copy-start(bf16[1024,2048]{1,0:T(8,128)(2,1)} %get-tuple-element.48.normed_hbm) | copy-start | bytes 12582916
  329.0 8.6 %copy-start.20 = (bf16[1024,1408]{1,0:T(8,128)(2,1)}, bf16[1024,1408]{1,0:T(8,128)(2,1)S(1)}, u32[]{:S(2)}) copy-start(bf16[1024,1408]{1,0:T(8,128)(2,1)S(1)} %get-tuple-element.53.gate_ref) | copy-start | bytes 8650756
  337.6 0.8 copy-start.9
  337.6 258.2 %reduce-scatter.8.cloned.1.call-start = ((), (), s32[]{:S(2)}) async-start(), calls=%async_computation.6 | async-start | bytes 6488064 | tf_op jit(solution)/shard_map/reduce_scatter | solution.py:1617
  424.4 1.3 copy-start.12
  425.7 6.3 %copy-start.11 = (bf16[1024,2048]{1,0:T(8,128)(2,1)S(1)}, bf16[1024,2048]{1,0:T(8,128)(2,1)}, u32[]{:S(2)}) copy-start(bf16[1024,2048]{1,0:T(8,128)(2,1)} %get-tuple-element.56) | copy-start | bytes 12582916
  425.7 6.3 %copy-start.14 = (bf16[512,2048]{1,0:T(8,128)(2,1)S(1)}, bf16[512,2048]{1,0:T(8,128)(2,1)}, u32[]{:S(2)}) copy-start(bf16[512,2048]{1,0:T(8,128)(2,1)} %get-tuple-element.57) | copy-start | bytes 6291460
  437.6 1.0 copy-start.1
  438.7 1.4 copy-start.2
  440.1 1.3 copy-start.3
  441.3 1.9 copy-start.4
  443.3 1.6 copy-start.5
  467.1 12.2 %copy-start = (bf16[1024,1536]{1,0:T(8,128)(2,1)}, bf16[1024,1536]{1,0:T(8,128)(2,1)S(1)}, u32[]{:S(2)}) copy-start(bf16[1024,1536]{1,0:T(8,128)(2,1)S(1)} %get-tuple-element.63.d_joined_hbm) | copy-start | bytes 9437188
  594.4 6.1 copy-start.6
  595.8 6.1 copy-start.7
  600.5 2.5 copy-start.10
  600.5 3.0 copy-start.8
Sparse Core Ops, SparseCore 0:
  254.4 59.1 all-gather.1
  315.9 63.0 reduce-scatter.3
  381.3 63.2 reduce-scatter.5
  446.7 78.4 reduce-scatter.7

commit v9 on v8

--- a/solution.py
+++ b/solution.py
@@ -1208,6 +1208,7 @@
         copy.start()
     for copy in local:
         copy.start()
+
     def gate_shard(row):
         tall = gate_hbm.shape[0]
         return gate_all.at[pl.ds(pl.multiple_of(row * tall, tall), tall), :]
@@ -1221,6 +1222,8 @@
         pltpu.make_async_copy(gate_hbm, gate_shard(row), late_sem.at[1]),
         pltpu.make_async_copy(up_hbm, up_shard(row), late_sem.at[2]),
     ]
+    for copy in late:
+        copy.start()
     rows_gather = CtxGather(place, rows_ref, rows_all, length, rows_sem)
     cot_gather = CtxGather(place, cot_ref, cot_all, length, cot_sem)
     out_line = LineGather(place, out_shard, line_out)
@@ -1320,12 +1323,10 @@
         if hop == min(2, place.lines - 1):
             cot_gather.second()
         absorb(hop - 1)
-    late[0].start()
-    late[1].start()
+    late[0].wait()
+    gate_line.send(1)
     absorb(place.lines - 1)
-    late[0].wait()
     late[1].wait()
-    gate_line.send(1)
 
     low = head_lanes((1, PAIR))
     pairs = joined_ref.shape[1] // (3 * PAIR)
@@ -1371,6 +1372,7 @@
     attend_pairs(0, pairs // 2)
     if place.lines > 1:
         pass_on(gate_line, 1)
+    up_line.send(1)
     attend_pairs(pairs // 2, pairs)
     for hop in range(place.lines):
         out_line.settle(hop)
@@ -1390,10 +1392,9 @@
         return pltpu.make_async_copy(resid_ref.at[rows, :], resid_hbm.at[rows, :], resid_sem.at[j])
 
     reduce.start()
+    reduce.relay()
     if place.lines > 2:
         pass_on(gate_line, 2)
-    up_line.send(1)
-    reduce.relay()
     for j in range(CHUNKS):
         rows = reduce.chunk(j)
         at = pl.multiple_of(me * length + j * reduce.size, reduce.size)

time: 617 us -> 569 us (0.922)
  Pallas kernels: 464 us -> 416 us
    pallas_call x1, Pallas kernels: 244 us -> 196 us  [forward(): pl.pallas_call(functools.partial(forward_kernel, dp, ctx, attend_step(ful...]
  transfers between devices with their start and end apart: 4 -> 4, of which waited for: 1 -> 1; matrix products, arithmetic and copies ran while one was open for 13% -> 14% of each run, Pallas kernels for 36% -> 39%
where the time goes in v9:
time: 569 us; the launch traced here: 563 us
  Pallas kernels  416 us (73%)
  matrix products  72.2 us (13%)
  waiting for transfers between devices  31.4 us (6%)
  local copies, waits for them, and re-layouts  20.3 us (4%)
  between operations  14.2 us (2%)
  other arithmetic  8.38 us (1%)
    pallas_call x1, Pallas kernels, forward(): pl.pallas_call(functools.partial(forward_kernel, dp, ctx, attend_step(ful...  196 us
    pallas_call x1, Pallas kernels, closing(): pl.pallas_call(functools.partial(closing_kernel, dp, ctx), in_specs=[HBM]...  113 us
    pallas_call x1, Pallas kernels, mix_back(): pl.pallas_call(functools.partial(mix_back_kernel, dp, ctx), in_specs=[vme...  85.5 us
    dot_general x4, matrix products, dot_tn(): lax.dot_general(a, b, (((0,), (0,)), ((), ())), preferred_element_type=f32)  34.2 us
    all_gather x1, waiting for transfers between devices, shards(): down_full = lax.all_gather(down_weight, 'dp', axis=1, tiled=True)  31.3 us
    pallas_call x1, Pallas kernels, attend_back(): pl.pallas_call(functools.partial(attend_back_kernel, step), grid=(pairs,)...  22.2 us
    dot_general x2, matrix products, dot(): return jnp.dot(a, b, preferred_element_type=f32)  19.2 us
    dot_general x2, matrix products, dot_nt(): lax.dot_general(a, b, (((1,), (1,)), ((), ())), preferred_element_type=f32)  18.7 us
  transfers between devices with their start and end apart: 4, of which 1 were waited for; matrix products, arithmetic and copies ran while one was open for 14% of the time, Pallas kernels for 39%

profile of v9, /device:TPU:0, one launch (start us, length us, event | category | flops | bytes accessed | tf_op | source)
XLA Modules:
  0.0 563.2 jit_solution(15485750574704537300)
XLA Ops:
  7.2 0.0 all-gather.2.cloned.1.call-start
  7.2 1.2 broadcast_in_dim.31.bias
  8.4 1.3 convert_reduce_fusion
  9.8 1.0 broadcast_in_dim.32.start_ref
  10.8 195.6 %shard_map.229 = (f32[4,2048]{1,0:T(4,128)}, bf16[2048,1536]{1,0:T(8,128)(2,1)}, bf16[512,2048]{1,0:T(8,128)(2,1)}, bf16[1024,2048]{1,0:T(8,128)(2,1)}, bf16[102...) custom-call(bf16[1,64]{1,0:T(2,128)(2,1)} %bitcast.50, ...), custom_call_target="tpu_custom_call" | custom-call | flops 6442450944 | bytes 419430400 | tf_op jit(solution)/shard_map/pallas_call | solution.py:1445
  206.4 0.0 all-gather.2.cloned.1.call-update
  206.4 0.4 reduce-scatter.4.cloned.1.call-start
  206.8 0.0 copy-start.16
  206.8 0.0 copy-start.17
  206.8 10.6 %fusion.2 = f32[1024,1408]{1,0:T(8,128)S(1)} fusion(bf16[1024,2048]{1,0:T(8,128)(2,1)} %get-tuple-element.48.normed_hbm, bf16[2048,1408]{1,0:T(8,128)(2,1)} %get-tuple-element.49.gate_weight_hbm), kind=kOutput, calls=%fused_computation.17 | convolution fusion | flops 5905580032 | bytes 15728640 | tf_op jit(solution)/shard_map/dot_general | solution.py:24
  217.5 0.0 copy-start.19
  217.5 0.0 copy-done.16
  217.5 0.0 copy-done.17
  217.5 0.0 copy-start.13
  217.5 8.6 %multiply_convert_fusion.2 = (bf16[1024,1408]{1,0:T(8,128)(2,1)S(1)}, f32[1024,1408]{1,0:T(8,128)}) fusion(f32[1024,1408]{1,0:T(8,128)S(1)} %fusion.2, bf16[1024,2048]{1,0:T(8,128)(2,1)S(1)} %copy-done.17, bf16[2048,1408]{1,0:T(8,128)(2,1)S(1)} %copy-done.16), kind=kOutput, calls=%fused_computation.5 | convolution fusion | flops 5914230784 | bytes 24379392 | tf_op jit(solution)/shard_map/dot_general | solution.py:24
  226.1 0.0 copy-done.19
  226.1 0.0 copy-done.13
  226.2 8.1 %convolution_convert_fusion.2 = bf16[1408,2048]{1,0:T(8,128)(2,1)} fusion(bf16[1024,1408]{1,0:T(8,128)(2,1)S(1)} %get-tuple-element.88.inner_hbm, bf16[1024,2048]{1,0:T(8,128)(2,1)S(1)} %copy-done.13), kind=kOutput, calls=%fused_computation.2 | convolution fusion | flops 5908463616 | bytes 12845056 | tf_op jit(solution)/shard_map/dot_general | solution.py:32
  234.3 0.0 copy-done.15
  234.3 0.0 reduce-scatter.4.cloned.1.call-update
  234.3 0.0 reduce-scatter.6.cloned.1.call-start
  234.4 31.3 %all-gather.2.cloned.1.call-done.down_hbm = bf16[1408,2048]{1,0:T(8,128)(2,1)} async-done(((bf16[1408,256]{1,0:T(8,128)(2,1)}), bf16[1408,2048]{1,0:T(8,128)(2,1)}) %all-gather.2.cloned.1.call-update) | async-done | bytes 5767184 | tf_op jit(solution)/shard_map/all_gather | solution.py:1590
  265.7 15.4 %multiply_convert_fusion = (bf16[1024,1408]{1,0:T(8,128)(2,1)}, bf16[1024,1408]{1,0:T(8,128)(2,1)S(1)}) fusion(f32[1024,1408]{1,0:T(8,128)} %copy-done.19, f32[1024,1408]{1,0:T(8,128)} %get-tuple-element.89, bf16[1024,2048]{1,0:T(8,128)(2,1)} %get-tuple-element.51, bf16[1408,2048]{1,0:T(8,128)(2,1)} %all-gather.2.cloned.1.call-done.down_hbm), kind=kOutput, calls=%fused_computation.3 | convolution fusion | flops 5924323328 | bytes 27262976 | tf_op jit(solution)/shard_map/dot_general | solution.py:28
  281.1 0.0 copy-done.18
  281.1 8.6 %convolution_convert_fusion.1 = bf16[2048,1408]{1,0:T(8,128)(2,1)} fusion(bf16[1024,2048]{1,0:T(8,128)(2,1)S(1)} %copy-done.18, bf16[1024,1408]{1,0:T(8,128)(2,1)S(1)} %get-tuple-element.53.gate_ref), kind=kOutput, calls=%fused_computation.1 | convolution fusion | flops 5908463616 | bytes 12845056 | tf_op jit(solution)/shard_map/dot_general | solution.py:32
  289.7 0.0 copy-done.20
  289.7 0.0 reduce-scatter.6.cloned.1.call-update
  289.7 0.2 reduce-scatter.8.cloned.1.call-start
  289.9 0.5 copy-done.9
  290.5 0.6 fusion.1
  291.1 85.5 %shard_map.230 = (f32[256,2048]{1,0:T(8,128)}, f32[2,2048]{1,0:T(2,128)}, bf16[1024,2048]{1,0:T(8,128)(2,1)}, bf16[1024,2048]{1,0:T(8,128)(2,1)}, bf16[2048,1408]{1,0:T(8,128)(2,1)}) custom-call(bf16[1024,1408]{1,0:T(8,128)(2,1)} %copy-done.20, bf16[1024,1408]{1,0:T(8,128)(2,1)} %get-tuple-element.80.up_ref, ...), custom_call_target="tpu_custom_call" | custom-call | flops 23622320128 | bytes 188743680 | tf_op jit(solution)/shard_map/pallas_call | solution.py:545
  376.5 0.0 copy-start.12
  376.5 0.0 reduce-scatter.8.cloned.1.call-update
  376.6 1.2 copy-done.12
  377.8 6.3 %convolution_convert_fusion.3 = bf16[512,2048]{1,0:T(8,128)(2,1)} fusion(bf16[1024,512]{1,0:T(8,128)(2,1)S(1)} %copy-done.12, bf16[1024,2048]{1,0:T(8,128)(2,1)} %get-tuple-element.56), kind=kOutput, calls=%fused_computation.9 | convolution fusion | flops 2148532224 | bytes 7340032 | tf_op jit(solution)/shard_map/dot_general | solution.py:32
  384.1 0.0 copy-done.11
  384.1 0.0 copy-done.14
  384.1 3.3 convolution_convert_fusion.4.grad_ref
  387.4 2.3 convert_element_type.45
  389.7 1.0 copy-done.1
  390.8 1.4 copy-done.2
  392.2 1.3 copy-done.3
  393.4 1.9 copy-done.4
  395.4 1.6 copy-done.5
  397.0 22.2 %shard_map.231 = (bf16[1024,1536]{1,0:T(8,128)(2,1)S(1)}, f32[1,1536]{1,0:T(1,128)S(1)}) custom-call(bf16[1024,1536]{1,0:T(8,128)(2,1)S(1)} %copy-done.4, bf16[1024,512]{1,0:T(8,128)(2,1)S(1)} %copy-done.3, f32[1024,512]{1,0:T(8,128)S(1)} %copy-done.5, f32[3,1024,128]{2,1,0:T(8,128)S(1)} %copy-done.2, s32[1024,128]{1,0:T(8,128)S(1)} %copy-done.1), custom_call_target="tpu_custom_call" | custom-call | flops 6039797760 | bytes 12582912 | tf_op jit(solution)/shard_map/pallas_call | solution.py:1113
  419.2 0.0 copy-start
  419.3 0.1 reshape.40
  419.3 0.1 reshape.41
  419.4 0.8 pad.4.bias_ref
  420.2 11.2 %convolution_convert_fusion = bf16[2048,1536]{1,0:T(8,128)(2,1)} fusion(bf16[1024,2048]{1,0:T(8,128)(2,1)} %get-tuple-element.65, bf16[1024,1536]{1,0:T(8,128)(2,1)S(1)} %get-tuple-element.63.d_joined_hbm), kind=kOutput, calls=%fused_computation | convolution fusion | flops 6445596672 | bytes 13631488 | tf_op jit(solution)/shard_map/dot_general | solution.py:32
  431.4 0.0 copy-done
  431.4 2.3 convert_element_type.46
  433.7 112.8 %shard_map.232 = (f32[256,2048]{1,0:T(8,128)}, f32[64,6144]{1,0:T(8,128)}, f32[64,2048]{1,0:T(8,128)}, bf16[256,2048]{1,0:T(8,128)(2,1)}, f32[4,64]{1,0:T(4,128)}, /*index=5*/f32[1,192]{1,0:T(1,128)}) custom-call(bf16[1024,1536]{1,0:T(8,128)(2,1)} %copy-done, bf16[2048,1536]{1,0:T(8,128)(2,1)} %get-tuple-element.64.weight_hbm, ...), custom_call_target="tpu_custom_call" | custom-call | flops 6442450944 | bytes 209715200 | tf_op jit(solution)/shard_map/pallas_call | solution.py:901
  546.5 0.0 copy-start.6
  546.5 1.4 slice_bitcast_fusion
  547.9 2.4 convert_element_type.49
  550.3 2.3 copy.35
  552.6 0.0 copy-done.6
  552.6 1.3 copy.36
  553.9 0.0 copy-done.7
  553.9 1.1 copy.37
  555.1 0.6 copy.38
  555.6 0.0 copy-done.8
  555.6 0.8 copy.39
  (20 shorter events, 0.1 us)
Async XLA Ops:
  7.2 258.5 %all-gather.2.cloned.1.call-start = ((), (), s32[]{:S(2)}) async-start(), calls=%async_computation.3 | async-start | bytes 6488064 | tf_op jit(solution)/shard_map/all_gather | solution.py:1590
  206.4 181.0 %reduce-scatter.4.cloned.1.call-start = ((), (), s32[]{:S(2)}) async-start(), calls=%async_computation.4 | async-start | bytes 6488064 | tf_op jit(solution)/shard_map/reduce_scatter | solution.py:1599
  206.8 10.6 %copy-start.16 = (bf16[2048,1408]{1,0:T(8,128)(2,1)S(1)}, bf16[2048,1408]{1,0:T(8,128)(2,1)}, u32[]{:S(2)}) copy-start(bf16[2048,1408]{1,0:T(8,128)(2,1)} %get-tuple-element.50.up_weight_hbm) | copy-start | bytes 17301508
  206.8 10.6 %copy-start.17 = (bf16[1024,2048]{1,0:T(8,128)(2,1)S(1)}, bf16[1024,2048]{1,0:T(8,128)(2,1)}, u32[]{:S(2)}) copy-start(bf16[1024,2048]{1,0:T(8,128)(2,1)} %get-tuple-element.48.normed_hbm) | copy-start | bytes 12582916
  217.5 8.7 %copy-start.19 = (f32[1024,1408]{1,0:T(8,128)}, f32[1024,1408]{1,0:T(8,128)S(1)}, u32[]{:S(2)}) copy-start(f32[1024,1408]{1,0:T(8,128)S(1)} %fusion.2) | copy-start | bytes 17301508
  217.5 8.7 %copy-start.13 = (bf16[1024,2048]{1,0:T(8,128)(2,1)S(1)}, bf16[1024,2048]{1,0:T(8,128)(2,1)}, u32[]{:S(2)}) copy-start(bf16[1024,2048]{1,0:T(8,128)(2,1)} %get-tuple-element.51) | copy-start | bytes 12582916
  226.1 8.2 %copy-start.15 = (bf16[1024,1408]{1,0:T(8,128)(2,1)}, bf16[1024,1408]{1,0:T(8,128)(2,1)S(1)}, u32[]{:S(2)}) copy-start(bf16[1024,1408]{1,0:T(8,128)(2,1)S(1)} %get-tuple-element.88.inner_hbm) | copy-start | bytes 8650756
  234.3 197.1 %reduce-scatter.6.cloned.1.call-start = ((), (), s32[]{:S(2)}) async-start(), calls=%async_computation.5 | async-start | bytes 6488064 | tf_op jit(solution)/shard_map/reduce_scatter | solution.py:1605
  265.7 15.4 %copy-start.18 = (bf16[1024,2048]{1,0:T(8,128)(2,1)S(1)}, bf16[1024,2048]{1,0:T(8,128)(2,1)}, u32[]{:S(2)}) copy-start(bf16[1024,2048]{1,0:T(8,128)(2,1)} %get-tuple-element.48.normed_hbm) | copy-start | bytes 12582916
  281.1 8.6 %copy-start.20 = (bf16[1024,1408]{1,0:T(8,128)(2,1)}, bf16[1024,1408]{1,0:T(8,128)(2,1)S(1)}, u32[]{:S(2)}) copy-start(bf16[1024,1408]{1,0:T(8,128)(2,1)S(1)} %get-tuple-element.53.gate_ref) | copy-start | bytes 8650756
  289.7 0.8 copy-start.9
  289.7 258.1 %reduce-scatter.8.cloned.1.call-start = ((), (), s32[]{:S(2)}) async-start(), calls=%async_computation.6 | async-start | bytes 6488064 | tf_op jit(solution)/shard_map/reduce_scatter | solution.py:1618
  376.5 1.3 copy-start.12
  377.8 6.3 %copy-start.11 = (bf16[1024,2048]{1,0:T(8,128)(2,1)S(1)}, bf16[1024,2048]{1,0:T(8,128)(2,1)}, u32[]{:S(2)}) copy-start(bf16[1024,2048]{1,0:T(8,128)(2,1)} %get-tuple-element.56) | copy-start | bytes 12582916
  377.8 6.3 %copy-start.14 = (bf16[512,2048]{1,0:T(8,128)(2,1)S(1)}, bf16[512,2048]{1,0:T(8,128)(2,1)}, u32[]{:S(2)}) copy-start(bf16[512,2048]{1,0:T(8,128)(2,1)} %get-tuple-element.57) | copy-start | bytes 6291460
  389.7 1.0 copy-start.1
  390.8 1.4 copy-start.2
  392.2 1.3 copy-start.3
  393.4 2.0 copy-start.4
  395.4 1.6 copy-start.5
  419.2 12.2 %copy-start = (bf16[1024,1536]{1,0:T(8,128)(2,1)}, bf16[1024,1536]{1,0:T(8,128)(2,1)S(1)}, u32[]{:S(2)}) copy-start(bf16[1024,1536]{1,0:T(8,128)(2,1)S(1)} %get-tuple-element.63.d_joined_hbm) | copy-start | bytes 9437188
  546.5 6.1 %copy-start.6 = (f32[256,2048]{1,0:T(8,128)S(1)}, f32[256,2048]{1,0:T(8,128)}, u32[]{:S(2)}) copy-start(f32[256,2048]{1,0:T(8,128)} %get-tuple-element.72) | copy-start | bytes 6291460
  547.9 6.1 %copy-start.7 = (f32[64,6144]{1,0:T(8,128)S(1)}, f32[64,6144]{1,0:T(8,128)}, u32[]{:S(2)}) copy-start(f32[64,6144]{1,0:T(8,128)} %get-tuple-element.106) | copy-start | bytes 4718596
  552.6 2.5 copy-start.10
  552.6 3.0 copy-start.8
Sparse Core Ops, SparseCore 0:
  206.5 59.1 all-gather.1
  268.0 63.0 reduce-scatter.3
  333.4 63.1 reduce-scatter.5
  398.8 78.3 reduce-scatter.7

commit v10 on v9

--- a/solution.py
+++ b/solution.py
@@ -439,28 +439,131 @@
     return ref[pl.ds(pl.multiple_of(col * size, size), size), :]
 
 
+class LineReduce:
+    def __init__(self, place, parts, own, pair, got, sems):
+        self.place, self.parts, self.own, self.pair, self.got, self.sems = place, parts, own, pair, got, sems
+
+    def load(self, line):
+        return pltpu.make_async_copy(
+            self.parts.at[2 * line + self.place.core], self.own.at[line], self.sems.at[6, line]
+        )
+
+    def swap(self, line):
+        row = 2 * line + 1 - self.place.core
+        return remote(
+            self.parts.at[row], self.pair.at[line], self.sems.at[0, line], self.sems.at[1, line], self.place.twin
+        )
+
+    def start(self):
+        for line in range(self.place.lines):
+            self.swap(line).start()
+
+    def add(self):
+        for line in range(self.place.lines):
+            self.load(line).wait()
+            self.swap(line).wait_recv()
+            self.pair[line] = (self.own[line].astype(f32) + self.pair[line].astype(f32)).astype(bf16)
+
+    def up(self, far):
+        part = self.place.line + far
+        return remote(
+            self.pair.at[part], self.got.at[part], self.sems.at[2, far], self.sems.at[3, far], self.place.above()
+        )
+
+    def down(self, far):
+        part = self.place.line - far
+        slot = part if far > 1 else self.place.lines
+        return remote(
+            self.pair.at[part], self.got.at[slot], self.sems.at[4, far], self.sems.at[5, far], self.place.below()
+        )
+
+    def came_up(self, far):
+        slot = self.got.at[self.place.line + far]
+        remote(slot, slot, self.sems.at[2, far + 1], self.sems.at[3, far + 1], self.place.twin).wait_recv()
+
+    def came_down(self, far):
+        slot = self.got.at[self.place.line - far if far else self.place.lines]
+        remote(slot, slot, self.sems.at[4, far + 1], self.sems.at[5, far + 1], self.place.twin).wait_recv()
+
+    def send(self, far):
+        place = self.place
+
+        @pl.when(place.line + far < place.lines)
+        def _():
+            @pl.when(place.line > 0)
+            def _():
+                self.came_up(far)
+                part = place.line + far
+                self.pair[part] = (self.pair[part].astype(f32) + self.got[part].astype(f32)).astype(bf16)
+
+            self.up(far).start()
+
+        @pl.when(place.line - far >= 0)
+        def _():
+            @pl.when(place.line < place.lines - 1)
+            def _():
+                self.came_down(far)
+                part = place.line - far
+                self.pair[part] = (self.pair[part].astype(f32) + self.got[part].astype(f32)).astype(bf16)
+
+            self.down(far).start()
+
+    def collect(self, out):
+        place = self.place
+        out[...] = self.pair[place.line].astype(f32)
+
+        @pl.when(place.line > 0)
+        def _():
+            self.came_up(0)
+            out[...] += self.got[place.line].astype(f32)
+
+        @pl.when(place.line < place.lines - 1)
+        def _():
+            self.came_down(0)
+            out[...] += self.got[place.lines].astype(f32)
+
+    def finish(self):
+        place = self.place
+        for line in range(place.lines):
+            self.swap(line).wait_send()
+        for far in range(1, place.lines):
+            pl.when(place.line + far < place.lines)(lambda: self.up(far).wait_send())
+            pl.when(place.line - far >= 0)(lambda: self.down(far).wait_send())
+
+    @staticmethod
+    def scratch(dp, tile):
+        return [
+            pltpu.VMEM((dp // 2,) + tile, bf16),
+            pltpu.VMEM((dp // 2,) + tile, bf16),
+            pltpu.VMEM((dp // 2 + 1,) + tile, bf16),
+            pltpu.SemaphoreType.DMA((7, dp // 2)),
+        ]
+
+
 def mix_back_kernel(
-    dp, ctx, gate_ref, up_ref, gate_weight_hbm, up_weight_hbm, inner_hbm, down_hbm, normed_hbm,
+    dp, ctx, gate_ref, up_ref, gate_weight_hbm, up_weight_hbm, inner_hbm, down_hbm, normed_hbm, gate_parts,
     resid_ref, cot_ref, gain_ref,
-    d_resid_hbm, sums_ref, wide_ref, branch_hbm, d_up_hbm,
-    total, sent, got, made, d_resid_ref, gate_weight_ref, up_weight_ref, inner_ref, down_ref, normed_ref, branch, d_up,
-    reduce_sem, spread_sem, load_sem, branch_sem, d_up_sem, d_resid_sem,
+    d_resid_hbm, sums_ref, wide_ref, branch_hbm, d_up_hbm, d_gate_ref,
+    total, sent, got, made, gate_weight_ref, up_weight_ref, inner, down_ref, normed, branch, d_up,
+    own, pair, line_got, line_sem,
+    reduce_sem, spread_sem, load_sem, inner_sem, normed_sem, branch_sem, d_up_sem, d_resid_sem,
 ):
     place = Place(dp)
+    size, width = cot_ref.shape
+    cols = normed.shape[2]
     loads = [
         pltpu.make_async_copy(src, dst, load_sem.at[i])
         for i, (src, dst) in enumerate(
-            (
-                (gate_weight_hbm, gate_weight_ref), (up_weight_hbm, up_weight_ref), (normed_hbm, normed_ref),
-                (inner_hbm, inner_ref), (down_hbm, down_ref),
-            )
+            ((gate_weight_hbm, gate_weight_ref), (up_weight_hbm, up_weight_ref), (down_hbm, down_ref))
         )
     ]
     for load in loads[:2]:
         load.start()
-    greet(place, ctx)
-    size, width = cot_ref.shape
-    cols = width // ctx // 2
+    greet_all(place, dp, ctx)
+    line = LineReduce(place, gate_parts, own, pair, line_got, line_sem)
+    line.start()
+    for i in range(place.lines):
+        line.load(i).start()
     for load in loads[:2]:
         load.wait()
 
@@ -469,6 +572,18 @@
             rows_of(up_ref, col, size), up_weight_ref[...]
         )
 
+    d_up_count, branch_count = width // cols, ctx
+
+    def normed_load(i):
+        return pltpu.make_async_copy(
+            normed_hbm.at[:, pl.ds(i * cols, cols)], normed.at[i % 2], normed_sem.at[i % 2]
+        )
+
+    def inner_load(i):
+        return pltpu.make_async_copy(
+            inner_hbm.at[pl.ds(i * size, size), :], inner.at[i % 2], inner_sem.at[i % 2]
+        )
+
     def d_up_copy(i):
         return pltpu.make_async_copy(
             d_up.at[i % 2], d_up_hbm.at[pl.ds(i * cols, cols), :], d_up_sem.at[i % 2]
@@ -480,36 +595,45 @@
         )
 
     def d_up_piece(i):
+        normed_load(i).wait()
+        if i > 1:
+            d_up_copy(i - 2).wait()
+        d_up[i % 2] = dot_tn(normed[i % 2], up_ref[...]).astype(bf16)
+        d_up_copy(i).start()
+        if i + 2 < d_up_count:
+            normed_load(i + 2).start()
+
+    def branch_piece(i):
         if i == 0:
             loads[2].wait()
-        if i > 1:
-            d_up_copy(i - 2).wait()
-        d_up[i % 2] = dot_tn(normed_ref[:, i * cols : (i + 1) * cols], up_ref[...]).astype(bf16)
-        d_up_copy(i).start()
-
-    def branch_piece(i):
-        if i == 0:
-            loads[3].wait()
-            loads[4].wait()
+        inner_load(i).wait()
         if i > 1:
             branch_copy(i - 2).wait()
-        branch[i % 2] = dot(inner_ref[i * size : (i + 1) * size, :], down_ref[...]).astype(bf16)
+        branch[i % 2] = dot(inner[i % 2], down_ref[...]).astype(bf16)
         branch_copy(i).start()
+        if i + 2 < branch_count:
+            inner_load(i + 2).start()
 
     def d_resid_copy(j):
         rows = reduce.chunk(j)
-        return pltpu.make_async_copy(d_resid_ref.at[rows, :], d_resid_hbm.at[rows, :], d_resid_sem.at[j])
-
-    pieces = [functools.partial(d_up_piece, i) for i in range(2 * ctx)]
-    pieces += [functools.partial(branch_piece, i) for i in range(ctx)]
+        return pltpu.make_async_copy(total.at[1, rows, :], d_resid_hbm.at[rows, :], d_resid_sem.at[j])
+
+    pieces = [functools.partial(d_up_piece, i) for i in range(d_up_count)]
+    pieces += [functools.partial(branch_piece, i) for i in range(branch_count)]
 
     reduce = CtxReduce(place, block, total, sent, got, reduce_sem)
     spread = CtxSpread(place, made, wide_ref, spread_sem)
-    reduce.start()
-    for load in loads[2:]:
-        load.start()
+    reduce.start_far()
+    loads[2].start()
+    for i in range(2):
+        normed_load(i).start()
+        inner_load(i).start()
+    reduce.start_near()
+    line.add()
+    line.send(place.lines - 1)
     reduce.relay()
     sums_ref[...] = jnp.zeros_like(sums_ref)
+    far = place.lines - 2
     for j in range(CHUNKS):
         for piece in pieces[2 * j : 2 * j + 2]:
             piece()
@@ -519,166 +643,83 @@
         sums_ref[0:1, :] += d_gain[None]
         sums_ref[1:2, :] += d_shift[None]
         grad = cot_ref[rows, :].astype(f32) + grad
-        d_resid_ref[rows, :] = grad
+        total[1, rows, :] = grad
         d_resid_copy(j).start()
         made[rows, :] = grad.astype(bf16)
         spread.send(j)
         if j:
             spread.relay(j - 1)
+        if j == 1 and far > 0:
+            line.send(far)
+            far -= 1
     pieces[2 * CHUNKS]()
     spread.relay(CHUNKS - 1)
+    while far > 0:
+        line.send(far)
+        far -= 1
     for piece in pieces[2 * CHUNKS + 1 :]:
         piece()
     spread.finish()
+    line.collect(d_gate_ref)
+    line.finish()
     reduce.finish()
     for i in (1, 2):
-        d_up_copy(2 * ctx - i).wait()
-        branch_copy(ctx - i).wait()
+        d_up_copy(d_up_count - i).wait()
+        branch_copy(branch_count - i).wait()
     for j in range(CHUNKS):
         d_resid_copy(j).wait()
 
 
-def mix_back(dp, ctx, d_gate, d_up, gate_weight, up_weight, inner, down, normed, resid, cot, gain):
+def mix_back(dp, ctx, d_gate, d_up, gate_weight, up_weight, inner, down, normed, gate_parts, resid, cot, gain):
     size, width = cot.shape
     hidden = d_up.shape[1]
+    own = width // dp
+    cols = width // ctx // 2
     vmem = pl.BlockSpec(memory_space=pltpu.VMEM)
     return pl.pallas_call(
         functools.partial(mix_back_kernel, dp, ctx),
-        in_specs=[vmem] * 2 + [HBM] * 5 + [vmem] * 3,
-        out_specs=[HBM, vmem, HBM, HBM, HBM],
+        in_specs=[vmem] * 2 + [HBM] * 6 + [vmem] * 3,
+        out_specs=[HBM, vmem, HBM, HBM, HBM, vmem],
         out_shape=[
             jax.ShapeDtypeStruct((size, width), f32),
             jax.ShapeDtypeStruct((2, width), f32),
             jax.ShapeDtypeStruct((ctx * size, width), bf16),
             jax.ShapeDtypeStruct((ctx * size, width), bf16),
             jax.ShapeDtypeStruct((width, hidden), bf16),
+            jax.ShapeDtypeStruct((own, hidden), f32),
         ],
         scratch_shapes=CtxReduce.scratch(size, width)[:3]
         + [
             pltpu.VMEM((size, width), bf16),
-            pltpu.VMEM((size, width), f32),
             pltpu.VMEM((width, hidden), bf16),
             pltpu.VMEM((width, hidden), bf16),
-            pltpu.VMEM((ctx * size, hidden), bf16),
+            pltpu.VMEM((2, size, hidden), bf16),
             pltpu.VMEM((hidden, width), bf16),
-            pltpu.VMEM((ctx * size, width), bf16),
+            pltpu.VMEM((2, ctx * size, cols), bf16),
             pltpu.VMEM((2, size, width), bf16),
-            pltpu.VMEM((2, width // ctx // 2, hidden), bf16),
+            pltpu.VMEM((2, cols, hidden), bf16),
+        ]
+        + LineReduce.scratch(dp, (own, hidden))
+        + [
             CtxReduce.scratch(size, width)[3],
             CtxSpread.scratch(),
-            pltpu.SemaphoreType.DMA((5,)),
+            pltpu.SemaphoreType.DMA((3,)),
+            pltpu.SemaphoreType.DMA((2,)),
+            pltpu.SemaphoreType.DMA((2,)),
             pltpu.SemaphoreType.DMA((2,)),
             pltpu.SemaphoreType.DMA((2,)),
             pltpu.SemaphoreType.DMA((CHUNKS,)),
         ],
         compiler_params=pltpu.CompilerParams(
-            collective_id=3, has_side_effects=True, vmem_limit_bytes=60 << 20
+            collective_id=3, has_side_effects=True, vmem_limit_bytes=62 << 20
         ),
         cost_estimate=pl.CostEstimate(
             flops=8 * d_gate.size * width, transcendentals=0, bytes_accessed=180 << 20
         ),
-    )(d_gate, d_up, gate_weight, up_weight, inner, down, normed, resid, cot, gain.reshape(1, width))
-
-
-class LineReduce:
-    def __init__(self, place, parts, own, pair, got, sems):
-        self.place, self.parts, self.own, self.pair, self.got, self.sems = place, parts, own, pair, got, sems
-
-    def load(self, line):
-        return pltpu.make_async_copy(
-            self.parts.at[2 * line + self.place.core], self.own.at[line], self.sems.at[6, line]
-        )
-
-    def swap(self, line):
-        row = 2 * line + 1 - self.place.core
-        return remote(
-            self.parts.at[row], self.pair.at[line], self.sems.at[0, line], self.sems.at[1, line], self.place.twin
-        )
-
-    def start(self):
-        for line in range(self.place.lines):
-            self.swap(line).start()
-
-    def add(self):
-        for line in range(self.place.lines):
-            self.load(line).wait()
-            self.swap(line).wait_recv()
-            self.pair[line] = (self.own[line].astype(f32) + self.pair[line].astype(f32)).astype(bf16)
-
-    def up(self, far):
-        part = self.place.line + far
-        return remote(
-            self.pair.at[part], self.got.at[part], self.sems.at[2, far], self.sems.at[3, far], self.place.above()
-        )
-
-    def down(self, far):
-        part = self.place.line - far
-        slot = part if far > 1 else self.place.lines
-        return remote(
-            self.pair.at[part], self.got.at[slot], self.sems.at[4, far], self.sems.at[5, far], self.place.below()
-        )
-
-    def came_up(self, far):
-        slot = self.got.at[self.place.line + far]
-        remote(slot, slot, self.sems.at[2, far + 1], self.sems.at[3, far + 1], self.place.twin).wait_recv()
-
-    def came_down(self, far):
-        slot = self.got.at[self.place.line - far if far else self.place.lines]
-        remote(slot, slot, self.sems.at[4, far + 1], self.sems.at[5, far + 1], self.place.twin).wait_recv()
-
-    def send(self, far):
-        place = self.place
-
-        @pl.when(place.line + far < place.lines)
-        def _():
-            @pl.when(place.line > 0)
-            def _():
-                self.came_up(far)
-                part = place.line + far
-                self.pair[part] = (self.pair[part].astype(f32) + self.got[part].astype(f32)).astype(bf16)
-
-            self.up(far).start()
-
-        @pl.when(place.line - far >= 0)
-        def _():
-            @pl.when(place.line < place.lines - 1)
-            def _():
-                self.came_down(far)
-                part = place.line - far
-                self.pair[part] = (self.pair[part].astype(f32) + self.got[part].astype(f32)).astype(bf16)
-
-            self.down(far).start()
-
-    def collect(self, out):
-        place = self.place
-        out[...] = self.pair[place.line].astype(f32)
-
-        @pl.when(place.line > 0)
-        def _():
-            self.came_up(0)
-            out[...] += self.got[place.line].astype(f32)
-
-        @pl.when(place.line < place.lines - 1)
-        def _():
-            self.came_down(0)
-            out[...] += self.got[place.lines].astype(f32)
-
-    def finish(self):
-        place = self.place
-        for line in range(place.lines):
-            self.swap(line).wait_send()
-        for far in range(1, place.lines):
-            pl.when(place.line + far < place.lines)(lambda: self.up(far).wait_send())
-            pl.when(place.line - far >= 0)(lambda: self.down(far).wait_send())
-
-    @staticmethod
-    def scratch(dp, tile):
-        return [
-            pltpu.VMEM((dp // 2,) + tile, bf16),
-            pltpu.VMEM((dp // 2,) + tile, bf16),
-            pltpu.VMEM((dp // 2 + 1,) + tile, bf16),
-            pltpu.SemaphoreType.DMA((7, dp // 2)),
-        ]
+    )(
+        d_gate, d_up, gate_weight, up_weight, inner, down, normed, gate_parts.reshape(dp, own, hidden),
+        resid, cot, gain.reshape(1, width),
+    )
 
 
 class CtxReduceReady:
@@ -1124,7 +1165,7 @@
         cost_estimate=pl.CostEstimate(
             flops=pairs * seen * PAIR * 20, transcendentals=pairs * seen * 2, bytes_accessed=full_len * width * 8
         ),
-    )(qkv, grad, lse, table, start)
+    )(*[pltpu.with_memory_space_constraint(x, pltpu.HBM) for x in (qkv, grad, lse, table, start)])
 
 
 def forward_kernel(
@@ -1601,14 +1642,13 @@
     d_gate = (d_inner * upward * sigma * (1.0 + gate * (1.0 - sigma))).astype(bf16)
     d_upward = (d_inner * swish).astype(bf16)
     d_gate_weight = dot_tn(normed_wide, d_gate).astype(bf16)
-    d_gate_ready, d_gate_weight = lax.optimization_barrier((d_gate, d_gate_weight))
-    d_gate_weight = lax.psum_scatter(d_gate_weight, "dp", scatter_dimension=0, tiled=True).astype(f32)
     if fused:
-        d_resid, sums_two, d_proj, branch, d_up_weight = mix_back(
-            dp, ctx, d_gate_ready, d_upward, gate_full, up_full, inner, down_full, normed_wide, resid,
+        d_resid, sums_two, d_proj, branch, d_up_weight, d_gate_weight = mix_back(
+            dp, ctx, d_gate, d_upward, gate_full, up_full, inner, down_full, normed_wide, d_gate_weight, resid,
             grad_rows, gain_two,
         )
     else:
+        d_gate_weight = lax.psum_scatter(d_gate_weight, "dp", scatter_dimension=0, tiled=True).astype(f32)
         branch = dot(inner, down_full)
         d_up_weight = dot_tn(normed_wide, d_upward).astype(bf16)
         d_normed_two = scatter_ctx(dot_nt(d_gate, gate_full) + dot_nt(d_upward, up_full), ctx)
@@ -1623,7 +1663,6 @@
     d_joined, d_bias = attend_back(qkv, d_attended, lse, table, start)
     d_joined_weight = dot_tn(normed_one, d_joined).astype(bf16)
     d_bias = d_bias.reshape(pairs, 3, 2, HD).transpose(1, 0, 2, 3)
-    d_joined, d_gate_weight = lax.optimization_barrier((d_joined, d_gate_weight))
     if fused:
         d_bias = jnp.pad(d_bias.reshape(dp, -1), ((0, 0), (0, width // dp - near * 3 * HD // dp)))
         grad_input, d_joined_weight, d_out_weight, output, vectors, d_bias = closing(

time: 569 us -> 564 us (level)
    pallas_call x1, Pallas kernels: 85.5 us -> 93.7 us  [mix_back(): pl.pallas_call(functools.partial(mix_back_kernel, dp, ctx), in_specs=[vme...]
    unnamed x47 -> x42, local copies, waits for them, and re-layouts: 15.2 us -> 10.6 us
  transfers between devices with their start and end apart: 4 -> 3, of which waited for: 1 -> 1; matrix products, arithmetic and copies ran while one was open for 14% -> 14% of each run, Pallas kernels for 39% -> 40%
where the time goes in v10:
time: 564 us; the launch traced here: 558 us
  Pallas kernels  421 us (75%)
  matrix products  72.1 us (13%)
  waiting for transfers between devices  28.7 us (5%)
  local copies, waits for them, and re-layouts  15.7 us (3%)
  between operations  14.4 us (3%)
  other arithmetic  6.08 us (1%)
    pallas_call x1, Pallas kernels, forward(): pl.pallas_call(functools.partial(forward_kernel, dp, ctx, attend_step(ful...  196 us
    pallas_call x1, Pallas kernels, closing(): pl.pallas_call(functools.partial(closing_kernel, dp, ctx), in_specs=[HBM]...  108 us
    pallas_call x1, Pallas kernels, mix_back(): pl.pallas_call(functools.partial(mix_back_kernel, dp, ctx), in_specs=[vme...  93.7 us
    dot_general x4, matrix products, dot_tn(): lax.dot_general(a, b, (((0,), (0,)), ((), ())), preferred_element_type=f32)  34.1 us
    all_gather x1, waiting for transfers between devices, shards(): down_full = lax.all_gather(down_weight, 'dp', axis=1, tiled=True)  28.6 us
    pallas_call x1, Pallas kernels, attend_back(): pl.pallas_call(functools.partial(attend_back_kernel, step), grid=(pairs,)...  23.8 us
    dot_general x2, matrix products, dot(): return jnp.dot(a, b, preferred_element_type=f32)  19.3 us
    dot_general x2, matrix products, dot_nt(): lax.dot_general(a, b, (((1,), (1,)), ((), ())), preferred_element_type=f32)  18.7 us
  transfers between devices with their start and end apart: 3, of which 1 were waited for; matrix products, arithmetic and copies ran while one was open for 14% of the time, Pallas kernels for 40%

profile of v10, /device:TPU:0, one launch (start us, length us, event | category | flops | bytes accessed | tf_op | source)
XLA Modules:
  0.0 558.3 jit_solution(9069837185802268310)
XLA Ops:
  7.2 0.0 all-gather.2.cloned.1.call-start
  7.2 1.2 broadcast_in_dim.31.bias
  8.4 1.3 convert_reduce_fusion
  9.8 1.0 broadcast_in_dim.32.start_ref
  10.8 195.6 %shard_map.229 = (f32[4,2048]{1,0:T(4,128)}, bf16[2048,1536]{1,0:T(8,128)(2,1)}, bf16[512,2048]{1,0:T(8,128)(2,1)}, bf16[1024,2048]{1,0:T(8,128)(2,1)}, bf16[102...) custom-call(bf16[1,64]{1,0:T(2,128)(2,1)} %bitcast.51, ...), custom_call_target="tpu_custom_call" | custom-call | flops 6442450944 | bytes 419430400 | tf_op jit(solution)/shard_map/pallas_call | solution.py:1486
  206.3 0.0 slice-start
  206.3 0.0 all-gather.2.cloned.1.call-update
  206.4 0.2 reduce-scatter.3.cloned.1.call-start
  206.6 0.0 slice-start.1
  206.6 0.0 copy-start.12
  206.6 10.6 %fusion.2 = f32[1024,1408]{1,0:T(8,128)S(1)} fusion(bf16[1024,2048]{1,0:T(8,128)(2,1)} %get-tuple-element.45.normed_hbm, bf16[2048,1408]{1,0:T(8,128)(2,1)} %get-tuple-element.46.gate_weight_hbm), kind=kOutput, calls=%fused_computation.17 | convolution fusion | flops 5905580032 | bytes 15728640 | tf_op jit(solution)/shard_map/dot_general | solution.py:24
  217.2 0.0 copy-start.14
  217.2 0.0 slice-done
  217.2 0.0 slice-done.1
  217.2 0.0 copy-done.12
  217.3 0.0 copy-start.9
  217.3 8.7 %multiply_convert_fusion.2 = (bf16[1024,1408]{1,0:T(8,128)(2,1)S(1)}, f32[1024,1408]{1,0:T(8,128)}) fusion(f32[1024,1408]{1,0:T(8,128)S(1)} %fusion.2, bf16[1024,2048]{1,0:T(8,128)(2,1)S(1)} %copy-done.12, bf16[2048,1408]{1,0:T(8,128)(2,1)S(1)} %bitcast.57), kind=kOutput, calls=%fused_computation.5 | convolution fusion | flops 5914230784 | bytes 24379392 | tf_op jit(solution)/shard_map/dot_general | solution.py:24
  225.9 0.0 copy-done.14
  225.9 0.0 copy-start.11
  226.0 1.6 copy-done.11
  227.6 0.0 copy-done.9
  227.6 8.1 %convolution_convert_fusion.2 = bf16[1408,2048]{1,0:T(8,128)(2,1)} fusion(bf16[1024,1408]{1,0:T(8,128)(2,1)S(1)} %get-tuple-element.82.inner_hbm, bf16[1024,2048]{1,0:T(8,128)(2,1)S(1)} %copy-done.9), kind=kOutput, calls=%fused_computation.2 | convolution fusion | flops 5908463616 | bytes 12845056 | tf_op jit(solution)/shard_map/dot_general | solution.py:32
  235.7 0.0 copy-start.5
  235.7 0.0 reduce-scatter.3.cloned.1.call-update
  235.7 0.3 reduce-scatter.5.cloned.1.call-start
  236.0 0.5 copy-done.5
  236.4 0.6 fusion.1
  237.0 28.6 %all-gather.2.cloned.1.call-done.down_hbm = bf16[1408,2048]{1,0:T(8,128)(2,1)} async-done(((bf16[1408,256]{1,0:T(8,128)(2,1)}), bf16[1408,2048]{1,0:T(8,128)(2,1)}) %all-gather.2.cloned.1.call-update) | async-done | bytes 5767184 | tf_op jit(solution)/shard_map/all_gather | solution.py:1631
  265.7 0.0 copy-start.13
  265.7 15.4 %multiply_convert_fusion = (bf16[1024,1408]{1,0:T(8,128)(2,1)}, bf16[1024,1408]{1,0:T(8,128)(2,1)S(1)}) fusion(f32[1024,1408]{1,0:T(8,128)} %copy-done.14, f32[1024,1408]{1,0:T(8,128)} %get-tuple-element.83, bf16[1024,2048]{1,0:T(8,128)(2,1)} %get-tuple-element.48, bf16[1408,2048]{1,0:T(8,128)(2,1)} %all-gather.2.cloned.1.call-done.down_hbm), kind=kOutput, calls=%fused_computation.3 | convolution fusion | flops 5924323328 | bytes 27262976 | tf_op jit(solution)/shard_map/dot_general | solution.py:28
  281.1 0.0 copy-done.13
  281.1 8.8 %convolution_convert_fusion.1 = bf16[2048,1408]{1,0:T(8,128)(2,1)} fusion(bf16[1024,2048]{1,0:T(8,128)(2,1)S(1)} %copy-done.13, bf16[1024,1408]{1,0:T(8,128)(2,1)S(1)} %get-tuple-element.75.gate_ref), kind=kOutput, calls=%fused_computation.1 | convolution fusion | flops 5908463616 | bytes 12845056 | tf_op jit(solution)/shard_map/dot_general | solution.py:32
  289.8 0.0 copy-done.15
  289.9 93.7 %shard_map.230 = (f32[256,2048]{1,0:T(8,128)}, f32[2,2048]{1,0:T(2,128)}, bf16[1024,2048]{1,0:T(8,128)(2,1)}, bf16[1024,2048]{1,0:T(8,128)(2,1)}, bf16[2048,1408]{1,0:T(8,128)(2,1)}, /*index=5*/f32[256,1408]{1,0:T(8,128)}) custom-call(bf16[1024,1408]{1,0:T(8,128)(2,1)} %copy-done.15, bf16[1024,1408]{1,0:T(8,128)(2,1)} %get-tuple-element.74.up_ref, ...), custom_call_target="tpu_custom_call" | custom-call | flops 23622320128 | bytes 188743680 | tf_op jit(solution)/shard_map/pallas_call | solution.py:679
  383.6 0.0 copy-start.8
  383.6 0.0 reduce-scatter.5.cloned.1.call-update
  383.6 1.2 copy-done.8
  384.8 6.0 %convolution_convert_fusion.3 = bf16[512,2048]{1,0:T(8,128)(2,1)} fusion(bf16[1024,512]{1,0:T(8,128)(2,1)S(1)} %copy-done.8, bf16[1024,2048]{1,0:T(8,128)(2,1)} %get-tuple-element.52), kind=kOutput, calls=%fused_computation.9 | convolution fusion | flops 2148532224 | bytes 7340032 | tf_op jit(solution)/shard_map/dot_general | solution.py:32
  390.9 0.0 copy-done.7
  390.9 0.0 copy-done.10
  390.9 3.3 convolution_convert_fusion.4.grad_ref
  394.2 2.3 convert_element_type.42
  396.5 23.8 %shard_map.231 = (bf16[1024,1536]{1,0:T(8,128)(2,1)S(1)}, f32[1,1536]{1,0:T(1,128)S(1)}) custom-call(bf16[1024,1536]{1,0:T(8,128)(2,1)} %get-tuple-element.43.qkv_ref, bf16[1024,512]{1,0:T(8,128)(2,1)} %convolution_convert_fusion.4.grad_ref, f32[1024,512]{1,0:T(8,128)} %get-tuple-element.56.lse_ref, f32[3,1024,128]{2,1,0:T(8,128)} %constant.8.clone.table_hbm.table_ref, ...), custom_call_target="tpu_custom_call" | custom-call | flops 6039797760 | bytes 12582912 | tf_op jit(solution)/shard_map/pallas_call | solution.py:1154
  420.3 0.0 copy-start
  420.4 0.1 reshape.44
  420.5 0.1 reshape.45
  420.5 0.8 pad.4.bias_ref
  421.4 11.2 %convolution_convert_fusion = bf16[2048,1536]{1,0:T(8,128)(2,1)} fusion(bf16[1024,2048]{1,0:T(8,128)(2,1)} %get-tuple-element.59, bf16[1024,1536]{1,0:T(8,128)(2,1)S(1)} %get-tuple-element.57.d_joined_hbm), kind=kOutput, calls=%fused_computation | convolution fusion | flops 6445596672 | bytes 13631488 | tf_op jit(solution)/shard_map/dot_general | solution.py:32
  432.5 0.0 copy-done
  432.5 107.8 %shard_map.232 = (f32[256,2048]{1,0:T(8,128)}, f32[64,6144]{1,0:T(8,128)}, f32[64,2048]{1,0:T(8,128)}, bf16[256,2048]{1,0:T(8,128)(2,1)}, f32[4,64]{1,0:T(4,128)}, /*index=5*/f32[1,192]{1,0:T(1,128)}) custom-call(bf16[1024,1536]{1,0:T(8,128)(2,1)} %copy-done, bf16[2048,1536]{1,0:T(8,128)(2,1)} %get-tuple-element.58.weight_hbm, ...), custom_call_target="tpu_custom_call" | custom-call | flops 6442450944 | bytes 209715200 | tf_op jit(solution)/shard_map/pallas_call | solution.py:942
  540.3 0.0 copy-start.1
  540.3 1.4 slice_bitcast_fusion
  541.7 2.4 convert_element_type.45
  544.1 2.3 copy.36
  546.4 0.0 copy-done.1
  546.4 1.3 copy.37
  547.8 0.0 copy-done.2
  547.8 1.1 copy.38
  548.9 0.0 copy-done.6
  548.9 0.6 copy.39
  549.5 0.0 copy-done.4
  549.5 0.8 copy.40
  550.3 0.0 copy-done.3
  550.3 1.1 copy.41
  (12 shorter events, 0.0 us)
Async XLA Ops:
  7.2 258.5 %all-gather.2.cloned.1.call-start = ((), (), s32[]{:S(2)}) async-start(), calls=%async_computation.2 | async-start | bytes 6488064 | tf_op jit(solution)/shard_map/all_gather | solution.py:1631
  206.3 10.9 %slice-start = ((s8[5767168]{0:T(1024)(128)(4,1)}), s8[1572864]{0:T(1024)(128)(4,1)S(1)}, s32[]{:S(2)}) async-start(s8[5767168]{0:T(1024)(128)(4,1)} %bitcast.56), calls=%async_computation.5 | async-start | bytes 3145728
  206.4 187.8 %reduce-scatter.3.cloned.1.call-start = ((), (), s32[]{:S(2)}) async-start(), calls=%async_computation.3 | async-start | bytes 6488064 | tf_op jit(solution)/shard_map/reduce_scatter | solution.py:1640
  206.6 10.7 %slice-start.1 = ((s8[5767168]{0:T(1024)(128)(4,1)}), s8[4194304]{0:T(1024)(128)(4,1)S(1)}, s32[]{:S(2)}) async-start(s8[5767168]{0:T(1024)(128)(4,1)} %bitcast.56), calls=%async_computation.6 | async-start | bytes 8388608
  206.6 10.6 %copy-start.12 = (bf16[1024,2048]{1,0:T(8,128)(2,1)S(1)}, bf16[1024,2048]{1,0:T(8,128)(2,1)}, u32[]{:S(2)}) copy-start(bf16[1024,2048]{1,0:T(8,128)(2,1)} %get-tuple-element.45.normed_hbm) | copy-start | bytes 12582916
  217.2 8.7 %copy-start.14 = (f32[1024,1408]{1,0:T(8,128)}, f32[1024,1408]{1,0:T(8,128)S(1)}, u32[]{:S(2)}) copy-start(f32[1024,1408]{1,0:T(8,128)S(1)} %fusion.2) | copy-start | bytes 17301508
  217.3 10.3 %copy-start.9 = (bf16[1024,2048]{1,0:T(8,128)(2,1)S(1)}, bf16[1024,2048]{1,0:T(8,128)(2,1)}, u32[]{:S(2)}) copy-start(bf16[1024,2048]{1,0:T(8,128)(2,1)} %get-tuple-element.48) | copy-start | bytes 12582916
  225.9 1.6 copy-start.11
  235.7 0.8 copy-start.5
  235.7 306.0 %reduce-scatter.5.cloned.1.call-start = ((), (), s32[]{:S(2)}) async-start(), calls=%async_computation.4 | async-start | bytes 6488064 | tf_op jit(solution)/shard_map/reduce_scatter | solution.py:1658
  265.7 15.4 %copy-start.13 = (bf16[1024,2048]{1,0:T(8,128)(2,1)S(1)}, bf16[1024,2048]{1,0:T(8,128)(2,1)}, u32[]{:S(2)}) copy-start(bf16[1024,2048]{1,0:T(8,128)(2,1)} %get-tuple-element.45.normed_hbm) | copy-start | bytes 12582916
  281.1 8.8 %copy-start.15 = (bf16[1024,1408]{1,0:T(8,128)(2,1)}, bf16[1024,1408]{1,0:T(8,128)(2,1)S(1)}, u32[]{:S(2)}) copy-start(bf16[1024,1408]{1,0:T(8,128)(2,1)S(1)} %get-tuple-element.75.gate_ref) | copy-start | bytes 8650756
  383.6 1.2 copy-start.8
  384.8 6.0 %copy-start.7 = (bf16[1024,2048]{1,0:T(8,128)(2,1)S(1)}, bf16[1024,2048]{1,0:T(8,128)(2,1)}, u32[]{:S(2)}) copy-start(bf16[1024,2048]{1,0:T(8,128)(2,1)} %get-tuple-element.52) | copy-start | bytes 12582916
  384.8 6.0 %copy-start.10 = (bf16[512,2048]{1,0:T(8,128)(2,1)S(1)}, bf16[512,2048]{1,0:T(8,128)(2,1)}, u32[]{:S(2)}) copy-start(bf16[512,2048]{1,0:T(8,128)(2,1)} %get-tuple-element.53) | copy-start | bytes 6291460
  420.3 12.2 %copy-start = (bf16[1024,1536]{1,0:T(8,128)(2,1)}, bf16[1024,1536]{1,0:T(8,128)(2,1)S(1)}, u32[]{:S(2)}) copy-start(bf16[1024,1536]{1,0:T(8,128)(2,1)S(1)} %get-tuple-element.57.d_joined_hbm) | copy-start | bytes 9437188
  540.3 6.1 %copy-start.1 = (f32[256,2048]{1,0:T(8,128)S(1)}, f32[256,2048]{1,0:T(8,128)}, u32[]{:S(2)}) copy-start(f32[256,2048]{1,0:T(8,128)} %get-tuple-element.66) | copy-start | bytes 6291460
  541.7 6.1 %copy-start.2 = (f32[64,6144]{1,0:T(8,128)S(1)}, f32[64,6144]{1,0:T(8,128)}, u32[]{:S(2)}) copy-start(f32[64,6144]{1,0:T(8,128)} %get-tuple-element.100) | copy-start | bytes 4718596
  546.4 2.5 copy-start.6
  546.4 3.0 copy-start.4
  546.4 3.8 copy-start.3
Sparse Core Ops, SparseCore 0:
  206.5 59.1 all-gather.1
  268.0 78.6 reduce-scatter.2
  383.8 66.0 reduce-scatter.4

commit v11 on v10

--- a/solution.py
+++ b/solution.py
@@ -541,16 +541,15 @@
 
 
 def mix_back_kernel(
-    dp, ctx, gate_ref, up_ref, gate_weight_hbm, up_weight_hbm, inner_hbm, down_hbm, normed_hbm, gate_parts,
+    dp, ctx, gate_ref, up_ref, gate_weight_hbm, up_weight_hbm, inner_hbm, down_hbm, gate_parts,
     resid_ref, cot_ref, gain_ref,
-    d_resid_hbm, sums_ref, wide_ref, branch_hbm, d_up_hbm, d_gate_ref,
-    total, sent, got, made, gate_weight_ref, up_weight_ref, inner, down_ref, normed, branch, d_up,
+    d_resid_hbm, sums_ref, wide_ref, branch_hbm, d_gate_ref,
+    total, sent, got, made, gate_weight_ref, up_weight_ref, inner, down_ref, branch,
     own, pair, line_got, line_sem,
-    reduce_sem, spread_sem, load_sem, inner_sem, normed_sem, branch_sem, d_up_sem, d_resid_sem,
+    reduce_sem, spread_sem, load_sem, inner_sem, branch_sem, d_resid_sem,
 ):
     place = Place(dp)
     size, width = cot_ref.shape
-    cols = normed.shape[2]
     loads = [
         pltpu.make_async_copy(src, dst, load_sem.at[i])
         for i, (src, dst) in enumerate(
@@ -572,36 +571,17 @@
             rows_of(up_ref, col, size), up_weight_ref[...]
         )
 
-    d_up_count, branch_count = width // cols, ctx
-
-    def normed_load(i):
-        return pltpu.make_async_copy(
-            normed_hbm.at[:, pl.ds(i * cols, cols)], normed.at[i % 2], normed_sem.at[i % 2]
-        )
+    branch_count = ctx
 
     def inner_load(i):
         return pltpu.make_async_copy(
             inner_hbm.at[pl.ds(i * size, size), :], inner.at[i % 2], inner_sem.at[i % 2]
         )
 
-    def d_up_copy(i):
-        return pltpu.make_async_copy(
-            d_up.at[i % 2], d_up_hbm.at[pl.ds(i * cols, cols), :], d_up_sem.at[i % 2]
-        )
-
     def branch_copy(i):
         return pltpu.make_async_copy(
             branch.at[i % 2], branch_hbm.at[pl.ds(i * size, size), :], branch_sem.at[i % 2]
         )
-
-    def d_up_piece(i):
-        normed_load(i).wait()
-        if i > 1:
-            d_up_copy(i - 2).wait()
-        d_up[i % 2] = dot_tn(normed[i % 2], up_ref[...]).astype(bf16)
-        d_up_copy(i).start()
-        if i + 2 < d_up_count:
-            normed_load(i + 2).start()
 
     def branch_piece(i):
         if i == 0:
@@ -618,15 +598,13 @@
         rows = reduce.chunk(j)
         return pltpu.make_async_copy(total.at[1, rows, :], d_resid_hbm.at[rows, :], d_resid_sem.at[j])
 
-    pieces = [functools.partial(d_up_piece, i) for i in range(d_up_count)]
-    pieces += [functools.partial(branch_piece, i) for i in range(branch_count)]
+    pieces = [functools.partial(branch_piece, i) for i in range(branch_count)]
 
     reduce = CtxReduce(place, block, total, sent, got, reduce_sem)
     spread = CtxSpread(place, made, wide_ref, spread_sem)
     reduce.start_far()
     loads[2].start()
     for i in range(2):
-        normed_load(i).start()
         inner_load(i).start()
     reduce.start_near()
     line.add()
@@ -635,7 +613,7 @@
     sums_ref[...] = jnp.zeros_like(sums_ref)
     far = place.lines - 2
     for j in range(CHUNKS):
-        for piece in pieces[2 * j : 2 * j + 2]:
+        for piece in pieces[j : j + 1]:
             piece()
         rows = reduce.chunk(j)
         scaled, inv_std = norm_stats(resid_ref[rows, :])
@@ -652,40 +630,36 @@
         if j == 1 and far > 0:
             line.send(far)
             far -= 1
-    pieces[2 * CHUNKS]()
     spread.relay(CHUNKS - 1)
     while far > 0:
         line.send(far)
         far -= 1
-    for piece in pieces[2 * CHUNKS + 1 :]:
+    for piece in pieces[CHUNKS:]:
         piece()
     spread.finish()
     line.collect(d_gate_ref)
     line.finish()
     reduce.finish()
     for i in (1, 2):
-        d_up_copy(d_up_count - i).wait()
         branch_copy(branch_count - i).wait()
     for j in range(CHUNKS):
         d_resid_copy(j).wait()
 
 
-def mix_back(dp, ctx, d_gate, d_up, gate_weight, up_weight, inner, down, normed, gate_parts, resid, cot, gain):
+def mix_back(dp, ctx, d_gate, d_up, gate_weight, up_weight, inner, down, gate_parts, resid, cot, gain):
     size, width = cot.shape
     hidden = d_up.shape[1]
     own = width // dp
-    cols = width // ctx // 2
     vmem = pl.BlockSpec(memory_space=pltpu.VMEM)
     return pl.pallas_call(
         functools.partial(mix_back_kernel, dp, ctx),
-        in_specs=[vmem] * 2 + [HBM] * 6 + [vmem] * 3,
-        out_specs=[HBM, vmem, HBM, HBM, HBM, vmem],
+        in_specs=[vmem] * 2 + [HBM] * 5 + [vmem] * 3,
+        out_specs=[HBM, vmem, HBM, HBM, vmem],
         out_shape=[
             jax.ShapeDtypeStruct((size, width), f32),
             jax.ShapeDtypeStruct((2, width), f32),
             jax.ShapeDtypeStruct((ctx * size, width), bf16),
             jax.ShapeDtypeStruct((ctx * size, width), bf16),
-            jax.ShapeDtypeStruct((width, hidden), bf16),
             jax.ShapeDtypeStruct((own, hidden), f32),
         ],
         scratch_shapes=CtxReduce.scratch(size, width)[:3]
@@ -695,17 +669,13 @@
             pltpu.VMEM((width, hidden), bf16),
             pltpu.VMEM((2, size, hidden), bf16),
             pltpu.VMEM((hidden, width), bf16),
-            pltpu.VMEM((2, ctx * size, cols), bf16),
             pltpu.VMEM((2, size, width), bf16),
-            pltpu.VMEM((2, cols, hidden), bf16),
         ]
         + LineReduce.scratch(dp, (own, hidden))
         + [
             CtxReduce.scratch(size, width)[3],
             CtxSpread.scratch(),
             pltpu.SemaphoreType.DMA((3,)),
-            pltpu.SemaphoreType.DMA((2,)),
-            pltpu.SemaphoreType.DMA((2,)),
             pltpu.SemaphoreType.DMA((2,)),
             pltpu.SemaphoreType.DMA((2,)),
             pltpu.SemaphoreType.DMA((CHUNKS,)),
@@ -717,7 +687,7 @@
             flops=8 * d_gate.size * width, transcendentals=0, bytes_accessed=180 << 20
         ),
     )(
-        d_gate, d_up, gate_weight, up_weight, inner, down, normed, gate_parts.reshape(dp, own, hidden),
+        d_gate, d_up, gate_weight, up_weight, inner, down, gate_parts.reshape(dp, own, hidden),
         resid, cot, gain.reshape(1, width),
     )
 
@@ -779,11 +749,11 @@
 
 def closing_kernel(
     dp, ctx,
-    d_joined_hbm, weight_hbm, qkv_parts, out_parts, branch_hbm, rows_hbm, d_resid_hbm, resid_hbm,
+    d_joined_hbm, weight_hbm, qkv_parts, branch_hbm, rows_hbm, d_resid_hbm, resid_hbm,
     gain_ref, sums_two_ref, bias_ref,
-    grad_ref, qkv_ref, out_ref, output_ref, vectors_ref, d_bias_ref,
+    grad_ref, qkv_ref, output_ref, vectors_ref, d_bias_ref,
     d_joined_ref, weight_ref, rows_ref, d_resid_ref, resid_ref, load_sem,
-    total, sent, got, reduce_sem, qkv_own, qkv_pair, qkv_got, qkv_sem, out_own, out_pair, out_got, out_sem,
+    total, sent, got, reduce_sem, qkv_own, qkv_pair, qkv_got, qkv_sem,
     have, branch_got, branch_sem, branch_load_sem,
     sums, tiles, tiles_got, small, small_sem, mine, swap_out, swap_in, swap_sem,
 ):
@@ -791,7 +761,6 @@
     me, row = place.col, place.row
     lines = [
         LineReduce(place, qkv_parts, qkv_own, qkv_pair, qkv_got, qkv_sem),
-        LineReduce(place, out_parts, out_own, out_pair, out_got, out_sem),
     ]
     loads = [
         pltpu.make_async_copy(src, dst, load_sem.at[i])
@@ -909,7 +878,6 @@
     for copy in swaps:
         copy.start()
     swap_in[me] = rows_of(swap_out, me, depth)
-    lines[1].collect(out_ref)
     for k in range(1, ctx):
         part = swap_in.at[place.other(k)]
         remote(part, part, swap_sem.at[0, k], swap_sem.at[1, k], place.across(k)).wait_recv()
@@ -932,21 +900,20 @@
     reduce.finish()
 
 
-def closing(dp, ctx, d_joined, weight, d_qkv, d_out, branch, rows, d_resid, resid, gain, sums_two, bias):
+def closing(dp, ctx, d_joined, weight, d_qkv, branch, rows, d_resid, resid, gain, sums_two, bias):
     size, width = rows.shape
     near = weight.shape[1]
-    own, tall = width // dp, d_out.shape[0] // dp
+    own = width // dp
     vmem = pl.BlockSpec(memory_space=pltpu.VMEM)
     reduce_scratch = CtxReduce.scratch(size, width)
     max_peers = max(dp, ctx)
     return pl.pallas_call(
         functools.partial(closing_kernel, dp, ctx),
-        in_specs=[HBM] * 8 + [vmem] * 3,
-        out_specs=[vmem] * 6,
+        in_specs=[HBM] * 7 + [vmem] * 3,
+        out_specs=[vmem] * 5,
         out_shape=[
             jax.ShapeDtypeStruct((size, width), f32),
             jax.ShapeDtypeStruct((own // ctx, 3 * width), f32),
-            jax.ShapeDtypeStruct((tall, width), f32),
             jax.ShapeDtypeStruct((size, width), bf16),
             jax.ShapeDtypeStruct((4, own // ctx), f32),
             jax.ShapeDtypeStruct((1, 3 * own // ctx), f32),
@@ -961,7 +928,6 @@
         ]
         + reduce_scratch
         + LineReduce.scratch(dp, (own, near))
-        + LineReduce.scratch(dp, (tall, width))
         + reduce_scratch[1:]
         + [
             pltpu.SemaphoreType.DMA((3,)),
@@ -982,7 +948,7 @@
             flops=2 * d_joined.size * width, transcendentals=0, bytes_accessed=200 << 20
         ),
     )(
-        d_joined, weight, d_qkv.reshape(dp, own, near), d_out.reshape(dp, tall, width), branch,
+        d_joined, weight, d_qkv.reshape(dp, own, near), branch,
         rows, d_resid, resid, gain.reshape(1, width), sums_two, bias,
     )
 
@@ -1642,31 +1608,34 @@
     d_gate = (d_inner * upward * sigma * (1.0 + gate * (1.0 - sigma))).astype(bf16)
     d_upward = (d_inner * swish).astype(bf16)
     d_gate_weight = dot_tn(normed_wide, d_gate).astype(bf16)
+    d_up_weight = dot_tn(normed_wide, d_upward).astype(bf16)
+    d_upward, d_up_weight = lax.optimization_barrier((d_upward, d_up_weight))
+    d_up_weight = lax.psum_scatter(d_up_weight, "dp", scatter_dimension=0, tiled=True).astype(f32)
     if fused:
-        d_resid, sums_two, d_proj, branch, d_up_weight, d_gate_weight = mix_back(
-            dp, ctx, d_gate, d_upward, gate_full, up_full, inner, down_full, normed_wide, d_gate_weight, resid,
+        d_resid, sums_two, d_proj, branch, d_gate_weight = mix_back(
+            dp, ctx, d_gate, d_upward, gate_full, up_full, inner, down_full, d_gate_weight, resid,
             grad_rows, gain_two,
         )
     else:
         d_gate_weight = lax.psum_scatter(d_gate_weight, "dp", scatter_dimension=0, tiled=True).astype(f32)
         branch = dot(inner, down_full)
-        d_up_weight = dot_tn(normed_wide, d_upward).astype(bf16)
         d_normed_two = scatter_ctx(dot_nt(d_gate, gate_full) + dot_nt(d_upward, up_full), ctx)
         grad, d_gain_two, d_shift_two = norm_backward(d_normed_two, scaled_two, inv_two, gain_two)
         d_resid = grad_rows.astype(f32) + grad
         d_proj = gather_ctx(d_resid.astype(bf16), ctx)
-    d_up_weight = lax.psum_scatter(d_up_weight, "dp", scatter_dimension=0, tiled=True).astype(f32)
 
     d_attended = dot_nt(d_proj, out_full).astype(bf16)
     d_out_weight = dot_tn(attended, d_proj).astype(bf16)
     d_attended, d_down = lax.optimization_barrier((d_attended, d_down))
     d_joined, d_bias = attend_back(qkv, d_attended, lse, table, start)
+    d_joined, d_up_weight, d_out_weight = lax.optimization_barrier((d_joined, d_up_weight, d_out_weight))
     d_joined_weight = dot_tn(normed_one, d_joined).astype(bf16)
     d_bias = d_bias.reshape(pairs, 3, 2, HD).transpose(1, 0, 2, 3)
     if fused:
+        d_out_weight = lax.psum_scatter(d_out_weight, "dp", scatter_dimension=0, tiled=True).astype(f32)
         d_bias = jnp.pad(d_bias.reshape(dp, -1), ((0, 0), (0, width // dp - near * 3 * HD // dp)))
-        grad_input, d_joined_weight, d_out_weight, output, vectors, d_bias = closing(
-            dp, ctx, d_joined, joined_weight, d_joined_weight, d_out_weight, branch, rows, d_resid, resid,
+        grad_input, d_joined_weight, output, vectors, d_bias = closing(
+            dp, ctx, d_joined, joined_weight, d_joined_weight, branch, rows, d_resid, resid,
             gain_one, sums_two, d_bias,
         )
         d_gain_one, d_shift_one, d_gain_two, d_shift_two = vectors

time: 564 us -> 602 us (1.067)
  Pallas kernels: 421 us -> 443 us
  matrix products: 72.1 us -> 84.4 us
    pallas_call x1, Pallas kernels: 93.7 us -> 121 us  [mix_back(): pl.pallas_call(functools.partial(mix_back_kernel, dp, ctx), in_specs=[vme...]
    dot_general x4 -> x5, matrix products: 34.1 us -> 44.6 us  [dot_tn(): lax.dot_general(a, b, (((0,), (0,)), ((), ())), preferred_element_type=f32)]
  transfers between devices with their start and end apart: 3 -> 4, of which waited for: 1 -> 1; matrix products, arithmetic and copies ran while one was open for 14% -> 15% of each run, Pallas kernels for 40% -> 42%
where the time goes in v11:
time: 602 us; the launch traced here: 596 us
  Pallas kernels  443 us (74%)
  matrix products  84.4 us (14%)
  waiting for transfers between devices  29.8 us (5%)
  local copies, waits for them, and re-layouts  15.1 us (3%)
  between operations  14.2 us (2%)
  other arithmetic  8.38 us (1%)
    pallas_call x1, Pallas kernels, forward(): pl.pallas_call(functools.partial(forward_kernel, dp, ctx, attend_step(ful...  196 us
    pallas_call x1, Pallas kernels, mix_back(): pl.pallas_call(functools.partial(mix_back_kernel, dp, ctx), in_specs=[vme...  121 us
    pallas_call x1, Pallas kernels, closing(): pl.pallas_call(functools.partial(closing_kernel, dp, ctx), in_specs=[HBM]...  103 us
    dot_general x5, matrix products, dot_tn(): lax.dot_general(a, b, (((0,), (0,)), ((), ())), preferred_element_type=f32)  44.6 us
    all_gather x1, waiting for transfers between devices, shards(): down_full = lax.all_gather(down_weight, 'dp', axis=1, tiled=True)  29.8 us
    pallas_call x1, Pallas kernels, attend_back(): pl.pallas_call(functools.partial(attend_back_kernel, step), grid=(pairs,)...  23.7 us
    dot_general x2, matrix products, dot_nt(): lax.dot_general(a, b, (((1,), (1,)), ((), ())), preferred_element_type=f32)  20.5 us
    dot_general x2, matrix products, dot(): return jnp.dot(a, b, preferred_element_type=f32)  19.2 us
  transfers between devices with their start and end apart: 4, of which 1 were waited for; matrix products, arithmetic and copies ran while one was open for 15% of the time, Pallas kernels for 42%

profile of v11, /device:TPU:0, one launch (start us, length us, event | category | flops | bytes accessed | tf_op | source)
XLA Modules:
  0.0 596.0 jit_solution(13126750364060922060)
XLA Ops:
  7.2 0.0 all-gather.2.cloned.1.call-start
  7.2 1.2 broadcast_in_dim.31.bias
  8.4 1.3 convert_reduce_fusion
  9.8 1.0 broadcast_in_dim.32.start_ref
  10.8 195.6 %shard_map.229 = (f32[4,2048]{1,0:T(4,128)}, bf16[2048,1536]{1,0:T(8,128)(2,1)}, bf16[512,2048]{1,0:T(8,128)(2,1)}, bf16[1024,2048]{1,0:T(8,128)(2,1)}, bf16[102...) custom-call(bf16[1,64]{1,0:T(2,128)(2,1)} %bitcast.51, ...), custom_call_target="tpu_custom_call" | custom-call | flops 6442450944 | bytes 419430400 | tf_op jit(solution)/shard_map/pallas_call | solution.py:1452
  206.3 0.0 slice-start
  206.3 0.0 all-gather.2.cloned.1.call-update
  206.4 0.4 reduce-scatter.4.cloned.1.call-start
  206.8 0.0 slice-start.1
  206.8 0.0 copy-start.9
  206.8 10.6 %fusion.2 = f32[1024,1408]{1,0:T(8,128)S(1)} fusion(bf16[1024,2048]{1,0:T(8,128)(2,1)} %get-tuple-element.48, bf16[2048,1408]{1,0:T(8,128)(2,1)} %get-tuple-element.49.gate_weight_hbm), kind=kOutput, calls=%fused_computation.18 | convolution fusion | flops 5905580032 | bytes 15728640 | tf_op jit(solution)/shard_map/dot_general | solution.py:24
  217.4 0.0 copy-start.11
  217.5 0.0 slice-done
  217.5 0.0 slice-done.1
  217.5 0.0 copy-done.9
  217.5 0.0 copy-start.7
  217.5 8.6 %multiply_convert_fusion.2 = (bf16[1024,1408]{1,0:T(8,128)(2,1)S(1)}, f32[1024,1408]{1,0:T(8,128)}) fusion(f32[1024,1408]{1,0:T(8,128)S(1)} %fusion.2, bf16[1024,2048]{1,0:T(8,128)(2,1)S(1)} %copy-done.9, bf16[2048,1408]{1,0:T(8,128)(2,1)S(1)} %bitcast.57), kind=kOutput, calls=%fused_computation.6 | convolution fusion | flops 5914230784 | bytes 24379392 | tf_op jit(solution)/shard_map/dot_general | solution.py:24
  226.1 0.0 copy-done.11
  226.1 1.6 copy-done.8
  227.7 0.0 copy-done.7
  227.7 8.1 %convolution_convert_fusion.3 = bf16[1408,2048]{1,0:T(8,128)(2,1)} fusion(bf16[1024,1408]{1,0:T(8,128)(2,1)S(1)} %get-tuple-element.88.inner_hbm, bf16[1024,2048]{1,0:T(8,128)(2,1)S(1)} %copy-done.7), kind=kOutput, calls=%fused_computation.3 | convolution fusion | flops 5908463616 | bytes 12845056 | tf_op jit(solution)/shard_map/dot_general | solution.py:32
  235.9 0.0 reduce-scatter.4.cloned.1.call-update
  235.9 0.0 reduce-scatter.6.cloned.1.call-start
  235.9 29.8 %all-gather.2.cloned.1.call-done.down_hbm = bf16[1408,2048]{1,0:T(8,128)(2,1)} async-done(((bf16[1408,256]{1,0:T(8,128)(2,1)}), bf16[1408,2048]{1,0:T(8,128)(2,1)}) %all-gather.2.cloned.1.call-update) | async-done | bytes 5767184 | tf_op jit(solution)/shard_map/all_gather | solution.py:1597
  265.7 14.3 %multiply_convert_fusion = (bf16[1024,1408]{1,0:T(8,128)(2,1)S(1)}, bf16[1024,1408]{1,0:T(8,128)(2,1)S(1)}) fusion(f32[1024,1408]{1,0:T(8,128)} %copy-done.11, f32[1024,1408]{1,0:T(8,128)} %get-tuple-element.89, bf16[1024,2048]{1,0:T(8,128)(2,1)} %get-tuple-element.51, bf16[1408,2048]{1,0:T(8,128)(2,1)} %all-gather.2.cloned.1.call-done.down_hbm), kind=kOutput, calls=%fused_computation.4 | convolution fusion | flops 5924323328 | bytes 27262976 | tf_op jit(solution)/shard_map/dot_general | solution.py:28
  280.0 0.0 copy-start.12
  280.0 0.0 copy-start.13
  280.0 1.6 copy-done.12
  281.6 0.0 copy-done.10
  281.6 8.5 %convolution_convert_fusion.2 = bf16[2048,1408]{1,0:T(8,128)(2,1)} fusion(bf16[1024,2048]{1,0:T(8,128)(2,1)S(1)} %copy-done.10, bf16[1024,1408]{1,0:T(8,128)(2,1)S(1)} %get-tuple-element.53.up_ref), kind=kOutput, calls=%fused_computation.2 | convolution fusion | flops 5908463616 | bytes 12845056 | tf_op jit(solution)/shard_map/dot_general | solution.py:32
  290.1 0.0 reduce-scatter.6.cloned.1.call-update
  290.1 0.2 reduce-scatter.8.cloned.1.call-start
  290.4 0.5 copy-done.4
  290.9 0.6 fusion.1
  291.5 0.0 copy-done.13
  291.5 11.0 %convolution_convert_fusion.1 = bf16[2048,1408]{1,0:T(8,128)(2,1)} fusion(bf16[1024,2048]{1,0:T(8,128)(2,1)} %get-tuple-element.48, bf16[1024,1408]{1,0:T(8,128)(2,1)S(1)} %get-tuple-element.81.gate_ref), kind=kOutput, calls=%fused_computation.1 | convolution fusion | flops 5908463616 | bytes 12845056 | tf_op jit(solution)/shard_map/dot_general | solution.py:32
  302.4 121.4 %shard_map.230 = (f32[256,2048]{1,0:T(8,128)}, f32[2,2048]{1,0:T(2,128)}, bf16[1024,2048]{1,0:T(8,128)(2,1)}, bf16[1024,2048]{1,0:T(8,128)(2,1)}, f32[256,1408]{1,0:T(8,128)}) custom-call(bf16[1024,1408]{1,0:T(8,128)(2,1)} %copy-done.13, bf16[1024,1408]{1,0:T(8,128)(2,1)} %copy-done.12, bf16[2048,1408]{1,0:T(8,128)(2,1)} %get-tuple-element.49.gate_weight_hbm, ...), custom_call_target="tpu_custom_call" | custom-call | flops 23622320128 | bytes 188743680 | tf_op jit(solution)/shard_map/pallas_call | solution.py:654
  423.9 0.0 copy-done.6
  423.9 5.9 convolution_convert_fusion.4
  429.8 6.3 %convolution_convert_fusion.5.grad_ref = bf16[1024,512]{1,0:T(8,128)(2,1)} fusion(bf16[1024,2048]{1,0:T(8,128)(2,1)} %get-tuple-element.56, bf16[512,2048]{1,0:T(8,128)(2,1)} %get-tuple-element.57), kind=kOutput, calls=%fused_computation.11 | convolution fusion | flops 2148007936 | bytes 7340032 | tf_op jit(solution)/shard_map/dot_general | solution.py:28
  436.1 2.3 convert_element_type.49
  438.4 23.7 %shard_map.231 = (bf16[1024,1536]{1,0:T(8,128)(2,1)S(1)}, f32[1,1536]{1,0:T(1,128)S(1)}) custom-call(bf16[1024,1536]{1,0:T(8,128)(2,1)} %get-tuple-element.46.qkv_ref, bf16[1024,512]{1,0:T(8,128)(2,1)} %convolution_convert_fusion.5.grad_ref, f32[1024,512]{1,0:T(8,128)} %get-tuple-element.60.lse_ref, f32[3,1024,128]{2,1,0:T(8,128)} %constant.8.clone.table_hbm.table_ref, ...), custom_call_target="tpu_custom_call" | custom-call | flops 6039797760 | bytes 12582912 | tf_op jit(solution)/shard_map/pallas_call | solution.py:1120
  462.1 0.0 copy-start
  462.1 0.0 reduce-scatter.6.cloned.1.call-done
  462.1 2.8 convert_element_type.50
  465.0 0.0 reduce-scatter.8.cloned.1.call-update
  465.0 0.1 reshape.40
  465.1 0.1 reshape.41
  465.2 0.6 pad.4.bias_ref
  465.8 11.0 %convolution_convert_fusion = bf16[2048,1536]{1,0:T(8,128)(2,1)} fusion(bf16[1024,2048]{1,0:T(8,128)(2,1)} %get-tuple-element.66, bf16[1024,1536]{1,0:T(8,128)(2,1)S(1)} %get-tuple-element.64.d_joined_hbm), kind=kOutput, calls=%fused_computation | convolution fusion | flops 6445596672 | bytes 13631488 | tf_op jit(solution)/shard_map/dot_general | solution.py:32
  476.8 0.0 copy-done
  476.8 102.7 %shard_map.232 = (f32[256,2048]{1,0:T(8,128)}, f32[64,6144]{1,0:T(8,128)}, bf16[256,2048]{1,0:T(8,128)(2,1)}, f32[4,64]{1,0:T(4,128)}, f32[1,192]{1,0:T(1,128)}) custom-call(bf16[1024,1536]{1,0:T(8,128)(2,1)} %copy-done, bf16[2048,1536]{1,0:T(8,128)(2,1)} %get-tuple-element.65.weight_hbm, bf16[8,256,1536]{2,1,0:T(8,128)(2,1)} %bitcast.41, ...), custom_call_target="tpu_custom_call" | custom-call | flops 6442450944 | bytes 209715200 | tf_op jit(solution)/shard_map/pallas_call | solution.py:910
  579.6 0.0 copy-start.1
  579.6 1.4 slice_bitcast_fusion
  580.9 1.9 convert_element_type.53
  582.8 2.3 copy.35
  585.1 0.0 copy-done.1
  585.2 1.3 copy.36
  586.5 0.0 copy-done.2
  586.5 1.1 copy.37
  587.6 0.0 copy-done.5
  587.6 0.6 copy.38
  588.2 0.0 copy-done.3
  588.2 1.1 copy.39
  (12 shorter events, 0.0 us)
Async XLA Ops:
  7.2 258.5 %all-gather.2.cloned.1.call-start = ((), (), s32[]{:S(2)}) async-start(), calls=%async_computation.3 | async-start | bytes 6488064 | tf_op jit(solution)/shard_map/all_gather | solution.py:1597
  206.3 11.1 %slice-start = ((s8[5767168]{0:T(1024)(128)(4,1)}), s8[1572864]{0:T(1024)(128)(4,1)S(1)}, s32[]{:S(2)}) async-start(s8[5767168]{0:T(1024)(128)(4,1)} %bitcast.56), calls=%async_computation.7 | async-start | bytes 3145728
  206.4 229.7 %reduce-scatter.4.cloned.1.call-start = ((), (), s32[]{:S(2)}) async-start(), calls=%async_computation.4 | async-start | bytes 6488064 | tf_op jit(solution)/shard_map/reduce_scatter | solution.py:1606
  206.8 10.7 %slice-start.1 = ((s8[5767168]{0:T(1024)(128)(4,1)}), s8[4194304]{0:T(1024)(128)(4,1)S(1)}, s32[]{:S(2)}) async-start(s8[5767168]{0:T(1024)(128)(4,1)} %bitcast.56), calls=%async_computation.8 | async-start | bytes 8388608
  206.8 10.7 %copy-start.9 = (bf16[1024,2048]{1,0:T(8,128)(2,1)S(1)}, bf16[1024,2048]{1,0:T(8,128)(2,1)}, u32[]{:S(2)}) copy-start(bf16[1024,2048]{1,0:T(8,128)(2,1)} %get-tuple-element.48) | copy-start | bytes 12582916
  217.4 8.7 %copy-start.11 = (f32[1024,1408]{1,0:T(8,128)}, f32[1024,1408]{1,0:T(8,128)S(1)}, u32[]{:S(2)}) copy-start(f32[1024,1408]{1,0:T(8,128)S(1)} %fusion.2) | copy-start | bytes 17301508
  217.5 10.2 %copy-start.7 = (bf16[1024,2048]{1,0:T(8,128)(2,1)S(1)}, bf16[1024,2048]{1,0:T(8,128)(2,1)}, u32[]{:S(2)}) copy-start(bf16[1024,2048]{1,0:T(8,128)(2,1)} %get-tuple-element.51) | copy-start | bytes 12582916
  226.1 1.6 copy-start.8
  235.9 226.2 %reduce-scatter.6.cloned.1.call-start = ((), (), s32[]{:S(2)}) async-start(), calls=%async_computation.5 | async-start | bytes 6488064 | tf_op jit(solution)/shard_map/reduce_scatter | solution.py:1613
  265.7 15.9 %copy-start.10 = (bf16[1024,2048]{1,0:T(8,128)(2,1)S(1)}, bf16[1024,2048]{1,0:T(8,128)(2,1)}, u32[]{:S(2)}) copy-start(bf16[1024,2048]{1,0:T(8,128)(2,1)} %get-tuple-element.48) | copy-start | bytes 12582916
  280.0 1.6 copy-start.12
  280.0 11.5 %copy-start.13 = (bf16[1024,1408]{1,0:T(8,128)(2,1)}, bf16[1024,1408]{1,0:T(8,128)(2,1)S(1)}, u32[]{:S(2)}) copy-start(bf16[1024,1408]{1,0:T(8,128)(2,1)S(1)} %get-tuple-element.81.gate_ref) | copy-start | bytes 8650756
  290.1 0.8 copy-start.4
  290.1 290.8 %reduce-scatter.8.cloned.1.call-start = ((), (), s32[]{:S(2)}) async-start(), calls=%async_computation.6 | async-start | bytes 2359296 | tf_op jit(solution)/shard_map/reduce_scatter | solution.py:1635
  302.4 121.4 %copy-start.6 = (bf16[1024,512]{1,0:T(8,128)(2,1)S(1)}, bf16[1024,512]{1,0:T(8,128)(2,1)}, u32[]{:S(2)}) copy-start(bf16[1024,512]{1,0:T(8,128)(2,1)} %get-tuple-element.63) | copy-start | bytes 3145732
  462.1 14.7 %copy-start = (bf16[1024,1536]{1,0:T(8,128)(2,1)}, bf16[1024,1536]{1,0:T(8,128)(2,1)S(1)}, u32[]{:S(2)}) copy-start(bf16[1024,1536]{1,0:T(8,128)(2,1)S(1)} %get-tuple-element.64.d_joined_hbm) | copy-start | bytes 9437188
  579.6 5.6 copy-start.1
  580.9 5.5 copy-start.2
  585.1 2.5 copy-start.5
  585.1 3.0 copy-start.3
Sparse Core Ops, SparseCore 0:
  206.5 59.1 all-gather.1
  268.0 68.8 reduce-scatter.3
  339.2 94.6 reduce-scatter.5
  465.1 41.4 reduce-scatter.7

commit v12 on v10

--- a/solution.py
+++ b/solution.py
@@ -649,7 +649,7 @@
         spread.send(j)
         if j:
             spread.relay(j - 1)
-        if j == 1 and far > 0:
+        if j % 2 == 0 and far > 0:
             line.send(far)
             far -= 1
     pieces[2 * CHUNKS]()
@@ -827,8 +827,8 @@
         line.add()
         line.send(place.lines - 1)
     reduce.start_near()
+    reduce.relay()
     branch.start()
-    reduce.relay()
     for far in range(place.lines - 2, 1, -1):
         for line in lines:
             line.send(far)

time: 564 us -> 552 us (0.979)
  Pallas kernels: 421 us -> 409 us
    pallas_call x1, Pallas kernels: 108 us -> 99.8 us  [closing(): pl.pallas_call(functools.partial(closing_kernel, dp, ctx), in_specs=[HBM]...]
  transfers between devices with their start and end apart: 3 -> 3, of which waited for: 1 -> 1; matrix products, arithmetic and copies ran while one was open for 14% -> 14% of each run, Pallas kernels for 40% -> 39%
where the time goes in v12:
time: 552 us; the launch traced here: 546 us
  Pallas kernels  409 us (74%)
  matrix products  72.1 us (13%)
  waiting for transfers between devices  28.7 us (5%)
  local copies, waits for them, and re-layouts  15.7 us (3%)
  between operations  14.4 us (3%)
  other arithmetic  6.08 us (1%)
    pallas_call x1, Pallas kernels, forward(): pl.pallas_call(functools.partial(forward_kernel, dp, ctx, attend_step(ful...  196 us
    pallas_call x1, Pallas kernels, closing(): pl.pallas_call(functools.partial(closing_kernel, dp, ctx), in_specs=[HBM]...  99.8 us
    pallas_call x1, Pallas kernels, mix_back(): pl.pallas_call(functools.partial(mix_back_kernel, dp, ctx), in_specs=[vme...  89.6 us
    dot_general x4, matrix products, dot_tn(): lax.dot_general(a, b, (((0,), (0,)), ((), ())), preferred_element_type=f32)  34.1 us
    all_gather x1, waiting for transfers between devices, shards(): down_full = lax.all_gather(down_weight, 'dp', axis=1, tiled=True)  28.6 us
    pallas_call x1, Pallas kernels, attend_back(): pl.pallas_call(functools.partial(attend_back_kernel, step), grid=(pairs,)...  23.8 us
    dot_general x2, matrix products, dot(): return jnp.dot(a, b, preferred_element_type=f32)  19.3 us
    dot_general x2, matrix products, dot_nt(): lax.dot_general(a, b, (((1,), (1,)), ((), ())), preferred_element_type=f32)  18.7 us
  transfers between devices with their start and end apart: 3, of which 1 were waited for; matrix products, arithmetic and copies ran while one was open for 14% of the time, Pallas kernels for 39%

profile of v12, /device:TPU:0, one launch (start us, length us, event | category | flops | bytes accessed | tf_op | source)
XLA Modules:
  0.0 546.2 jit_solution(2569424560633994615)
XLA Ops:
  7.2 0.0 all-gather.2.cloned.1.call-start
  7.2 1.2 broadcast_in_dim.31.bias
  8.4 1.3 convert_reduce_fusion
  9.8 1.0 broadcast_in_dim.32.start_ref
  10.8 195.6 %shard_map.229 = (f32[4,2048]{1,0:T(4,128)}, bf16[2048,1536]{1,0:T(8,128)(2,1)}, bf16[512,2048]{1,0:T(8,128)(2,1)}, bf16[1024,2048]{1,0:T(8,128)(2,1)}, bf16[102...) custom-call(bf16[1,64]{1,0:T(2,128)(2,1)} %bitcast.51, ...), custom_call_target="tpu_custom_call" | custom-call | flops 6442450944 | bytes 419430400 | tf_op jit(solution)/shard_map/pallas_call | solution.py:1486
  206.3 0.0 slice-start
  206.3 0.0 all-gather.2.cloned.1.call-update
  206.4 0.2 reduce-scatter.3.cloned.1.call-start
  206.6 0.0 slice-start.1
  206.6 0.0 copy-start.12
  206.6 10.6 %fusion.2 = f32[1024,1408]{1,0:T(8,128)S(1)} fusion(bf16[1024,2048]{1,0:T(8,128)(2,1)} %get-tuple-element.45.normed_hbm, bf16[2048,1408]{1,0:T(8,128)(2,1)} %get-tuple-element.46.gate_weight_hbm), kind=kOutput, calls=%fused_computation.17 | convolution fusion | flops 5905580032 | bytes 15728640 | tf_op jit(solution)/shard_map/dot_general | solution.py:24
  217.2 0.0 copy-start.14
  217.2 0.0 slice-done
  217.2 0.0 slice-done.1
  217.2 0.0 copy-done.12
  217.3 0.0 copy-start.9
  217.3 8.7 %multiply_convert_fusion.2 = (bf16[1024,1408]{1,0:T(8,128)(2,1)S(1)}, f32[1024,1408]{1,0:T(8,128)}) fusion(f32[1024,1408]{1,0:T(8,128)S(1)} %fusion.2, bf16[1024,2048]{1,0:T(8,128)(2,1)S(1)} %copy-done.12, bf16[2048,1408]{1,0:T(8,128)(2,1)S(1)} %bitcast.57), kind=kOutput, calls=%fused_computation.5 | convolution fusion | flops 5914230784 | bytes 24379392 | tf_op jit(solution)/shard_map/dot_general | solution.py:24
  225.9 0.0 copy-done.14
  225.9 0.0 copy-start.11
  226.0 1.6 copy-done.11
  227.6 0.0 copy-done.9
  227.6 8.1 %convolution_convert_fusion.2 = bf16[1408,2048]{1,0:T(8,128)(2,1)} fusion(bf16[1024,1408]{1,0:T(8,128)(2,1)S(1)} %get-tuple-element.82.inner_hbm, bf16[1024,2048]{1,0:T(8,128)(2,1)S(1)} %copy-done.9), kind=kOutput, calls=%fused_computation.2 | convolution fusion | flops 5908463616 | bytes 12845056 | tf_op jit(solution)/shard_map/dot_general | solution.py:32
  235.7 0.0 copy-start.5
  235.7 0.0 reduce-scatter.3.cloned.1.call-update
  235.7 0.3 reduce-scatter.5.cloned.1.call-start
  236.0 0.5 copy-done.5
  236.4 0.6 fusion.1
  237.0 28.6 %all-gather.2.cloned.1.call-done.down_hbm = bf16[1408,2048]{1,0:T(8,128)(2,1)} async-done(((bf16[1408,256]{1,0:T(8,128)(2,1)}), bf16[1408,2048]{1,0:T(8,128)(2,1)}) %all-gather.2.cloned.1.call-update) | async-done | bytes 5767184 | tf_op jit(solution)/shard_map/all_gather | solution.py:1631
  265.7 0.0 copy-start.13
  265.7 15.4 %multiply_convert_fusion = (bf16[1024,1408]{1,0:T(8,128)(2,1)}, bf16[1024,1408]{1,0:T(8,128)(2,1)S(1)}) fusion(f32[1024,1408]{1,0:T(8,128)} %copy-done.14, f32[1024,1408]{1,0:T(8,128)} %get-tuple-element.83, bf16[1024,2048]{1,0:T(8,128)(2,1)} %get-tuple-element.48, bf16[1408,2048]{1,0:T(8,128)(2,1)} %all-gather.2.cloned.1.call-done.down_hbm), kind=kOutput, calls=%fused_computation.3 | convolution fusion | flops 5924323328 | bytes 27262976 | tf_op jit(solution)/shard_map/dot_general | solution.py:28
  281.1 0.0 copy-done.13
  281.1 8.8 %convolution_convert_fusion.1 = bf16[2048,1408]{1,0:T(8,128)(2,1)} fusion(bf16[1024,2048]{1,0:T(8,128)(2,1)S(1)} %copy-done.13, bf16[1024,1408]{1,0:T(8,128)(2,1)S(1)} %get-tuple-element.75.gate_ref), kind=kOutput, calls=%fused_computation.1 | convolution fusion | flops 5908463616 | bytes 12845056 | tf_op jit(solution)/shard_map/dot_general | solution.py:32
  289.8 0.0 copy-done.15
  289.9 89.6 %shard_map.230 = (f32[256,2048]{1,0:T(8,128)}, f32[2,2048]{1,0:T(2,128)}, bf16[1024,2048]{1,0:T(8,128)(2,1)}, bf16[1024,2048]{1,0:T(8,128)(2,1)}, bf16[2048,1408]{1,0:T(8,128)(2,1)}, /*index=5*/f32[256,1408]{1,0:T(8,128)}) custom-call(bf16[1024,1408]{1,0:T(8,128)(2,1)} %copy-done.15, bf16[1024,1408]{1,0:T(8,128)(2,1)} %get-tuple-element.74.up_ref, ...), custom_call_target="tpu_custom_call" | custom-call | flops 23622320128 | bytes 188743680 | tf_op jit(solution)/shard_map/pallas_call | solution.py:679
  379.4 0.0 copy-start.8
  379.4 0.0 reduce-scatter.5.cloned.1.call-update
  379.5 1.2 copy-done.8
  380.7 6.0 %convolution_convert_fusion.3 = bf16[512,2048]{1,0:T(8,128)(2,1)} fusion(bf16[1024,512]{1,0:T(8,128)(2,1)S(1)} %copy-done.8, bf16[1024,2048]{1,0:T(8,128)(2,1)} %get-tuple-element.52), kind=kOutput, calls=%fused_computation.9 | convolution fusion | flops 2148532224 | bytes 7340032 | tf_op jit(solution)/shard_map/dot_general | solution.py:32
  386.7 0.0 copy-done.7
  386.7 0.0 copy-done.10
  386.7 3.3 convolution_convert_fusion.4.grad_ref
  390.0 2.3 convert_element_type.42
  392.3 23.8 %shard_map.231 = (bf16[1024,1536]{1,0:T(8,128)(2,1)S(1)}, f32[1,1536]{1,0:T(1,128)S(1)}) custom-call(bf16[1024,1536]{1,0:T(8,128)(2,1)} %get-tuple-element.43.qkv_ref, bf16[1024,512]{1,0:T(8,128)(2,1)} %convolution_convert_fusion.4.grad_ref, f32[1024,512]{1,0:T(8,128)} %get-tuple-element.56.lse_ref, f32[3,1024,128]{2,1,0:T(8,128)} %constant.8.clone.table_hbm.table_ref, ...), custom_call_target="tpu_custom_call" | custom-call | flops 6039797760 | bytes 12582912 | tf_op jit(solution)/shard_map/pallas_call | solution.py:1154
  416.2 0.0 copy-start
  416.2 0.1 reshape.44
  416.3 0.1 reshape.45
  416.4 0.8 pad.4.bias_ref
  417.2 11.2 %convolution_convert_fusion = bf16[2048,1536]{1,0:T(8,128)(2,1)} fusion(bf16[1024,2048]{1,0:T(8,128)(2,1)} %get-tuple-element.59, bf16[1024,1536]{1,0:T(8,128)(2,1)S(1)} %get-tuple-element.57.d_joined_hbm), kind=kOutput, calls=%fused_computation | convolution fusion | flops 6445596672 | bytes 13631488 | tf_op jit(solution)/shard_map/dot_general | solution.py:32
  428.4 0.0 copy-done
  428.4 99.8 %shard_map.232 = (f32[256,2048]{1,0:T(8,128)}, f32[64,6144]{1,0:T(8,128)}, f32[64,2048]{1,0:T(8,128)}, bf16[256,2048]{1,0:T(8,128)(2,1)}, f32[4,64]{1,0:T(4,128)}, /*index=5*/f32[1,192]{1,0:T(1,128)}) custom-call(bf16[1024,1536]{1,0:T(8,128)(2,1)} %copy-done, bf16[2048,1536]{1,0:T(8,128)(2,1)} %get-tuple-element.58.weight_hbm, ...), custom_call_target="tpu_custom_call" | custom-call | flops 6442450944 | bytes 209715200 | tf_op jit(solution)/shard_map/pallas_call | solution.py:942
  528.2 0.0 copy-start.1
  528.2 1.4 slice_bitcast_fusion
  529.6 2.4 convert_element_type.45
  532.0 2.3 copy.36
  534.3 0.0 copy-done.1
  534.3 1.3 copy.37
  535.6 0.0 copy-done.2
  535.6 1.1 copy.38
  536.8 0.0 copy-done.6
  536.8 0.6 copy.39
  537.4 0.0 copy-done.4
  537.4 0.8 copy.40
  538.2 0.0 copy-done.3
  538.2 1.1 copy.41
  (12 shorter events, 0.0 us)
Async XLA Ops:
  7.2 258.5 %all-gather.2.cloned.1.call-start = ((), (), s32[]{:S(2)}) async-start(), calls=%async_computation.2 | async-start | bytes 6488064 | tf_op jit(solution)/shard_map/all_gather | solution.py:1631
  206.3 10.9 %slice-start = ((s8[5767168]{0:T(1024)(128)(4,1)}), s8[1572864]{0:T(1024)(128)(4,1)S(1)}, s32[]{:S(2)}) async-start(s8[5767168]{0:T(1024)(128)(4,1)} %bitcast.56), calls=%async_computation.5 | async-start | bytes 3145728
  206.4 183.7 %reduce-scatter.3.cloned.1.call-start = ((), (), s32[]{:S(2)}) async-start(), calls=%async_computation.3 | async-start | bytes 6488064 | tf_op jit(solution)/shard_map/reduce_scatter | solution.py:1640
  206.6 10.7 %slice-start.1 = ((s8[5767168]{0:T(1024)(128)(4,1)}), s8[4194304]{0:T(1024)(128)(4,1)S(1)}, s32[]{:S(2)}) async-start(s8[5767168]{0:T(1024)(128)(4,1)} %bitcast.56), calls=%async_computation.6 | async-start | bytes 8388608
  206.6 10.6 %copy-start.12 = (bf16[1024,2048]{1,0:T(8,128)(2,1)S(1)}, bf16[1024,2048]{1,0:T(8,128)(2,1)}, u32[]{:S(2)}) copy-start(bf16[1024,2048]{1,0:T(8,128)(2,1)} %get-tuple-element.45.normed_hbm) | copy-start | bytes 12582916
  217.2 8.7 %copy-start.14 = (f32[1024,1408]{1,0:T(8,128)}, f32[1024,1408]{1,0:T(8,128)S(1)}, u32[]{:S(2)}) copy-start(f32[1024,1408]{1,0:T(8,128)S(1)} %fusion.2) | copy-start | bytes 17301508
  217.3 10.3 %copy-start.9 = (bf16[1024,2048]{1,0:T(8,128)(2,1)S(1)}, bf16[1024,2048]{1,0:T(8,128)(2,1)}, u32[]{:S(2)}) copy-start(bf16[1024,2048]{1,0:T(8,128)(2,1)} %get-tuple-element.48) | copy-start | bytes 12582916
  225.9 1.6 copy-start.11
  235.7 0.8 copy-start.5
  235.7 293.9 %reduce-scatter.5.cloned.1.call-start = ((), (), s32[]{:S(2)}) async-start(), calls=%async_computation.4 | async-start | bytes 6488064 | tf_op jit(solution)/shard_map/reduce_scatter | solution.py:1658
  265.7 15.4 %copy-start.13 = (bf16[1024,2048]{1,0:T(8,128)(2,1)S(1)}, bf16[1024,2048]{1,0:T(8,128)(2,1)}, u32[]{:S(2)}) copy-start(bf16[1024,2048]{1,0:T(8,128)(2,1)} %get-tuple-element.45.normed_hbm) | copy-start | bytes 12582916
  281.1 8.8 %copy-start.15 = (bf16[1024,1408]{1,0:T(8,128)(2,1)}, bf16[1024,1408]{1,0:T(8,128)(2,1)S(1)}, u32[]{:S(2)}) copy-start(bf16[1024,1408]{1,0:T(8,128)(2,1)S(1)} %get-tuple-element.75.gate_ref) | copy-start | bytes 8650756
  379.4 1.2 copy-start.8
  380.7 6.0 %copy-start.7 = (bf16[1024,2048]{1,0:T(8,128)(2,1)S(1)}, bf16[1024,2048]{1,0:T(8,128)(2,1)}, u32[]{:S(2)}) copy-start(bf16[1024,2048]{1,0:T(8,128)(2,1)} %get-tuple-element.52) | copy-start | bytes 12582916
  380.7 6.0 %copy-start.10 = (bf16[512,2048]{1,0:T(8,128)(2,1)S(1)}, bf16[512,2048]{1,0:T(8,128)(2,1)}, u32[]{:S(2)}) copy-start(bf16[512,2048]{1,0:T(8,128)(2,1)} %get-tuple-element.53) | copy-start | bytes 6291460
  416.2 12.2 %copy-start = (bf16[1024,1536]{1,0:T(8,128)(2,1)}, bf16[1024,1536]{1,0:T(8,128)(2,1)S(1)}, u32[]{:S(2)}) copy-start(bf16[1024,1536]{1,0:T(8,128)(2,1)S(1)} %get-tuple-element.57.d_joined_hbm) | copy-start | bytes 9437188
  528.2 6.1 %copy-start.1 = (f32[256,2048]{1,0:T(8,128)S(1)}, f32[256,2048]{1,0:T(8,128)}, u32[]{:S(2)}) copy-start(f32[256,2048]{1,0:T(8,128)} %get-tuple-element.66) | copy-start | bytes 6291460
  529.6 6.1 %copy-start.2 = (f32[64,6144]{1,0:T(8,128)S(1)}, f32[64,6144]{1,0:T(8,128)}, u32[]{:S(2)}) copy-start(f32[64,6144]{1,0:T(8,128)} %get-tuple-element.100) | copy-start | bytes 4718596
  534.3 2.5 copy-start.6
  534.3 3.0 copy-start.4
  534.3 3.8 copy-start.3
Sparse Core Ops, SparseCore 0:
  206.5 59.1 all-gather.1
  268.0 81.3 reduce-scatter.2
  379.6 65.2 reduce-scatter.4

commit v13 on v12

--- a/solution.py
+++ b/solution.py
@@ -1410,10 +1410,10 @@
             line.send(hop + 1)
 
     table_copy.wait()
+    up_line.send(1)
     attend_pairs(0, pairs // 2)
     if place.lines > 1:
         pass_on(gate_line, 1)
-    up_line.send(1)
     attend_pairs(pairs // 2, pairs)
     for hop in range(place.lines):
         out_line.settle(hop)
@@ -1447,12 +1447,14 @@
         spread.send(j)
         if j:
             spread.relay(j - 1)
-        if j == 1 and place.lines > 1:
+        if j == 0 and place.lines > 1:
             pass_on(up_line, 1)
+        if j == 3 and place.lines > 2:
+            pass_on(up_line, 2)
     spread.relay(CHUNKS - 1)
     for hop in range(3, place.lines):
         pass_on(gate_line, hop)
-    for hop in range(2, place.lines):
+    for hop in range(3, place.lines):
         pass_on(up_line, hop)
     spread.finish()
     for line in (gate_line, up_line):

time: 552 us -> 545 us (0.987)
  Pallas kernels: 409 us -> 400 us
    pallas_call x1, Pallas kernels: 196 us -> 187 us  [forward(): pl.pallas_call(functools.partial(forward_kernel, dp, ctx, attend_step(ful...]
  transfers between devices with their start and end apart: 3 -> 3, of which waited for: 1 -> 1; matrix products, arithmetic and copies ran while one was open for 14% -> 14% of each run, Pallas kernels for 39% -> 40%
where the time goes in v13:
time: 545 us; the launch traced here: 539 us
  Pallas kernels  400 us (73%)
  matrix products  72.1 us (13%)
  waiting for transfers between devices  29.5 us (5%)
  local copies, waits for them, and re-layouts  15.7 us (3%)
  between operations  14.4 us (3%)
  other arithmetic  6.08 us (1%)
    pallas_call x1, Pallas kernels, forward(): pl.pallas_call(functools.partial(forward_kernel, dp, ctx, attend_step(ful...  187 us
    pallas_call x1, Pallas kernels, closing(): pl.pallas_call(functools.partial(closing_kernel, dp, ctx), in_specs=[HBM]...  99.8 us
    pallas_call x1, Pallas kernels, mix_back(): pl.pallas_call(functools.partial(mix_back_kernel, dp, ctx), in_specs=[vme...  89.6 us
    dot_general x4, matrix products, dot_tn(): lax.dot_general(a, b, (((0,), (0,)), ((), ())), preferred_element_type=f32)  34.1 us
    all_gather x1, waiting for transfers between devices, shards(): down_full = lax.all_gather(down_weight, 'dp', axis=1, tiled=True)  29.5 us
    pallas_call x1, Pallas kernels, attend_back(): pl.pallas_call(functools.partial(attend_back_kernel, step), grid=(pairs,)...  23.8 us
    dot_general x2, matrix products, dot(): return jnp.dot(a, b, preferred_element_type=f32)  19.3 us
    dot_general x2, matrix products, dot_nt(): lax.dot_general(a, b, (((1,), (1,)), ((), ())), preferred_element_type=f32)  18.7 us
  transfers between devices with their start and end apart: 3, of which 1 were waited for; matrix products, arithmetic and copies ran while one was open for 14% of the time, Pallas kernels for 40%

profile of v13, /device:TPU:0, one launch (start us, length us, event | category | flops | bytes accessed | tf_op | source)
XLA Modules:
  0.0 538.8 jit_solution(14428226074034522648)
XLA Ops:
  7.2 0.0 all-gather.2.cloned.1.call-start
  7.2 1.2 broadcast_in_dim.31.bias
  8.4 1.3 convert_reduce_fusion
  9.8 1.0 broadcast_in_dim.32.start_ref
  10.8 187.3 %shard_map.229 = (f32[4,2048]{1,0:T(4,128)}, bf16[2048,1536]{1,0:T(8,128)(2,1)}, bf16[512,2048]{1,0:T(8,128)(2,1)}, bf16[1024,2048]{1,0:T(8,128)(2,1)}, bf16[102...) custom-call(bf16[1,64]{1,0:T(2,128)(2,1)} %bitcast.51, ...), custom_call_target="tpu_custom_call" | custom-call | flops 6442450944 | bytes 419430400 | tf_op jit(solution)/shard_map/pallas_call | solution.py:1488
  198.0 0.0 slice-start
  198.1 0.0 all-gather.2.cloned.1.call-update
  198.1 0.2 reduce-scatter.3.cloned.1.call-start
  198.3 0.0 slice-start.1
  198.3 0.0 copy-start.12
  198.3 10.6 %fusion.2 = f32[1024,1408]{1,0:T(8,128)S(1)} fusion(bf16[1024,2048]{1,0:T(8,128)(2,1)} %get-tuple-element.45.normed_hbm, bf16[2048,1408]{1,0:T(8,128)(2,1)} %get-tuple-element.46.gate_weight_hbm), kind=kOutput, calls=%fused_computation.17 | convolution fusion | flops 5905580032 | bytes 15728640 | tf_op jit(solution)/shard_map/dot_general | solution.py:24
  208.9 0.0 copy-start.14
  208.9 0.0 slice-done
  208.9 0.0 slice-done.1
  209.0 0.0 copy-done.12
  209.0 0.0 copy-start.9
  209.0 8.7 %multiply_convert_fusion.2 = (bf16[1024,1408]{1,0:T(8,128)(2,1)S(1)}, f32[1024,1408]{1,0:T(8,128)}) fusion(f32[1024,1408]{1,0:T(8,128)S(1)} %fusion.2, bf16[1024,2048]{1,0:T(8,128)(2,1)S(1)} %copy-done.12, bf16[2048,1408]{1,0:T(8,128)(2,1)S(1)} %bitcast.57), kind=kOutput, calls=%fused_computation.5 | convolution fusion | flops 5914230784 | bytes 24379392 | tf_op jit(solution)/shard_map/dot_general | solution.py:24
  217.7 0.0 copy-done.14
  217.7 0.0 copy-start.11
  217.7 1.6 copy-done.11
  219.3 0.0 copy-done.9
  219.3 8.1 %convolution_convert_fusion.2 = bf16[1408,2048]{1,0:T(8,128)(2,1)} fusion(bf16[1024,1408]{1,0:T(8,128)(2,1)S(1)} %get-tuple-element.82.inner_hbm, bf16[1024,2048]{1,0:T(8,128)(2,1)S(1)} %copy-done.9), kind=kOutput, calls=%fused_computation.2 | convolution fusion | flops 5908463616 | bytes 12845056 | tf_op jit(solution)/shard_map/dot_general | solution.py:32
  227.4 0.0 copy-start.5
  227.4 0.0 reduce-scatter.3.cloned.1.call-update
  227.4 0.3 reduce-scatter.5.cloned.1.call-start
  227.7 0.5 copy-done.5
  228.2 0.6 fusion.1
  228.8 29.5 %all-gather.2.cloned.1.call-done.down_hbm = bf16[1408,2048]{1,0:T(8,128)(2,1)} async-done(((bf16[1408,256]{1,0:T(8,128)(2,1)}), bf16[1408,2048]{1,0:T(8,128)(2,1)}) %all-gather.2.cloned.1.call-update) | async-done | bytes 5767184 | tf_op jit(solution)/shard_map/all_gather | solution.py:1633
  258.3 0.0 copy-start.13
  258.3 15.4 %multiply_convert_fusion = (bf16[1024,1408]{1,0:T(8,128)(2,1)}, bf16[1024,1408]{1,0:T(8,128)(2,1)S(1)}) fusion(f32[1024,1408]{1,0:T(8,128)} %copy-done.14, f32[1024,1408]{1,0:T(8,128)} %get-tuple-element.83, bf16[1024,2048]{1,0:T(8,128)(2,1)} %get-tuple-element.48, bf16[1408,2048]{1,0:T(8,128)(2,1)} %all-gather.2.cloned.1.call-done.down_hbm), kind=kOutput, calls=%fused_computation.3 | convolution fusion | flops 5924323328 | bytes 27262976 | tf_op jit(solution)/shard_map/dot_general | solution.py:28
  273.6 0.0 copy-done.13
  273.6 8.8 %convolution_convert_fusion.1 = bf16[2048,1408]{1,0:T(8,128)(2,1)} fusion(bf16[1024,2048]{1,0:T(8,128)(2,1)S(1)} %copy-done.13, bf16[1024,1408]{1,0:T(8,128)(2,1)S(1)} %get-tuple-element.75.gate_ref), kind=kOutput, calls=%fused_computation.1 | convolution fusion | flops 5908463616 | bytes 12845056 | tf_op jit(solution)/shard_map/dot_general | solution.py:32
  282.4 0.0 copy-done.15
  282.4 89.6 %shard_map.230 = (f32[256,2048]{1,0:T(8,128)}, f32[2,2048]{1,0:T(2,128)}, bf16[1024,2048]{1,0:T(8,128)(2,1)}, bf16[1024,2048]{1,0:T(8,128)(2,1)}, bf16[2048,1408]{1,0:T(8,128)(2,1)}, /*index=5*/f32[256,1408]{1,0:T(8,128)}) custom-call(bf16[1024,1408]{1,0:T(8,128)(2,1)} %copy-done.15, bf16[1024,1408]{1,0:T(8,128)(2,1)} %get-tuple-element.74.up_ref, ...), custom_call_target="tpu_custom_call" | custom-call | flops 23622320128 | bytes 188743680 | tf_op jit(solution)/shard_map/pallas_call | solution.py:679
  372.0 0.0 copy-start.8
  372.0 0.0 reduce-scatter.5.cloned.1.call-update
  372.0 1.2 copy-done.8
  373.2 6.0 %convolution_convert_fusion.3 = bf16[512,2048]{1,0:T(8,128)(2,1)} fusion(bf16[1024,512]{1,0:T(8,128)(2,1)S(1)} %copy-done.8, bf16[1024,2048]{1,0:T(8,128)(2,1)} %get-tuple-element.52), kind=kOutput, calls=%fused_computation.9 | convolution fusion | flops 2148532224 | bytes 7340032 | tf_op jit(solution)/shard_map/dot_general | solution.py:32
  379.3 0.0 copy-done.7
  379.3 0.0 copy-done.10
  379.3 3.3 convolution_convert_fusion.4.grad_ref
  382.6 2.3 convert_element_type.42
  384.9 23.8 %shard_map.231 = (bf16[1024,1536]{1,0:T(8,128)(2,1)S(1)}, f32[1,1536]{1,0:T(1,128)S(1)}) custom-call(bf16[1024,1536]{1,0:T(8,128)(2,1)} %get-tuple-element.43.qkv_ref, bf16[1024,512]{1,0:T(8,128)(2,1)} %convolution_convert_fusion.4.grad_ref, f32[1024,512]{1,0:T(8,128)} %get-tuple-element.56.lse_ref, f32[3,1024,128]{2,1,0:T(8,128)} %constant.8.clone.table_hbm.table_ref, ...), custom_call_target="tpu_custom_call" | custom-call | flops 6039797760 | bytes 12582912 | tf_op jit(solution)/shard_map/pallas_call | solution.py:1154
  408.8 0.0 copy-start
  408.8 0.1 reshape.44
  408.9 0.1 reshape.45
  409.0 0.8 pad.4.bias_ref
  409.8 11.2 %convolution_convert_fusion = bf16[2048,1536]{1,0:T(8,128)(2,1)} fusion(bf16[1024,2048]{1,0:T(8,128)(2,1)} %get-tuple-element.59, bf16[1024,1536]{1,0:T(8,128)(2,1)S(1)} %get-tuple-element.57.d_joined_hbm), kind=kOutput, calls=%fused_computation | convolution fusion | flops 6445596672 | bytes 13631488 | tf_op jit(solution)/shard_map/dot_general | solution.py:32
  421.0 0.0 copy-done
  421.0 99.8 %shard_map.232 = (f32[256,2048]{1,0:T(8,128)}, f32[64,6144]{1,0:T(8,128)}, f32[64,2048]{1,0:T(8,128)}, bf16[256,2048]{1,0:T(8,128)(2,1)}, f32[4,64]{1,0:T(4,128)}, /*index=5*/f32[1,192]{1,0:T(1,128)}) custom-call(bf16[1024,1536]{1,0:T(8,128)(2,1)} %copy-done, bf16[2048,1536]{1,0:T(8,128)(2,1)} %get-tuple-element.58.weight_hbm, ...), custom_call_target="tpu_custom_call" | custom-call | flops 6442450944 | bytes 209715200 | tf_op jit(solution)/shard_map/pallas_call | solution.py:942
  520.8 0.0 copy-start.1
  520.8 1.4 slice_bitcast_fusion
  522.2 2.4 convert_element_type.45
  524.6 2.3 copy.36
  526.9 0.0 copy-done.1
  526.9 1.3 copy.37
  528.2 0.0 copy-done.2
  528.2 1.1 copy.38
  529.4 0.0 copy-done.6
  529.4 0.6 copy.39
  529.9 0.0 copy-done.4
  529.9 0.8 copy.40
  530.7 0.0 copy-done.3
  530.7 1.1 copy.41
  (12 shorter events, 0.0 us)
Async XLA Ops:
  7.2 251.1 %all-gather.2.cloned.1.call-start = ((), (), s32[]{:S(2)}) async-start(), calls=%async_computation.2 | async-start | bytes 6488064 | tf_op jit(solution)/shard_map/all_gather | solution.py:1633
  198.0 10.9 %slice-start = ((s8[5767168]{0:T(1024)(128)(4,1)}), s8[1572864]{0:T(1024)(128)(4,1)S(1)}, s32[]{:S(2)}) async-start(s8[5767168]{0:T(1024)(128)(4,1)} %bitcast.56), calls=%async_computation.5 | async-start | bytes 3145728
  198.1 184.5 %reduce-scatter.3.cloned.1.call-start = ((), (), s32[]{:S(2)}) async-start(), calls=%async_computation.3 | async-start | bytes 6488064 | tf_op jit(solution)/shard_map/reduce_scatter | solution.py:1642
  198.3 10.6 %slice-start.1 = ((s8[5767168]{0:T(1024)(128)(4,1)}), s8[4194304]{0:T(1024)(128)(4,1)S(1)}, s32[]{:S(2)}) async-start(s8[5767168]{0:T(1024)(128)(4,1)} %bitcast.56), calls=%async_computation.6 | async-start | bytes 8388608
  198.3 10.6 %copy-start.12 = (bf16[1024,2048]{1,0:T(8,128)(2,1)S(1)}, bf16[1024,2048]{1,0:T(8,128)(2,1)}, u32[]{:S(2)}) copy-start(bf16[1024,2048]{1,0:T(8,128)(2,1)} %get-tuple-element.45.normed_hbm) | copy-start | bytes 12582916
  208.9 8.8 %copy-start.14 = (f32[1024,1408]{1,0:T(8,128)}, f32[1024,1408]{1,0:T(8,128)S(1)}, u32[]{:S(2)}) copy-start(f32[1024,1408]{1,0:T(8,128)S(1)} %fusion.2) | copy-start | bytes 17301508
  209.0 10.3 %copy-start.9 = (bf16[1024,2048]{1,0:T(8,128)(2,1)S(1)}, bf16[1024,2048]{1,0:T(8,128)(2,1)}, u32[]{:S(2)}) copy-start(bf16[1024,2048]{1,0:T(8,128)(2,1)} %get-tuple-element.48) | copy-start | bytes 12582916
  217.7 1.6 copy-start.11
  227.4 0.8 copy-start.5
  227.4 294.7 %reduce-scatter.5.cloned.1.call-start = ((), (), s32[]{:S(2)}) async-start(), calls=%async_computation.4 | async-start | bytes 6488064 | tf_op jit(solution)/shard_map/reduce_scatter | solution.py:1660
  258.3 15.4 %copy-start.13 = (bf16[1024,2048]{1,0:T(8,128)(2,1)S(1)}, bf16[1024,2048]{1,0:T(8,128)(2,1)}, u32[]{:S(2)}) copy-start(bf16[1024,2048]{1,0:T(8,128)(2,1)} %get-tuple-element.45.normed_hbm) | copy-start | bytes 12582916
  273.6 8.8 %copy-start.15 = (bf16[1024,1408]{1,0:T(8,128)(2,1)}, bf16[1024,1408]{1,0:T(8,128)(2,1)S(1)}, u32[]{:S(2)}) copy-start(bf16[1024,1408]{1,0:T(8,128)(2,1)S(1)} %get-tuple-element.75.gate_ref) | copy-start | bytes 8650756
  372.0 1.2 copy-start.8
  373.2 6.0 %copy-start.7 = (bf16[1024,2048]{1,0:T(8,128)(2,1)S(1)}, bf16[1024,2048]{1,0:T(8,128)(2,1)}, u32[]{:S(2)}) copy-start(bf16[1024,2048]{1,0:T(8,128)(2,1)} %get-tuple-element.52) | copy-start | bytes 12582916
  373.2 6.0 %copy-start.10 = (bf16[512,2048]{1,0:T(8,128)(2,1)S(1)}, bf16[512,2048]{1,0:T(8,128)(2,1)}, u32[]{:S(2)}) copy-start(bf16[512,2048]{1,0:T(8,128)(2,1)} %get-tuple-element.53) | copy-start | bytes 6291460
  408.8 12.2 %copy-start = (bf16[1024,1536]{1,0:T(8,128)(2,1)}, bf16[1024,1536]{1,0:T(8,128)(2,1)S(1)}, u32[]{:S(2)}) copy-start(bf16[1024,1536]{1,0:T(8,128)(2,1)S(1)} %get-tuple-element.57.d_joined_hbm) | copy-start | bytes 9437188
  520.8 6.1 %copy-start.1 = (f32[256,2048]{1,0:T(8,128)S(1)}, f32[256,2048]{1,0:T(8,128)}, u32[]{:S(2)}) copy-start(f32[256,2048]{1,0:T(8,128)} %get-tuple-element.66) | copy-start | bytes 6291460
  522.2 6.1 %copy-start.2 = (f32[64,6144]{1,0:T(8,128)S(1)}, f32[64,6144]{1,0:T(8,128)}, u32[]{:S(2)}) copy-start(f32[64,6144]{1,0:T(8,128)} %get-tuple-element.100) | copy-start | bytes 4718596
  526.9 2.5 copy-start.6
  526.9 3.0 copy-start.4
  526.9 3.8 copy-start.3
Sparse Core Ops, SparseCore 0:
  198.2 60.0 all-gather.1
  260.6 81.3 reduce-scatter.2
  372.2 65.2 reduce-scatter.4

commit v14 on v13

--- a/solution.py
+++ b/solution.py
@@ -458,11 +458,24 @@
         for line in range(self.place.lines):
             self.swap(line).start()
 
-    def add(self):
-        for line in range(self.place.lines):
-            self.load(line).wait()
-            self.swap(line).wait_recv()
-            self.pair[line] = (self.own[line].astype(f32) + self.pair[line].astype(f32)).astype(bf16)
+    def add_at(self, line):
+        self.load(line).wait()
+        self.swap(line).wait_recv()
+        self.pair[line] = (self.own[line].astype(f32) + self.pair[line].astype(f32)).astype(bf16)
+
+    def add(self, far):
+        place = self.place
+        if far == 0:
+            self.add_at(place.line)
+            return
+        pl.when(place.line + far < place.lines)(lambda: self.add_at(place.line + far))
+        pl.when(place.line - far >= 0)(lambda: self.add_at(place.line - far))
+
+    def begin(self):
+        for far in range(self.place.lines - 1, -1, -1):
+            self.add(far)
+            if far == self.place.lines - 1:
+                self.send(far)
 
     def up(self, far):
         part = self.place.line + far
@@ -629,8 +642,7 @@
         normed_load(i).start()
         inner_load(i).start()
     reduce.start_near()
-    line.add()
-    line.send(place.lines - 1)
+    line.begin()
     reduce.relay()
     sums_ref[...] = jnp.zeros_like(sums_ref)
     far = place.lines - 2
@@ -824,8 +836,7 @@
     )
     reduce.start_far()
     for line in lines:
-        line.add()
-        line.send(place.lines - 1)
+        line.begin()
     reduce.start_near()
     reduce.relay()
     branch.start()

time: 545 us -> 545 us (level)
  no operation moved by 1% of the time
where the time goes in v14:
time: 545 us; the launch traced here: 539 us
  Pallas kernels  401 us (74%)
  matrix products  72.1 us (13%)
  waiting for transfers between devices  29.5 us (5%)
  local copies, waits for them, and re-layouts  15.7 us (3%)
  between operations  14.4 us (3%)
  other arithmetic  6.08 us (1%)
    pallas_call x1, Pallas kernels, forward(): pl.pallas_call(functools.partial(forward_kernel, dp, ctx, attend_step(ful...  187 us
    pallas_call x1, Pallas kernels, closing(): pl.pallas_call(functools.partial(closing_kernel, dp, ctx), in_specs=[HBM]...  101 us
    pallas_call x1, Pallas kernels, mix_back(): pl.pallas_call(functools.partial(mix_back_kernel, dp, ctx), in_specs=[vme...  89.3 us
    dot_general x4, matrix products, dot_tn(): lax.dot_general(a, b, (((0,), (0,)), ((), ())), preferred_element_type=f32)  34.1 us
    all_gather x1, waiting for transfers between devices, shards(): down_full = lax.all_gather(down_weight, 'dp', axis=1, tiled=True)  29.5 us
    pallas_call x1, Pallas kernels, attend_back(): pl.pallas_call(functools.partial(attend_back_kernel, step), grid=(pairs,)...  23.8 us
    dot_general x2, matrix products, dot(): return jnp.dot(a, b, preferred_element_type=f32)  19.3 us
    dot_general x2, matrix products, dot_nt(): lax.dot_general(a, b, (((1,), (1,)), ((), ())), preferred_element_type=f32)  18.7 us
  transfers between devices with their start and end apart: 3, of which 1 were waited for; matrix products, arithmetic and copies ran while one was open for 14% of the time, Pallas kernels for 40%

profile of v14, /device:TPU:0, one launch (start us, length us, event | category | flops | bytes accessed | tf_op | source)
XLA Modules:
  0.0 539.4 jit_solution(2683707344969559328)
XLA Ops:
  7.2 0.0 all-gather.2.cloned.1.call-start
  7.2 1.2 broadcast_in_dim.31.bias
  8.4 1.3 convert_reduce_fusion
  9.8 1.0 broadcast_in_dim.32.start_ref
  10.8 187.3 %shard_map.229 = (f32[4,2048]{1,0:T(4,128)}, bf16[2048,1536]{1,0:T(8,128)(2,1)}, bf16[512,2048]{1,0:T(8,128)(2,1)}, bf16[1024,2048]{1,0:T(8,128)(2,1)}, bf16[102...) custom-call(bf16[1,64]{1,0:T(2,128)(2,1)} %bitcast.51, ...), custom_call_target="tpu_custom_call" | custom-call | flops 6442450944 | bytes 419430400 | tf_op jit(solution)/shard_map/pallas_call | solution.py:1499
  198.0 0.0 slice-start
  198.1 0.0 all-gather.2.cloned.1.call-update
  198.1 0.2 reduce-scatter.3.cloned.1.call-start
  198.3 0.0 slice-start.1
  198.3 0.0 copy-start.12
  198.3 10.6 %fusion.2 = f32[1024,1408]{1,0:T(8,128)S(1)} fusion(bf16[1024,2048]{1,0:T(8,128)(2,1)} %get-tuple-element.45.normed_hbm, bf16[2048,1408]{1,0:T(8,128)(2,1)} %get-tuple-element.46.gate_weight_hbm), kind=kOutput, calls=%fused_computation.17 | convolution fusion | flops 5905580032 | bytes 15728640 | tf_op jit(solution)/shard_map/dot_general | solution.py:24
  208.9 0.0 copy-start.14
  208.9 0.0 slice-done
  208.9 0.0 slice-done.1
  209.0 0.0 copy-done.12
  209.0 0.0 copy-start.9
  209.0 8.7 %multiply_convert_fusion.2 = (bf16[1024,1408]{1,0:T(8,128)(2,1)S(1)}, f32[1024,1408]{1,0:T(8,128)}) fusion(f32[1024,1408]{1,0:T(8,128)S(1)} %fusion.2, bf16[1024,2048]{1,0:T(8,128)(2,1)S(1)} %copy-done.12, bf16[2048,1408]{1,0:T(8,128)(2,1)S(1)} %bitcast.57), kind=kOutput, calls=%fused_computation.5 | convolution fusion | flops 5914230784 | bytes 24379392 | tf_op jit(solution)/shard_map/dot_general | solution.py:24
  217.7 0.0 copy-done.14
  217.7 1.6 copy-done.11
  219.3 0.0 copy-done.9
  219.3 8.1 %convolution_convert_fusion.2 = bf16[1408,2048]{1,0:T(8,128)(2,1)} fusion(bf16[1024,1408]{1,0:T(8,128)(2,1)S(1)} %get-tuple-element.82.inner_hbm, bf16[1024,2048]{1,0:T(8,128)(2,1)S(1)} %copy-done.9), kind=kOutput, calls=%fused_computation.2 | convolution fusion | flops 5908463616 | bytes 12845056 | tf_op jit(solution)/shard_map/dot_general | solution.py:32
  227.4 0.0 copy-start.5
  227.4 0.0 reduce-scatter.3.cloned.1.call-update
  227.4 0.3 reduce-scatter.5.cloned.1.call-start
  227.7 0.5 copy-done.5
  228.2 0.6 fusion.1
  228.8 29.5 %all-gather.2.cloned.1.call-done.down_hbm = bf16[1408,2048]{1,0:T(8,128)(2,1)} async-done(((bf16[1408,256]{1,0:T(8,128)(2,1)}), bf16[1408,2048]{1,0:T(8,128)(2,1)}) %all-gather.2.cloned.1.call-update) | async-done | bytes 5767184 | tf_op jit(solution)/shard_map/all_gather | solution.py:1644
  258.3 0.0 copy-start.13
  258.3 15.4 %multiply_convert_fusion = (bf16[1024,1408]{1,0:T(8,128)(2,1)}, bf16[1024,1408]{1,0:T(8,128)(2,1)S(1)}) fusion(f32[1024,1408]{1,0:T(8,128)} %copy-done.14, f32[1024,1408]{1,0:T(8,128)} %get-tuple-element.83, bf16[1024,2048]{1,0:T(8,128)(2,1)} %get-tuple-element.48, bf16[1408,2048]{1,0:T(8,128)(2,1)} %all-gather.2.cloned.1.call-done.down_hbm), kind=kOutput, calls=%fused_computation.3 | convolution fusion | flops 5924323328 | bytes 27262976 | tf_op jit(solution)/shard_map/dot_general | solution.py:28
  273.6 0.0 copy-start.15
  273.6 0.0 copy-done.13
  273.6 8.8 %convolution_convert_fusion.1 = bf16[2048,1408]{1,0:T(8,128)(2,1)} fusion(bf16[1024,2048]{1,0:T(8,128)(2,1)S(1)} %copy-done.13, bf16[1024,1408]{1,0:T(8,128)(2,1)S(1)} %get-tuple-element.75.gate_ref), kind=kOutput, calls=%fused_computation.1 | convolution fusion | flops 5908463616 | bytes 12845056 | tf_op jit(solution)/shard_map/dot_general | solution.py:32
  282.4 0.0 copy-done.15
  282.4 89.3 %shard_map.230 = (f32[256,2048]{1,0:T(8,128)}, f32[2,2048]{1,0:T(2,128)}, bf16[1024,2048]{1,0:T(8,128)(2,1)}, bf16[1024,2048]{1,0:T(8,128)(2,1)}, bf16[2048,1408]{1,0:T(8,128)(2,1)}, /*index=5*/f32[256,1408]{1,0:T(8,128)}) custom-call(bf16[1024,1408]{1,0:T(8,128)(2,1)} %copy-done.15, bf16[1024,1408]{1,0:T(8,128)(2,1)} %get-tuple-element.74.up_ref, ...), custom_call_target="tpu_custom_call" | custom-call | flops 23622320128 | bytes 188743680 | tf_op jit(solution)/shard_map/pallas_call | solution.py:691
  371.8 0.0 copy-start.8
  371.8 0.0 reduce-scatter.5.cloned.1.call-update
  371.8 1.2 copy-done.8
  373.0 6.0 %convolution_convert_fusion.3 = bf16[512,2048]{1,0:T(8,128)(2,1)} fusion(bf16[1024,512]{1,0:T(8,128)(2,1)S(1)} %copy-done.8, bf16[1024,2048]{1,0:T(8,128)(2,1)} %get-tuple-element.52), kind=kOutput, calls=%fused_computation.9 | convolution fusion | flops 2148532224 | bytes 7340032 | tf_op jit(solution)/shard_map/dot_general | solution.py:32
  379.0 0.0 copy-done.7
  379.0 0.0 copy-done.10
  379.0 3.3 convolution_convert_fusion.4.grad_ref
  382.4 2.3 convert_element_type.42
  384.7 23.8 %shard_map.231 = (bf16[1024,1536]{1,0:T(8,128)(2,1)S(1)}, f32[1,1536]{1,0:T(1,128)S(1)}) custom-call(bf16[1024,1536]{1,0:T(8,128)(2,1)} %get-tuple-element.43.qkv_ref, bf16[1024,512]{1,0:T(8,128)(2,1)} %convolution_convert_fusion.4.grad_ref, f32[1024,512]{1,0:T(8,128)} %get-tuple-element.56.lse_ref, f32[3,1024,128]{2,1,0:T(8,128)} %constant.8.clone.table_hbm.table_ref, ...), custom_call_target="tpu_custom_call" | custom-call | flops 6039797760 | bytes 12582912 | tf_op jit(solution)/shard_map/pallas_call | solution.py:1165
  408.5 0.0 copy-start
  408.5 0.1 reshape.44
  408.6 0.1 reshape.45
  408.7 0.8 pad.4.bias_ref
  409.5 11.2 %convolution_convert_fusion = bf16[2048,1536]{1,0:T(8,128)(2,1)} fusion(bf16[1024,2048]{1,0:T(8,128)(2,1)} %get-tuple-element.59, bf16[1024,1536]{1,0:T(8,128)(2,1)S(1)} %get-tuple-element.57.d_joined_hbm), kind=kOutput, calls=%fused_computation | convolution fusion | flops 6445596672 | bytes 13631488 | tf_op jit(solution)/shard_map/dot_general | solution.py:32
  420.7 0.0 copy-done
  420.7 100.7 %shard_map.232 = (f32[256,2048]{1,0:T(8,128)}, f32[64,6144]{1,0:T(8,128)}, f32[64,2048]{1,0:T(8,128)}, bf16[256,2048]{1,0:T(8,128)(2,1)}, f32[4,64]{1,0:T(4,128)}, /*index=5*/f32[1,192]{1,0:T(1,128)}) custom-call(bf16[1024,1536]{1,0:T(8,128)(2,1)} %copy-done, bf16[2048,1536]{1,0:T(8,128)(2,1)} %get-tuple-element.58.weight_hbm, ...), custom_call_target="tpu_custom_call" | custom-call | flops 6442450944 | bytes 209715200 | tf_op jit(solution)/shard_map/pallas_call | solution.py:953
  521.4 0.0 copy-start.1
  521.4 1.4 slice_bitcast_fusion
  522.8 2.4 convert_element_type.45
  525.2 2.3 copy.36
  527.5 0.0 copy-done.1
  527.5 1.3 copy.37
  528.9 0.0 copy-done.2
  528.9 1.1 copy.38
  530.0 0.0 copy-done.6
  530.0 0.6 copy.39
  530.6 0.0 copy-done.4
  530.6 0.8 copy.40
  531.4 0.0 copy-done.3
  531.4 1.1 copy.41
  (12 shorter events, 0.0 us)
Async XLA Ops:
  7.2 251.1 %all-gather.2.cloned.1.call-start = ((), (), s32[]{:S(2)}) async-start(), calls=%async_computation.2 | async-start | bytes 6488064 | tf_op jit(solution)/shard_map/all_gather | solution.py:1644
  198.0 10.9 %slice-start = ((s8[5767168]{0:T(1024)(128)(4,1)}), s8[1572864]{0:T(1024)(128)(4,1)S(1)}, s32[]{:S(2)}) async-start(s8[5767168]{0:T(1024)(128)(4,1)} %bitcast.56), calls=%async_computation.5 | async-start | bytes 3145728
  198.1 184.3 %reduce-scatter.3.cloned.1.call-start = ((), (), s32[]{:S(2)}) async-start(), calls=%async_computation.3 | async-start | bytes 6488064 | tf_op jit(solution)/shard_map/reduce_scatter | solution.py:1653
  198.3 10.6 %slice-start.1 = ((s8[5767168]{0:T(1024)(128)(4,1)}), s8[4194304]{0:T(1024)(128)(4,1)S(1)}, s32[]{:S(2)}) async-start(s8[5767168]{0:T(1024)(128)(4,1)} %bitcast.56), calls=%async_computation.6 | async-start | bytes 8388608
  198.3 10.6 %copy-start.12 = (bf16[1024,2048]{1,0:T(8,128)(2,1)S(1)}, bf16[1024,2048]{1,0:T(8,128)(2,1)}, u32[]{:S(2)}) copy-start(bf16[1024,2048]{1,0:T(8,128)(2,1)} %get-tuple-element.45.normed_hbm) | copy-start | bytes 12582916
  208.9 8.8 %copy-start.14 = (f32[1024,1408]{1,0:T(8,128)}, f32[1024,1408]{1,0:T(8,128)S(1)}, u32[]{:S(2)}) copy-start(f32[1024,1408]{1,0:T(8,128)S(1)} %fusion.2) | copy-start | bytes 17301508
  209.0 10.3 %copy-start.9 = (bf16[1024,2048]{1,0:T(8,128)(2,1)S(1)}, bf16[1024,2048]{1,0:T(8,128)(2,1)}, u32[]{:S(2)}) copy-start(bf16[1024,2048]{1,0:T(8,128)(2,1)} %get-tuple-element.48) | copy-start | bytes 12582916
  217.7 1.6 copy-start.11
  227.4 0.8 copy-start.5
  227.4 295.4 %reduce-scatter.5.cloned.1.call-start = ((), (), s32[]{:S(2)}) async-start(), calls=%async_computation.4 | async-start | bytes 6488064 | tf_op jit(solution)/shard_map/reduce_scatter | solution.py:1671
  258.3 15.4 %copy-start.13 = (bf16[1024,2048]{1,0:T(8,128)(2,1)S(1)}, bf16[1024,2048]{1,0:T(8,128)(2,1)}, u32[]{:S(2)}) copy-start(bf16[1024,2048]{1,0:T(8,128)(2,1)} %get-tuple-element.45.normed_hbm) | copy-start | bytes 12582916
  273.6 8.8 %copy-start.15 = (bf16[1024,1408]{1,0:T(8,128)(2,1)}, bf16[1024,1408]{1,0:T(8,128)(2,1)S(1)}, u32[]{:S(2)}) copy-start(bf16[1024,1408]{1,0:T(8,128)(2,1)S(1)} %get-tuple-element.75.gate_ref) | copy-start | bytes 8650756
  371.8 1.2 copy-start.8
  373.0 6.0 %copy-start.7 = (bf16[1024,2048]{1,0:T(8,128)(2,1)S(1)}, bf16[1024,2048]{1,0:T(8,128)(2,1)}, u32[]{:S(2)}) copy-start(bf16[1024,2048]{1,0:T(8,128)(2,1)} %get-tuple-element.52) | copy-start | bytes 12582916
  373.0 6.0 %copy-start.10 = (bf16[512,2048]{1,0:T(8,128)(2,1)S(1)}, bf16[512,2048]{1,0:T(8,128)(2,1)}, u32[]{:S(2)}) copy-start(bf16[512,2048]{1,0:T(8,128)(2,1)} %get-tuple-element.53) | copy-start | bytes 6291460
  408.5 12.2 %copy-start = (bf16[1024,1536]{1,0:T(8,128)(2,1)}, bf16[1024,1536]{1,0:T(8,128)(2,1)S(1)}, u32[]{:S(2)}) copy-start(bf16[1024,1536]{1,0:T(8,128)(2,1)S(1)} %get-tuple-element.57.d_joined_hbm) | copy-start | bytes 9437188
  521.4 6.1 %copy-start.1 = (f32[256,2048]{1,0:T(8,128)S(1)}, f32[256,2048]{1,0:T(8,128)}, u32[]{:S(2)}) copy-start(f32[256,2048]{1,0:T(8,128)} %get-tuple-element.66) | copy-start | bytes 6291460
  522.8 6.1 %copy-start.2 = (f32[64,6144]{1,0:T(8,128)S(1)}, f32[64,6144]{1,0:T(8,128)}, u32[]{:S(2)}) copy-start(f32[64,6144]{1,0:T(8,128)} %get-tuple-element.100) | copy-start | bytes 4718596
  527.5 2.5 copy-start.6
  527.5 3.0 copy-start.4
  527.5 3.8 copy-start.3
Sparse Core Ops, SparseCore 0:
  198.2 60.0 all-gather.1
  260.6 81.8 reduce-scatter.2
  371.9 69.1 reduce-scatter.4
